TPU v7x, 128 devices: a whole 4x4x4 slice. The times are simulated.
128 devices in a mesh: wide: 16 (over x_lo, y, core), narrow: 8 (over z, x_hi).
Axes of the slice: x: 4 (x_hi: 2, x_lo: 2; x = x_hi * 2 + x_lo), y: 4, z: 4, core: 2. Of those that a mesh axis runs over, the one named last changes fastest.
Arguments:
- tokens: bfloat16 [4096, 2048], P('wide', 'narrow'), may hold values from -6 to 6
- norm_gain: bfloat16 [2048], replicated, may hold values from 0.25 to 1.75
- router: bfloat16 [2048, 8], replicated, may hold values from -0.125 to 0.125
- routes: int32 [4096, 2], P('wide'), may hold values from 0 to 7, all different within a row
- kv_weight: bfloat16 [4096, 2048], P('narrow', 'wide'), may hold values from -0.125 to 0.125
- query_weight: bfloat16 [16384, 2048], P('narrow', 'wide'), may hold values from -0.125 to 0.125
- out_weight: bfloat16 [16384, 2048], P('narrow', 'wide'), may hold values from -0.09375 to 0.09375
- prefix_cache: bfloat16 [12288, 4096], P('wide', 'narrow'), may hold values from -225 to 225
- suffix_lengths: int32 [4], replicated, may hold values from 1 to 3328, 4096 in all
- prefix_lengths: int32 [4], replicated, may hold values from 1 to 6144, 12288 in all
Outputs:
- mixed: bfloat16 [4096, 2048], P('wide', 'narrow')
Inputs may be any that keep to these rules, and one draw needn't show every extreme that they name: `routes`: each token names 2 different experts. `suffix_lengths`: they sum to 4096. `prefix_lengths`: they sum to 12288.
All inputs are finite; a program needn't handle non-finite values.
Results may differ from a plain program's by a relative error of at most 0.012.
The roundings to bfloat16 on the way count: a program that leaves them out, or rounds other values in their place, can miss the bound.
Values may be sent and summed in bfloat16 or wider, within the bound.
No kernel may reach another device: no remote copies, remote signals or barrier semaphores. Data moves between devices by JAX's collectives and lax.ppermute only.
A program may use at most 320 MiB of HBM per device.

v0:
```python
import math

import jax
import jax.numpy as jnp
from jax import lax
from jax.sharding import PartitionSpec as P

H = 128
E = 8


eps = 1e-06
floor_value = -1e30


def tenant_of(positions, lengths):
    bounds = jnp.cumsum(lengths)
    return jnp.sum((positions[:, None] >= bounds[None, :]).astype(jnp.int32), axis=1)


def attend(carried, queries, key_block, value_block, allowed, scaling):
    highest, totals, summed = carried
    scores = (
        jnp.einsum("hrd,nhd->hrn", queries, key_block, preferred_element_type=jnp.float32) * scaling
    )
    scores = jnp.where(allowed[None, :, :], scores, -jnp.inf)
    new_highest = jnp.maximum(highest, jnp.max(scores, axis=2))
    weights = jnp.exp(scores - new_highest[:, :, None])
    factor = jnp.exp(highest - new_highest)
    totals = totals * factor + jnp.sum(weights, axis=2)
    summed = summed * factor[:, :, None] + jnp.einsum(
        "hrn,nhd->hrd",
        weights,
        value_block.astype(jnp.float32),
        precision=lax.Precision.HIGHEST,
        preferred_element_type=jnp.float32,
    )
    return (new_highest, totals, summed)


def over_blocks(
    carried, queries, cache_rows, row_tenant, row_index, key_tenant, key_index, scaling, causal
):
    length = cache_rows.shape[0]
    block_size = math.gcd(length, 512)
    steps_count = length // block_size
    cache_blocks = cache_rows.reshape((steps_count, block_size) + cache_rows.shape[1:])
    tenant_blocks = key_tenant.reshape(steps_count, block_size)
    index_blocks = key_index.reshape(steps_count, block_size)

    def advance(current, inputs):
        rows_here, tenant_here, index_here = inputs
        allowed = row_tenant[:, None] == tenant_here[None, :]
        if causal:
            allowed = allowed & (index_here[None, :] <= row_index[:, None])
        return (
            attend(
                current, queries, rows_here[:, :, 0, :], rows_here[:, :, 1, :], allowed, scaling
            ),
            None,
        )

    carried, unused = lax.scan(advance, carried, (cache_blocks, tenant_blocks, index_blocks))
    return carried


def on_device(
    tokens,
    norm_gain,
    router,
    routes,
    kv_weight,
    query_weight,
    out_weight,
    prefix_cache,
    suffix_lengths,
    prefix_lengths,
):
    whole = lax.all_gather(tokens, "narrow", axis=1, tiled=True)
    tok_rows = whole.shape[0]
    local_heads = kv_weight.shape[0] // (2 * H)
    slot_count = routes.shape[1]
    scaling = H ** (-0.5)
    floats = whole.astype(jnp.float32)
    normed = (
        floats
        * lax.rsqrt(jnp.mean(floats * floats, axis=1, keepdims=True) + eps)
        * norm_gain.astype(jnp.float32)
    ).astype(jnp.bfloat16)
    logits = jnp.dot(normed, router, preferred_element_type=jnp.float32)
    one_hot = routes[:, :, None] == jnp.arange(E, dtype=jnp.int32)[None, None, :]
    chosen = jnp.sum(jnp.where(one_hot, logits[:, None, :], 0.0), axis=2)
    gate_values = jax.nn.softmax(chosen, axis=1)
    choose = one_hot.astype(jnp.bfloat16)
    kv_part = lax.dot_general(
        normed,
        lax.all_gather(kv_weight, "wide", axis=1, tiled=True),
        (((1,), (1,)), ((), ())),
        preferred_element_type=jnp.float32,
    )
    query_part = lax.dot_general(
        normed,
        lax.all_gather(query_weight, "wide", axis=1, tiled=True),
        (((1,), (1,)), ((), ())),
        preferred_element_type=jnp.float32,
    )
    kv_local = kv_part.astype(jnp.bfloat16).reshape(tok_rows, local_heads, 2, H)
    query_all = query_part.astype(jnp.bfloat16).reshape(tok_rows, local_heads, E, H)
    selected = jnp.einsum(
        "tje,thed->htjd", choose, query_all, preferred_element_type=jnp.float32
    ).astype(jnp.bfloat16)
    row_count = tok_rows * slot_count
    queries = selected.reshape(local_heads, row_count, H)
    first_token = lax.axis_index("wide") * tok_rows
    token_index = first_token + jnp.arange(tok_rows, dtype=jnp.int32)
    row_index = jnp.repeat(token_index, slot_count)
    row_tenant = tenant_of(row_index, suffix_lengths)
    start_carry = (
        jnp.full((local_heads, row_count), floor_value, jnp.float32),
        jnp.zeros((local_heads, row_count), jnp.float32),
        jnp.zeros((local_heads, row_count, H), jnp.float32),
    )
    shard_piece = lax.all_gather(prefix_cache, "wide", axis=0, tiled=True)
    piece_rows = shard_piece.shape[0]
    slot_index = jnp.arange(piece_rows, dtype=jnp.int32)
    slot_tenant = tenant_of(slot_index, prefix_lengths)
    cache_rows = shard_piece.reshape(piece_rows, local_heads, 2, H)
    carried = over_blocks(
        start_carry,
        queries,
        cache_rows,
        row_tenant,
        row_index,
        slot_tenant,
        slot_index,
        scaling,
        False,
    )
    shard_piece = lax.all_gather(kv_local, "wide", axis=0, tiled=True)
    piece_rows = shard_piece.shape[0]
    key_index = jnp.arange(piece_rows, dtype=jnp.int32)
    key_tenant = tenant_of(key_index, suffix_lengths)
    carried = over_blocks(
        carried, queries, shard_piece, row_tenant, row_index, key_tenant, key_index, scaling, True
    )
    highest, totals, summed = carried
    attended = (summed / totals[:, :, None]).reshape(local_heads, tok_rows, slot_count, H)
    weighted = (attended * gate_values[None, :, :, None]).astype(jnp.bfloat16)
    padded = (
        jnp.einsum("tje,htjd->thed", choose, weighted, preferred_element_type=jnp.float32)
        .astype(jnp.bfloat16)
        .reshape(tok_rows, local_heads * E * H)
    )
    partial_out = jnp.dot(
        padded,
        lax.all_gather(out_weight, "wide", axis=1, tiled=True),
        preferred_element_type=jnp.float32,
    )
    return lax.psum_scatter(partial_out, "narrow", scatter_dimension=1, tiled=True).astype(
        jnp.bfloat16
    )


def solution(mesh):
    placed = (
        P("wide", "narrow"),
        P(),
        P(),
        P("wide", None),
        P("narrow", "wide"),
        P("narrow", "wide"),
        P("narrow", "wide"),
        P("wide", "narrow"),
        P(),
        P(),
    )
    return jax.shard_map(
        on_device, mesh=mesh, in_specs=placed, out_specs=P("wide", "narrow"), check_vma=False
    )
```

profile of v0, /device:TPU:3, one launch (start us, length us, event | category | flops | bytes accessed | tf_op | source)
XLA Modules:
  0.0 495.6 jit_solution(3596680702898717761)
XLA Ops:
  10.1 45.6 %all-gather.9.cloned.1.call-done = bf16[256,2048]{1,0:T(8,128)(2,1)} async-done(((bf16[256,256]{1,0:T(8,128)(2,1)}), bf16[256,2048]{1,0:T(8,128)(2,1)}) %all-gather.9.cloned.1.call-update) | async-done | bytes 1048592 | tf_op jit(solution)/shard_map/all_gather | solution.py:79
  57.2 37.3 %all-gather.13.cloned.1.call-done = bf16[512,2048]{1,0:T(8,128)(2,1)} async-done(((bf16[512,128]{1,0:T(8,128)(2,1)}), bf16[512,2048]{1,0:T(8,128)(2,1)}) %all-gather.13.cloned.1.call-update) | async-done | bytes 2097168 | tf_op jit(solution)/shard_map/all_gather | solution.py:97
  94.5 2.7 convolution_convert_fusion.2
  102.0 56.0 %all-gather.11.cloned.1.call-done = bf16[2048,2048]{1,0:T(8,128)(2,1)} async-done(((bf16[2048,128]{1,0:T(8,128)(2,1)}), bf16[2048,2048]{1,0:T(8,128)(2,1)}) %all-gather.11.cloned.1.call-update) | async-done | bytes 8388624 | tf_op jit(solution)/shard_map/all_gather | solution.py:103
  158.0 5.8 %fusion.15 = bf16[32,8,16,128]{3,1,2,0:T(8,128)(2,1)S(1)} fusion(bf16[2048,2048]{1,0:T(8,128)(2,1)} %all-gather.11.cloned.1.call-done, bf16[256,2048]{1,0:T(8,128)(2,1)S(1)} %copy-done.1, f32[2048]{0:T(1024)S(1)} %convert_element_type.48, f32[256]{0:T(256)S(1)} %add_rsqrt_fusion), kind=kOutput, calls=%fused_computation.41 | convolution fusion | flops 2150105088 | bytes 10494976 | tf_op jit(solution)/shard_map/dot_general | solution.py:101
  165.5 64.8 %all-gather.7.cloned.1.call-done = bf16[12288,512]{1,0:T(8,128)(2,1)} async-done(((bf16[768,512]{1,0:T(8,128)(2,1)}), bf16[12288,512]{1,0:T(8,128)(2,1)}) %all-gather.7.cloned.1.call-update) | async-done | bytes 12582928 | tf_op jit(solution)/shard_map/all_gather | solution.py:123
  230.3 18.2 %reshape.233 = bf16[24,512,2,2,128]{4,3,2,1,0:T(2,128)(2,1)} reshape(bf16[12288,512]{1,0:T(8,128)(2,1)} %all-gather.7.cloned.1.call-done) | data formatting | bytes 25165824 | tf_op jit(solution)/shard_map/reshape;reshape | solution.py:47
  248.5 112.6 %while.31 = (s32[]{:T(128)}, f32[2,512]{1,0:T(2,128)S(1)}, f32[2,512]{1,0:T(2,128)S(1)}, f32[2,512,128]{2,1,0:T(8,128)S(1)}, s32[512]{0:T(512)S(1)}, /*index=5*/...) while((s32[]{:T(128)}, f32[2,512]{1,0:T(2,128)S(1)}, ...), condition=%wide.region_8.9_spmd.clone, body=%wide.region_5.8_spmd.clone.sunk | while | flops 943330304 | bytes 11870357 | solution.py:63
  251.2 2.0 fusion.61
  255.9 2.0 fusion.61
  260.6 2.0 fusion.61
  265.3 2.0 fusion.61
  270.0 2.0 fusion.61
  274.7 2.0 fusion.61
  279.4 2.0 fusion.61
  284.1 2.0 fusion.61
  288.7 2.0 fusion.61
  293.4 2.0 fusion.61
  298.2 2.0 fusion.61
  302.9 2.0 fusion.61
  307.6 2.0 fusion.61
  312.3 2.0 fusion.61
  317.0 2.0 fusion.61
  321.7 2.0 fusion.61
  326.4 2.0 fusion.61
  331.1 2.0 fusion.61
  340.4 2.0 fusion.61
  349.8 2.0 fusion.61
  359.2 2.0 fusion.61
  361.2 43.5 %while.30 = (s32[]{:T(128)}, f32[2,512]{1,0:T(2,128)S(1)}, f32[2,512]{1,0:T(2,128)S(1)}, f32[2,512,128]{2,1,0:T(8,128)S(1)}, s32[512]{0:T(512)S(1)}, /*index=5*/...) while((s32[]{:T(128)}, f32[2,512]{1,0:T(2,128)S(1)}, ...), condition=%wide.region_13.14_spmd.clone, body=%wide.region_10.13_spmd.clone.sunk | while | flops 943720448 | bytes 9789041 | solution.py:63
  406.3 7.1 %fusion.17 = f32[256,2048]{1,0:T(8,128)} fusion(bf16[2048,2048]{1,0:T(8,128)(2,1)} %all-gather.17.cloned.1.call-done, bf16[32,8,16,128]{3,2,1,0:T(8,128)(2,1)S(1)} %bitcast.97), kind=kOutput, calls=%fused_computation.45 | convolution fusion | flops 2147483648 | bytes 11534336 | tf_op jit(solution)/shard_map/dot_general | solution.py:154
  413.4 73.7 %reduce-scatter.2.cloned.1.call-done = f32[256,256]{1,0:T(8,128)} async-done(((f32[256,2048]{1,0:T(8,128)}), f32[256,256]{1,0:T(8,128)}) %reduce-scatter.2.cloned.1.call-update) | async-done | bytes 262160 | tf_op jit(solution)/shard_map/reduce_scatter | solution.py:159
  (412 shorter events, 126.8 us)
Async XLA Ops:
  6.5 93.5 %copy-start = (bf16[2048,8]{0,1:T(8,128)(2,1)S(1)}, bf16[2048,8]{0,1:T(8,128)(2,1)}, u32[]{:S(2)}) copy-start(bf16[2048,8]{0,1:T(8,128)(2,1)} %param.16) | copy-start | bytes 98308
  6.5 49.1 %all-gather.9.cloned.1.call-start = ((), (), s32[]{:S(2)}) async-start(), calls=%async_computation.2 | async-start | bytes 1179648 | tf_op jit(solution)/shard_map/all_gather | solution.py:79
  7.3 87.3 %all-gather.13.cloned.1.call-start = ((), (), s32[]{:S(2)}) async-start(), calls=%async_computation.4 | async-start | bytes 2228224 | tf_op jit(solution)/shard_map/all_gather | solution.py:97
  8.0 150.0 %all-gather.11.cloned.1.call-start = ((), (), s32[]{:S(2)}) async-start(), calls=%async_computation.3 | async-start | bytes 8912896 | tf_op jit(solution)/shard_map/all_gather | solution.py:103
  8.7 221.5 %all-gather.7.cloned.1.call-start = ((), (), s32[]{:S(2)}) async-start(), calls=%async_computation.1 | async-start | bytes 13369344 | tf_op jit(solution)/shard_map/all_gather | solution.py:123
  9.3 351.9 %all-gather.15.cloned.1.call-start = ((), (), s32[]{:S(2)}) async-start(), calls=%async_computation.5 | async-start | bytes 4456448 | tf_op jit(solution)/shard_map/all_gather | solution.py:139
  57.2 41.6 %copy-start.3 = (s32[256,2]{0,1:T(2,128)S(1)}, s32[256,2]{0,1:T(2,128)}, u32[]{:S(2)}) copy-start(s32[256,2]{0,1:T(2,128)} %param.17) | copy-start | bytes 6148
  57.2 41.7 %copy-start.4 = (s32[4]{0:T(128)S(1)}, s32[4]{0:T(128)}, u32[]{:S(2)}) copy-start(s32[4]{0:T(128)} %param.22) | copy-start | bytes 52
  97.2 2.3 copy-start.5
  97.2 2.8 copy-start.1
  98.1 308.2 %all-gather.17.cloned.1.call-start = ((), (), s32[]{:S(2)}) async-start(), calls=%async_computation.6 | async-start | bytes 8912896 | tf_op jit(solution)/shard_map/all_gather | solution.py:156
  98.6 388.5 %reduce-scatter.2.cloned.1.call-start = ((), (), s32[]{:S(2)}) async-start(), calls=%async_computation.7 | async-start | bytes 2359296 | tf_op jit(solution)/shard_map/reduce_scatter | solution.py:159
  253.2 1.8 copy-start.2
  257.9 1.8 copy-start.2
  262.6 1.8 copy-start.2
  267.3 1.8 copy-start.2
  272.0 1.8 copy-start.2
  276.7 1.8 copy-start.2
  281.3 1.8 copy-start.2
  286.0 1.8 copy-start.2
  290.7 1.8 copy-start.2
  295.4 1.8 copy-start.2
  300.2 1.8 copy-start.2
  304.8 1.8 copy-start.2
  309.5 1.9 copy-start.2
  314.3 1.8 copy-start.2
  319.0 1.8 copy-start.2
  323.7 1.8 copy-start.2
  328.4 1.8 copy-start.2
  333.0 1.8 copy-start.2
  347.1 1.8 copy-start.2
  351.8 1.8 copy-start.2
  (4 other events, 7.1 us)
Sparse Core Ops, SparseCore 0:
  9.5 46.0 all-gather.8
  57.3 37.2 all-gather.12
  96.2 61.8 all-gather.10
  159.6 70.6 all-gather.6
  231.8 38.1 all-gather.14
  271.4 61.6 all-gather.16
  413.5 73.5 reduce-scatter.1
where the time goes:
time: 500 us; the launch traced here: 496 us
  waiting for transfers between devices  281 us (56%)
  matrix products  106 us (21%)
  local copies, waits for them, and re-layouts  68.4 us (14%)
  other arithmetic  24.2 us (5%)
  between operations  13.7 us (3%)
    reduce_scatter x1, waiting for transfers between devices, on_device(): lax.psum_scatter(partial_out, 'narrow', scatter_dimension=1, tiled=True)  73.7 us
    all_gather x1, waiting for transfers between devices, on_device(): shard_piece = lax.all_gather(prefix_cache, 'wide', axis=0, tiled=True)  64.8 us
    dot_general x32, matrix products, attend(): jnp.einsum('hrn,nhd->hrd', weights, value_block.astype(jnp.float32), prec...  62.4 us
    all_gather x1, waiting for transfers between devices, on_device(): lax.all_gather(query_weight, 'wide', axis=1, tiled=True)  56 us
    all_gather x1, waiting for transfers between devices, on_device(): whole = lax.all_gather(tokens, 'narrow', axis=1, tiled=True)  45.6 us
    all_gather x1, waiting for transfers between devices, on_device(): lax.all_gather(kv_weight, 'wide', axis=1, tiled=True)  37.3 us
    dynamic_slice x80, local copies, waits for them, and re-layouts, over_blocks(): lax.scan(advance, carried, (cache_blocks, tenant_blocks, index_blocks))  37.1 us
    dot_general x32, matrix products, attend(): jnp.einsum('hrd,nhd->hrn', queries, key_block, preferred_element_type=jnp...  25.4 us
  transfers between devices with their start and end apart: 7, of which 5 were waited for; matrix products, arithmetic and copies ran while one was open for 38% of the time, Pallas kernels for 0%

commit v1 on v0

v1 whole, which is shorter than its diff:
```python
import functools
import math

import jax
import jax.numpy as jnp
from jax import lax
from jax.experimental import pallas as pl
from jax.experimental.pallas import tpu as pltpu
from jax.sharding import Mesh
from jax.sharding import PartitionSpec as P

H = 128
E = 8
EPS = 1e-06
FLOOR = -1e30
AXES = ("xl", "y", "c", "z", "xh")
SIZES = (2, 4, 2, 4, 2)
WIDE = ("xl", "y", "c")
NARROW = ("z", "xh")
BF16 = jnp.bfloat16
F32 = jnp.float32
SCALE2 = H ** (-0.5) * math.log2(math.e)
CK = 512
R = 512
CHUNKS = 8
TILES = 8
DUMMY = 8
UNROLL = 4

SMEM = pl.BlockSpec(memory_space=pltpu.SMEM)
VMEM = pl.BlockSpec(memory_space=pltpu.VMEM)
HBM = pl.BlockSpec(memory_space=pltpu.HBM)


def along_y(x, k):
    return lax.ppermute(x, "y", [(i, (i + k) % 4) for i in range(4)])


def along_z(x, k):
    return lax.ppermute(x, "z", [(i, (i + k) % 4) for i in range(4)])


def across_x(x):
    return lax.ppermute(x, "xl", [(0, 1), (1, 0)])


def across_far(x):
    return lax.ppermute(x, "xh", [(0, 1), (1, 0)])


def across_core(x):
    return lax.ppermute(x, "c", [(0, 1), (1, 0)])


def tie(a, b):
    return lax.optimization_barrier((a, b))


def gather_chips(w):
    a = across_x(w)
    yp, ym = along_y(w, 1), along_y(w, 3)
    ap, am = along_y(a, 1), along_y(a, 3)
    far0, far1 = along_y(yp[0], 1), along_y(ym[1], 3)
    afar0, afar1 = across_x(far0), across_x(far1)
    return [w, a, yp, ym, ap, am, far0, far1, afar0, afar1]


def chip_order():
    xl, y = lax.axis_index("xl"), lax.axis_index("y")
    pairs = [
        (xl, y),
        (1 - xl, y),
        (xl, y + 3),
        (xl, y + 1),
        (1 - xl, y + 3),
        (1 - xl, y + 1),
        (xl, y + 2),
        (1 - xl, y + 2),
    ]
    return [a * 4 + lax.rem(b, 4) for a, b in pairs]


def nt_dot(a, b):
    return lax.dot_general(a, b, (((1,), (1,)), ((), ())), preferred_element_type=F32)


def run(copies):
    for c in copies:
        c.start()
    for c in copies:
        c.wait()


def norm_kernel(idx, gain, b0, b1, b2, b3, normed, held, sem):
    refs = (b0, b1, b2, b3)
    run([pltpu.make_async_copy(r, held.at[i], sem.at[i]) for i, r in enumerate(refs)])
    total = jnp.zeros((256, 1), F32)
    for k in range(8):
        v = held[k // 2, k % 2].astype(F32)
        total = total + jnp.sum(v * v, axis=1, keepdims=True)
    scale = lax.rsqrt(total * (1.0 / 2048) + EPS)
    for k in range(8):
        src = idx[k]
        v = held[k // 2, k % 2].astype(F32) * scale * gain[src].astype(F32)
        normed[src, 0] = v[:, :H].astype(BF16)
        normed[src, 1] = v[:, H:].astype(BF16)


def normalise(idx, gain, blocks):
    return pl.pallas_call(
        norm_kernel,
        out_shape=jax.ShapeDtypeStruct((8, 2, 256, H), BF16),
        in_specs=[SMEM, VMEM] + [HBM] * 4,
        out_specs=VMEM,
        scratch_shapes=[pltpu.VMEM((4, 2, 256, 256), BF16), pltpu.SemaphoreType.DMA((4,))],
        compiler_params=pltpu.CompilerParams(vmem_limit_bytes=8 << 20),
        cost_estimate=pl.CostEstimate(flops=1 << 24, bytes_accessed=2 << 20, transcendentals=0),
        name="normalise",
    )(idx, gain, *blocks)


def project_kernel(idx, routes, router, own, other, *refs):
    blocks = refs[:10]
    q_out, kv_out, gates, xs, held, sel, sem = refs[10:]
    core = idx[8]
    rows_of = [pl.multiple_of(core * 256, 256), pl.multiple_of((1 - core) * 256, 256)]
    x_copies = [
        pltpu.make_async_copy(r, xs.at[:, :, pl.ds(at, 256)], sem.at[5 + i])
        for i, (r, at) in enumerate(zip((own, other), rows_of))
    ]

    def tile_copies(r):
        at = pl.ds(r * 256, 256)
        copies = []
        for k in range(10):
            if k < 6:
                src, dst = blocks[k].at[:, at], held.at[k, :, at]
            else:
                src, dst = blocks[k].at[at], held.at[6 + (k - 6) // 2, (k - 6) % 2, at]
            copies.append(pltpu.make_async_copy(src, dst, sem.at[r]))
        return copies

    tiles = [tile_copies(r) for r in range(5)]
    for c in x_copies:
        c.start()
    for group in tiles:
        for c in group:
            c.start()
    for c in x_copies:
        c.wait()
    logits = jnp.zeros((512, E), F32)
    for nb in range(8):
        for side in range(2):
            logits += jnp.dot(xs[nb, side], router[nb, side], preferred_element_type=F32)
    lane = lax.broadcasted_iota(jnp.int32, (512, E), 1)
    chosen = [
        jnp.sum(jnp.where(routes[:, j : j + 1] == lane, logits, 0.0), axis=1, keepdims=True)
        for j in range(2)
    ]
    top = jnp.maximum(chosen[0], chosen[1])
    e0, e1 = jnp.exp(chosen[0] - top), jnp.exp(chosen[1] - top)
    gates[:, 0:1] = e0 / (e0 + e1)
    gates[:, 1:2] = e1 / (e0 + e1)

    for r in range(5):
        for c in tiles[r]:
            c.wait()
        acc = jnp.zeros((512, 256), F32)
        for i in range(8):
            nb = idx[i]
            x = jnp.concatenate([xs[nb, core], xs[nb, 1 - core]], axis=1)
            at = slice(r * 256, (r + 1) * 256)
            w = jnp.concatenate([held[i, 0, at], held[i, 1, at]], axis=1)
            acc += nt_dot(x, w)
        if r == 4:
            kv_out[...] = acc.astype(BF16)
            continue
        for j in range(2):
            value = jnp.zeros((512, H), F32) if r == 0 else sel[j]
            for e in range(2):
                hit = routes[:, j : j + 1] == 2 * r + e
                value = jnp.where(hit, acc[:, e * H : (e + 1) * H], value)
            if r < 3:
                sel[j] = value
            else:
                for half in range(2):
                    at = (half * 2 + j) * 256
                    q_out[at : at + 256] = value[half * 256 : (half + 1) * 256].astype(BF16)


def project(idx, routes, router, own, other, blocks):
    return pl.pallas_call(
        project_kernel,
        out_shape=(
            jax.ShapeDtypeStruct((1024, H), BF16),
            jax.ShapeDtypeStruct((512, 2 * H), BF16),
            jax.ShapeDtypeStruct((512, 2), F32),
        ),
        in_specs=[SMEM, VMEM, VMEM] + [HBM] * 12,
        out_specs=(VMEM, VMEM, VMEM),
        scratch_shapes=[
            pltpu.VMEM((8, 2, 512, H), BF16),
            pltpu.VMEM((8, 2, 1280, H), BF16),
            pltpu.VMEM((2, 512, H), F32),
            pltpu.SemaphoreType.DMA((7,)),
        ],
        compiler_params=pltpu.CompilerParams(vmem_limit_bytes=20 << 20),
        cost_estimate=pl.CostEstimate(flops=6 << 30, bytes_accessed=8 << 20, transcendentals=0),
        name="project",
    )(idx, routes, router, own, other, *blocks)


def attend_kernel(idx, ends_s, ends_p, q0, q1, q2, q3, cache0, cache1, kv0, kv1, *refs):
    outs = refs[:4]
    q, keep, limits, top, tot, acc, sa, sb, chunk_of, tile_of, sem = refs[4:]
    core = idx[0]
    copies = [
        pltpu.make_async_copy(r, q.at[pl.ds(1024 * b, 1024)], sem.at[b])
        for b, r in enumerate((q0, q1, q2, q3))
    ]
    for i, r in enumerate((cache0, cache1)):
        for side in range(2):
            at = pl.multiple_of(i * 1536 + 768 * (core if side == 0 else 1 - core), 256)
            copies.append(
                pltpu.make_async_copy(r.at[side], keep.at[pl.ds(at, 768)], sem.at[4 + 2 * i + side])
            )
    for i, r in enumerate((kv0, kv1)):
        copies.append(
            pltpu.make_async_copy(r, keep.at[pl.ds(3072 + 512 * i, 512)], sem.at[8 + i])
        )
    for c in copies:
        c.start()

    se, pe = [ends_s[0]], [ends_p[0]]
    for k in range(1, 4):
        se.append(se[-1] + ends_s[k])
        pe.append(pe[-1] + ends_p[k])

    def allowed_of(token):
        lo, hi, own = 0 * token, 0 * token + pe[0], 0 * token
        for k in range(3):
            later = token >= se[k]
            lo = jnp.where(later, pe[k], lo)
            hi = jnp.where(later, pe[k + 1], hi)
            own = jnp.where(later, se[k], own)
        return lo, hi, own

    for t in range(TILES):
        first = idx[1 + t // 2] + (t % 2) * 256
        token = first + lax.rem(lax.broadcasted_iota(jnp.int32, (1, R), 1), 256)
        lo, hi, own = allowed_of(token)
        limits[t, 0:1] = lo
        limits[t, 1:2] = hi
        limits[t, 2:3] = own
        limits[t, 3:4] = token + 1
    limits[DUMMY] = jnp.zeros((4, R), jnp.int32)
    top[...] = jnp.full(top.shape, FLOOR, F32)
    tot[...] = jnp.zeros(tot.shape, F32)
    acc[...] = jnp.zeros(acc.shape, F32)

    def base_of(i):
        slot = jnp.where(i < 3, idx[5] + i * CK, idx[6] + (i - 3) * CK)
        return jnp.where(i < 6, slot, jnp.where(i == 6, idx[7], idx[8]))

    def collect(want_full, start):
        def visit(n, count):
            i, t = n // TILES, lax.rem(n, TILES)
            base = base_of(i)
            first = idx[1 + t // 2] + lax.rem(t, 2) * 256
            last = first + 255
            lo_a, hi_a, own_a = allowed_of(first)
            lo_b, hi_b, own_b = allowed_of(last)
            pre = i < 6
            lo_first, lo_last = jnp.where(pre, lo_a, own_a), jnp.where(pre, lo_b, own_b)
            hi_first, hi_last = jnp.where(pre, hi_a, first + 1), jnp.where(pre, hi_b, last + 1)
            some = (base + CK > lo_first) & (base < hi_last)
            full = (base >= lo_last) & (base + CK <= hi_first)
            hit = full if want_full else (some & jnp.logical_not(full))

            @pl.when(hit)
            def _():
                chunk_of[count] = i
                tile_of[count] = t

            return count + hit.astype(jnp.int32)

        count = lax.fori_loop(0, CHUNKS * TILES, visit, start)
        rounds = (count + UNROLL - 1) // UNROLL
        for k in range(UNROLL):
            chunk_of[count + k] = 0
            tile_of[count + k] = DUMMY
        return rounds

    full_rounds = collect(True, 0)
    all_rounds = collect(False, full_rounds * UNROLL)
    for c in copies:
        c.wait()
    q[4096:4608] = jnp.zeros((R, H), BF16)

    def scores(n, out):
        keys = keep[pl.ds(pl.multiple_of(chunk_of[n] * CK, CK), CK), :H]
        out[...] = nt_dot(keys, q[pl.ds(pl.multiple_of(tile_of[n] * R, R), R), :])

    def consume(n, s_ref, masked):
        i, t = chunk_of[n], tile_of[n]
        s = s_ref[...]
        if masked:
            pos = base_of(i) + lax.broadcasted_iota(jnp.int32, (CK, R), 0)
            kind = jnp.where(i < 6, 0, 2)
            lo, hi = limits[t, pl.ds(kind, 1)], limits[t, pl.ds(kind + 1, 1)]
            s = jnp.where((pos >= lo) & (pos < hi), s, -jnp.inf)
        old = top[t]
        new = jnp.maximum(old, jnp.max(s, axis=0, keepdims=True))
        p = jnp.exp2(s * SCALE2 - new * SCALE2)
        factor = jnp.exp2((old - new) * SCALE2)
        top[t] = new
        tot[t] = tot[t] * factor + jnp.sum(p, axis=0, keepdims=True)
        values = keep[pl.ds(pl.multiple_of(i * CK, CK), CK), H:]
        acc[t] = acc[t] * factor + lax.dot_general(
            values, p.astype(BF16), (((0,), (0,)), ((), ())), preferred_element_type=F32
        )

    def rounds(masked):
        def body(n, _):
            for k in range(UNROLL):
                cur, nxt = (sa, sb) if k % 2 == 0 else (sb, sa)
                scores(n * UNROLL + k + 1, nxt)
                consume(n * UNROLL + k, cur, masked)
            return 0

        return body

    chunk_of[all_rounds * UNROLL] = 0
    tile_of[all_rounds * UNROLL] = DUMMY
    scores(0, sa)
    lax.fori_loop(0, full_rounds, rounds(False), 0)
    lax.fori_loop(full_rounds, all_rounds, rounds(True), 0)

    for t in range(TILES):
        total = tot[t]
        safe = jnp.where(total > 0.0, total, 1.0)
        cols = slice((t % 2) * R, (t % 2 + 1) * R)
        out = outs[t // 2]
        out[0:H, cols] = (acc[t] / safe).astype(BF16)
        lse = jnp.where(total > 0.0, top[t] * SCALE2 + jnp.log2(safe), FLOOR)
        high = lse.astype(BF16).astype(F32)
        mid = (lse - high).astype(BF16).astype(F32)
        low = lse - high - mid
        row = lax.broadcasted_iota(jnp.int32, (16, R), 0)
        packed = jnp.where(row == 0, high, jnp.where(row == 1, mid, jnp.where(row == 2, low, 0.0)))
        out[H : H + 16, cols] = packed.astype(BF16)


def attend(idx, suffix_lengths, prefix_lengths, qs, caches, kvs):
    return pl.pallas_call(
        attend_kernel,
        out_shape=tuple(jax.ShapeDtypeStruct((H + 16, 1024), BF16) for _ in range(4)),
        in_specs=[SMEM] * 3 + [HBM] * 8,
        out_specs=tuple([VMEM] * 4),
        scratch_shapes=[
            pltpu.VMEM((9 * R, H), BF16),
            pltpu.VMEM((CHUNKS * CK, 2 * H), BF16),
            pltpu.VMEM((TILES + 1, 4, R), jnp.int32),
            pltpu.VMEM((TILES + 1, 1, R), F32),
            pltpu.VMEM((TILES + 1, 1, R), F32),
            pltpu.VMEM((TILES + 1, H, R), F32),
            pltpu.VMEM((CK, R), F32),
            pltpu.VMEM((CK, R), F32),
            pltpu.SMEM((CHUNKS * TILES + 4 * UNROLL,), jnp.int32),
            pltpu.SMEM((CHUNKS * TILES + 4 * UNROLL,), jnp.int32),
            pltpu.SemaphoreType.DMA((10,)),
        ],
        compiler_params=pltpu.CompilerParams(vmem_limit_bytes=20 << 20),
        cost_estimate=pl.CostEstimate(
            flops=12 << 30, bytes_accessed=6 << 20, transcendentals=10 << 20
        ),
        name="attend",
    )(idx, suffix_lengths, prefix_lengths, *qs, *caches, *kvs)


def combine_kernel(gates, p0, p1, p2, p3, out):
    parts = (p0, p1, p2, p3)
    lses = []
    for p in parts:
        rows = p[H : H + 16].astype(F32)
        lses.append(rows[0:1] + rows[1:2] + rows[2:3])
    high = jnp.maximum(jnp.maximum(lses[0], lses[1]), jnp.maximum(lses[2], lses[3]))
    share = [jnp.exp2(v - high) for v in lses]
    norm = gates[...] / (share[0] + share[1] + share[2] + share[3])
    for at in range(0, 1024, 256):
        cols = slice(at, at + 256)
        total = jnp.zeros((H, 256), F32)
        for p, s in zip(parts, share):
            total += p[0:H, cols].astype(F32) * s[:, cols]
        out[cols] = jnp.transpose(total * norm[:, cols]).astype(BF16)


def combine(gates, parts):
    return pl.pallas_call(
        combine_kernel,
        out_shape=jax.ShapeDtypeStruct((1024, H), BF16),
        in_specs=[VMEM] * 5,
        out_specs=VMEM,
        compiler_params=pltpu.CompilerParams(vmem_limit_bytes=8 << 20),
        cost_estimate=pl.CostEstimate(flops=1 << 22, bytes_accessed=2 << 20, transcendentals=0),
        name="combine",
    )(gates, *parts)


def out_kernel(idx, routes, own, other, *refs):
    blocks = refs[:10]
    outs = refs[10:14]
    held, padded, sem = refs[14:]
    core = idx[8]
    copies = []
    for k in range(10):
        if k < 6:
            src, dst = blocks[k], held.at[idx[k]]
        else:
            src, dst = blocks[k], held.at[idx[6 + (k - 6) // 2], (k - 6) % 2]
        copies.append(pltpu.make_async_copy(src, dst, sem.at[k]))
    for c in copies:
        c.start()
    for side, source in enumerate((own, other)):
        for half in range(2):
            for e in range(E):
                value = jnp.zeros((256, H), F32)
                for j in range(2):
                    hit = routes[half * 256 : (half + 1) * 256, j : j + 1] == e
                    at = (half * 2 + j) * 256
                    value = jnp.where(hit, source[at : at + 256].astype(F32), value)
                padded[side, half * 256 : (half + 1) * 256, e * H : (e + 1) * H] = value.astype(
                    BF16
                )
    for c in copies:
        c.wait()
    for dz in range(4):
        value = jnp.zeros((512, 256), F32)
        for side in range(2):
            head = core if side == 0 else 1 - core
            w = jnp.concatenate(
                [held[idx[9 + 2 * dz], head], held[idx[10 + 2 * dz], head]], axis=1
            )
            value += jnp.dot(padded[side], w, preferred_element_type=F32)
        for s in range(2):
            outs[dz][s] = value[:, s * H : (s + 1) * H].astype(outs[dz].dtype)


def project_out(idx, routes, own, other, blocks):
    return pl.pallas_call(
        out_kernel,
        out_shape=(jax.ShapeDtypeStruct((2, 512, H), F32),)
        + tuple(jax.ShapeDtypeStruct((2, 512, H), BF16) for _ in range(3)),
        in_specs=[SMEM, VMEM, VMEM, VMEM] + [HBM] * 10,
        out_specs=tuple([VMEM] * 4),
        scratch_shapes=[
            pltpu.VMEM((8, 2, 1024, H), BF16),
            pltpu.VMEM((2, 512, 1024), BF16),
            pltpu.SemaphoreType.DMA((10,)),
        ],
        compiler_params=pltpu.CompilerParams(vmem_limit_bytes=20 << 20),
        cost_estimate=pl.CostEstimate(flops=4 << 30, bytes_accessed=6 << 20, transcendentals=0),
        name="project_out",
    )(idx, routes, own, other, *blocks)


def on_device(
    tokens,
    norm_gain,
    router,
    routes,
    kv_weight,
    query_weight,
    out_weight,
    prefix_cache,
    suffix_lengths,
    prefix_lengths,
):
    xl, y, c = (lax.axis_index(a) for a in WIDE)
    z, xh = (lax.axis_index(a) for a in NARROW)
    first_core = c == 0
    chips = chip_order()

    def table(values):
        return jnp.stack([jnp.asarray(v, jnp.int32) for v in values])

    def head_rows(w, h):
        rows = w.shape[0] // 2
        return lax.dynamic_slice_in_dim(w, h * rows, rows, 0)

    def weights_of(h):
        return jnp.concatenate([head_rows(query_weight, h), head_rows(kv_weight, h)], axis=0)

    pair = jnp.stack([tokens, across_far(tokens)])
    blocks = [pair] + [along_z(pair, k) for k in (1, 2, 3)]
    w = jnp.stack([weights_of(c), across_core(weights_of(1 - c))])
    gathered = gather_chips(w)
    other_routes = across_core(routes)
    both_routes = jnp.where(
        first_core,
        jnp.concatenate([routes, other_routes]),
        jnp.concatenate([other_routes, routes]),
    )

    def cache_of(h):
        return lax.dynamic_slice_in_dim(prefix_cache, h * 2 * H, 2 * H, 1)

    cache = jnp.stack([cache_of(c), across_core(cache_of(1 - c))])
    cache_out, gathered[1] = tie(cache, gathered[1])
    caches = [cache, across_x(cache_out)]

    token_src = [lax.rem(z + 4 - dz, 4) * 2 + (xh ^ s) for dz in range(4) for s in range(2)]
    normed = normalise(table(token_src), norm_gain.reshape(8, 1, 256), blocks)
    q, kv, gates = project(
        table(chips + [c]),
        both_routes,
        router.reshape(8, 2, H, E),
        normed,
        across_core(normed),
        gathered,
    )
    out_weight, q = tie(out_weight, q)
    out_blocks = gather_chips(out_weight.reshape(2, 1024, H))

    kvs = [kv, across_x(kv)]
    qs = [q] + [along_y(q, k) for k in (1, 2, 3)]
    firsts = [(xl * 4 + lax.rem(y + 4 - k, 4)) * 512 for k in range(4)]
    mine, partner = xl * 4 + y, (1 - xl) * 4 + y
    at = [c] + firsts + [mine * 1536, partner * 1536, mine * 512, partner * 512]
    parts = list(attend(table(at), suffix_lengths, prefix_lengths, qs, caches, kvs))
    for k in range(1, 4):
        parts[k] = along_y(parts[k], 4 - k)
    gate_row = gates.reshape(2, 256, 2).transpose(0, 2, 1).reshape(1, 1024)
    attended = combine(gate_row, parts)

    dests = [lax.rem(z + dz, 4) * 2 + (xh ^ s) for dz in range(4) for s in range(2)]
    sums = project_out(
        table(chips + [c] + dests), both_routes, attended, across_core(attended), out_blocks
    )
    total = sums[0]
    for k in (1, 2, 3):
        total = total + along_z(sums[k], k).astype(F32)
    total = total[0] + across_far(total[1].astype(BF16)).astype(F32)
    here = lax.dynamic_slice_in_dim(total, c * 256, 256, 0).astype(BF16)
    there = lax.dynamic_slice_in_dim(total, (1 - c) * 256, 256, 0).astype(BF16)
    there = across_core(there)
    return jnp.where(
        first_core,
        jnp.concatenate([here, there], axis=1),
        jnp.concatenate([there, here], axis=1),
    )


def solution(mesh):
    fine = Mesh(mesh.devices.reshape(SIZES), AXES)
    placed = (
        P(WIDE, NARROW),
        P(),
        P(),
        P(WIDE, None),
        P(NARROW, WIDE),
        P(NARROW, WIDE),
        P(NARROW, WIDE),
        P(WIDE, NARROW),
        P(),
        P(),
    )
    return jax.shard_map(
        on_device, mesh=fine, in_specs=placed, out_specs=P(WIDE, NARROW), check_vma=False
    )
```

time: 500 us -> 184 us (0.37)
  waiting for transfers between devices: 281 us -> 65.8 us
  matrix products: 106 us -> 0 us
  starting transfers between devices: 0.23 us -> 61.4 us
  local copies, waits for them, and re-layouts: 68.4 us -> 16.2 us
  Pallas kernels: 0 us -> 37.9 us
  other arithmetic: 24.2 us -> 2.13 us
  between operations: 13.7 us -> 0.27 us
    all_gather x6 -> x0, waiting for transfers between devices: 204 us -> none  [the longest x1 64.8 us: on_device(): shard_piece = lax.all_gather(prefix_cache, 'wide', axis=0, tiled=True)]
    dot_general x70 -> x0, matrix products: 106 us -> none  [the longest x32 62.4 us: attend(): jnp.einsum('hrn,nhd->hrd', weights, value_block.astype(jnp.float32), prec...]
    reduce_scatter x1 -> x0, waiting for transfers between devices: 73.7 us -> none  [on_device(): lax.psum_scatter(partial_out, 'narrow', scatter_dimension=1, tiled=True)]
    ppermute x0 -> x40, waiting for transfers between devices: none -> 65.8 us  [the longest x8 24.1 us: across_x(): return lax.ppermute(x, 'xl', [(0, 1), (1, 0)])]
    ppermute x0 -> x40, starting transfers between devices: none -> 61.4 us  [the longest x6 23.6 us: across_core(): return lax.ppermute(x, 'c', [(0, 1), (1, 0)])]
    pallas_call x0 -> x5, Pallas kernels: none -> 37.9 us  [the longest x1 20 us: attend(): pl.pallas_call(attend_kernel, out_shape=tuple((jax.ShapeDtypeStruct((H +...]
    dynamic_slice x80 -> x2, local copies, waits for them, and re-layouts: 37.1 us -> 1.95 us  [head_rows(): return lax.dynamic_slice_in_dim(w, h * rows, rows, 0)]
    another operation x1 -> x5, local copies, waits for them, and re-layouts: 18.2 us -> 1.15 us  [the longest x1 0.81 us: on_device(): cache = jnp.stack([cache_of(c), across_core(cache_of(1 - c))])]
  transfers between devices with their start and end apart: 7 -> 40, of which waited for: 5 -> 18; matrix products, arithmetic and copies ran while one was open for 38% -> 3% of each run, Pallas kernels for 0% -> 18%
where the time goes in v1:
time: 184 us
  waiting for transfers between devices  65.8 us (36%)
  starting transfers between devices  61.4 us (33%)
  Pallas kernels  37.9 us (21%)
  local copies, waits for them, and re-layouts  16.2 us (9%)
  other arithmetic  2.13 us (1%)
    ppermute x8, waiting for transfers between devices, across_x(): return lax.ppermute(x, 'xl', [(0, 1), (1, 0)])  24.1 us
    ppermute x6, starting transfers between devices, across_core(): return lax.ppermute(x, 'c', [(0, 1), (1, 0)])  23.6 us
    ppermute x18, starting transfers between devices, along_y(): return lax.ppermute(x, 'y', [(i, (i + k) % 4) for i in range(4)])  22.7 us
    pallas_call x1, Pallas kernels, attend(): pl.pallas_call(attend_kernel, out_shape=tuple((jax.ShapeDtypeStruct((H +...  20 us
    ppermute x6, waiting for transfers between devices, along_z(): return lax.ppermute(x, 'z', [(i, (i + k) % 4) for i in range(4)])  16.9 us
    ppermute x18, waiting for transfers between devices, along_y(): return lax.ppermute(x, 'y', [(i, (i + k) % 4) for i in range(4)])  14.8 us
    pallas_call x1, Pallas kernels, project(): pl.pallas_call(project_kernel, out_shape=(jax.ShapeDtypeStruct((1024, H),...  10.8 us
    unnamed x39, local copies, waits for them, and re-layouts  9.39 us
  transfers between devices with their start and end apart: 40, of which 18 were waited for; matrix products, arithmetic and copies ran while one was open for 3% of the time, Pallas kernels for 18%

profile of v1, /device:TPU:3, one launch (start us, length us, event | category | flops | bytes accessed | tf_op | source)
XLA Modules:
  0.0 183.7 jit_solution(9990685845928242794)
XLA Ops:
  4.1 1.4 collective-permute-start.9
  5.4 1.8 %collective-permute-start.1 = (bf16[256,256]{1,0:T(8,128)(2,1)S(1)}, bf16[256,256]{1,0:T(8,128)(2,1)S(1)}, u32[]{:S(2)}, u32[]{:S(2)}) collective-permute-start(bf16[256,256]{1,0:T(8,128)(2,1)S(1)} %copy-done.15), channel_id=1, source_target_pairs={{0,1},{1,0},{2,3},{3,2},{4,5},{5,4},{6,7},{7,6},{8,9},{9,8},{10,11... | collective-permute-start | bytes 393224 | tf_op jit(solution)/shard_map/ppermute | solution.py:48
  7.3 4.0 %collective-permute-done.1 = bf16[256,256]{1,0:T(8,128)(2,1)S(1)} collective-permute-done((bf16[256,256]{1,0:T(8,128)(2,1)S(1)}, bf16[256,256]{1,0:T(8,128)(2,1)S(1)}, u32[]{:S(2)}, u32[]{:S(2)}) %collective-permute-start.1) | collective-permute-done | bytes 131104 | tf_op jit(solution)/shard_map/ppermute | solution.py:48
  11.4 1.7 collective-permute-start.2
  13.1 3.3 %collective-permute-start.3 = (bf16[2,256,256]{2,1,0:T(8,128)(2,1)S(1)}, bf16[2,256,256]{2,1,0:T(8,128)(2,1)S(1)}, u32[]{:S(2)}, u32[]{:S(2)}) collective-permute-start(bf16[2,256,256]{2,1,0:T(8,128)(2,1)S(1)} %pad_maximum_fusion.3.b0), channel_id=1, source_target_pairs={{0,4},{2,6},{4,0},{6,2},{1,5},{3,7},{5,1},{7,3},{8,12},{10,14},{12... | collective-permute-start | bytes 786440 | tf_op jit(solution)/shard_map/ppermute | solution.py:40
  17.1 2.5 %collective-permute-start.10 = (bf16[2,1280,128]{2,1,0:T(8,128)(2,1)S(1)}, bf16[2,1280,128]{2,1,0:T(8,128)(2,1)}, u32[]{:S(2)}, u32[]{:S(2)}) collective-permute-start(bf16[2,1280,128]{2,1,0:T(8,128)(2,1)S(1)} %pad_maximum_fusion.1.refs_0_), channel_id=1, source_target_pairs={{0,48},{16,0},{32,16},{48,32},{1,49},{17,1},{33,17},{49,33},{2,50}... | collective-permute-start | bytes 1966088 | tf_op jit(solution)/shard_map/ppermute | solution.py:36
  21.2 2.3 %collective-permute-start = (s32[256,2]{0,1:T(2,128)S(1)}, s32[256,2]{0,1:T(2,128)S(1)}, u32[]{:S(2)}, u32[]{:S(2)}) collective-permute-start(s32[256,2]{0,1:T(2,128)S(1)} %copy-done.18), channel_id=1, source_target_pairs={{0,8},{8,0},{1,9},{9,1},{2,10},{10,2},{3,11},{11,3},{4,12},{12,4},... | collective-permute-start | bytes 6152 | tf_op jit(solution)/shard_map/ppermute | solution.py:52
  23.6 3.2 %collective-permute-done.3.b2 = bf16[2,256,256]{2,1,0:T(8,128)(2,1)S(1)} collective-permute-done((bf16[2,256,256]{2,1,0:T(8,128)(2,1)S(1)}, bf16[2,256,256]{2,1,0:T(8,128)(2,1)S(1)}, u32[]{:S(2)}, u32[]{:S(2)}) %collective-permute-start.3) | collective-permute-done | bytes 262176 | tf_op jit(solution)/shard_map/ppermute | solution.py:40
  26.8 2.4 %collective-permute-start.7 = (bf16[768,256]{1,0:T(8,128)(2,1)S(1)}, bf16[768,256]{1,0:T(8,128)(2,1)}, u32[]{:S(2)}, u32[]{:S(2)}) collective-permute-start(bf16[768,256]{1,0:T(8,128)(2,1)S(1)} %get-tuple-element.36), channel_id=1, source_target_pairs={{0,8},{8,0},{1,9},{9,1},{2,10},{10,2},{3,11},{11,3},{4,12},{12,4},... | collective-permute-start | bytes 1179656 | tf_op jit(solution)/shard_map/ppermute | solution.py:52
  32.6 1.7 slice_bitcast_fusion
  34.3 2.5 %collective-permute-start.14 = (bf16[1280,128]{1,0:T(8,128)(2,1)}, bf16[1280,128]{1,0:T(8,128)(2,1)}, u32[]{:S(2)}, u32[]{:S(2)}) collective-permute-start(bf16[1280,128]{1,0:T(8,128)(2,1)} %slice_bitcast_fusion), channel_id=1, source_target_pairs={{0,48},{16,0},{32,16},{48,32},{1,49},{17,1},{33,17},{49,33},{2,50}... | collective-permute-start | bytes 983048 | tf_op jit(solution)/shard_map/ppermute | solution.py:36
  36.9 8.9 %collective-permute-done.8.refs_1_ = bf16[2,1280,128]{2,1,0:T(8,128)(2,1)} collective-permute-done((bf16[2,1280,128]{2,1,0:T(8,128)(2,1)S(1)}, bf16[2,1280,128]{2,1,0:T(8,128)(2,1)}, u32[]{:S(2)}, u32[]{:S(2)}) %collective-permute-start.8) | collective-permute-done | bytes 655392 | tf_op jit(solution)/shard_map/ppermute | solution.py:44
  47.0 1.4 collective-permute-start.12
  53.0 9.8 %collective-permute-done.11.refs_4_ = bf16[2,1280,128]{2,1,0:T(8,128)(2,1)} collective-permute-done((bf16[2,1280,128]{2,1,0:T(8,128)(2,1)}, bf16[2,1280,128]{2,1,0:T(8,128)(2,1)}, u32[]{:S(2)}, u32[]{:S(2)}) %collective-permute-start.11) | collective-permute-done | bytes 655392 | tf_op jit(solution)/shard_map/ppermute | solution.py:36
  62.7 2.3 %collective-permute-done.16.refs_9_ = bf16[1280,128]{1,0:T(8,128)(2,1)S(1)} collective-permute-done((bf16[1280,128]{1,0:T(8,128)(2,1)}, bf16[1280,128]{1,0:T(8,128)(2,1)S(1)}, u32[]{:S(2)}, u32[]{:S(2)}) %collective-permute-start.16) | collective-permute-done | bytes 327712 | tf_op jit(solution)/shard_map/ppermute | solution.py:44
  65.0 10.8 %project.1 = (bf16[1024,128]{1,0:T(8,128)(2,1)}, bf16[512,256]{1,0:T(8,128)(2,1)}, f32[512,2]{1,0:T(8,128)S(1)}) custom-call(s32[9]{0:T(128)S(1)} %stack.154.idx, s32[512,2]{1,0:T(8,128)S(1)} %broadcast_select_fusion.routes, bf16[8,2,128,8]{3,2,1,0:T(8,128)(2,1)S(1)} %bitcast.53, bf16[8,2,256,128]{3,2,1,0:T(8,128)(2,1)S(1)} %normalise.1.own, ...), custom_call_target="tpu_custom_call" | custom-call | flops 6442450944 | bytes 8388608 | tf_op jit(solution)/shard_map/project/pallas_call | solution.py:192
  76.2 2.5 %collective-permute-start.18 = (bf16[1024,128]{1,0:T(8,128)(2,1)}, bf16[1024,128]{1,0:T(8,128)(2,1)S(1)}, u32[]{:S(2)}, u32[]{:S(2)}) collective-permute-start(bf16[1024,128]{1,0:T(8,128)(2,1)} %get-tuple-element.23.q0), channel_id=1, source_target_pairs={{0,32},{16,48},{32,0},{48,16},{1,33},{17,49},{33,1},{49,17},{2,34}... | collective-permute-start | bytes 786440 | tf_op jit(solution)/shard_map/ppermute | solution.py:36
  80.0 2.0 %collective-permute-done.20.cache1 = bf16[2,768,256]{2,1,0:T(8,128)(2,1)} collective-permute-done((bf16[2,768,256]{2,1,0:T(8,128)(2,1)S(1)}, bf16[2,768,256]{2,1,0:T(8,128)(2,1)}, u32[]{:S(2)}, u32[]{:S(2)}) %collective-permute-start.20) | collective-permute-done | bytes 786464 | tf_op jit(solution)/shard_map/ppermute | solution.py:44
  83.5 3.1 %collective-permute-done.18.q2 = bf16[1024,128]{1,0:T(8,128)(2,1)S(1)} collective-permute-done((bf16[1024,128]{1,0:T(8,128)(2,1)}, bf16[1024,128]{1,0:T(8,128)(2,1)S(1)}, u32[]{:S(2)}, u32[]{:S(2)}) %collective-permute-start.18) | collective-permute-done | bytes 262176 | tf_op jit(solution)/shard_map/ppermute | solution.py:36
  92.5 20.0 %attend.1 = (bf16[144,1024]{1,0:T(8,128)(2,1)S(1)}, bf16[144,1024]{1,0:T(8,128)(2,1)S(1)}, bf16[144,1024]{1,0:T(8,128)(2,1)S(1)}, bf16[144,1024]{1,0:T(8,128)(2,1)S(1)}) custom-call(s32[9]{0:T(128)S(1)} %stack.175.idx, s32[4]{0:T(128)S(1)} %copy-done.11, s32[4]{0:T(128)S(1)} %copy-done.12, bf16[1024,128]{1,0:T(8,128)(2,1)} %get-tuple-element.23.q0, ...), custom_call_target="tpu_custom_call" | custom-call | flops 12884901888 | bytes 6291456 | tf_op jit(solution)/shard_map/attend/pallas_call | solution.py:355
  116.8 1.4 collective-permute-start.32
  119.9 4.0 %collective-permute-start.30 = (bf16[2,1024,128]{2,1,0:T(8,128)(2,1)}, bf16[2,1024,128]{2,1,0:T(8,128)(2,1)}, u32[]{:S(2)}, u32[]{:S(2)}) collective-permute-start(bf16[2,1024,128]{2,1,0:T(8,128)(2,1)} %collective-permute-done.26.refs_1_), channel_id=1, source_target_pairs={{0,48},{16,0},{32,16},{48,32},{1,49},{17,1},{33,17},{49,33},{2,50}... | collective-permute-start | bytes 1572872 | tf_op jit(solution)/shard_map/ppermute | solution.py:36
  124.3 15.8 %collective-permute-start.25 = (bf16[1024,128]{1,0:T(8,128)(2,1)S(1)}, bf16[1024,128]{1,0:T(8,128)(2,1)S(1)}, u32[]{:S(2)}, u32[]{:S(2)}) collective-permute-start(bf16[1024,128]{1,0:T(8,128)(2,1)S(1)} %combine.1.own), channel_id=1, source_target_pairs={{0,8},{8,0},{1,9},{9,1},{2,10},{10,2},{3,11},{11,3},{4,12},{12,4},... | collective-permute-start | bytes 786440 | tf_op jit(solution)/shard_map/ppermute | solution.py:52
  141.7 5.3 %collective-permute-done.33.refs_8_ = bf16[1024,128]{1,0:T(8,128)(2,1)S(1)} collective-permute-done((bf16[1024,128]{1,0:T(8,128)(2,1)}, bf16[1024,128]{1,0:T(8,128)(2,1)S(1)}, u32[]{:S(2)}, u32[]{:S(2)}) %collective-permute-start.33) | collective-permute-done | bytes 262176 | tf_op jit(solution)/shard_map/ppermute | solution.py:44
  147.0 5.6 %collective-permute-done.34.refs_9_ = bf16[1024,128]{1,0:T(8,128)(2,1)S(1)} collective-permute-done((bf16[1024,128]{1,0:T(8,128)(2,1)}, bf16[1024,128]{1,0:T(8,128)(2,1)S(1)}, u32[]{:S(2)}, u32[]{:S(2)}) %collective-permute-start.34) | collective-permute-done | bytes 262176 | tf_op jit(solution)/shard_map/ppermute | solution.py:44
  153.6 5.5 %project_out.1 = (f32[2,512,128]{2,1,0:T(8,128)S(1)}, bf16[2,512,128]{2,1,0:T(8,128)(2,1)S(1)}, bf16[2,512,128]{2,1,0:T(8,128)(2,1)S(1)}, bf16[2,512,128]{2,1,0:T(8,128)(2,1)S(1)}) custom-call(s32[17]{0:T(128)S(1)} %stack.153.idx, s32[512,2]{1,0:T(8,128)S(1)} %broadcast_select_fusion.routes, bf16[1024,128]{1,0:T(8,128)(2,1)S(1)} %combine.1.own, ...), custom_call_target="tpu_custom_call" | custom-call | flops 4294967296 | bytes 6291456 | tf_op jit(solution)/shard_map/project_out/pallas_call | solution.py:450
  159.3 1.3 collective-permute-start.35
  160.7 4.3 %collective-permute-done.37 = bf16[2,512,128]{2,1,0:T(8,128)(2,1)S(1)} collective-permute-done((bf16[2,512,128]{2,1,0:T(8,128)(2,1)S(1)}, bf16[2,512,128]{2,1,0:T(8,128)(2,1)S(1)}, u32[]{:S(2)}, u32[]{:S(2)}) %collective-permute-start.37) | collective-permute-done | bytes 262176 | tf_op jit(solution)/shard_map/ppermute | solution.py:40
  166.2 8.1 %collective-permute-done.35 = bf16[2,512,128]{2,1,0:T(8,128)(2,1)S(1)} collective-permute-done((bf16[2,512,128]{2,1,0:T(8,128)(2,1)S(1)}, bf16[2,512,128]{2,1,0:T(8,128)(2,1)S(1)}, u32[]{:S(2)}, u32[]{:S(2)}) %collective-permute-start.35) | collective-permute-done | bytes 262176 | tf_op jit(solution)/shard_map/ppermute | solution.py:40
  174.4 1.9 %collective-permute-start.38 = (bf16[512,128]{1,0:T(8,128)(2,1)S(1)}, bf16[512,128]{1,0:T(8,128)(2,1)S(1)}, u32[]{:S(2)}, u32[]{:S(2)}) collective-permute-start(bf16[512,128]{1,0:T(8,128)(2,1)S(1)} %fusion.1), channel_id=1, source_target_pairs={{0,1},{1,0},{2,3},{3,2},{4,5},{5,4},{6,7},{7,6},{8,9},{9,8},{10,11... | collective-permute-start | bytes 393224 | tf_op jit(solution)/shard_map/ppermute | solution.py:48
  176.4 3.8 %collective-permute-done.38 = bf16[512,128]{1,0:T(8,128)(2,1)S(1)} collective-permute-done((bf16[512,128]{1,0:T(8,128)(2,1)S(1)}, bf16[512,128]{1,0:T(8,128)(2,1)S(1)}, u32[]{:S(2)}, u32[]{:S(2)}) %collective-permute-start.38) | collective-permute-done | bytes 131104 | tf_op jit(solution)/shard_map/ppermute | solution.py:48
  180.2 1.8 %collective-permute-start.39 = (bf16[256,128]{1,0:T(8,128)(2,1)S(1)}, bf16[256,128]{1,0:T(8,128)(2,1)S(1)}, u32[]{:S(2)}, u32[]{:S(2)}) collective-permute-start(bf16[256,128]{1,0:T(8,128)(2,1)S(1)} %get-tuple-element.40), channel_id=1, source_target_pairs={{0,8},{8,0},{1,9},{9,1},{2,10},{10,2},{3,11},{11,3},{4,12},{12,4},... | collective-permute-start | bytes 196616 | tf_op jit(solution)/shard_map/ppermute | solution.py:52
  (120 shorter events, 36.7 us)
Async XLA Ops:
  4.1 26.7 %collective-permute-start.9 = (bf16[2,1280,128]{2,1,0:T(8,128)(2,1)S(1)}, bf16[2,1280,128]{2,1,0:T(8,128)(2,1)S(1)}, u32[]{:S(2)}, u32[]{:S(2)}) collective-permute-start(bf16[2,1280,128]{2,1,0:T(8,128)(2,1)S(1)} %pad_maximum_fusion.1.refs_0_), channel_id=1, source_target_pairs={{0,16},{16,32},{32,48},{48,0},{1,17},{17,33},{33,49},{49,1},{2,18}... | collective-permute-start | bytes 1966088 | tf_op jit(solution)/shard_map/ppermute | solution.py:36
  11.4 9.9 %collective-permute-start.2 = (bf16[2,256,256]{2,1,0:T(8,128)(2,1)S(1)}, bf16[2,256,256]{2,1,0:T(8,128)(2,1)S(1)}, u32[]{:S(2)}, u32[]{:S(2)}) collective-permute-start(bf16[2,256,256]{2,1,0:T(8,128)(2,1)S(1)} %pad_maximum_fusion.3.b0), channel_id=1, source_target_pairs={{0,2},{2,4},{4,6},{6,0},{1,3},{3,5},{5,7},{7,1},{8,10},{10,12},{12... | collective-permute-start | bytes 786440 | tf_op jit(solution)/shard_map/ppermute | solution.py:40
  13.1 13.7 %collective-permute-start.3 = (bf16[2,256,256]{2,1,0:T(8,128)(2,1)S(1)}, bf16[2,256,256]{2,1,0:T(8,128)(2,1)S(1)}, u32[]{:S(2)}, u32[]{:S(2)}) collective-permute-start(bf16[2,256,256]{2,1,0:T(8,128)(2,1)S(1)} %pad_maximum_fusion.3.b0), channel_id=1, source_target_pairs={{0,4},{2,6},{4,0},{6,2},{1,5},{3,7},{5,1},{7,3},{8,12},{10,14},{12... | collective-permute-start | bytes 786440 | tf_op jit(solution)/shard_map/ppermute | solution.py:40
  16.4 12.9 %collective-permute-start.4 = (bf16[2,256,256]{2,1,0:T(8,128)(2,1)S(1)}, bf16[2,256,256]{2,1,0:T(8,128)(2,1)S(1)}, u32[]{:S(2)}, u32[]{:S(2)}) collective-permute-start(bf16[2,256,256]{2,1,0:T(8,128)(2,1)S(1)} %pad_maximum_fusion.3.b0), channel_id=1, source_target_pairs={{0,6},{2,0},{4,2},{6,4},{1,7},{3,1},{5,3},{7,5},{8,14},{10,8},{12,... | collective-permute-start | bytes 786440 | tf_op jit(solution)/shard_map/ppermute | solution.py:40
  17.1 14.5 %collective-permute-start.10 = (bf16[2,1280,128]{2,1,0:T(8,128)(2,1)S(1)}, bf16[2,1280,128]{2,1,0:T(8,128)(2,1)}, u32[]{:S(2)}, u32[]{:S(2)}) collective-permute-start(bf16[2,1280,128]{2,1,0:T(8,128)(2,1)S(1)} %pad_maximum_fusion.1.refs_0_), channel_id=1, source_target_pairs={{0,48},{16,0},{32,16},{48,32},{1,49},{17,1},{33,17},{49,33},{2,50}... | collective-permute-start | bytes 1966088 | tf_op jit(solution)/shard_map/ppermute | solution.py:36
  21.2 13.1 %collective-permute-start = (s32[256,2]{0,1:T(2,128)S(1)}, s32[256,2]{0,1:T(2,128)S(1)}, u32[]{:S(2)}, u32[]{:S(2)}) collective-permute-start(s32[256,2]{0,1:T(2,128)S(1)} %copy-done.18), channel_id=1, source_target_pairs={{0,8},{8,0},{1,9},{9,1},{2,10},{10,2},{3,11},{11,3},{4,12},{12,4},... | collective-permute-start | bytes 6152 | tf_op jit(solution)/shard_map/ppermute | solution.py:52
  26.8 20.2 %collective-permute-start.7 = (bf16[768,256]{1,0:T(8,128)(2,1)S(1)}, bf16[768,256]{1,0:T(8,128)(2,1)}, u32[]{:S(2)}, u32[]{:S(2)}) collective-permute-start(bf16[768,256]{1,0:T(8,128)(2,1)S(1)} %get-tuple-element.36), channel_id=1, source_target_pairs={{0,8},{8,0},{1,9},{9,1},{2,10},{10,2},{3,11},{11,3},{4,12},{12,4},... | collective-permute-start | bytes 1179656 | tf_op jit(solution)/shard_map/ppermute | solution.py:52
  29.2 16.5 %collective-permute-start.8 = (bf16[2,1280,128]{2,1,0:T(8,128)(2,1)S(1)}, bf16[2,1280,128]{2,1,0:T(8,128)(2,1)}, u32[]{:S(2)}, u32[]{:S(2)}) collective-permute-start(bf16[2,1280,128]{2,1,0:T(8,128)(2,1)S(1)} %pad_maximum_fusion.1.refs_0_), channel_id=1, source_target_pairs={{0,64},{64,0},{1,65},{65,1},{2,66},{66,2},{3,67},{67,3},{4,68},{68... | collective-permute-start | bytes 1966088 | tf_op jit(solution)/shard_map/ppermute | solution.py:44
  30.8 21.8 %collective-permute-start.5 = (bf16[8,2,256,128]{3,2,1,0:T(8,128)(2,1)S(1)}, bf16[8,2,256,128]{3,2,1,0:T(8,128)(2,1)}, u32[]{:S(2)}, u32[]{:S(2)}) collective-permute-start(bf16[8,2,256,128]{3,2,1,0:T(8,128)(2,1)S(1)} %normalise.1.own), channel_id=1, source_target_pairs={{0,8},{8,0},{1,9},{9,1},{2,10},{10,2},{3,11},{11,3},{4,12},{12,4},... | collective-permute-start | bytes 3145736 | tf_op jit(solution)/shard_map/ppermute | solution.py:52
  31.6 18.2 %collective-permute-start.13 = (bf16[1280,128]{1,0:T(8,128)(2,1)S(1)}, bf16[1280,128]{1,0:T(8,128)(2,1)}, u32[]{:S(2)}, u32[]{:S(2)}) collective-permute-start(bf16[1280,128]{1,0:T(8,128)(2,1)S(1)} %slice_bitcast_fusion.1), channel_id=1, source_target_pairs={{0,16},{16,32},{32,48},{48,0},{1,17},{17,33},{33,49},{49,1},{2,18}... | collective-permute-start | bytes 983048 | tf_op jit(solution)/shard_map/ppermute | solution.py:36
  34.3 15.9 %collective-permute-start.14 = (bf16[1280,128]{1,0:T(8,128)(2,1)}, bf16[1280,128]{1,0:T(8,128)(2,1)}, u32[]{:S(2)}, u32[]{:S(2)}) collective-permute-start(bf16[1280,128]{1,0:T(8,128)(2,1)} %slice_bitcast_fusion), channel_id=1, source_target_pairs={{0,48},{16,0},{32,16},{48,32},{1,49},{17,1},{33,17},{49,33},{2,50}... | collective-permute-start | bytes 983048 | tf_op jit(solution)/shard_map/ppermute | solution.py:36
  45.7 17.0 %collective-permute-start.11 = (bf16[2,1280,128]{2,1,0:T(8,128)(2,1)}, bf16[2,1280,128]{2,1,0:T(8,128)(2,1)}, u32[]{:S(2)}, u32[]{:S(2)}) collective-permute-start(bf16[2,1280,128]{2,1,0:T(8,128)(2,1)} %collective-permute-done.8.refs_1_), channel_id=1, source_target_pairs={{0,16},{16,32},{32,48},{48,0},{1,17},{17,33},{33,49},{49,1},{2,18}... | collective-permute-start | bytes 1966088 | tf_op jit(solution)/shard_map/ppermute | solution.py:36
  47.0 15.7 %collective-permute-start.12 = (bf16[2,1280,128]{2,1,0:T(8,128)(2,1)}, bf16[2,1280,128]{2,1,0:T(8,128)(2,1)}, u32[]{:S(2)}, u32[]{:S(2)}) collective-permute-start(bf16[2,1280,128]{2,1,0:T(8,128)(2,1)} %collective-permute-done.8.refs_1_), channel_id=1, source_target_pairs={{0,48},{16,0},{32,16},{48,32},{1,49},{17,1},{33,17},{49,33},{2,50}... | collective-permute-start | bytes 1966088 | tf_op jit(solution)/shard_map/ppermute | solution.py:36
  49.9 12.9 %collective-permute-start.15 = (bf16[1280,128]{1,0:T(8,128)(2,1)}, bf16[1280,128]{1,0:T(8,128)(2,1)S(1)}, u32[]{:S(2)}, u32[]{:S(2)}) collective-permute-start(bf16[1280,128]{1,0:T(8,128)(2,1)} %collective-permute-done.13.refs_6_), channel_id=1, source_target_pairs={{0,64},{64,0},{1,65},{65,1},{2,66},{66,2},{3,67},{67,3},{4,68},{68... | collective-permute-start | bytes 983048 | tf_op jit(solution)/shard_map/ppermute | solution.py:44
  50.2 14.8 %collective-permute-start.16 = (bf16[1280,128]{1,0:T(8,128)(2,1)}, bf16[1280,128]{1,0:T(8,128)(2,1)S(1)}, u32[]{:S(2)}, u32[]{:S(2)}) collective-permute-start(bf16[1280,128]{1,0:T(8,128)(2,1)} %collective-permute-done.14.refs_7_), channel_id=1, source_target_pairs={{0,64},{64,0},{1,65},{65,1},{2,66},{66,2},{3,67},{67,3},{4,68},{68... | collective-permute-start | bytes 983048 | tf_op jit(solution)/shard_map/ppermute | solution.py:44
  52.6 29.4 %collective-permute-start.20 = (bf16[2,768,256]{2,1,0:T(8,128)(2,1)S(1)}, bf16[2,768,256]{2,1,0:T(8,128)(2,1)}, u32[]{:S(2)}, u32[]{:S(2)}) collective-permute-start(bf16[2,768,256]{2,1,0:T(8,128)(2,1)S(1)} %pad_maximum_fusion.cache0), channel_id=1, source_target_pairs={{0,64},{64,0},{1,65},{65,1},{2,66},{66,2},{3,67},{67,3},{4,68},{68... | collective-permute-start | bytes 2359304 | tf_op jit(solution)/shard_map/ppermute | solution.py:44
  75.8 6.9 %collective-permute-start.17 = (bf16[1024,128]{1,0:T(8,128)(2,1)}, bf16[1024,128]{1,0:T(8,128)(2,1)S(1)}, u32[]{:S(2)}, u32[]{:S(2)}) collective-permute-start(bf16[1024,128]{1,0:T(8,128)(2,1)} %get-tuple-element.23.q0), channel_id=1, source_target_pairs={{0,16},{16,32},{32,48},{48,0},{1,17},{17,33},{33,49},{49,1},{2,18}... | collective-permute-start | bytes 786440 | tf_op jit(solution)/shard_map/ppermute | solution.py:36
  76.2 10.4 %collective-permute-start.18 = (bf16[1024,128]{1,0:T(8,128)(2,1)}, bf16[1024,128]{1,0:T(8,128)(2,1)S(1)}, u32[]{:S(2)}, u32[]{:S(2)}) collective-permute-start(bf16[1024,128]{1,0:T(8,128)(2,1)} %get-tuple-element.23.q0), channel_id=1, source_target_pairs={{0,32},{16,48},{32,0},{48,16},{1,33},{17,49},{33,1},{49,17},{2,34}... | collective-permute-start | bytes 786440 | tf_op jit(solution)/shard_map/ppermute | solution.py:36
  78.7 8.6 %collective-permute-start.19 = (bf16[1024,128]{1,0:T(8,128)(2,1)}, bf16[1024,128]{1,0:T(8,128)(2,1)S(1)}, u32[]{:S(2)}, u32[]{:S(2)}) collective-permute-start(bf16[1024,128]{1,0:T(8,128)(2,1)} %get-tuple-element.23.q0), channel_id=1, source_target_pairs={{0,48},{16,0},{32,16},{48,32},{1,49},{17,1},{33,17},{49,33},{2,50}... | collective-permute-start | bytes 786440 | tf_op jit(solution)/shard_map/ppermute | solution.py:36
  79.6 8.4 %collective-permute-start.21 = (bf16[512,256]{1,0:T(8,128)(2,1)}, bf16[512,256]{1,0:T(8,128)(2,1)S(1)}, u32[]{:S(2)}, u32[]{:S(2)}) collective-permute-start(bf16[512,256]{1,0:T(8,128)(2,1)} %get-tuple-element.25.kv0), channel_id=1, source_target_pairs={{0,64},{64,0},{1,65},{65,1},{2,66},{66,2},{3,67},{67,3},{4,68},{68... | collective-permute-start | bytes 786440 | tf_op jit(solution)/shard_map/ppermute | solution.py:44
  82.0 34.8 %collective-permute-start.26 = (bf16[2,1024,128]{2,1,0:T(8,128)(2,1)}, bf16[2,1024,128]{2,1,0:T(8,128)(2,1)}, u32[]{:S(2)}, u32[]{:S(2)}) collective-permute-start(bf16[2,1024,128]{2,1,0:T(8,128)(2,1)} %bitcast.55), channel_id=1, source_target_pairs={{0,64},{64,0},{1,65},{65,1},{2,66},{66,2},{3,67},{67,3},{4,68},{68... | collective-permute-start | bytes 1572872 | tf_op jit(solution)/shard_map/ppermute | solution.py:44
  83.4 30.0 %collective-permute-start.27 = (bf16[2,1024,128]{2,1,0:T(8,128)(2,1)}, bf16[2,1024,128]{2,1,0:T(8,128)(2,1)S(1)}, u32[]{:S(2)}, u32[]{:S(2)}) collective-permute-start(bf16[2,1024,128]{2,1,0:T(8,128)(2,1)} %bitcast.56), channel_id=1, source_target_pairs={{0,16},{16,32},{32,48},{48,0},{1,17},{17,33},{33,49},{49,1},{2,18}... | collective-permute-start | bytes 1572872 | tf_op jit(solution)/shard_map/ppermute | solution.py:36
  87.3 27.5 %collective-permute-start.28 = (bf16[2,1024,128]{2,1,0:T(8,128)(2,1)}, bf16[2,1024,128]{2,1,0:T(8,128)(2,1)S(1)}, u32[]{:S(2)}, u32[]{:S(2)}) collective-permute-start(bf16[2,1024,128]{2,1,0:T(8,128)(2,1)} %bitcast.57), channel_id=1, source_target_pairs={{0,48},{16,0},{32,16},{48,32},{1,49},{17,1},{33,17},{49,33},{2,50}... | collective-permute-start | bytes 1572872 | tf_op jit(solution)/shard_map/ppermute | solution.py:36
  112.6 7.3 %collective-permute-start.23 = (bf16[144,1024]{1,0:T(8,128)(2,1)S(1)}, bf16[144,1024]{1,0:T(8,128)(2,1)S(1)}, u32[]{:S(2)}, u32[]{:S(2)}) collective-permute-start(bf16[144,1024]{1,0:T(8,128)(2,1)S(1)} %get-tuple-element.28), channel_id=1, source_target_pairs={{0,32},{16,48},{32,0},{48,16},{1,33},{17,49},{33,1},{49,17},{2,34}... | collective-permute-start | bytes 884744 | tf_op jit(solution)/shard_map/ppermute | solution.py:36
  113.5 10.5 %collective-permute-start.24 = (bf16[144,1024]{1,0:T(8,128)(2,1)S(1)}, bf16[144,1024]{1,0:T(8,128)(2,1)S(1)}, u32[]{:S(2)}, u32[]{:S(2)}) collective-permute-start(bf16[144,1024]{1,0:T(8,128)(2,1)S(1)} %get-tuple-element.29), channel_id=1, source_target_pairs={{0,16},{16,32},{32,48},{48,0},{1,17},{17,33},{33,49},{49,1},{2,18}... | collective-permute-start | bytes 884744 | tf_op jit(solution)/shard_map/ppermute | solution.py:36
  114.8 25.3 %collective-permute-start.31 = (bf16[1024,128]{1,0:T(8,128)(2,1)}, bf16[1024,128]{1,0:T(8,128)(2,1)}, u32[]{:S(2)}, u32[]{:S(2)}) collective-permute-start(bf16[1024,128]{1,0:T(8,128)(2,1)} %slice_bitcast_fusion.4), channel_id=1, source_target_pairs={{0,16},{16,32},{32,48},{48,0},{1,17},{17,33},{33,49},{49,1},{2,18}... | collective-permute-start | bytes 786440 | tf_op jit(solution)/shard_map/ppermute | solution.py:36
  116.8 23.6 %collective-permute-start.32 = (bf16[1024,128]{1,0:T(8,128)(2,1)}, bf16[1024,128]{1,0:T(8,128)(2,1)}, u32[]{:S(2)}, u32[]{:S(2)}) collective-permute-start(bf16[1024,128]{1,0:T(8,128)(2,1)} %slice_bitcast_fusion.3), channel_id=1, source_target_pairs={{0,48},{16,0},{32,16},{48,32},{1,49},{17,1},{33,17},{49,33},{2,50}... | collective-permute-start | bytes 786440 | tf_op jit(solution)/shard_map/ppermute | solution.py:36
  118.2 34.4 %collective-permute-start.29 = (bf16[2,1024,128]{2,1,0:T(8,128)(2,1)}, bf16[2,1024,128]{2,1,0:T(8,128)(2,1)}, u32[]{:S(2)}, u32[]{:S(2)}) collective-permute-start(bf16[2,1024,128]{2,1,0:T(8,128)(2,1)} %collective-permute-done.26.refs_1_), channel_id=1, source_target_pairs={{0,16},{16,32},{32,48},{48,0},{1,17},{17,33},{33,49},{49,1},{2,18}... | collective-permute-start | bytes 1572872 | tf_op jit(solution)/shard_map/ppermute | solution.py:36
  119.9 32.7 %collective-permute-start.30 = (bf16[2,1024,128]{2,1,0:T(8,128)(2,1)}, bf16[2,1024,128]{2,1,0:T(8,128)(2,1)}, u32[]{:S(2)}, u32[]{:S(2)}) collective-permute-start(bf16[2,1024,128]{2,1,0:T(8,128)(2,1)} %collective-permute-done.26.refs_1_), channel_id=1, source_target_pairs={{0,48},{16,0},{32,16},{48,32},{1,49},{17,1},{33,17},{49,33},{2,50}... | collective-permute-start | bytes 1572872 | tf_op jit(solution)/shard_map/ppermute | solution.py:36
  124.3 17.4 %collective-permute-start.25 = (bf16[1024,128]{1,0:T(8,128)(2,1)S(1)}, bf16[1024,128]{1,0:T(8,128)(2,1)S(1)}, u32[]{:S(2)}, u32[]{:S(2)}) collective-permute-start(bf16[1024,128]{1,0:T(8,128)(2,1)S(1)} %combine.1.own), channel_id=1, source_target_pairs={{0,8},{8,0},{1,9},{9,1},{2,10},{10,2},{3,11},{11,3},{4,12},{12,4},... | collective-permute-start | bytes 786440 | tf_op jit(solution)/shard_map/ppermute | solution.py:52
  140.4 12.2 %collective-permute-start.34 = (bf16[1024,128]{1,0:T(8,128)(2,1)}, bf16[1024,128]{1,0:T(8,128)(2,1)S(1)}, u32[]{:S(2)}, u32[]{:S(2)}) collective-permute-start(bf16[1024,128]{1,0:T(8,128)(2,1)} %collective-permute-done.32.refs_7_), channel_id=1, source_target_pairs={{0,64},{64,0},{1,65},{65,1},{2,66},{66,2},{3,67},{67,3},{4,68},{68... | collective-permute-start | bytes 786440 | tf_op jit(solution)/shard_map/ppermute | solution.py:44
  159.3 15.0 %collective-permute-start.35 = (bf16[2,512,128]{2,1,0:T(8,128)(2,1)S(1)}, bf16[2,512,128]{2,1,0:T(8,128)(2,1)S(1)}, u32[]{:S(2)}, u32[]{:S(2)}) collective-permute-start(bf16[2,512,128]{2,1,0:T(8,128)(2,1)S(1)} %get-tuple-element.32), channel_id=1, source_target_pairs={{0,2},{2,4},{4,6},{6,0},{1,3},{3,5},{5,7},{7,1},{8,10},{10,12},{12... | collective-permute-start | bytes 786440 | tf_op jit(solution)/shard_map/ppermute | solution.py:40
  (27 other events, 105.5 us)

commit v2 on v1

--- a/solution.py
+++ b/solution.py
@@ -30,6 +30,7 @@
 SMEM = pl.BlockSpec(memory_space=pltpu.SMEM)
 VMEM = pl.BlockSpec(memory_space=pltpu.VMEM)
 HBM = pl.BlockSpec(memory_space=pltpu.HBM)
+ANY = pl.BlockSpec(memory_space=pl.ANY)
 
 
 def along_y(x, k):
@@ -56,28 +57,24 @@
     return lax.optimization_barrier((a, b))
 
 
-def gather_chips(w):
-    a = across_x(w)
-    yp, ym = along_y(w, 1), along_y(w, 3)
-    ap, am = along_y(a, 1), along_y(a, 3)
-    far0, far1 = along_y(yp[0], 1), along_y(ym[1], 3)
+def gather_parts(w0, w1):
+    ym0, yp0, a0 = along_y(w0, 3), along_y(w0, 1), across_x(w0)
+    ym1, yp1, a1 = along_y(w1, 3), along_y(w1, 1), across_x(w1)
+    far0, far1 = along_y(yp0, 1), along_y(ym1, 3)
+    am0, ap0 = along_y(a0, 3), along_y(a0, 1)
+    am1, ap1 = along_y(a1, 3), along_y(a1, 1)
     afar0, afar1 = across_x(far0), across_x(far1)
-    return [w, a, yp, ym, ap, am, far0, far1, afar0, afar1]
+    pairs = [(w0, w1), (a0, a1), (ym0, ym1), (am0, am1), (far0, far1), (afar0, afar1), (yp0, yp1), (ap0, ap1)]
+    return [part for pair in pairs for part in pair]
 
 
 def chip_order():
     xl, y = lax.axis_index("xl"), lax.axis_index("y")
-    pairs = [
-        (xl, y),
-        (1 - xl, y),
-        (xl, y + 3),
-        (xl, y + 1),
-        (1 - xl, y + 3),
-        (1 - xl, y + 1),
-        (xl, y + 2),
-        (1 - xl, y + 2),
-    ]
-    return [a * 4 + lax.rem(b, 4) for a, b in pairs]
+    return [(xl ^ dx) * 4 + lax.rem(y + dy, 4) for dy in range(4) for dx in range(2)]
+
+
+def pin(arrays):
+    return [pltpu.with_memory_space_constraint(a, pltpu.HBM) for a in arrays]
 
 
 def nt_dot(a, b):
@@ -100,16 +97,14 @@
         total = total + jnp.sum(v * v, axis=1, keepdims=True)
     scale = lax.rsqrt(total * (1.0 / 2048) + EPS)
     for k in range(8):
-        src = idx[k]
-        v = held[k // 2, k % 2].astype(F32) * scale * gain[src].astype(F32)
-        normed[src, 0] = v[:, :H].astype(BF16)
-        normed[src, 1] = v[:, H:].astype(BF16)
+        v = held[k // 2, k % 2].astype(F32) * scale * gain[idx[k]].astype(F32)
+        normed[:, pl.ds(pl.multiple_of(idx[8 + k] * 256, 256), 256)] = v.astype(BF16)
 
 
 def normalise(idx, gain, blocks):
     return pl.pallas_call(
         norm_kernel,
-        out_shape=jax.ShapeDtypeStruct((8, 2, 256, H), BF16),
+        out_shape=jax.ShapeDtypeStruct((256, 2048), BF16),
         in_specs=[SMEM, VMEM] + [HBM] * 4,
         out_specs=VMEM,
         scratch_shapes=[pltpu.VMEM((4, 2, 256, 256), BF16), pltpu.SemaphoreType.DMA((4,))],
@@ -119,39 +114,36 @@
     )(idx, gain, *blocks)
 
 
+GROUPS = ((0, 512), (512, 768))
+
+
 def project_kernel(idx, routes, router, own, other, *refs):
-    blocks = refs[:10]
-    q_out, kv_out, gates, xs, held, sel, sem = refs[10:]
+    blocks = refs[:16]
+    q_out, kv_out, gates, xs, held, sel, sem = refs[16:]
     core = idx[8]
-    rows_of = [pl.multiple_of(core * 256, 256), pl.multiple_of((1 - core) * 256, 256)]
-    x_copies = [
-        pltpu.make_async_copy(r, xs.at[:, :, pl.ds(at, 256)], sem.at[5 + i])
-        for i, (r, at) in enumerate(zip((own, other), rows_of))
-    ]
-
-    def tile_copies(r):
-        at = pl.ds(r * 256, 256)
-        copies = []
-        for k in range(10):
-            if k < 6:
-                src, dst = blocks[k].at[:, at], held.at[k, :, at]
-            else:
-                src, dst = blocks[k].at[at], held.at[6 + (k - 6) // 2, (k - 6) % 2, at]
-            copies.append(pltpu.make_async_copy(src, dst, sem.at[r]))
-        return copies
-
-    tiles = [tile_copies(r) for r in range(5)]
-    for c in x_copies:
+    copies = []
+    for i, r in enumerate((own, other)):
+        at = pl.multiple_of((core if i == 0 else 1 - core) * 256, 256)
+        copies.append(pltpu.make_async_copy(r, xs.at[pl.ds(at, 256)], sem.at[32 + i]))
+    for g, (start, rows) in enumerate(GROUPS):
+        for k in range(16):
+            lane = (k // 2) * 256 + H * (core if k % 2 == 0 else 1 - core)
+            at = pl.ds(pl.multiple_of(lane, H), H)
+            copies.append(
+                pltpu.make_async_copy(
+                    blocks[k].at[pl.ds(start, rows)],
+                    held.at[pl.ds(start, rows), at],
+                    sem.at[16 * g + k],
+                )
+            )
+    for c in copies:
         c.start()
-    for group in tiles:
-        for c in group:
-            c.start()
-    for c in x_copies:
+    for c in copies[:2]:
         c.wait()
     logits = jnp.zeros((512, E), F32)
-    for nb in range(8):
-        for side in range(2):
-            logits += jnp.dot(xs[nb, side], router[nb, side], preferred_element_type=F32)
+    for i in range(8):
+        part = router[:, pl.ds(pl.multiple_of(idx[i] * 256, 256), 256)]
+        logits += nt_dot(xs[:, i * 256 : (i + 1) * 256], part)
     lane = lax.broadcasted_iota(jnp.int32, (512, E), 1)
     chosen = [
         jnp.sum(jnp.where(routes[:, j : j + 1] == lane, logits, 0.0), axis=1, keepdims=True)
@@ -163,15 +155,13 @@
     gates[:, 1:2] = e1 / (e0 + e1)
 
     for r in range(5):
-        for c in tiles[r]:
-            c.wait()
-        acc = jnp.zeros((512, 256), F32)
-        for i in range(8):
-            nb = idx[i]
-            x = jnp.concatenate([xs[nb, core], xs[nb, 1 - core]], axis=1)
-            at = slice(r * 256, (r + 1) * 256)
-            w = jnp.concatenate([held[i, 0, at], held[i, 1, at]], axis=1)
-            acc += nt_dot(x, w)
+        if r == 0:
+            for c in copies[2:18]:
+                c.wait()
+        if r == 2:
+            for c in copies[18:]:
+                c.wait()
+        acc = nt_dot(xs[...], held[r * 256 : (r + 1) * 256])
         if r == 4:
             kv_out[...] = acc.astype(BF16)
             continue
@@ -196,18 +186,18 @@
             jax.ShapeDtypeStruct((512, 2 * H), BF16),
             jax.ShapeDtypeStruct((512, 2), F32),
         ),
-        in_specs=[SMEM, VMEM, VMEM] + [HBM] * 12,
+        in_specs=[SMEM, VMEM, VMEM] + [HBM] * 18,
         out_specs=(VMEM, VMEM, VMEM),
         scratch_shapes=[
-            pltpu.VMEM((8, 2, 512, H), BF16),
-            pltpu.VMEM((8, 2, 1280, H), BF16),
+            pltpu.VMEM((512, 2048), BF16),
+            pltpu.VMEM((1280, 2048), BF16),
             pltpu.VMEM((2, 512, H), F32),
-            pltpu.SemaphoreType.DMA((7,)),
+            pltpu.SemaphoreType.DMA((34,)),
         ],
         compiler_params=pltpu.CompilerParams(vmem_limit_bytes=20 << 20),
         cost_estimate=pl.CostEstimate(flops=6 << 30, bytes_accessed=8 << 20, transcendentals=0),
         name="project",
-    )(idx, routes, router, own, other, *blocks)
+    )(idx, routes, router, *pin([own, other, *blocks]))
 
 
 def attend_kernel(idx, ends_s, ends_p, q0, q1, q2, q3, cache0, cache1, kv0, kv1, *refs):
@@ -375,7 +365,7 @@
             flops=12 << 30, bytes_accessed=6 << 20, transcendentals=10 << 20
         ),
         name="attend",
-    )(idx, suffix_lengths, prefix_lengths, *qs, *caches, *kvs)
+    )(idx, suffix_lengths, prefix_lengths, *pin([*qs, *caches, *kvs]))
 
 
 def combine_kernel(gates, p0, p1, p2, p3, out):
@@ -408,17 +398,13 @@
 
 
 def out_kernel(idx, routes, own, other, *refs):
-    blocks = refs[:10]
-    outs = refs[10:14]
-    held, padded, sem = refs[14:]
+    blocks = refs[:8]
+    outs = refs[8:12]
+    held, padded, sem = refs[12:]
     core = idx[8]
-    copies = []
-    for k in range(10):
-        if k < 6:
-            src, dst = blocks[k], held.at[idx[k]]
-        else:
-            src, dst = blocks[k], held.at[idx[6 + (k - 6) // 2], (k - 6) % 2]
-        copies.append(pltpu.make_async_copy(src, dst, sem.at[k]))
+    copies = [
+        pltpu.make_async_copy(r, held.at[idx[k]], sem.at[k]) for k, r in enumerate(blocks)
+    ]
     for c in copies:
         c.start()
     for side, source in enumerate((own, other)):
@@ -438,8 +424,9 @@
         value = jnp.zeros((512, 256), F32)
         for side in range(2):
             head = core if side == 0 else 1 - core
+            rows = pl.ds(pl.multiple_of(head * 1024, 1024), 1024)
             w = jnp.concatenate(
-                [held[idx[9 + 2 * dz], head], held[idx[10 + 2 * dz], head]], axis=1
+                [held[idx[9 + 2 * dz], rows], held[idx[10 + 2 * dz], rows]], axis=1
             )
             value += jnp.dot(padded[side], w, preferred_element_type=F32)
         for s in range(2):
@@ -451,17 +438,17 @@
         out_kernel,
         out_shape=(jax.ShapeDtypeStruct((2, 512, H), F32),)
         + tuple(jax.ShapeDtypeStruct((2, 512, H), BF16) for _ in range(3)),
-        in_specs=[SMEM, VMEM, VMEM, VMEM] + [HBM] * 10,
+        in_specs=[SMEM, VMEM, VMEM, VMEM] + [HBM] * 8,
         out_specs=tuple([VMEM] * 4),
         scratch_shapes=[
-            pltpu.VMEM((8, 2, 1024, H), BF16),
+            pltpu.VMEM((8, 2048, H), BF16),
             pltpu.VMEM((2, 512, 1024), BF16),
-            pltpu.SemaphoreType.DMA((10,)),
+            pltpu.SemaphoreType.DMA((8,)),
         ],
         compiler_params=pltpu.CompilerParams(vmem_limit_bytes=20 << 20),
         cost_estimate=pl.CostEstimate(flops=4 << 30, bytes_accessed=6 << 20, transcendentals=0),
         name="project_out",
-    )(idx, routes, own, other, *blocks)
+    )(idx, routes, own, other, *pin(blocks))
 
 
 def on_device(
@@ -491,10 +478,9 @@
     def weights_of(h):
         return jnp.concatenate([head_rows(query_weight, h), head_rows(kv_weight, h)], axis=0)
 
+    gathered = gather_parts(weights_of(c), across_core(weights_of(1 - c)))
     pair = jnp.stack([tokens, across_far(tokens)])
     blocks = [pair] + [along_z(pair, k) for k in (1, 2, 3)]
-    w = jnp.stack([weights_of(c), across_core(weights_of(1 - c))])
-    gathered = gather_chips(w)
     other_routes = across_core(routes)
     both_routes = jnp.where(
         first_core,
@@ -506,30 +492,31 @@
         return lax.dynamic_slice_in_dim(prefix_cache, h * 2 * H, 2 * H, 1)
 
     cache = jnp.stack([cache_of(c), across_core(cache_of(1 - c))])
-    cache_out, gathered[1] = tie(cache, gathered[1])
+    cache_out, gathered[2] = tie(cache, gathered[2])
     caches = [cache, across_x(cache_out)]
 
     token_src = [lax.rem(z + 4 - dz, 4) * 2 + (xh ^ s) for dz in range(4) for s in range(2)]
-    normed = normalise(table(token_src), norm_gain.reshape(8, 1, 256), blocks)
+    places = [lax.rem(lax.rem(v, 4) + 4 - y, 4) * 2 + (v // 4 ^ xl) for v in token_src]
+    normed = normalise(table(token_src + places), norm_gain.reshape(8, 1, 256), blocks)
+    out_early, gathered[7] = tie(out_weight, gathered[7])
+    o_ym, o_yp, o_a = along_y(out_early, 3), along_y(out_early, 1), across_x(out_early)
     q, kv, gates = project(
-        table(chips + [c]),
-        both_routes,
-        router.reshape(8, 2, H, E),
-        normed,
-        across_core(normed),
-        gathered,
+        table(chips + [c]), both_routes, router.T, normed, across_core(normed), gathered
     )
-    out_weight, q = tie(out_weight, q)
-    out_blocks = gather_chips(out_weight.reshape(2, 1024, H))
-
     kvs = [kv, across_x(kv)]
-    qs = [q] + [along_y(q, k) for k in (1, 2, 3)]
+    q_out, o_a, o_ym, o_yp = lax.optimization_barrier((q, o_a, o_ym, o_yp))
+    qs = [q] + [along_y(q_out, k) for k in (1, 2, 3)]
+    out_late, o_a_late, qs[2] = lax.optimization_barrier((out_weight, o_a, qs[2]))
+    o_far, o_am, o_ap = along_y(out_late, 2), along_y(o_a_late, 3), along_y(o_a_late, 1)
+
     firsts = [(xl * 4 + lax.rem(y + 4 - k, 4)) * 512 for k in range(4)]
     mine, partner = xl * 4 + y, (1 - xl) * 4 + y
     at = [c] + firsts + [mine * 1536, partner * 1536, mine * 512, partner * 512]
     parts = list(attend(table(at), suffix_lengths, prefix_lengths, qs, caches, kvs))
+    parts[1:], o_far, o_am, o_ap = lax.optimization_barrier((parts[1:], o_far, o_am, o_ap))
     for k in range(1, 4):
         parts[k] = along_y(parts[k], 4 - k)
+    out_blocks = [out_weight, o_a, o_ym, o_am, o_far, across_x(o_far), o_yp, o_ap]
     gate_row = gates.reshape(2, 256, 2).transpose(0, 2, 1).reshape(1, 1024)
     attended = combine(gate_row, parts)
 

time: 184 us -> 188 us (1.022)
  waiting for transfers between devices: 65.8 us -> 88.5 us
  local copies, waits for them, and re-layouts: 16.2 us -> 4.23 us
  starting transfers between devices: 61.4 us -> 56.7 us
  Pallas kernels: 37.9 us -> 33.8 us
    ppermute x18 -> x21, waiting for transfers between devices: 14.8 us -> 36 us  [along_y(): return lax.ppermute(x, 'y', [(i, (i + k) % 4) for i in range(4)])]
    ppermute x6, starting transfers between devices: 23.6 us -> 7.74 us  [across_core(): return lax.ppermute(x, 'c', [(0, 1), (1, 0)])]
    unnamed x39 -> x48, local copies, waits for them, and re-layouts: 9.39 us -> 1.38 us
    ppermute x18 -> x21, starting transfers between devices: 22.7 us -> 28.6 us  [along_y(): return lax.ppermute(x, 'y', [(i, (i + k) % 4) for i in range(4)])]
    pallas_call x1, Pallas kernels: 10.8 us -> 7.4 us  [project(): pl.pallas_call(project_kernel, out_shape=(jax.ShapeDtypeStruct((1024, H),...]
    squeeze x4 -> x0, local copies, waits for them, and re-layouts: 3.19 us -> none  [gather_chips(): far0, far1 = (along_y(yp[0], 1), along_y(ym[1], 3))]
    ppermute x8, waiting for transfers between devices: 24.1 us -> 26.9 us  [across_x(): return lax.ppermute(x, 'xl', [(0, 1), (1, 0)])]
    ppermute x8, starting transfers between devices: 4.1 us -> 6.9 us  [across_x(): return lax.ppermute(x, 'xl', [(0, 1), (1, 0)])]
  transfers between devices with their start and end apart: 40 -> 43, of which waited for: 18 -> 24; matrix products, arithmetic and copies ran while one was open for 3% -> 2% of each run, Pallas kernels for 18% -> 14%
where the time goes in v2:
time: 188 us; the launch traced here: 186 us
  waiting for transfers between devices  88.5 us (47%)
  starting transfers between devices  56.7 us (30%)
  Pallas kernels  33.8 us (18%)
  local copies, waits for them, and re-layouts  4.23 us (2%)
  other arithmetic  2.47 us (1%)
    ppermute x21, waiting for transfers between devices, along_y(): return lax.ppermute(x, 'y', [(i, (i + k) % 4) for i in range(4)])  36 us
    ppermute x21, starting transfers between devices, along_y(): return lax.ppermute(x, 'y', [(i, (i + k) % 4) for i in range(4)])  28.6 us
    ppermute x8, waiting for transfers between devices, across_x(): return lax.ppermute(x, 'xl', [(0, 1), (1, 0)])  26.9 us
    pallas_call x1, Pallas kernels, attend(): pl.pallas_call(attend_kernel, out_shape=tuple((jax.ShapeDtypeStruct((H +...  17.6 us
    ppermute x6, waiting for transfers between devices, along_z(): return lax.ppermute(x, 'z', [(i, (i + k) % 4) for i in range(4)])  16.7 us
    ppermute x6, starting transfers between devices, along_z(): return lax.ppermute(x, 'z', [(i, (i + k) % 4) for i in range(4)])  9.46 us
    ppermute x6, starting transfers between devices, across_core(): return lax.ppermute(x, 'c', [(0, 1), (1, 0)])  7.74 us
    pallas_call x1, Pallas kernels, project(): pl.pallas_call(project_kernel, out_shape=(jax.ShapeDtypeStruct((1024, H),...  7.4 us
  transfers between devices with their start and end apart: 43, of which 24 were waited for; matrix products, arithmetic and copies ran while one was open for 2% of the time, Pallas kernels for 14%

profile of v2, /device:TPU:3, one launch (start us, length us, event | category | flops | bytes accessed | tf_op | source)
XLA Modules:
  0.0 186.1 jit_solution(438022403461535205)
XLA Ops:
  0.7 1.8 collective-permute-start.1
  4.5 3.0 %collective-permute-done.1 = bf16[256,256]{1,0:T(8,128)(2,1)S(1)} collective-permute-done((bf16[256,256]{1,0:T(8,128)(2,1)}, bf16[256,256]{1,0:T(8,128)(2,1)S(1)}, u32[]{:S(2)}, u32[]{:S(2)}) %collective-permute-start.1) | collective-permute-done | bytes 131104 | tf_op jit(solution)/shard_map/ppermute | solution.py:49
  7.6 1.7 collective-permute-start.2
  9.3 3.3 %collective-permute-start.3 = (bf16[2,256,256]{2,1,0:T(8,128)(2,1)S(1)}, bf16[2,256,256]{2,1,0:T(8,128)(2,1)S(1)}, u32[]{:S(2)}, u32[]{:S(2)}) collective-permute-start(bf16[2,256,256]{2,1,0:T(8,128)(2,1)S(1)} %pad_maximum_fusion.3.b0), channel_id=1, source_target_pairs={{0,4},{2,6},{4,0},{6,2},{1,5},{3,7},{5,1},{7,3},{8,12},{10,14},{12... | collective-permute-start | bytes 786440 | tf_op jit(solution)/shard_map/ppermute | solution.py:41
  17.3 2.7 %collective-permute-start.10 = (bf16[1280,128]{1,0:T(8,128)(2,1)}, bf16[1280,128]{1,0:T(8,128)(2,1)}, u32[]{:S(2)}, u32[]{:S(2)}) collective-permute-start(bf16[1280,128]{1,0:T(8,128)(2,1)} %pad_maximum_fusion.1.refs_0_), channel_id=1, source_target_pairs={{0,48},{16,0},{32,16},{48,32},{1,49},{17,1},{33,17},{49,33},{2,50}... | collective-permute-start | bytes 983048 | tf_op jit(solution)/shard_map/ppermute | solution.py:37
  20.0 3.7 %collective-permute-done.3.b2 = bf16[2,256,256]{2,1,0:T(8,128)(2,1)S(1)} collective-permute-done((bf16[2,256,256]{2,1,0:T(8,128)(2,1)S(1)}, bf16[2,256,256]{2,1,0:T(8,128)(2,1)S(1)}, u32[]{:S(2)}, u32[]{:S(2)}) %collective-permute-start.3) | collective-permute-done | bytes 262176 | tf_op jit(solution)/shard_map/ppermute | solution.py:41
  25.1 2.0 %collective-permute-start.7 = (bf16[768,256]{1,0:T(8,128)(2,1)S(1)}, bf16[768,256]{1,0:T(8,128)(2,1)S(1)}, u32[]{:S(2)}, u32[]{:S(2)}) collective-permute-start(bf16[768,256]{1,0:T(8,128)(2,1)S(1)} %get-tuple-element.62), channel_id=1, source_target_pairs={{0,8},{8,0},{1,9},{9,1},{2,10},{10,2},{3,11},{11,3},{4,12},{12,4},... | collective-permute-start | bytes 1179656 | tf_op jit(solution)/shard_map/ppermute | solution.py:53
  34.4 4.9 %collective-permute-done.9.refs_3_ = bf16[1280,128]{1,0:T(8,128)(2,1)} collective-permute-done((bf16[1280,128]{1,0:T(8,128)(2,1)}, bf16[1280,128]{1,0:T(8,128)(2,1)}, u32[]{:S(2)}, u32[]{:S(2)}) %collective-permute-start.9) | collective-permute-done | bytes 327712 | tf_op jit(solution)/shard_map/ppermute | solution.py:45
  42.0 4.3 %collective-permute-done.12.refs_6_ = bf16[1280,128]{1,0:T(8,128)(2,1)S(1)} collective-permute-done((bf16[1280,128]{1,0:T(8,128)(2,1)}, bf16[1280,128]{1,0:T(8,128)(2,1)S(1)}, u32[]{:S(2)}, u32[]{:S(2)}) %collective-permute-start.12) | collective-permute-done | bytes 327712 | tf_op jit(solution)/shard_map/ppermute | solution.py:37
  46.3 2.5 %collective-permute-start.16 = (bf16[1280,128]{1,0:T(8,128)(2,1)}, bf16[1280,128]{1,0:T(8,128)(2,1)}, u32[]{:S(2)}, u32[]{:S(2)}) collective-permute-start(bf16[1280,128]{1,0:T(8,128)(2,1)} %collective-permute-done.11.refs_5_), channel_id=1, source_target_pairs={{0,48},{16,0},{32,16},{48,32},{1,49},{17,1},{33,17},{49,33},{2,50}... | collective-permute-start | bytes 983048 | tf_op jit(solution)/shard_map/ppermute | solution.py:37
  50.7 2.6 %collective-permute-done.13.refs_7_ = bf16[1280,128]{1,0:T(8,128)(2,1)} collective-permute-done((bf16[1280,128]{1,0:T(8,128)(2,1)}, bf16[1280,128]{1,0:T(8,128)(2,1)}, u32[]{:S(2)}, u32[]{:S(2)}) %collective-permute-start.13) | collective-permute-done | bytes 327712 | tf_op jit(solution)/shard_map/ppermute | solution.py:37
  54.5 5.8 %collective-permute-done.16.refs_9_ = bf16[1280,128]{1,0:T(8,128)(2,1)} collective-permute-done((bf16[1280,128]{1,0:T(8,128)(2,1)}, bf16[1280,128]{1,0:T(8,128)(2,1)}, u32[]{:S(2)}, u32[]{:S(2)}) %collective-permute-start.16) | collective-permute-done | bytes 327712 | tf_op jit(solution)/shard_map/ppermute | solution.py:37
  63.2 1.8 collective-permute-done.21.refs_15_
  65.8 2.6 %collective-permute-done.18.refs_11_ = bf16[1280,128]{1,0:T(8,128)(2,1)S(1)} collective-permute-done((bf16[1280,128]{1,0:T(8,128)(2,1)}, bf16[1280,128]{1,0:T(8,128)(2,1)S(1)}, u32[]{:S(2)}, u32[]{:S(2)}) %collective-permute-start.18) | collective-permute-done | bytes 327712 | tf_op jit(solution)/shard_map/ppermute | solution.py:45
  69.8 7.4 %project.1 = (bf16[1024,128]{1,0:T(8,128)(2,1)S(1)}, bf16[512,256]{1,0:T(8,128)(2,1)S(1)}, f32[512,2]{1,0:T(8,128)S(1)}) custom-call(s32[9]{0:T(128)S(1)} %stack.169.idx, s32[512,2]{1,0:T(8,128)S(1)} %broadcast_select_fusion.routes, bf16[8,2048]{1,0:T(8,128)(2,1)S(1)} %bitcast.50, bf16[256,2048]{1,0:T(8,128)(2,1)} %copy-done, ...), custom_call_target="tpu_custom_call" | custom-call | flops 6442450944 | bytes 8388608 | tf_op jit(solution)/shard_map/project/pallas_call | solution.py:182
  77.2 19.4 %collective-permute-done.22.refs_1_ = bf16[2048,128]{1,0:T(8,128)(2,1)} collective-permute-done((bf16[2048,128]{1,0:T(8,128)(2,1)}, bf16[2048,128]{1,0:T(8,128)(2,1)}, u32[]{:S(2)}, u32[]{:S(2)}) %collective-permute-start.22) | collective-permute-done | bytes 524320 | tf_op jit(solution)/shard_map/ppermute | solution.py:45
  96.7 2.7 %collective-permute-start.26 = (bf16[1024,128]{1,0:T(8,128)(2,1)S(1)}, bf16[1024,128]{1,0:T(8,128)(2,1)S(1)}, u32[]{:S(2)}, u32[]{:S(2)}) collective-permute-start(bf16[1024,128]{1,0:T(8,128)(2,1)S(1)} %get-tuple-element.38.q0), channel_id=1, source_target_pairs={{0,32},{16,48},{32,0},{48,16},{1,33},{17,49},{33,1},{49,17},{2,34}... | collective-permute-start | bytes 786440 | tf_op jit(solution)/shard_map/ppermute | solution.py:37
  101.1 2.1 %collective-permute-start.27 = (bf16[1024,128]{1,0:T(8,128)(2,1)S(1)}, bf16[1024,128]{1,0:T(8,128)(2,1)}, u32[]{:S(2)}, u32[]{:S(2)}) collective-permute-start(bf16[1024,128]{1,0:T(8,128)(2,1)S(1)} %get-tuple-element.38.q0), channel_id=1, source_target_pairs={{0,48},{16,0},{32,16},{48,32},{1,49},{17,1},{33,17},{49,33},{2,50}... | collective-permute-start | bytes 786440 | tf_op jit(solution)/shard_map/ppermute | solution.py:37
  103.9 2.6 %collective-permute-start.31 = (bf16[2048,128]{1,0:T(8,128)(2,1)}, bf16[2048,128]{1,0:T(8,128)(2,1)S(1)}, u32[]{:S(2)}, u32[]{:S(2)}) collective-permute-start(bf16[2048,128]{1,0:T(8,128)(2,1)} %collective-permute-done.22.refs_1_), channel_id=1, source_target_pairs={{0,48},{16,0},{32,16},{48,32},{1,49},{17,1},{33,17},{49,33},{2,50}... | collective-permute-start | bytes 1572872 | tf_op jit(solution)/shard_map/ppermute | solution.py:37
  108.0 2.8 %collective-permute-done.25.q1 = bf16[1024,128]{1,0:T(8,128)(2,1)} collective-permute-done((bf16[1024,128]{1,0:T(8,128)(2,1)S(1)}, bf16[1024,128]{1,0:T(8,128)(2,1)}, u32[]{:S(2)}, u32[]{:S(2)}) %collective-permute-start.25) | collective-permute-done | bytes 262176 | tf_op jit(solution)/shard_map/ppermute | solution.py:37
  110.9 17.6 %attend.1 = (bf16[144,1024]{1,0:T(8,128)(2,1)S(1)}, bf16[144,1024]{1,0:T(8,128)(2,1)S(1)}, bf16[144,1024]{1,0:T(8,128)(2,1)S(1)}, bf16[144,1024]{1,0:T(8,128)(2,1)S(1)}) custom-call(s32[9]{0:T(128)S(1)} %stack.195.idx, s32[4]{0:T(128)S(1)} %copy-done.4, s32[4]{0:T(128)S(1)} %copy-done.5, bf16[1024,128]{1,0:T(8,128)(2,1)} %copy-done.1, ...), custom_call_target="tpu_custom_call" | custom-call | flops 12884901888 | bytes 6291456 | tf_op jit(solution)/shard_map/attend/pallas_call | solution.py:345
  128.5 2.5 %collective-permute-done.30.refs_4_ = bf16[2048,128]{1,0:T(8,128)(2,1)} collective-permute-done((bf16[2048,128]{1,0:T(8,128)(2,1)}, bf16[2048,128]{1,0:T(8,128)(2,1)}, u32[]{:S(2)}, u32[]{:S(2)}) %collective-permute-start.30) | collective-permute-done | bytes 524320 | tf_op jit(solution)/shard_map/ppermute | solution.py:37
  131.1 3.7 %collective-permute-start.33 = (bf16[144,1024]{1,0:T(8,128)(2,1)S(1)}, bf16[144,1024]{1,0:T(8,128)(2,1)S(1)}, u32[]{:S(2)}, u32[]{:S(2)}) collective-permute-start(bf16[144,1024]{1,0:T(8,128)(2,1)S(1)} %get-tuple-element.49), channel_id=1, source_target_pairs={{0,48},{16,0},{32,16},{48,32},{1,49},{17,1},{33,17},{49,33},{2,50}... | collective-permute-start | bytes 884744 | tf_op jit(solution)/shard_map/ppermute | solution.py:37
  137.1 4.0 %collective-permute-done.33.p1 = bf16[144,1024]{1,0:T(8,128)(2,1)S(1)} collective-permute-done((bf16[144,1024]{1,0:T(8,128)(2,1)S(1)}, bf16[144,1024]{1,0:T(8,128)(2,1)S(1)}, u32[]{:S(2)}, u32[]{:S(2)}) %collective-permute-start.33) | collective-permute-done | bytes 294944 | tf_op jit(solution)/shard_map/ppermute | solution.py:37
  141.9 8.6 %collective-permute-done.35.p3 = bf16[144,1024]{1,0:T(8,128)(2,1)S(1)} collective-permute-done((bf16[144,1024]{1,0:T(8,128)(2,1)S(1)}, bf16[144,1024]{1,0:T(8,128)(2,1)S(1)}, u32[]{:S(2)}, u32[]{:S(2)}) %collective-permute-start.35) | collective-permute-done | bytes 294944 | tf_op jit(solution)/shard_map/ppermute | solution.py:37
  150.8 1.8 collective-permute-start.36
  153.8 7.1 %project_out.1 = (f32[2,512,128]{2,1,0:T(8,128)S(1)}, bf16[2,512,128]{2,1,0:T(8,128)(2,1)S(1)}, bf16[2,512,128]{2,1,0:T(8,128)(2,1)S(1)}, bf16[2,512,128]{2,1,0:T(8,128)(2,1)S(1)}) custom-call(s32[17]{0:T(128)S(1)} %stack.168.idx, s32[512,2]{1,0:T(8,128)S(1)} %broadcast_select_fusion.routes, bf16[1024,128]{1,0:T(8,128)(2,1)S(1)} %combine.1.own, ...), custom_call_target="tpu_custom_call" | custom-call | flops 4294967296 | bytes 6291456 | tf_op jit(solution)/shard_map/project_out/pallas_call | solution.py:437
  161.4 2.5 %collective-permute-start.39 = (bf16[2,512,128]{2,1,0:T(8,128)(2,1)S(1)}, bf16[2,512,128]{2,1,0:T(8,128)(2,1)S(1)}, u32[]{:S(2)}, u32[]{:S(2)}) collective-permute-start(bf16[2,512,128]{2,1,0:T(8,128)(2,1)S(1)} %get-tuple-element.59), channel_id=1, source_target_pairs={{0,4},{2,6},{4,0},{6,2},{1,5},{3,7},{5,1},{7,3},{8,12},{10,14},{12... | collective-permute-start | bytes 786440 | tf_op jit(solution)/shard_map/ppermute | solution.py:41
  164.7 3.9 %collective-permute-done.40 = bf16[2,512,128]{2,1,0:T(8,128)(2,1)S(1)} collective-permute-done((bf16[2,512,128]{2,1,0:T(8,128)(2,1)S(1)}, bf16[2,512,128]{2,1,0:T(8,128)(2,1)S(1)}, u32[]{:S(2)}, u32[]{:S(2)}) %collective-permute-start.40) | collective-permute-done | bytes 262176 | tf_op jit(solution)/shard_map/ppermute | solution.py:41
  170.1 6.6 %collective-permute-done.38 = bf16[2,512,128]{2,1,0:T(8,128)(2,1)S(1)} collective-permute-done((bf16[2,512,128]{2,1,0:T(8,128)(2,1)S(1)}, bf16[2,512,128]{2,1,0:T(8,128)(2,1)S(1)}, u32[]{:S(2)}, u32[]{:S(2)}) %collective-permute-start.38) | collective-permute-done | bytes 262176 | tf_op jit(solution)/shard_map/ppermute | solution.py:41
  176.8 2.2 %collective-permute-start.41 = (bf16[512,128]{1,0:T(8,128)(2,1)S(1)}, bf16[512,128]{1,0:T(8,128)(2,1)S(1)}, u32[]{:S(2)}, u32[]{:S(2)}) collective-permute-start(bf16[512,128]{1,0:T(8,128)(2,1)S(1)} %fusion.1), channel_id=1, source_target_pairs={{0,1},{1,0},{2,3},{3,2},{4,5},{5,4},{6,7},{7,6},{8,9},{9,8},{10,11... | collective-permute-start | bytes 393224 | tf_op jit(solution)/shard_map/ppermute | solution.py:49
  179.1 3.9 %collective-permute-done.41 = bf16[512,128]{1,0:T(8,128)(2,1)S(1)} collective-permute-done((bf16[512,128]{1,0:T(8,128)(2,1)S(1)}, bf16[512,128]{1,0:T(8,128)(2,1)S(1)}, u32[]{:S(2)}, u32[]{:S(2)}) %collective-permute-start.41) | collective-permute-done | bytes 131104 | tf_op jit(solution)/shard_map/ppermute | solution.py:49
  (130 shorter events, 41.3 us)
Async XLA Ops:
  0.0 16.2 %collective-permute-start = (s32[256,2]{0,1:T(2,128)}, s32[256,2]{0,1:T(2,128)S(1)}, u32[]{:S(2)}, u32[]{:S(2)}) collective-permute-start(s32[256,2]{0,1:T(2,128)} %param.13), channel_id=1, source_target_pairs={{0,8},{8,0},{1,9},{9,1},{2,10},{10,2},{3,11},{11,3},{4,12},{12,4},... | collective-permute-start | bytes 6152 | tf_op jit(solution)/shard_map/ppermute | solution.py:53
  7.6 9.7 %collective-permute-start.2 = (bf16[2,256,256]{2,1,0:T(8,128)(2,1)S(1)}, bf16[2,256,256]{2,1,0:T(8,128)(2,1)S(1)}, u32[]{:S(2)}, u32[]{:S(2)}) collective-permute-start(bf16[2,256,256]{2,1,0:T(8,128)(2,1)S(1)} %pad_maximum_fusion.3.b0), channel_id=1, source_target_pairs={{0,2},{2,4},{4,6},{6,0},{1,3},{3,5},{5,7},{7,1},{8,10},{10,12},{12... | collective-permute-start | bytes 786440 | tf_op jit(solution)/shard_map/ppermute | solution.py:41
  9.3 14.5 %collective-permute-start.3 = (bf16[2,256,256]{2,1,0:T(8,128)(2,1)S(1)}, bf16[2,256,256]{2,1,0:T(8,128)(2,1)S(1)}, u32[]{:S(2)}, u32[]{:S(2)}) collective-permute-start(bf16[2,256,256]{2,1,0:T(8,128)(2,1)S(1)} %pad_maximum_fusion.3.b0), channel_id=1, source_target_pairs={{0,4},{2,6},{4,0},{6,2},{1,5},{3,7},{5,1},{7,3},{8,12},{10,14},{12... | collective-permute-start | bytes 786440 | tf_op jit(solution)/shard_map/ppermute | solution.py:41
  13.3 16.0 %collective-permute-start.6 = (bf16[1280,128]{1,0:T(8,128)(2,1)}, bf16[1280,128]{1,0:T(8,128)(2,1)}, u32[]{:S(2)}, u32[]{:S(2)}) collective-permute-start(bf16[1280,128]{1,0:T(8,128)(2,1)} %pad_maximum_fusion.2), channel_id=1, source_target_pairs={{0,8},{8,0},{1,9},{9,1},{2,10},{10,2},{3,11},{11,3},{4,12},{12,4},... | collective-permute-start | bytes 983048 | tf_op jit(solution)/shard_map/ppermute | solution.py:53
  14.7 10.5 %collective-permute-start.4 = (bf16[2,256,256]{2,1,0:T(8,128)(2,1)S(1)}, bf16[2,256,256]{2,1,0:T(8,128)(2,1)S(1)}, u32[]{:S(2)}, u32[]{:S(2)}) collective-permute-start(bf16[2,256,256]{2,1,0:T(8,128)(2,1)S(1)} %pad_maximum_fusion.3.b0), channel_id=1, source_target_pairs={{0,6},{2,0},{4,2},{6,4},{1,7},{3,1},{5,3},{7,5},{8,14},{10,8},{12,... | collective-permute-start | bytes 786440 | tf_op jit(solution)/shard_map/ppermute | solution.py:41
  16.2 13.6 %collective-permute-start.8 = (bf16[1280,128]{1,0:T(8,128)(2,1)}, bf16[1280,128]{1,0:T(8,128)(2,1)}, u32[]{:S(2)}, u32[]{:S(2)}) collective-permute-start(bf16[1280,128]{1,0:T(8,128)(2,1)} %pad_maximum_fusion.1.refs_0_), channel_id=1, source_target_pairs={{0,64},{64,0},{1,65},{65,1},{2,66},{66,2},{3,67},{67,3},{4,68},{68... | collective-permute-start | bytes 983048 | tf_op jit(solution)/shard_map/ppermute | solution.py:45
  17.3 12.8 %collective-permute-start.10 = (bf16[1280,128]{1,0:T(8,128)(2,1)}, bf16[1280,128]{1,0:T(8,128)(2,1)}, u32[]{:S(2)}, u32[]{:S(2)}) collective-permute-start(bf16[1280,128]{1,0:T(8,128)(2,1)} %pad_maximum_fusion.1.refs_0_), channel_id=1, source_target_pairs={{0,48},{16,0},{32,16},{48,32},{1,49},{17,1},{33,17},{49,33},{2,50}... | collective-permute-start | bytes 983048 | tf_op jit(solution)/shard_map/ppermute | solution.py:37
  23.8 9.2 %collective-permute-start.14 = (bf16[1280,128]{1,0:T(8,128)(2,1)}, bf16[1280,128]{1,0:T(8,128)(2,1)}, u32[]{:S(2)}, u32[]{:S(2)}) collective-permute-start(bf16[1280,128]{1,0:T(8,128)(2,1)} %pad_maximum_fusion.1.refs_0_), channel_id=1, source_target_pairs={{0,16},{16,32},{32,48},{48,0},{1,17},{17,33},{33,49},{49,1},{2,18}... | collective-permute-start | bytes 983048 | tf_op jit(solution)/shard_map/ppermute | solution.py:37
  25.1 9.2 %collective-permute-start.7 = (bf16[768,256]{1,0:T(8,128)(2,1)S(1)}, bf16[768,256]{1,0:T(8,128)(2,1)S(1)}, u32[]{:S(2)}, u32[]{:S(2)}) collective-permute-start(bf16[768,256]{1,0:T(8,128)(2,1)S(1)} %get-tuple-element.62), channel_id=1, source_target_pairs={{0,8},{8,0},{1,9},{9,1},{2,10},{10,2},{3,11},{11,3},{4,12},{12,4},... | collective-permute-start | bytes 1179656 | tf_op jit(solution)/shard_map/ppermute | solution.py:53
  29.3 40.4 %collective-permute-start.5 = (bf16[256,2048]{1,0:T(8,128)(2,1)S(1)}, bf16[256,2048]{1,0:T(8,128)(2,1)}, u32[]{:S(2)}, u32[]{:S(2)}) collective-permute-start(bf16[256,2048]{1,0:T(8,128)(2,1)S(1)} %normalise.1.own), channel_id=1, source_target_pairs={{0,8},{8,0},{1,9},{9,1},{2,10},{10,2},{3,11},{11,3},{4,12},{12,4},... | collective-permute-start | bytes 3145736 | tf_op jit(solution)/shard_map/ppermute | solution.py:53
  29.8 9.5 %collective-permute-start.9 = (bf16[1280,128]{1,0:T(8,128)(2,1)}, bf16[1280,128]{1,0:T(8,128)(2,1)}, u32[]{:S(2)}, u32[]{:S(2)}) collective-permute-start(bf16[1280,128]{1,0:T(8,128)(2,1)} %collective-permute-done.6.refs_1_), channel_id=1, source_target_pairs={{0,64},{64,0},{1,65},{65,1},{2,66},{66,2},{3,67},{67,3},{4,68},{68... | collective-permute-start | bytes 983048 | tf_op jit(solution)/shard_map/ppermute | solution.py:45
  30.1 10.5 %collective-permute-start.11 = (bf16[1280,128]{1,0:T(8,128)(2,1)}, bf16[1280,128]{1,0:T(8,128)(2,1)}, u32[]{:S(2)}, u32[]{:S(2)}) collective-permute-start(bf16[1280,128]{1,0:T(8,128)(2,1)} %collective-permute-done.6.refs_1_), channel_id=1, source_target_pairs={{0,48},{16,0},{32,16},{48,32},{1,49},{17,1},{33,17},{49,33},{2,50}... | collective-permute-start | bytes 983048 | tf_op jit(solution)/shard_map/ppermute | solution.py:37
  33.0 13.3 %collective-permute-start.12 = (bf16[1280,128]{1,0:T(8,128)(2,1)}, bf16[1280,128]{1,0:T(8,128)(2,1)S(1)}, u32[]{:S(2)}, u32[]{:S(2)}) collective-permute-start(bf16[1280,128]{1,0:T(8,128)(2,1)} %collective-permute-done.8.refs_2_), channel_id=1, source_target_pairs={{0,48},{16,0},{32,16},{48,32},{1,49},{17,1},{33,17},{49,33},{2,50}... | collective-permute-start | bytes 983048 | tf_op jit(solution)/shard_map/ppermute | solution.py:37
  34.4 15.4 %collective-permute-start.15 = (bf16[1280,128]{1,0:T(8,128)(2,1)}, bf16[1280,128]{1,0:T(8,128)(2,1)}, u32[]{:S(2)}, u32[]{:S(2)}) collective-permute-start(bf16[1280,128]{1,0:T(8,128)(2,1)} %collective-permute-done.14.refs_12_), channel_id=1, source_target_pairs={{0,16},{16,32},{32,48},{48,0},{1,17},{17,33},{33,49},{49,1},{2,18}... | collective-permute-start | bytes 983048 | tf_op jit(solution)/shard_map/ppermute | solution.py:37
  39.3 11.2 %collective-permute-start.19 = (bf16[1280,128]{1,0:T(8,128)(2,1)}, bf16[1280,128]{1,0:T(8,128)(2,1)S(1)}, u32[]{:S(2)}, u32[]{:S(2)}) collective-permute-start(bf16[1280,128]{1,0:T(8,128)(2,1)} %collective-permute-done.6.refs_1_), channel_id=1, source_target_pairs={{0,16},{16,32},{32,48},{48,0},{1,17},{17,33},{33,49},{49,1},{2,18}... | collective-permute-start | bytes 983048 | tf_op jit(solution)/shard_map/ppermute | solution.py:37
  40.6 12.7 %collective-permute-start.13 = (bf16[1280,128]{1,0:T(8,128)(2,1)}, bf16[1280,128]{1,0:T(8,128)(2,1)}, u32[]{:S(2)}, u32[]{:S(2)}) collective-permute-start(bf16[1280,128]{1,0:T(8,128)(2,1)} %collective-permute-done.9.refs_3_), channel_id=1, source_target_pairs={{0,48},{16,0},{32,16},{48,32},{1,49},{17,1},{33,17},{49,33},{2,50}... | collective-permute-start | bytes 983048 | tf_op jit(solution)/shard_map/ppermute | solution.py:37
  46.3 14.0 %collective-permute-start.16 = (bf16[1280,128]{1,0:T(8,128)(2,1)}, bf16[1280,128]{1,0:T(8,128)(2,1)}, u32[]{:S(2)}, u32[]{:S(2)}) collective-permute-start(bf16[1280,128]{1,0:T(8,128)(2,1)} %collective-permute-done.11.refs_5_), channel_id=1, source_target_pairs={{0,48},{16,0},{32,16},{48,32},{1,49},{17,1},{33,17},{49,33},{2,50}... | collective-permute-start | bytes 983048 | tf_op jit(solution)/shard_map/ppermute | solution.py:37
  49.7 11.9 %collective-permute-start.20 = (bf16[1280,128]{1,0:T(8,128)(2,1)}, bf16[1280,128]{1,0:T(8,128)(2,1)S(1)}, u32[]{:S(2)}, u32[]{:S(2)}) collective-permute-start(bf16[1280,128]{1,0:T(8,128)(2,1)} %collective-permute-done.8.refs_2_), channel_id=1, source_target_pairs={{0,16},{16,32},{32,48},{48,0},{1,17},{17,33},{33,49},{49,1},{2,18}... | collective-permute-start | bytes 983048 | tf_op jit(solution)/shard_map/ppermute | solution.py:37
  50.5 14.6 %collective-permute-start.21 = (bf16[1280,128]{1,0:T(8,128)(2,1)}, bf16[1280,128]{1,0:T(8,128)(2,1)S(1)}, u32[]{:S(2)}, u32[]{:S(2)}) collective-permute-start(bf16[1280,128]{1,0:T(8,128)(2,1)} %collective-permute-done.9.refs_3_), channel_id=1, source_target_pairs={{0,16},{16,32},{32,48},{48,0},{1,17},{17,33},{33,49},{49,1},{2,18}... | collective-permute-start | bytes 983048 | tf_op jit(solution)/shard_map/ppermute | solution.py:37
  61.7 44.8 %collective-permute-start.28 = (bf16[2,768,256]{2,1,0:T(8,128)(2,1)S(1)}, bf16[2,768,256]{2,1,0:T(8,128)(2,1)S(1)}, u32[]{:S(2)}, u32[]{:S(2)}) collective-permute-start(bf16[2,768,256]{2,1,0:T(8,128)(2,1)S(1)} %pad_maximum_fusion.cache0), channel_id=1, source_target_pairs={{0,64},{64,0},{1,65},{65,1},{2,66},{66,2},{3,67},{67,3},{4,68},{68... | collective-permute-start | bytes 2359304 | tf_op jit(solution)/shard_map/ppermute | solution.py:45
  62.0 34.6 %collective-permute-start.22 = (bf16[2048,128]{1,0:T(8,128)(2,1)}, bf16[2048,128]{1,0:T(8,128)(2,1)}, u32[]{:S(2)}, u32[]{:S(2)}) collective-permute-start(bf16[2048,128]{1,0:T(8,128)(2,1)} %refs_0_.1), channel_id=1, source_target_pairs={{0,64},{64,0},{1,65},{65,1},{2,66},{66,2},{3,67},{67,3},{4,68},{68... | collective-permute-start | bytes 1572872 | tf_op jit(solution)/shard_map/ppermute | solution.py:45
  65.1 31.6 %collective-permute-start.23 = (bf16[2048,128]{1,0:T(8,128)(2,1)}, bf16[2048,128]{1,0:T(8,128)(2,1)S(1)}, u32[]{:S(2)}, u32[]{:S(2)}) collective-permute-start(bf16[2048,128]{1,0:T(8,128)(2,1)} %refs_0_.1), channel_id=1, source_target_pairs={{0,48},{16,0},{32,16},{48,32},{1,49},{17,1},{33,17},{49,33},{2,50}... | collective-permute-start | bytes 1572872 | tf_op jit(solution)/shard_map/ppermute | solution.py:37
  68.4 28.2 %collective-permute-start.24 = (bf16[2048,128]{1,0:T(8,128)(2,1)}, bf16[2048,128]{1,0:T(8,128)(2,1)S(1)}, u32[]{:S(2)}, u32[]{:S(2)}) collective-permute-start(bf16[2048,128]{1,0:T(8,128)(2,1)} %refs_0_.1), channel_id=1, source_target_pairs={{0,16},{16,32},{32,48},{48,0},{1,17},{17,33},{33,49},{49,1},{2,18}... | collective-permute-start | bytes 1572872 | tf_op jit(solution)/shard_map/ppermute | solution.py:37
  100.6 10.3 %collective-permute-start.25 = (bf16[1024,128]{1,0:T(8,128)(2,1)S(1)}, bf16[1024,128]{1,0:T(8,128)(2,1)}, u32[]{:S(2)}, u32[]{:S(2)}) collective-permute-start(bf16[1024,128]{1,0:T(8,128)(2,1)S(1)} %get-tuple-element.38.q0), channel_id=1, source_target_pairs={{0,16},{16,32},{32,48},{48,0},{1,17},{17,33},{33,49},{49,1},{2,18}... | collective-permute-start | bytes 786440 | tf_op jit(solution)/shard_map/ppermute | solution.py:37
  101.1 9.7 %collective-permute-start.27 = (bf16[1024,128]{1,0:T(8,128)(2,1)S(1)}, bf16[1024,128]{1,0:T(8,128)(2,1)}, u32[]{:S(2)}, u32[]{:S(2)}) collective-permute-start(bf16[1024,128]{1,0:T(8,128)(2,1)S(1)} %get-tuple-element.38.q0), channel_id=1, source_target_pairs={{0,48},{16,0},{32,16},{48,32},{1,49},{17,1},{33,17},{49,33},{2,50}... | collective-permute-start | bytes 786440 | tf_op jit(solution)/shard_map/ppermute | solution.py:37
  103.9 27.2 %collective-permute-start.31 = (bf16[2048,128]{1,0:T(8,128)(2,1)}, bf16[2048,128]{1,0:T(8,128)(2,1)S(1)}, u32[]{:S(2)}, u32[]{:S(2)}) collective-permute-start(bf16[2048,128]{1,0:T(8,128)(2,1)} %collective-permute-done.22.refs_1_), channel_id=1, source_target_pairs={{0,48},{16,0},{32,16},{48,32},{1,49},{17,1},{33,17},{49,33},{2,50}... | collective-permute-start | bytes 1572872 | tf_op jit(solution)/shard_map/ppermute | solution.py:37
  106.4 24.6 %collective-permute-start.32 = (bf16[2048,128]{1,0:T(8,128)(2,1)}, bf16[2048,128]{1,0:T(8,128)(2,1)S(1)}, u32[]{:S(2)}, u32[]{:S(2)}) collective-permute-start(bf16[2048,128]{1,0:T(8,128)(2,1)} %collective-permute-done.22.refs_1_), channel_id=1, source_target_pairs={{0,16},{16,32},{32,48},{48,0},{1,17},{17,33},{33,49},{49,1},{2,18}... | collective-permute-start | bytes 1572872 | tf_op jit(solution)/shard_map/ppermute | solution.py:37
  106.5 24.6 %collective-permute-start.30 = (bf16[2048,128]{1,0:T(8,128)(2,1)}, bf16[2048,128]{1,0:T(8,128)(2,1)}, u32[]{:S(2)}, u32[]{:S(2)}) collective-permute-start(bf16[2048,128]{1,0:T(8,128)(2,1)} %refs_0_.1), channel_id=1, source_target_pairs={{0,32},{16,48},{32,0},{48,16},{1,33},{17,49},{33,1},{49,17},{2,34}... | collective-permute-start | bytes 1572872 | tf_op jit(solution)/shard_map/ppermute | solution.py:37
  131.1 10.0 %collective-permute-start.33 = (bf16[144,1024]{1,0:T(8,128)(2,1)S(1)}, bf16[144,1024]{1,0:T(8,128)(2,1)S(1)}, u32[]{:S(2)}, u32[]{:S(2)}) collective-permute-start(bf16[144,1024]{1,0:T(8,128)(2,1)S(1)} %get-tuple-element.49), channel_id=1, source_target_pairs={{0,48},{16,0},{32,16},{48,32},{1,49},{17,1},{33,17},{49,33},{2,50}... | collective-permute-start | bytes 884744 | tf_op jit(solution)/shard_map/ppermute | solution.py:37
  135.2 15.3 %collective-permute-start.35 = (bf16[144,1024]{1,0:T(8,128)(2,1)S(1)}, bf16[144,1024]{1,0:T(8,128)(2,1)S(1)}, u32[]{:S(2)}, u32[]{:S(2)}) collective-permute-start(bf16[144,1024]{1,0:T(8,128)(2,1)S(1)} %get-tuple-element.51), channel_id=1, source_target_pairs={{0,16},{16,32},{32,48},{48,0},{1,17},{17,33},{33,49},{49,1},{2,18}... | collective-permute-start | bytes 884744 | tf_op jit(solution)/shard_map/ppermute | solution.py:37
  135.7 17.0 %collective-permute-start.37 = (bf16[2048,128]{1,0:T(8,128)(2,1)}, bf16[2048,128]{1,0:T(8,128)(2,1)}, u32[]{:S(2)}, u32[]{:S(2)}) collective-permute-start(bf16[2048,128]{1,0:T(8,128)(2,1)} %collective-permute-done.30.refs_4_), channel_id=1, source_target_pairs={{0,64},{64,0},{1,65},{65,1},{2,66},{66,2},{3,67},{67,3},{4,68},{68... | collective-permute-start | bytes 1572872 | tf_op jit(solution)/shard_map/ppermute | solution.py:45
  163.9 12.8 %collective-permute-start.38 = (bf16[2,512,128]{2,1,0:T(8,128)(2,1)S(1)}, bf16[2,512,128]{2,1,0:T(8,128)(2,1)S(1)}, u32[]{:S(2)}, u32[]{:S(2)}) collective-permute-start(bf16[2,512,128]{2,1,0:T(8,128)(2,1)S(1)} %get-tuple-element.58), channel_id=1, source_target_pairs={{0,2},{2,4},{4,6},{6,0},{1,3},{3,5},{5,7},{7,1},{8,10},{10,12},{12... | collective-permute-start | bytes 786440 | tf_op jit(solution)/shard_map/ppermute | solution.py:41
  (35 other events, 305.9 us)

commit v3 on v2

--- a/solution.py
+++ b/solution.py
@@ -57,9 +57,13 @@
     return lax.optimization_barrier((a, b))
 
 
-def gather_parts(w0, w1):
-    ym0, yp0, a0 = along_y(w0, 3), along_y(w0, 1), across_x(w0)
-    ym1, yp1, a1 = along_y(w1, 3), along_y(w1, 1), across_x(w1)
+def first_step(w):
+    return along_y(w, 3), along_y(w, 1), across_x(w)
+
+
+def gather_parts(w0, w1, step0, step1):
+    ym0, yp0, a0 = step0
+    ym1, yp1, a1 = step1
     far0, far1 = along_y(yp0, 1), along_y(ym1, 3)
     am0, ap0 = along_y(a0, 3), along_y(a0, 1)
     am1, ap1 = along_y(a1, 3), along_y(a1, 1)
@@ -397,16 +401,12 @@
     )(gates, *parts)
 
 
-def out_kernel(idx, routes, own, other, *refs):
-    blocks = refs[:8]
-    outs = refs[8:12]
-    held, padded, sem = refs[12:]
+def out_kernel(idx, routes, own, other, blocks, *refs):
+    outs = refs[:4]
+    held, padded, sem = refs[4:]
     core = idx[8]
-    copies = [
-        pltpu.make_async_copy(r, held.at[idx[k]], sem.at[k]) for k, r in enumerate(blocks)
-    ]
-    for c in copies:
-        c.start()
+    copy = pltpu.make_async_copy(blocks, held, sem.at[0])
+    copy.start()
     for side, source in enumerate((own, other)):
         for half in range(2):
             for e in range(E):
@@ -418,15 +418,14 @@
                 padded[side, half * 256 : (half + 1) * 256, e * H : (e + 1) * H] = value.astype(
                     BF16
                 )
-    for c in copies:
-        c.wait()
+    copy.wait()
     for dz in range(4):
         value = jnp.zeros((512, 256), F32)
         for side in range(2):
             head = core if side == 0 else 1 - core
             rows = pl.ds(pl.multiple_of(head * 1024, 1024), 1024)
             w = jnp.concatenate(
-                [held[idx[9 + 2 * dz], rows], held[idx[10 + 2 * dz], rows]], axis=1
+                [held[idx[2 * dz], rows], held[idx[2 * dz + 1], rows]], axis=1
             )
             value += jnp.dot(padded[side], w, preferred_element_type=F32)
         for s in range(2):
@@ -438,17 +437,17 @@
         out_kernel,
         out_shape=(jax.ShapeDtypeStruct((2, 512, H), F32),)
         + tuple(jax.ShapeDtypeStruct((2, 512, H), BF16) for _ in range(3)),
-        in_specs=[SMEM, VMEM, VMEM, VMEM] + [HBM] * 8,
+        in_specs=[SMEM, VMEM, VMEM, VMEM, HBM],
         out_specs=tuple([VMEM] * 4),
         scratch_shapes=[
             pltpu.VMEM((8, 2048, H), BF16),
             pltpu.VMEM((2, 512, 1024), BF16),
-            pltpu.SemaphoreType.DMA((8,)),
+            pltpu.SemaphoreType.DMA((1,)),
         ],
         compiler_params=pltpu.CompilerParams(vmem_limit_bytes=20 << 20),
         cost_estimate=pl.CostEstimate(flops=4 << 30, bytes_accessed=6 << 20, transcendentals=0),
         name="project_out",
-    )(idx, routes, own, other, *pin(blocks))
+    )(idx, routes, own, other, *pin([blocks]))
 
 
 def on_device(
@@ -467,6 +466,7 @@
     z, xh = (lax.axis_index(a) for a in NARROW)
     first_core = c == 0
     chips = chip_order()
+    out_all = lax.all_gather(out_weight, ("xl", "y"), axis=0)
 
     def table(values):
         return jnp.stack([jnp.asarray(v, jnp.int32) for v in values])
@@ -478,9 +478,14 @@
     def weights_of(h):
         return jnp.concatenate([head_rows(query_weight, h), head_rows(kv_weight, h)], axis=0)
 
-    gathered = gather_parts(weights_of(c), across_core(weights_of(1 - c)))
+    w0, w1 = weights_of(c), across_core(weights_of(1 - c))
+    step0 = first_step(w0)
     pair = jnp.stack([tokens, across_far(tokens)])
+    pair, step0 = tie(pair, step0)
+    step1 = first_step(w1)
     blocks = [pair] + [along_z(pair, k) for k in (1, 2, 3)]
+    blocks, step1 = tie(blocks, step1)
+    gathered = gather_parts(w0, w1, step0, step1)
     other_routes = across_core(routes)
     both_routes = jnp.where(
         first_core,
@@ -492,37 +497,31 @@
         return lax.dynamic_slice_in_dim(prefix_cache, h * 2 * H, 2 * H, 1)
 
     cache = jnp.stack([cache_of(c), across_core(cache_of(1 - c))])
-    cache_out, gathered[2] = tie(cache, gathered[2])
+    cache_out, step1 = tie(cache, step1)
     caches = [cache, across_x(cache_out)]
+    gathered, caches = tie(gathered, caches)
 
     token_src = [lax.rem(z + 4 - dz, 4) * 2 + (xh ^ s) for dz in range(4) for s in range(2)]
     places = [lax.rem(lax.rem(v, 4) + 4 - y, 4) * 2 + (v // 4 ^ xl) for v in token_src]
     normed = normalise(table(token_src + places), norm_gain.reshape(8, 1, 256), blocks)
-    out_early, gathered[7] = tie(out_weight, gathered[7])
-    o_ym, o_yp, o_a = along_y(out_early, 3), along_y(out_early, 1), across_x(out_early)
     q, kv, gates = project(
         table(chips + [c]), both_routes, router.T, normed, across_core(normed), gathered
     )
     kvs = [kv, across_x(kv)]
-    q_out, o_a, o_ym, o_yp = lax.optimization_barrier((q, o_a, o_ym, o_yp))
-    qs = [q] + [along_y(q_out, k) for k in (1, 2, 3)]
-    out_late, o_a_late, qs[2] = lax.optimization_barrier((out_weight, o_a, qs[2]))
-    o_far, o_am, o_ap = along_y(out_late, 2), along_y(o_a_late, 3), along_y(o_a_late, 1)
+    qs = [q] + [along_y(q, k) for k in (1, 2, 3)]
 
     firsts = [(xl * 4 + lax.rem(y + 4 - k, 4)) * 512 for k in range(4)]
     mine, partner = xl * 4 + y, (1 - xl) * 4 + y
     at = [c] + firsts + [mine * 1536, partner * 1536, mine * 512, partner * 512]
     parts = list(attend(table(at), suffix_lengths, prefix_lengths, qs, caches, kvs))
-    parts[1:], o_far, o_am, o_ap = lax.optimization_barrier((parts[1:], o_far, o_am, o_ap))
     for k in range(1, 4):
         parts[k] = along_y(parts[k], 4 - k)
-    out_blocks = [out_weight, o_a, o_ym, o_am, o_far, across_x(o_far), o_yp, o_ap]
     gate_row = gates.reshape(2, 256, 2).transpose(0, 2, 1).reshape(1, 1024)
     attended = combine(gate_row, parts)
 
     dests = [lax.rem(z + dz, 4) * 2 + (xh ^ s) for dz in range(4) for s in range(2)]
     sums = project_out(
-        table(chips + [c] + dests), both_routes, attended, across_core(attended), out_blocks
+        table(dests + [c]), both_routes, attended, across_core(attended), out_all
     )
     total = sums[0]
     for k in (1, 2, 3):

time: 188 us -> 208 us (1.11)
  between operations: 0.41 us -> 13.8 us
  waiting for transfers between devices: 88.5 us -> 95.3 us
    ppermute x8 -> x6, waiting for transfers between devices: 26.9 us -> 5.05 us  [across_x(): return lax.ppermute(x, 'xl', [(0, 1), (1, 0)])]
    ppermute x21 -> x16, waiting for transfers between devices: 36 us -> 56.7 us  [along_y(): return lax.ppermute(x, 'y', [(i, (i + k) % 4) for i in range(4)])]
    ppermute x21 -> x16, starting transfers between devices: 28.6 us -> 16.1 us  [along_y(): return lax.ppermute(x, 'y', [(i, (i + k) % 4) for i in range(4)])]
    ppermute x6, starting transfers between devices: 7.74 us -> 17 us  [across_core(): return lax.ppermute(x, 'c', [(0, 1), (1, 0)])]
    ppermute x2, waiting for transfers between devices: 6.93 us -> 13.1 us  [across_far(): return lax.ppermute(x, 'xh', [(0, 1), (1, 0)])]
    pallas_call x1, Pallas kernels: 17.6 us -> 20.6 us  [attend(): pl.pallas_call(attend_kernel, out_shape=tuple((jax.ShapeDtypeStruct((H +...]
    ppermute x8 -> x6, starting transfers between devices: 6.9 us -> 7.48 us  [across_x(): return lax.ppermute(x, 'xl', [(0, 1), (1, 0)])]
  transfers between devices with their start and end apart: 43 -> 37, of which waited for: 24 -> 23; matrix products, arithmetic and copies ran while one was open for 2% -> 2% of each run, Pallas kernels for 14% -> 14%
where the time goes in v3:
time: 208 us; the launch traced here: 207 us
  waiting for transfers between devices  95.3 us (46%)
  starting transfers between devices  56.2 us (27%)
  Pallas kernels  34.9 us (17%)
  between operations  13.8 us (7%)
  local copies, waits for them, and re-layouts  5.02 us (2%)
    ppermute x16, waiting for transfers between devices, along_y(): return lax.ppermute(x, 'y', [(i, (i + k) % 4) for i in range(4)])  56.7 us
    pallas_call x1, Pallas kernels, attend(): pl.pallas_call(attend_kernel, out_shape=tuple((jax.ShapeDtypeStruct((H +...  20.6 us
    ppermute x6, starting transfers between devices, across_core(): return lax.ppermute(x, 'c', [(0, 1), (1, 0)])  17 us
    ppermute x6, waiting for transfers between devices, along_z(): return lax.ppermute(x, 'z', [(i, (i + k) % 4) for i in range(4)])  16.9 us
    ppermute x16, starting transfers between devices, along_y(): return lax.ppermute(x, 'y', [(i, (i + k) % 4) for i in range(4)])  16.1 us
    ppermute x2, waiting for transfers between devices, across_far(): return lax.ppermute(x, 'xh', [(0, 1), (1, 0)])  13.1 us
    ppermute x6, starting transfers between devices, along_z(): return lax.ppermute(x, 'z', [(i, (i + k) % 4) for i in range(4)])  11.3 us
    ppermute x6, starting transfers between devices, across_x(): return lax.ppermute(x, 'xl', [(0, 1), (1, 0)])  7.48 us
  transfers between devices with their start and end apart: 37, of which 23 were waited for; matrix products, arithmetic and copies ran while one was open for 2% of the time, Pallas kernels for 14%

profile of v3, /device:TPU:3, one launch (start us, length us, event | category | flops | bytes accessed | tf_op | source)
XLA Modules:
  0.0 207.0 jit_solution(5484310525048963985)
XLA Ops:
  9.3 2.8 %collective-permute-start.2 = (bf16[1280,128]{1,0:T(8,128)(2,1)S(1)}, bf16[1280,128]{1,0:T(8,128)(2,1)S(1)}, u32[]{:S(2)}, u32[]{:S(2)}) collective-permute-start(bf16[1280,128]{1,0:T(8,128)(2,1)S(1)} %pad_maximum_fusion.1.refs_0_), channel_id=1, source_target_pairs={{0,48},{16,0},{32,16},{48,32},{1,49},{17,1},{33,17},{49,33},{2,50}... | collective-permute-start | bytes 983048 | tf_op jit(solution)/shard_map/ppermute | solution.py:37
  12.4 2.1 %collective-permute-start.1 = (bf16[256,256]{1,0:T(8,128)(2,1)}, bf16[256,256]{1,0:T(8,128)(2,1)S(1)}, u32[]{:S(2)}, u32[]{:S(2)}) collective-permute-start(bf16[256,256]{1,0:T(8,128)(2,1)} %param.10), channel_id=1, source_target_pairs={{0,1},{1,0},{2,3},{3,2},{4,5},{5,4},{6,7},{7,6},{8,9},{9,8},{10,11... | collective-permute-start | bytes 393224 | tf_op jit(solution)/shard_map/ppermute | solution.py:49
  16.1 9.3 %collective-permute-done.1 = bf16[256,256]{1,0:T(8,128)(2,1)S(1)} collective-permute-done((bf16[256,256]{1,0:T(8,128)(2,1)}, bf16[256,256]{1,0:T(8,128)(2,1)S(1)}, u32[]{:S(2)}, u32[]{:S(2)}) %collective-permute-start.1) | collective-permute-done | bytes 131104 | tf_op jit(solution)/shard_map/ppermute | solution.py:49
  27.1 2.0 collective-permute-start.5
  29.1 4.0 %collective-permute-start.6 = (bf16[2,256,256]{2,1,0:T(8,128)(2,1)S(1)}, bf16[2,256,256]{2,1,0:T(8,128)(2,1)S(1)}, u32[]{:S(2)}, u32[]{:S(2)}) collective-permute-start(bf16[2,256,256]{2,1,0:T(8,128)(2,1)S(1)} %pad_maximum_fusion.3.b0), channel_id=1, source_target_pairs={{0,4},{2,6},{4,0},{6,2},{1,5},{3,7},{5,1},{7,3},{8,12},{10,14},{12... | collective-permute-start | bytes 786440 | tf_op jit(solution)/shard_map/ppermute | solution.py:41
  33.5 2.3 %collective-permute-start.9 = (bf16[1280,128]{1,0:T(8,128)(2,1)}, bf16[1280,128]{1,0:T(8,128)(2,1)}, u32[]{:S(2)}, u32[]{:S(2)}) collective-permute-start(bf16[1280,128]{1,0:T(8,128)(2,1)} %collective-permute-done.8.refs_1_), channel_id=1, source_target_pairs={{0,48},{16,0},{32,16},{48,32},{1,49},{17,1},{33,17},{49,33},{2,50}... | collective-permute-start | bytes 983048 | tf_op jit(solution)/shard_map/ppermute | solution.py:37
  36.2 1.9 collective-permute-start.11
  38.1 2.5 %collective-permute-done.6.b2 = bf16[2,256,256]{2,1,0:T(8,128)(2,1)S(1)} collective-permute-done((bf16[2,256,256]{2,1,0:T(8,128)(2,1)S(1)}, bf16[2,256,256]{2,1,0:T(8,128)(2,1)S(1)}, u32[]{:S(2)}, u32[]{:S(2)}) %collective-permute-start.6) | collective-permute-done | bytes 262176 | tf_op jit(solution)/shard_map/ppermute | solution.py:41
  40.5 5.5 %collective-permute-start.21 = (bf16[768,256]{1,0:T(8,128)(2,1)S(1)}, bf16[768,256]{1,0:T(8,128)(2,1)S(1)}, u32[]{:S(2)}, u32[]{:S(2)}) collective-permute-start(bf16[768,256]{1,0:T(8,128)(2,1)S(1)} %get-tuple-element.88), channel_id=1, source_target_pairs={{0,8},{8,0},{1,9},{9,1},{2,10},{10,2},{3,11},{11,3},{4,12},{12,4},... | collective-permute-start | bytes 1179656 | tf_op jit(solution)/shard_map/ppermute | solution.py:53
  46.2 4.5 %collective-permute-done.9.refs_5_ = bf16[1280,128]{1,0:T(8,128)(2,1)} collective-permute-done((bf16[1280,128]{1,0:T(8,128)(2,1)}, bf16[1280,128]{1,0:T(8,128)(2,1)}, u32[]{:S(2)}, u32[]{:S(2)}) %collective-permute-start.9) | collective-permute-done | bytes 327712 | tf_op jit(solution)/shard_map/ppermute | solution.py:37
  50.7 4.0 %collective-permute-done.10.refs_13_ = bf16[1280,128]{1,0:T(8,128)(2,1)} collective-permute-done((bf16[1280,128]{1,0:T(8,128)(2,1)}, bf16[1280,128]{1,0:T(8,128)(2,1)}, u32[]{:S(2)}, u32[]{:S(2)}) %collective-permute-start.10) | collective-permute-done | bytes 327712 | tf_op jit(solution)/shard_map/ppermute | solution.py:37
  56.0 6.3 %collective-permute-start.12 = (bf16[256,2048]{1,0:T(8,128)(2,1)S(1)}, bf16[256,2048]{1,0:T(8,128)(2,1)}, u32[]{:S(2)}, u32[]{:S(2)}) collective-permute-start(bf16[256,2048]{1,0:T(8,128)(2,1)S(1)} %normalise.1.own), channel_id=1, source_target_pairs={{0,8},{8,0},{1,9},{9,1},{2,10},{10,2},{3,11},{11,3},{4,12},{12,4},... | collective-permute-start | bytes 3145736 | tf_op jit(solution)/shard_map/ppermute | solution.py:53
  63.9 1.8 collective-permute-start.22
  67.4 9.8 %collective-permute-done.13.refs_6_ = bf16[1280,128]{1,0:T(8,128)(2,1)S(1)} collective-permute-done((bf16[1280,128]{1,0:T(8,128)(2,1)}, bf16[1280,128]{1,0:T(8,128)(2,1)S(1)}, u32[]{:S(2)}, u32[]{:S(2)}) %collective-permute-start.13) | collective-permute-done | bytes 327712 | tf_op jit(solution)/shard_map/ppermute | solution.py:37
  77.2 3.3 %collective-permute-start.14 = (bf16[1280,128]{1,0:T(8,128)(2,1)}, bf16[1280,128]{1,0:T(8,128)(2,1)S(1)}, u32[]{:S(2)}, u32[]{:S(2)}) collective-permute-start(bf16[1280,128]{1,0:T(8,128)(2,1)} %collective-permute-done.11.refs_3_), channel_id=1, source_target_pairs={{0,48},{16,0},{32,16},{48,32},{1,49},{17,1},{33,17},{49,33},{2,50}... | collective-permute-start | bytes 983048 | tf_op jit(solution)/shard_map/ppermute | solution.py:37
  80.7 6.7 %collective-permute-done.19.refs_14_ = bf16[1280,128]{1,0:T(8,128)(2,1)S(1)} collective-permute-done((bf16[1280,128]{1,0:T(8,128)(2,1)}, bf16[1280,128]{1,0:T(8,128)(2,1)S(1)}, u32[]{:S(2)}, u32[]{:S(2)}) %collective-permute-start.19) | collective-permute-done | bytes 327712 | tf_op jit(solution)/shard_map/ppermute | solution.py:37
  88.6 5.8 %collective-permute-done.16.refs_9_ = bf16[1280,128]{1,0:T(8,128)(2,1)} collective-permute-done((bf16[1280,128]{1,0:T(8,128)(2,1)}, bf16[1280,128]{1,0:T(8,128)(2,1)}, u32[]{:S(2)}, u32[]{:S(2)}) %collective-permute-start.16) | collective-permute-done | bytes 327712 | tf_op jit(solution)/shard_map/ppermute | solution.py:37
  96.0 1.7 collective-permute-done.20.refs_15_
  97.8 5.0 %collective-permute-done.18.refs_11_ = bf16[1280,128]{1,0:T(8,128)(2,1)} collective-permute-done((bf16[1280,128]{1,0:T(8,128)(2,1)}, bf16[1280,128]{1,0:T(8,128)(2,1)}, u32[]{:S(2)}, u32[]{:S(2)}) %collective-permute-start.18) | collective-permute-done | bytes 327712 | tf_op jit(solution)/shard_map/ppermute | solution.py:45
  102.8 7.4 %project.1 = (bf16[1024,128]{1,0:T(8,128)(2,1)S(1)}, bf16[512,256]{1,0:T(8,128)(2,1)S(1)}, f32[512,2]{1,0:T(8,128)S(1)}) custom-call(s32[9]{0:T(128)S(1)} %stack.161.idx, s32[512,2]{1,0:T(8,128)S(1)} %broadcast_select_fusion.routes, bf16[8,2048]{1,0:T(8,128)(2,1)S(1)} %bitcast.51, bf16[256,2048]{1,0:T(8,128)(2,1)} %copy-done, ...), custom_call_target="tpu_custom_call" | custom-call | flops 6442450944 | bytes 8388608 | tf_op jit(solution)/shard_map/project/pallas_call | solution.py:186
  110.3 4.5 %collective-permute-start.24 = (bf16[1024,128]{1,0:T(8,128)(2,1)S(1)}, bf16[1024,128]{1,0:T(8,128)(2,1)S(1)}, u32[]{:S(2)}, u32[]{:S(2)}) collective-permute-start(bf16[1024,128]{1,0:T(8,128)(2,1)S(1)} %get-tuple-element.75.q0), channel_id=1, source_target_pairs={{0,32},{16,48},{32,0},{48,16},{1,33},{17,49},{33,1},{49,17},{2,34}... | collective-permute-start | bytes 786440 | tf_op jit(solution)/shard_map/ppermute | solution.py:37
  116.2 1.9 collective-permute-done.23.q1
  118.1 6.5 %collective-permute-done.24.q2 = bf16[1024,128]{1,0:T(8,128)(2,1)S(1)} collective-permute-done((bf16[1024,128]{1,0:T(8,128)(2,1)S(1)}, bf16[1024,128]{1,0:T(8,128)(2,1)S(1)}, u32[]{:S(2)}, u32[]{:S(2)}) %collective-permute-start.24) | collective-permute-done | bytes 262176 | tf_op jit(solution)/shard_map/ppermute | solution.py:37
  126.7 20.6 %attend.1 = (bf16[144,1024]{1,0:T(8,128)(2,1)S(1)}, bf16[144,1024]{1,0:T(8,128)(2,1)S(1)}, bf16[144,1024]{1,0:T(8,128)(2,1)S(1)}, bf16[144,1024]{1,0:T(8,128)(2,1)S(1)}) custom-call(s32[9]{0:T(128)S(1)} %stack.187.idx, s32[4]{0:T(128)S(1)} %copy-done.4, s32[4]{0:T(128)S(1)} %copy-done.5, bf16[1024,128]{1,0:T(8,128)(2,1)} %copy-done.1, ...), custom_call_target="tpu_custom_call" | custom-call | flops 12884901888 | bytes 6291456 | tf_op jit(solution)/shard_map/attend/pallas_call | solution.py:349
  149.0 4.4 %collective-permute-done.27.p1 = bf16[144,1024]{1,0:T(8,128)(2,1)S(1)} collective-permute-done((bf16[144,1024]{1,0:T(8,128)(2,1)S(1)}, bf16[144,1024]{1,0:T(8,128)(2,1)S(1)}, u32[]{:S(2)}, u32[]{:S(2)}) %collective-permute-start.27) | collective-permute-done | bytes 294944 | tf_op jit(solution)/shard_map/ppermute | solution.py:37
  155.1 8.8 %collective-permute-done.29.p3 = bf16[144,1024]{1,0:T(8,128)(2,1)S(1)} collective-permute-done((bf16[144,1024]{1,0:T(8,128)(2,1)S(1)}, bf16[144,1024]{1,0:T(8,128)(2,1)S(1)}, u32[]{:S(2)}, u32[]{:S(2)}) %collective-permute-start.29) | collective-permute-done | bytes 294944 | tf_op jit(solution)/shard_map/ppermute | solution.py:37
  166.6 5.2 %project_out.1 = (f32[2,512,128]{2,1,0:T(8,128)S(1)}, bf16[2,512,128]{2,1,0:T(8,128)(2,1)S(1)}, bf16[2,512,128]{2,1,0:T(8,128)(2,1)S(1)}, bf16[2,512,128]{2,1,0:T(8,128)(2,1)S(1)}) custom-call(s32[9]{0:T(128)S(1)} %stack.152.idx, s32[512,2]{1,0:T(8,128)S(1)} %broadcast_select_fusion.routes, bf16[1024,128]{1,0:T(8,128)(2,1)S(1)} %combine.1.own, ...), custom_call_target="tpu_custom_call" | custom-call | flops 4294967296 | bytes 6291456 | tf_op jit(solution)/shard_map/project_out/pallas_call | solution.py:436
  171.8 4.0 %collective-permute-start.33 = (bf16[2,512,128]{2,1,0:T(8,128)(2,1)S(1)}, bf16[2,512,128]{2,1,0:T(8,128)(2,1)S(1)}, u32[]{:S(2)}, u32[]{:S(2)}) collective-permute-start(bf16[2,512,128]{2,1,0:T(8,128)(2,1)S(1)} %get-tuple-element.86), channel_id=1, source_target_pairs={{0,6},{2,0},{4,2},{6,4},{1,7},{3,1},{5,3},{7,5},{8,14},{10,8},{12,... | collective-permute-start | bytes 786440 | tf_op jit(solution)/shard_map/ppermute | solution.py:41
  176.7 10.0 %collective-permute-done.33 = bf16[2,512,128]{2,1,0:T(8,128)(2,1)S(1)} collective-permute-done((bf16[2,512,128]{2,1,0:T(8,128)(2,1)S(1)}, bf16[2,512,128]{2,1,0:T(8,128)(2,1)S(1)}, u32[]{:S(2)}, u32[]{:S(2)}) %collective-permute-start.33) | collective-permute-done | bytes 262176 | tf_op jit(solution)/shard_map/ppermute | solution.py:41
  186.7 4.1 %collective-permute-done.31 = bf16[2,512,128]{2,1,0:T(8,128)(2,1)S(1)} collective-permute-done((bf16[2,512,128]{2,1,0:T(8,128)(2,1)S(1)}, bf16[2,512,128]{2,1,0:T(8,128)(2,1)S(1)}, u32[]{:S(2)}, u32[]{:S(2)}) %collective-permute-start.31) | collective-permute-done | bytes 262176 | tf_op jit(solution)/shard_map/ppermute | solution.py:41
  190.9 2.1 %collective-permute-start.34 = (bf16[512,128]{1,0:T(8,128)(2,1)S(1)}, bf16[512,128]{1,0:T(8,128)(2,1)S(1)}, u32[]{:S(2)}, u32[]{:S(2)}) collective-permute-start(bf16[512,128]{1,0:T(8,128)(2,1)S(1)} %fusion.1), channel_id=1, source_target_pairs={{0,1},{1,0},{2,3},{3,2},{4,5},{5,4},{6,7},{7,6},{8,9},{9,8},{10,11... | collective-permute-start | bytes 393224 | tf_op jit(solution)/shard_map/ppermute | solution.py:49
  193.1 3.8 %collective-permute-done.34 = bf16[512,128]{1,0:T(8,128)(2,1)S(1)} collective-permute-done((bf16[512,128]{1,0:T(8,128)(2,1)S(1)}, bf16[512,128]{1,0:T(8,128)(2,1)S(1)}, u32[]{:S(2)}, u32[]{:S(2)}) %collective-permute-start.34) | collective-permute-done | bytes 131104 | tf_op jit(solution)/shard_map/ppermute | solution.py:49
  (113 shorter events, 28.4 us)
Async XLA Ops:
  6.5 160.0 %all-gather.3.cloned.1.call-start = ((), (), s32[]{:S(2)}) async-start(), calls=%async_computation | async-start | bytes 4718592 | tf_op jit(solution)/shard_map/all_gather | solution.py:469
  9.3 17.1 %collective-permute-start.2 = (bf16[1280,128]{1,0:T(8,128)(2,1)S(1)}, bf16[1280,128]{1,0:T(8,128)(2,1)S(1)}, u32[]{:S(2)}, u32[]{:S(2)}) collective-permute-start(bf16[1280,128]{1,0:T(8,128)(2,1)S(1)} %pad_maximum_fusion.1.refs_0_), channel_id=1, source_target_pairs={{0,48},{16,0},{32,16},{48,32},{1,49},{17,1},{33,17},{49,33},{2,50}... | collective-permute-start | bytes 983048 | tf_op jit(solution)/shard_map/ppermute | solution.py:37
  12.1 14.3 %collective-permute-start.3 = (bf16[1280,128]{1,0:T(8,128)(2,1)S(1)}, bf16[1280,128]{1,0:T(8,128)(2,1)S(1)}, u32[]{:S(2)}, u32[]{:S(2)}) collective-permute-start(bf16[1280,128]{1,0:T(8,128)(2,1)S(1)} %pad_maximum_fusion.1.refs_0_), channel_id=1, source_target_pairs={{0,16},{16,32},{32,48},{48,0},{1,17},{17,33},{33,49},{49,1},{2,18}... | collective-permute-start | bytes 983048 | tf_op jit(solution)/shard_map/ppermute | solution.py:37
  12.1 14.3 %collective-permute-start.4 = (bf16[1280,128]{1,0:T(8,128)(2,1)S(1)}, bf16[1280,128]{1,0:T(8,128)(2,1)S(1)}, u32[]{:S(2)}, u32[]{:S(2)}) collective-permute-start(bf16[1280,128]{1,0:T(8,128)(2,1)S(1)} %pad_maximum_fusion.1.refs_0_), channel_id=1, source_target_pairs={{0,64},{64,0},{1,65},{65,1},{2,66},{66,2},{3,67},{67,3},{4,68},{68... | collective-permute-start | bytes 983048 | tf_op jit(solution)/shard_map/ppermute | solution.py:45
  12.4 13.1 %collective-permute-start.1 = (bf16[256,256]{1,0:T(8,128)(2,1)}, bf16[256,256]{1,0:T(8,128)(2,1)S(1)}, u32[]{:S(2)}, u32[]{:S(2)}) collective-permute-start(bf16[256,256]{1,0:T(8,128)(2,1)} %param.10), channel_id=1, source_target_pairs={{0,1},{1,0},{2,3},{3,2},{4,5},{5,4},{6,7},{7,6},{8,9},{9,8},{10,11... | collective-permute-start | bytes 393224 | tf_op jit(solution)/shard_map/ppermute | solution.py:49
  14.5 19.0 %collective-permute-start.8 = (bf16[1280,128]{1,0:T(8,128)(2,1)S(1)}, bf16[1280,128]{1,0:T(8,128)(2,1)}, u32[]{:S(2)}, u32[]{:S(2)}) collective-permute-start(bf16[1280,128]{1,0:T(8,128)(2,1)S(1)} %pad_maximum_fusion.2), channel_id=1, source_target_pairs={{0,8},{8,0},{1,9},{9,1},{2,10},{10,2},{3,11},{11,3},{4,12},{12,4},... | collective-permute-start | bytes 983048 | tf_op jit(solution)/shard_map/ppermute | solution.py:53
  27.1 9.0 %collective-permute-start.5 = (bf16[2,256,256]{2,1,0:T(8,128)(2,1)S(1)}, bf16[2,256,256]{2,1,0:T(8,128)(2,1)S(1)}, u32[]{:S(2)}, u32[]{:S(2)}) collective-permute-start(bf16[2,256,256]{2,1,0:T(8,128)(2,1)S(1)} %pad_maximum_fusion.3.b0), channel_id=1, source_target_pairs={{0,2},{2,4},{4,6},{6,0},{1,3},{3,5},{5,7},{7,1},{8,10},{10,12},{12... | collective-permute-start | bytes 786440 | tf_op jit(solution)/shard_map/ppermute | solution.py:41
  29.1 11.4 %collective-permute-start.6 = (bf16[2,256,256]{2,1,0:T(8,128)(2,1)S(1)}, bf16[2,256,256]{2,1,0:T(8,128)(2,1)S(1)}, u32[]{:S(2)}, u32[]{:S(2)}) collective-permute-start(bf16[2,256,256]{2,1,0:T(8,128)(2,1)S(1)} %pad_maximum_fusion.3.b0), channel_id=1, source_target_pairs={{0,4},{2,6},{4,0},{6,2},{1,5},{3,7},{5,1},{7,3},{8,12},{10,14},{12... | collective-permute-start | bytes 786440 | tf_op jit(solution)/shard_map/ppermute | solution.py:41
  33.2 13.0 %collective-permute-start.7 = (bf16[2,256,256]{2,1,0:T(8,128)(2,1)S(1)}, bf16[2,256,256]{2,1,0:T(8,128)(2,1)S(1)}, u32[]{:S(2)}, u32[]{:S(2)}) collective-permute-start(bf16[2,256,256]{2,1,0:T(8,128)(2,1)S(1)} %pad_maximum_fusion.3.b0), channel_id=1, source_target_pairs={{0,6},{2,0},{4,2},{6,4},{1,7},{3,1},{5,3},{7,5},{8,14},{10,8},{12,... | collective-permute-start | bytes 786440 | tf_op jit(solution)/shard_map/ppermute | solution.py:41
  33.5 17.2 %collective-permute-start.9 = (bf16[1280,128]{1,0:T(8,128)(2,1)}, bf16[1280,128]{1,0:T(8,128)(2,1)}, u32[]{:S(2)}, u32[]{:S(2)}) collective-permute-start(bf16[1280,128]{1,0:T(8,128)(2,1)} %collective-permute-done.8.refs_1_), channel_id=1, source_target_pairs={{0,48},{16,0},{32,16},{48,32},{1,49},{17,1},{33,17},{49,33},{2,50}... | collective-permute-start | bytes 983048 | tf_op jit(solution)/shard_map/ppermute | solution.py:37
  35.8 18.9 %collective-permute-start.10 = (bf16[1280,128]{1,0:T(8,128)(2,1)}, bf16[1280,128]{1,0:T(8,128)(2,1)}, u32[]{:S(2)}, u32[]{:S(2)}) collective-permute-start(bf16[1280,128]{1,0:T(8,128)(2,1)} %collective-permute-done.8.refs_1_), channel_id=1, source_target_pairs={{0,16},{16,32},{32,48},{48,0},{1,17},{17,33},{33,49},{49,1},{2,18}... | collective-permute-start | bytes 983048 | tf_op jit(solution)/shard_map/ppermute | solution.py:37
  36.2 18.5 %collective-permute-start.11 = (bf16[1280,128]{1,0:T(8,128)(2,1)}, bf16[1280,128]{1,0:T(8,128)(2,1)}, u32[]{:S(2)}, u32[]{:S(2)}) collective-permute-start(bf16[1280,128]{1,0:T(8,128)(2,1)} %collective-permute-done.8.refs_1_), channel_id=1, source_target_pairs={{0,64},{64,0},{1,65},{65,1},{2,66},{66,2},{3,67},{67,3},{4,68},{68... | collective-permute-start | bytes 983048 | tf_op jit(solution)/shard_map/ppermute | solution.py:45
  40.5 23.3 %collective-permute-start.21 = (bf16[768,256]{1,0:T(8,128)(2,1)S(1)}, bf16[768,256]{1,0:T(8,128)(2,1)S(1)}, u32[]{:S(2)}, u32[]{:S(2)}) collective-permute-start(bf16[768,256]{1,0:T(8,128)(2,1)S(1)} %get-tuple-element.88), channel_id=1, source_target_pairs={{0,8},{8,0},{1,9},{9,1},{2,10},{10,2},{3,11},{11,3},{4,12},{12,4},... | collective-permute-start | bytes 1179656 | tf_op jit(solution)/shard_map/ppermute | solution.py:53
  56.0 46.7 %collective-permute-start.12 = (bf16[256,2048]{1,0:T(8,128)(2,1)S(1)}, bf16[256,2048]{1,0:T(8,128)(2,1)}, u32[]{:S(2)}, u32[]{:S(2)}) collective-permute-start(bf16[256,2048]{1,0:T(8,128)(2,1)S(1)} %normalise.1.own), channel_id=1, source_target_pairs={{0,8},{8,0},{1,9},{9,1},{2,10},{10,2},{3,11},{11,3},{4,12},{12,4},... | collective-permute-start | bytes 3145736 | tf_op jit(solution)/shard_map/ppermute | solution.py:53
  62.3 14.9 %collective-permute-start.13 = (bf16[1280,128]{1,0:T(8,128)(2,1)}, bf16[1280,128]{1,0:T(8,128)(2,1)S(1)}, u32[]{:S(2)}, u32[]{:S(2)}) collective-permute-start(bf16[1280,128]{1,0:T(8,128)(2,1)} %copy-done.13), channel_id=1, source_target_pairs={{0,48},{16,0},{32,16},{48,32},{1,49},{17,1},{33,17},{49,33},{2,50}... | collective-permute-start | bytes 983048 | tf_op jit(solution)/shard_map/ppermute | solution.py:37
  62.7 17.8 %collective-permute-start.15 = (bf16[1280,128]{1,0:T(8,128)(2,1)}, bf16[1280,128]{1,0:T(8,128)(2,1)}, u32[]{:S(2)}, u32[]{:S(2)}) collective-permute-start(bf16[1280,128]{1,0:T(8,128)(2,1)} %copy-done.12), channel_id=1, source_target_pairs={{0,16},{16,32},{32,48},{48,0},{1,17},{17,33},{33,49},{49,1},{2,18}... | collective-permute-start | bytes 983048 | tf_op jit(solution)/shard_map/ppermute | solution.py:37
  63.9 38.9 %collective-permute-start.22 = (bf16[2,768,256]{2,1,0:T(8,128)(2,1)S(1)}, bf16[2,768,256]{2,1,0:T(8,128)(2,1)}, u32[]{:S(2)}, u32[]{:S(2)}) collective-permute-start(bf16[2,768,256]{2,1,0:T(8,128)(2,1)S(1)} %pad_maximum_fusion.cache0), channel_id=1, source_target_pairs={{0,64},{64,0},{1,65},{65,1},{2,66},{66,2},{3,67},{67,3},{4,68},{68... | collective-permute-start | bytes 2359304 | tf_op jit(solution)/shard_map/ppermute | solution.py:45
  67.4 20.0 %collective-permute-start.19 = (bf16[1280,128]{1,0:T(8,128)(2,1)}, bf16[1280,128]{1,0:T(8,128)(2,1)S(1)}, u32[]{:S(2)}, u32[]{:S(2)}) collective-permute-start(bf16[1280,128]{1,0:T(8,128)(2,1)} %copy-done.13), channel_id=1, source_target_pairs={{0,16},{16,32},{32,48},{48,0},{1,17},{17,33},{33,49},{49,1},{2,18}... | collective-permute-start | bytes 983048 | tf_op jit(solution)/shard_map/ppermute | solution.py:37
  77.2 10.3 %collective-permute-start.14 = (bf16[1280,128]{1,0:T(8,128)(2,1)}, bf16[1280,128]{1,0:T(8,128)(2,1)S(1)}, u32[]{:S(2)}, u32[]{:S(2)}) collective-permute-start(bf16[1280,128]{1,0:T(8,128)(2,1)} %collective-permute-done.11.refs_3_), channel_id=1, source_target_pairs={{0,48},{16,0},{32,16},{48,32},{1,49},{17,1},{33,17},{49,33},{2,50}... | collective-permute-start | bytes 983048 | tf_op jit(solution)/shard_map/ppermute | solution.py:37
  80.5 14.0 %collective-permute-start.16 = (bf16[1280,128]{1,0:T(8,128)(2,1)}, bf16[1280,128]{1,0:T(8,128)(2,1)}, u32[]{:S(2)}, u32[]{:S(2)}) collective-permute-start(bf16[1280,128]{1,0:T(8,128)(2,1)} %collective-permute-done.9.refs_5_), channel_id=1, source_target_pairs={{0,48},{16,0},{32,16},{48,32},{1,49},{17,1},{33,17},{49,33},{2,50}... | collective-permute-start | bytes 983048 | tf_op jit(solution)/shard_map/ppermute | solution.py:37
  87.4 10.4 %collective-permute-start.20 = (bf16[1280,128]{1,0:T(8,128)(2,1)}, bf16[1280,128]{1,0:T(8,128)(2,1)}, u32[]{:S(2)}, u32[]{:S(2)}) collective-permute-start(bf16[1280,128]{1,0:T(8,128)(2,1)} %collective-permute-done.11.refs_3_), channel_id=1, source_target_pairs={{0,16},{16,32},{32,48},{48,0},{1,17},{17,33},{33,49},{49,1},{2,18}... | collective-permute-start | bytes 983048 | tf_op jit(solution)/shard_map/ppermute | solution.py:37
  87.4 8.6 %collective-permute-start.17 = (bf16[1280,128]{1,0:T(8,128)(2,1)}, bf16[1280,128]{1,0:T(8,128)(2,1)}, u32[]{:S(2)}, u32[]{:S(2)}) collective-permute-start(bf16[1280,128]{1,0:T(8,128)(2,1)} %collective-permute-done.15.refs_8_), channel_id=1, source_target_pairs={{0,64},{64,0},{1,65},{65,1},{2,66},{66,2},{3,67},{67,3},{4,68},{68... | collective-permute-start | bytes 983048 | tf_op jit(solution)/shard_map/ppermute | solution.py:45
  94.5 8.3 %collective-permute-start.18 = (bf16[1280,128]{1,0:T(8,128)(2,1)}, bf16[1280,128]{1,0:T(8,128)(2,1)}, u32[]{:S(2)}, u32[]{:S(2)}) collective-permute-start(bf16[1280,128]{1,0:T(8,128)(2,1)} %collective-permute-done.16.refs_9_), channel_id=1, source_target_pairs={{0,64},{64,0},{1,65},{65,1},{2,66},{66,2},{3,67},{67,3},{4,68},{68... | collective-permute-start | bytes 983048 | tf_op jit(solution)/shard_map/ppermute | solution.py:45
  110.3 7.8 %collective-permute-start.23 = (bf16[1024,128]{1,0:T(8,128)(2,1)S(1)}, bf16[1024,128]{1,0:T(8,128)(2,1)S(1)}, u32[]{:S(2)}, u32[]{:S(2)}) collective-permute-start(bf16[1024,128]{1,0:T(8,128)(2,1)S(1)} %get-tuple-element.75.q0), channel_id=1, source_target_pairs={{0,16},{16,32},{32,48},{48,0},{1,17},{17,33},{33,49},{49,1},{2,18}... | collective-permute-start | bytes 786440 | tf_op jit(solution)/shard_map/ppermute | solution.py:37
  110.3 14.3 %collective-permute-start.24 = (bf16[1024,128]{1,0:T(8,128)(2,1)S(1)}, bf16[1024,128]{1,0:T(8,128)(2,1)S(1)}, u32[]{:S(2)}, u32[]{:S(2)}) collective-permute-start(bf16[1024,128]{1,0:T(8,128)(2,1)S(1)} %get-tuple-element.75.q0), channel_id=1, source_target_pairs={{0,32},{16,48},{32,0},{48,16},{1,33},{17,49},{33,1},{49,17},{2,34}... | collective-permute-start | bytes 786440 | tf_op jit(solution)/shard_map/ppermute | solution.py:37
  114.9 10.4 %collective-permute-start.25 = (bf16[1024,128]{1,0:T(8,128)(2,1)S(1)}, bf16[1024,128]{1,0:T(8,128)(2,1)S(1)}, u32[]{:S(2)}, u32[]{:S(2)}) collective-permute-start(bf16[1024,128]{1,0:T(8,128)(2,1)S(1)} %get-tuple-element.75.q0), channel_id=1, source_target_pairs={{0,48},{16,0},{32,16},{48,32},{1,49},{17,1},{33,17},{49,33},{2,50}... | collective-permute-start | bytes 786440 | tf_op jit(solution)/shard_map/ppermute | solution.py:37
  114.9 10.4 %collective-permute-start.26 = (bf16[512,256]{1,0:T(8,128)(2,1)S(1)}, bf16[512,256]{1,0:T(8,128)(2,1)S(1)}, u32[]{:S(2)}, u32[]{:S(2)}) collective-permute-start(bf16[512,256]{1,0:T(8,128)(2,1)S(1)} %get-tuple-element.78.kv0), channel_id=1, source_target_pairs={{0,64},{64,0},{1,65},{65,1},{2,66},{66,2},{3,67},{67,3},{4,68},{68... | collective-permute-start | bytes 786440 | tf_op jit(solution)/shard_map/ppermute | solution.py:45
  147.4 7.7 %collective-permute-start.28 = (bf16[144,1024]{1,0:T(8,128)(2,1)S(1)}, bf16[144,1024]{1,0:T(8,128)(2,1)S(1)}, u32[]{:S(2)}, u32[]{:S(2)}) collective-permute-start(bf16[144,1024]{1,0:T(8,128)(2,1)S(1)} %get-tuple-element.81), channel_id=1, source_target_pairs={{0,32},{16,48},{32,0},{48,16},{1,33},{17,49},{33,1},{49,17},{2,34}... | collective-permute-start | bytes 884744 | tf_op jit(solution)/shard_map/ppermute | solution.py:37
  147.5 16.4 %collective-permute-start.29 = (bf16[144,1024]{1,0:T(8,128)(2,1)S(1)}, bf16[144,1024]{1,0:T(8,128)(2,1)S(1)}, u32[]{:S(2)}, u32[]{:S(2)}) collective-permute-start(bf16[144,1024]{1,0:T(8,128)(2,1)S(1)} %get-tuple-element.82), channel_id=1, source_target_pairs={{0,16},{16,32},{32,48},{48,0},{1,17},{17,33},{33,49},{49,1},{2,18}... | collective-permute-start | bytes 884744 | tf_op jit(solution)/shard_map/ppermute | solution.py:37
  171.8 14.9 %collective-permute-start.33 = (bf16[2,512,128]{2,1,0:T(8,128)(2,1)S(1)}, bf16[2,512,128]{2,1,0:T(8,128)(2,1)S(1)}, u32[]{:S(2)}, u32[]{:S(2)}) collective-permute-start(bf16[2,512,128]{2,1,0:T(8,128)(2,1)S(1)} %get-tuple-element.86), channel_id=1, source_target_pairs={{0,6},{2,0},{4,2},{6,4},{1,7},{3,1},{5,3},{7,5},{8,14},{10,8},{12,... | collective-permute-start | bytes 786440 | tf_op jit(solution)/shard_map/ppermute | solution.py:41
  175.8 10.9 %collective-permute-start.32 = (bf16[2,512,128]{2,1,0:T(8,128)(2,1)S(1)}, bf16[2,512,128]{2,1,0:T(8,128)(2,1)S(1)}, u32[]{:S(2)}, u32[]{:S(2)}) collective-permute-start(bf16[2,512,128]{2,1,0:T(8,128)(2,1)S(1)} %get-tuple-element.85), channel_id=1, source_target_pairs={{0,4},{2,6},{4,0},{6,2},{1,5},{3,7},{5,1},{7,3},{8,12},{10,14},{12... | collective-permute-start | bytes 786440 | tf_op jit(solution)/shard_map/ppermute | solution.py:41
  175.9 14.9 %collective-permute-start.31 = (bf16[2,512,128]{2,1,0:T(8,128)(2,1)S(1)}, bf16[2,512,128]{2,1,0:T(8,128)(2,1)S(1)}, u32[]{:S(2)}, u32[]{:S(2)}) collective-permute-start(bf16[2,512,128]{2,1,0:T(8,128)(2,1)S(1)} %get-tuple-element.84), channel_id=1, source_target_pairs={{0,2},{2,4},{4,6},{6,0},{1,3},{3,5},{5,7},{7,1},{8,10},{10,12},{12... | collective-permute-start | bytes 786440 | tf_op jit(solution)/shard_map/ppermute | solution.py:41
  (26 other events, 493.3 us)
Sparse Core Ops, SparseCore 0:
  9.0 69.9 all-gather.2

commit v4 on v2

--- a/solution.py
+++ b/solution.py
@@ -57,9 +57,13 @@
     return lax.optimization_barrier((a, b))
 
 
-def gather_parts(w0, w1):
-    ym0, yp0, a0 = along_y(w0, 3), along_y(w0, 1), across_x(w0)
-    ym1, yp1, a1 = along_y(w1, 3), along_y(w1, 1), across_x(w1)
+def first_step(w):
+    return along_y(w, 3), along_y(w, 1), across_x(w)
+
+
+def gather_parts(w0, w1, step0, step1):
+    ym0, yp0, a0 = step0
+    ym1, yp1, a1 = step1
     far0, far1 = along_y(yp0, 1), along_y(ym1, 3)
     am0, ap0 = along_y(a0, 3), along_y(a0, 1)
     am1, ap1 = along_y(a1, 3), along_y(a1, 1)
@@ -478,9 +482,14 @@
     def weights_of(h):
         return jnp.concatenate([head_rows(query_weight, h), head_rows(kv_weight, h)], axis=0)
 
-    gathered = gather_parts(weights_of(c), across_core(weights_of(1 - c)))
+    w0, w1 = weights_of(c), across_core(weights_of(1 - c))
+    step0 = first_step(w0)
     pair = jnp.stack([tokens, across_far(tokens)])
+    pair, step0 = tie(pair, step0)
+    step1 = first_step(w1)
     blocks = [pair] + [along_z(pair, k) for k in (1, 2, 3)]
+    blocks, step1 = tie(blocks, step1)
+    gathered = gather_parts(w0, w1, step0, step1)
     other_routes = across_core(routes)
     both_routes = jnp.where(
         first_core,
@@ -492,8 +501,9 @@
         return lax.dynamic_slice_in_dim(prefix_cache, h * 2 * H, 2 * H, 1)
 
     cache = jnp.stack([cache_of(c), across_core(cache_of(1 - c))])
-    cache_out, gathered[2] = tie(cache, gathered[2])
+    cache_out, step1 = tie(cache, step1)
     caches = [cache, across_x(cache_out)]
+    gathered, caches = tie(gathered, caches)
 
     token_src = [lax.rem(z + 4 - dz, 4) * 2 + (xh ^ s) for dz in range(4) for s in range(2)]
     places = [lax.rem(lax.rem(v, 4) + 4 - y, 4) * 2 + (v // 4 ^ xl) for v in token_src]
@@ -506,7 +516,7 @@
     kvs = [kv, across_x(kv)]
     q_out, o_a, o_ym, o_yp = lax.optimization_barrier((q, o_a, o_ym, o_yp))
     qs = [q] + [along_y(q_out, k) for k in (1, 2, 3)]
-    out_late, o_a_late, qs[2] = lax.optimization_barrier((out_weight, o_a, qs[2]))
+    out_late, o_a_late, kvs[1] = lax.optimization_barrier((out_weight, o_a, kvs[1]))
     o_far, o_am, o_ap = along_y(out_late, 2), along_y(o_a_late, 3), along_y(o_a_late, 1)
 
     firsts = [(xl * 4 + lax.rem(y + 4 - k, 4)) * 512 for k in range(4)]

time: 188 us -> 182 us (0.968); the launches traced: 186 us -> 183 us
  waiting for transfers between devices: 88.5 us -> 81 us
  local copies, waits for them, and re-layouts: 4.23 us -> 6.43 us
  starting transfers between devices: 56.7 us -> 58.7 us
    ppermute x8, waiting for transfers between devices: 26.9 us -> 6.74 us  [across_x(): return lax.ppermute(x, 'xl', [(0, 1), (1, 0)])]
    ppermute x2, waiting for transfers between devices: 6.93 us -> 13.7 us  [across_far(): return lax.ppermute(x, 'xh', [(0, 1), (1, 0)])]
    ppermute x21, waiting for transfers between devices: 36 us -> 40.8 us  [along_y(): return lax.ppermute(x, 'y', [(i, (i + k) % 4) for i in range(4)])]
    ppermute x6, starting transfers between devices: 7.74 us -> 11 us  [across_core(): return lax.ppermute(x, 'c', [(0, 1), (1, 0)])]
    unnamed x48 -> x60, local copies, waits for them, and re-layouts: 1.38 us -> 3.58 us
  transfers between devices with their start and end apart: 43 -> 43, of which waited for: 24 -> 24; matrix products, arithmetic and copies ran while one was open for 2% -> 1% of each run, Pallas kernels for 14% -> 15%
where the time goes in v4:
time: 182 us; the launch traced here: 183 us
  waiting for transfers between devices  81 us (45%)
  starting transfers between devices  58.7 us (32%)
  Pallas kernels  35.1 us (19%)
  local copies, waits for them, and re-layouts  6.43 us (4%)
    ppermute x21, waiting for transfers between devices, along_y(): return lax.ppermute(x, 'y', [(i, (i + k) % 4) for i in range(4)])  40.8 us
    ppermute x21, starting transfers between devices, along_y(): return lax.ppermute(x, 'y', [(i, (i + k) % 4) for i in range(4)])  26.7 us
    pallas_call x1, Pallas kernels, attend(): pl.pallas_call(attend_kernel, out_shape=tuple((jax.ShapeDtypeStruct((H +...  18.9 us
    ppermute x6, waiting for transfers between devices, along_z(): return lax.ppermute(x, 'z', [(i, (i + k) % 4) for i in range(4)])  16.9 us
    ppermute x2, waiting for transfers between devices, across_far(): return lax.ppermute(x, 'xh', [(0, 1), (1, 0)])  13.7 us
    ppermute x6, starting transfers between devices, across_core(): return lax.ppermute(x, 'c', [(0, 1), (1, 0)])  11 us
    ppermute x6, starting transfers between devices, along_z(): return lax.ppermute(x, 'z', [(i, (i + k) % 4) for i in range(4)])  10.6 us
    ppermute x8, starting transfers between devices, across_x(): return lax.ppermute(x, 'xl', [(0, 1), (1, 0)])  8.18 us
  transfers between devices with their start and end apart: 43, of which 24 were waited for; matrix products, arithmetic and copies ran while one was open for 1% of the time, Pallas kernels for 15%

profile of v4, /device:TPU:3, one launch (start us, length us, event | category | flops | bytes accessed | tf_op | source)
XLA Modules:
  0.0 182.7 jit_solution(17382346069905371092)
XLA Ops:
  2.1 2.8 %collective-permute-start.2 = (bf16[1280,128]{1,0:T(8,128)(2,1)S(1)}, bf16[1280,128]{1,0:T(8,128)(2,1)S(1)}, u32[]{:S(2)}, u32[]{:S(2)}) collective-permute-start(bf16[1280,128]{1,0:T(8,128)(2,1)S(1)} %pad_maximum_fusion.1.refs_0_), channel_id=1, source_target_pairs={{0,48},{16,0},{32,16},{48,32},{1,49},{17,1},{33,17},{49,33},{2,50}... | collective-permute-start | bytes 983048 | tf_op jit(solution)/shard_map/ppermute | solution.py:37
  5.1 2.1 %collective-permute-start.1 = (bf16[256,256]{1,0:T(8,128)(2,1)S(1)}, bf16[256,256]{1,0:T(8,128)(2,1)S(1)}, u32[]{:S(2)}, u32[]{:S(2)}) collective-permute-start(bf16[256,256]{1,0:T(8,128)(2,1)S(1)} %copy-done.9), channel_id=1, source_target_pairs={{0,1},{1,0},{2,3},{3,2},{4,5},{5,4},{6,7},{7,6},{8,9},{9,8},{10,11... | collective-permute-start | bytes 393224 | tf_op jit(solution)/shard_map/ppermute | solution.py:49
  8.9 7.7 %collective-permute-done.1 = bf16[256,256]{1,0:T(8,128)(2,1)S(1)} collective-permute-done((bf16[256,256]{1,0:T(8,128)(2,1)S(1)}, bf16[256,256]{1,0:T(8,128)(2,1)S(1)}, u32[]{:S(2)}, u32[]{:S(2)}) %collective-permute-start.1) | collective-permute-done | bytes 131104 | tf_op jit(solution)/shard_map/ppermute | solution.py:49
  16.7 1.7 collective-permute-start.5
  18.4 3.3 %collective-permute-start.6 = (bf16[2,256,256]{2,1,0:T(8,128)(2,1)S(1)}, bf16[2,256,256]{2,1,0:T(8,128)(2,1)S(1)}, u32[]{:S(2)}, u32[]{:S(2)}) collective-permute-start(bf16[2,256,256]{2,1,0:T(8,128)(2,1)S(1)} %pad_maximum_fusion.3.b0), channel_id=1, source_target_pairs={{0,4},{2,6},{4,0},{6,2},{1,5},{3,7},{5,1},{7,3},{8,12},{10,14},{12... | collective-permute-start | bytes 786440 | tf_op jit(solution)/shard_map/ppermute | solution.py:41
  22.4 2.4 %collective-permute-start.9 = (bf16[1280,128]{1,0:T(8,128)(2,1)S(1)}, bf16[1280,128]{1,0:T(8,128)(2,1)S(1)}, u32[]{:S(2)}, u32[]{:S(2)}) collective-permute-start(bf16[1280,128]{1,0:T(8,128)(2,1)S(1)} %collective-permute-done.8.refs_1_), channel_id=1, source_target_pairs={{0,48},{16,0},{32,16},{48,32},{1,49},{17,1},{33,17},{49,33},{2,50}... | collective-permute-start | bytes 983048 | tf_op jit(solution)/shard_map/ppermute | solution.py:37
  26.5 4.9 %collective-permute-done.6.b2 = bf16[2,256,256]{2,1,0:T(8,128)(2,1)S(1)} collective-permute-done((bf16[2,256,256]{2,1,0:T(8,128)(2,1)S(1)}, bf16[2,256,256]{2,1,0:T(8,128)(2,1)S(1)}, u32[]{:S(2)}, u32[]{:S(2)}) %collective-permute-start.6) | collective-permute-done | bytes 262176 | tf_op jit(solution)/shard_map/ppermute | solution.py:41
  31.4 3.1 %collective-permute-start.21 = (bf16[768,256]{1,0:T(8,128)(2,1)S(1)}, bf16[768,256]{1,0:T(8,128)(2,1)S(1)}, u32[]{:S(2)}, u32[]{:S(2)}) collective-permute-start(bf16[768,256]{1,0:T(8,128)(2,1)S(1)} %get-tuple-element.118), channel_id=1, source_target_pairs={{0,8},{8,0},{1,9},{9,1},{2,10},{10,2},{3,11},{11,3},{4,12},{12,4},... | collective-permute-start | bytes 1179656 | tf_op jit(solution)/shard_map/ppermute | solution.py:53
  38.8 1.9 %collective-permute-start.13 = (bf16[1280,128]{1,0:T(8,128)(2,1)}, bf16[1280,128]{1,0:T(8,128)(2,1)S(1)}, u32[]{:S(2)}, u32[]{:S(2)}) collective-permute-start(bf16[1280,128]{1,0:T(8,128)(2,1)} %collective-permute-done.4.refs_2_), channel_id=1, source_target_pairs={{0,48},{16,0},{32,16},{48,32},{1,49},{17,1},{33,17},{49,33},{2,50}... | collective-permute-start | bytes 983048 | tf_op jit(solution)/shard_map/ppermute | solution.py:37
  40.8 1.6 collective-permute-start.22
  44.3 4.2 %collective-permute-done.13.refs_6_ = bf16[1280,128]{1,0:T(8,128)(2,1)S(1)} collective-permute-done((bf16[1280,128]{1,0:T(8,128)(2,1)}, bf16[1280,128]{1,0:T(8,128)(2,1)S(1)}, u32[]{:S(2)}, u32[]{:S(2)}) %collective-permute-start.13) | collective-permute-done | bytes 327712 | tf_op jit(solution)/shard_map/ppermute | solution.py:37
  48.4 2.6 %collective-permute-start.14 = (bf16[1280,128]{1,0:T(8,128)(2,1)}, bf16[1280,128]{1,0:T(8,128)(2,1)S(1)}, u32[]{:S(2)}, u32[]{:S(2)}) collective-permute-start(bf16[1280,128]{1,0:T(8,128)(2,1)} %collective-permute-done.11.refs_3_), channel_id=1, source_target_pairs={{0,48},{16,0},{32,16},{48,32},{1,49},{17,1},{33,17},{49,33},{2,50}... | collective-permute-start | bytes 983048 | tf_op jit(solution)/shard_map/ppermute | solution.py:37
  51.8 5.7 %collective-permute-done.19.refs_14_ = bf16[1280,128]{1,0:T(8,128)(2,1)S(1)} collective-permute-done((bf16[1280,128]{1,0:T(8,128)(2,1)}, bf16[1280,128]{1,0:T(8,128)(2,1)S(1)}, u32[]{:S(2)}, u32[]{:S(2)}) %collective-permute-start.19) | collective-permute-done | bytes 327712 | tf_op jit(solution)/shard_map/ppermute | solution.py:37
  57.5 1.6 collective-permute-start.17
  59.1 5.1 %collective-permute-done.16.refs_9_ = bf16[1280,128]{1,0:T(8,128)(2,1)} collective-permute-done((bf16[1280,128]{1,0:T(8,128)(2,1)S(1)}, bf16[1280,128]{1,0:T(8,128)(2,1)}, u32[]{:S(2)}, u32[]{:S(2)}) %collective-permute-start.16) | collective-permute-done | bytes 327712 | tf_op jit(solution)/shard_map/ppermute | solution.py:37
  66.6 6.7 %collective-permute-done.18.refs_11_ = bf16[1280,128]{1,0:T(8,128)(2,1)} collective-permute-done((bf16[1280,128]{1,0:T(8,128)(2,1)}, bf16[1280,128]{1,0:T(8,128)(2,1)}, u32[]{:S(2)}, u32[]{:S(2)}) %collective-permute-start.18) | collective-permute-done | bytes 327712 | tf_op jit(solution)/shard_map/ppermute | solution.py:45
  74.9 3.1 %collective-permute-start.24 = (bf16[2048,128]{1,0:T(8,128)(2,1)S(1)}, bf16[2048,128]{1,0:T(8,128)(2,1)S(1)}, u32[]{:S(2)}, u32[]{:S(2)}) collective-permute-start(bf16[2048,128]{1,0:T(8,128)(2,1)S(1)} %copy-done.12), channel_id=1, source_target_pairs={{0,48},{16,0},{32,16},{48,32},{1,49},{17,1},{33,17},{49,33},{2,50}... | collective-permute-start | bytes 1572872 | tf_op jit(solution)/shard_map/ppermute | solution.py:37
  78.0 7.4 %project.1 = (bf16[1024,128]{1,0:T(8,128)(2,1)S(1)}, bf16[512,256]{1,0:T(8,128)(2,1)S(1)}, f32[512,2]{1,0:T(8,128)S(1)}) custom-call(s32[9]{0:T(128)S(1)} %stack.169.idx, s32[512,2]{1,0:T(8,128)S(1)} %broadcast_select_fusion.routes, bf16[8,2048]{1,0:T(8,128)(2,1)S(1)} %bitcast.50, bf16[256,2048]{1,0:T(8,128)(2,1)} %copy-done, ...), custom_call_target="tpu_custom_call" | custom-call | flops 6442450944 | bytes 8388608 | tf_op jit(solution)/shard_map/project/pallas_call | solution.py:186
  86.6 3.1 %collective-permute-done.25.refs_6_ = bf16[2048,128]{1,0:T(8,128)(2,1)S(1)} collective-permute-done((bf16[2048,128]{1,0:T(8,128)(2,1)S(1)}, bf16[2048,128]{1,0:T(8,128)(2,1)S(1)}, u32[]{:S(2)}, u32[]{:S(2)}) %collective-permute-start.25) | collective-permute-done | bytes 524320 | tf_op jit(solution)/shard_map/ppermute | solution.py:37
  94.2 5.3 %collective-permute-done.26.q1 = bf16[1024,128]{1,0:T(8,128)(2,1)S(1)} collective-permute-done((bf16[1024,128]{1,0:T(8,128)(2,1)S(1)}, bf16[1024,128]{1,0:T(8,128)(2,1)S(1)}, u32[]{:S(2)}, u32[]{:S(2)}) %collective-permute-start.26) | collective-permute-done | bytes 262176 | tf_op jit(solution)/shard_map/ppermute | solution.py:37
  101.0 18.9 %attend.1 = (bf16[144,1024]{1,0:T(8,128)(2,1)S(1)}, bf16[144,1024]{1,0:T(8,128)(2,1)S(1)}, bf16[144,1024]{1,0:T(8,128)(2,1)S(1)}, bf16[144,1024]{1,0:T(8,128)(2,1)S(1)}) custom-call(s32[9]{0:T(128)S(1)} %stack.195.idx, s32[4]{0:T(128)S(1)} %copy-done.4, s32[4]{0:T(128)S(1)} %copy-done.5, bf16[1024,128]{1,0:T(8,128)(2,1)} %copy-done.1, ...), custom_call_target="tpu_custom_call" | custom-call | flops 12884901888 | bytes 6291456 | tf_op jit(solution)/shard_map/attend/pallas_call | solution.py:349
  119.9 2.5 %collective-permute-done.30.refs_4_ = bf16[2048,128]{1,0:T(8,128)(2,1)} collective-permute-done((bf16[2048,128]{1,0:T(8,128)(2,1)S(1)}, bf16[2048,128]{1,0:T(8,128)(2,1)}, u32[]{:S(2)}, u32[]{:S(2)}) %collective-permute-start.30) | collective-permute-done | bytes 524320 | tf_op jit(solution)/shard_map/ppermute | solution.py:37
  122.5 8.3 %collective-permute-start.33 = (bf16[144,1024]{1,0:T(8,128)(2,1)S(1)}, bf16[144,1024]{1,0:T(8,128)(2,1)S(1)}, u32[]{:S(2)}, u32[]{:S(2)}) collective-permute-start(bf16[144,1024]{1,0:T(8,128)(2,1)S(1)} %get-tuple-element.105), channel_id=1, source_target_pairs={{0,48},{16,0},{32,16},{48,32},{1,49},{17,1},{33,17},{49,33},{2,50}... | collective-permute-start | bytes 884744 | tf_op jit(solution)/shard_map/ppermute | solution.py:37
  131.6 6.0 %collective-permute-done.33.p1 = bf16[144,1024]{1,0:T(8,128)(2,1)S(1)} collective-permute-done((bf16[144,1024]{1,0:T(8,128)(2,1)S(1)}, bf16[144,1024]{1,0:T(8,128)(2,1)S(1)}, u32[]{:S(2)}, u32[]{:S(2)}) %collective-permute-start.33) | collective-permute-done | bytes 294944 | tf_op jit(solution)/shard_map/ppermute | solution.py:37
  137.9 6.8 %collective-permute-done.35.p3 = bf16[144,1024]{1,0:T(8,128)(2,1)S(1)} collective-permute-done((bf16[144,1024]{1,0:T(8,128)(2,1)S(1)}, bf16[144,1024]{1,0:T(8,128)(2,1)S(1)}, u32[]{:S(2)}, u32[]{:S(2)}) %collective-permute-start.35) | collective-permute-done | bytes 294944 | tf_op jit(solution)/shard_map/ppermute | solution.py:37
  145.1 3.3 %collective-permute-start.36 = (bf16[1024,128]{1,0:T(8,128)(2,1)S(1)}, bf16[1024,128]{1,0:T(8,128)(2,1)S(1)}, u32[]{:S(2)}, u32[]{:S(2)}) collective-permute-start(bf16[1024,128]{1,0:T(8,128)(2,1)S(1)} %combine.1.own), channel_id=1, source_target_pairs={{0,8},{8,0},{1,9},{9,1},{2,10},{10,2},{3,11},{11,3},{4,12},{12,4},... | collective-permute-start | bytes 786440 | tf_op jit(solution)/shard_map/ppermute | solution.py:53
  149.5 7.1 %project_out.1 = (f32[2,512,128]{2,1,0:T(8,128)S(1)}, bf16[2,512,128]{2,1,0:T(8,128)(2,1)S(1)}, bf16[2,512,128]{2,1,0:T(8,128)(2,1)S(1)}, bf16[2,512,128]{2,1,0:T(8,128)(2,1)S(1)}) custom-call(s32[17]{0:T(128)S(1)} %stack.168.idx, s32[512,2]{1,0:T(8,128)S(1)} %broadcast_select_fusion.routes, bf16[1024,128]{1,0:T(8,128)(2,1)S(1)} %combine.1.own, ...), custom_call_target="tpu_custom_call" | custom-call | flops 4294967296 | bytes 6291456 | tf_op jit(solution)/shard_map/project_out/pallas_call | solution.py:441
  158.0 2.8 %collective-permute-start.39 = (bf16[2,512,128]{2,1,0:T(8,128)(2,1)S(1)}, bf16[2,512,128]{2,1,0:T(8,128)(2,1)S(1)}, u32[]{:S(2)}, u32[]{:S(2)}) collective-permute-start(bf16[2,512,128]{2,1,0:T(8,128)(2,1)S(1)} %get-tuple-element.115), channel_id=1, source_target_pairs={{0,4},{2,6},{4,0},{6,2},{1,5},{3,7},{5,1},{7,3},{8,12},{10,14},{12... | collective-permute-start | bytes 786440 | tf_op jit(solution)/shard_map/ppermute | solution.py:41
  161.5 2.7 %collective-permute-done.40 = bf16[2,512,128]{2,1,0:T(8,128)(2,1)S(1)} collective-permute-done((bf16[2,512,128]{2,1,0:T(8,128)(2,1)S(1)}, bf16[2,512,128]{2,1,0:T(8,128)(2,1)S(1)}, u32[]{:S(2)}, u32[]{:S(2)}) %collective-permute-start.40) | collective-permute-done | bytes 262176 | tf_op jit(solution)/shard_map/ppermute | solution.py:41
  164.2 2.5 %collective-permute-done.39 = bf16[2,512,128]{2,1,0:T(8,128)(2,1)S(1)} collective-permute-done((bf16[2,512,128]{2,1,0:T(8,128)(2,1)S(1)}, bf16[2,512,128]{2,1,0:T(8,128)(2,1)S(1)}, u32[]{:S(2)}, u32[]{:S(2)}) %collective-permute-start.39) | collective-permute-done | bytes 262176 | tf_op jit(solution)/shard_map/ppermute | solution.py:41
  166.7 6.6 %collective-permute-done.38 = bf16[2,512,128]{2,1,0:T(8,128)(2,1)S(1)} collective-permute-done((bf16[2,512,128]{2,1,0:T(8,128)(2,1)S(1)}, bf16[2,512,128]{2,1,0:T(8,128)(2,1)S(1)}, u32[]{:S(2)}, u32[]{:S(2)}) %collective-permute-start.38) | collective-permute-done | bytes 262176 | tf_op jit(solution)/shard_map/ppermute | solution.py:41
  173.6 6.1 %collective-permute-done.41 = bf16[512,128]{1,0:T(8,128)(2,1)S(1)} collective-permute-done((bf16[512,128]{1,0:T(8,128)(2,1)S(1)}, bf16[512,128]{1,0:T(8,128)(2,1)S(1)}, u32[]{:S(2)}, u32[]{:S(2)}) %collective-permute-start.41) | collective-permute-done | bytes 131104 | tf_op jit(solution)/shard_map/ppermute | solution.py:49
  (142 shorter events, 32.4 us)
Async XLA Ops:
  2.1 14.5 %collective-permute-start.2 = (bf16[1280,128]{1,0:T(8,128)(2,1)S(1)}, bf16[1280,128]{1,0:T(8,128)(2,1)S(1)}, u32[]{:S(2)}, u32[]{:S(2)}) collective-permute-start(bf16[1280,128]{1,0:T(8,128)(2,1)S(1)} %pad_maximum_fusion.1.refs_0_), channel_id=1, source_target_pairs={{0,48},{16,0},{32,16},{48,32},{1,49},{17,1},{33,17},{49,33},{2,50}... | collective-permute-start | bytes 983048 | tf_op jit(solution)/shard_map/ppermute | solution.py:37
  4.9 11.8 %collective-permute-start.3 = (bf16[1280,128]{1,0:T(8,128)(2,1)S(1)}, bf16[1280,128]{1,0:T(8,128)(2,1)S(1)}, u32[]{:S(2)}, u32[]{:S(2)}) collective-permute-start(bf16[1280,128]{1,0:T(8,128)(2,1)S(1)} %pad_maximum_fusion.1.refs_0_), channel_id=1, source_target_pairs={{0,16},{16,32},{32,48},{48,0},{1,17},{17,33},{33,49},{49,1},{2,18}... | collective-permute-start | bytes 983048 | tf_op jit(solution)/shard_map/ppermute | solution.py:37
  4.9 11.8 %collective-permute-start.4 = (bf16[1280,128]{1,0:T(8,128)(2,1)S(1)}, bf16[1280,128]{1,0:T(8,128)(2,1)}, u32[]{:S(2)}, u32[]{:S(2)}) collective-permute-start(bf16[1280,128]{1,0:T(8,128)(2,1)S(1)} %pad_maximum_fusion.1.refs_0_), channel_id=1, source_target_pairs={{0,64},{64,0},{1,65},{65,1},{2,66},{66,2},{3,67},{67,3},{4,68},{68... | collective-permute-start | bytes 983048 | tf_op jit(solution)/shard_map/ppermute | solution.py:45
  5.1 11.4 %collective-permute-start.1 = (bf16[256,256]{1,0:T(8,128)(2,1)S(1)}, bf16[256,256]{1,0:T(8,128)(2,1)S(1)}, u32[]{:S(2)}, u32[]{:S(2)}) collective-permute-start(bf16[256,256]{1,0:T(8,128)(2,1)S(1)} %copy-done.9), channel_id=1, source_target_pairs={{0,1},{1,0},{2,3},{3,2},{4,5},{5,4},{6,7},{7,6},{8,9},{9,8},{10,11... | collective-permute-start | bytes 393224 | tf_op jit(solution)/shard_map/ppermute | solution.py:49
  7.3 15.1 %collective-permute-start.8 = (bf16[1280,128]{1,0:T(8,128)(2,1)S(1)}, bf16[1280,128]{1,0:T(8,128)(2,1)S(1)}, u32[]{:S(2)}, u32[]{:S(2)}) collective-permute-start(bf16[1280,128]{1,0:T(8,128)(2,1)S(1)} %pad_maximum_fusion.2), channel_id=1, source_target_pairs={{0,8},{8,0},{1,9},{9,1},{2,10},{10,2},{3,11},{11,3},{4,12},{12,4},... | collective-permute-start | bytes 983048 | tf_op jit(solution)/shard_map/ppermute | solution.py:53
  18.4 13.1 %collective-permute-start.6 = (bf16[2,256,256]{2,1,0:T(8,128)(2,1)S(1)}, bf16[2,256,256]{2,1,0:T(8,128)(2,1)S(1)}, u32[]{:S(2)}, u32[]{:S(2)}) collective-permute-start(bf16[2,256,256]{2,1,0:T(8,128)(2,1)S(1)} %pad_maximum_fusion.3.b0), channel_id=1, source_target_pairs={{0,4},{2,6},{4,0},{6,2},{1,5},{3,7},{5,1},{7,3},{8,12},{10,14},{12... | collective-permute-start | bytes 786440 | tf_op jit(solution)/shard_map/ppermute | solution.py:41
  21.7 13.7 %collective-permute-start.7 = (bf16[2,256,256]{2,1,0:T(8,128)(2,1)S(1)}, bf16[2,256,256]{2,1,0:T(8,128)(2,1)S(1)}, u32[]{:S(2)}, u32[]{:S(2)}) collective-permute-start(bf16[2,256,256]{2,1,0:T(8,128)(2,1)S(1)} %pad_maximum_fusion.3.b0), channel_id=1, source_target_pairs={{0,6},{2,0},{4,2},{6,4},{1,7},{3,1},{5,3},{7,5},{8,14},{10,8},{12,... | collective-permute-start | bytes 786440 | tf_op jit(solution)/shard_map/ppermute | solution.py:41
  22.4 13.0 %collective-permute-start.9 = (bf16[1280,128]{1,0:T(8,128)(2,1)S(1)}, bf16[1280,128]{1,0:T(8,128)(2,1)S(1)}, u32[]{:S(2)}, u32[]{:S(2)}) collective-permute-start(bf16[1280,128]{1,0:T(8,128)(2,1)S(1)} %collective-permute-done.8.refs_1_), channel_id=1, source_target_pairs={{0,48},{16,0},{32,16},{48,32},{1,49},{17,1},{33,17},{49,33},{2,50}... | collective-permute-start | bytes 983048 | tf_op jit(solution)/shard_map/ppermute | solution.py:37
  24.8 10.6 %collective-permute-start.10 = (bf16[1280,128]{1,0:T(8,128)(2,1)S(1)}, bf16[1280,128]{1,0:T(8,128)(2,1)S(1)}, u32[]{:S(2)}, u32[]{:S(2)}) collective-permute-start(bf16[1280,128]{1,0:T(8,128)(2,1)S(1)} %collective-permute-done.8.refs_1_), channel_id=1, source_target_pairs={{0,16},{16,32},{32,48},{48,0},{1,17},{17,33},{33,49},{49,1},{2,18}... | collective-permute-start | bytes 983048 | tf_op jit(solution)/shard_map/ppermute | solution.py:37
  24.9 11.9 %collective-permute-start.11 = (bf16[1280,128]{1,0:T(8,128)(2,1)S(1)}, bf16[1280,128]{1,0:T(8,128)(2,1)}, u32[]{:S(2)}, u32[]{:S(2)}) collective-permute-start(bf16[1280,128]{1,0:T(8,128)(2,1)S(1)} %collective-permute-done.8.refs_1_), channel_id=1, source_target_pairs={{0,64},{64,0},{1,65},{65,1},{2,66},{66,2},{3,67},{67,3},{4,68},{68... | collective-permute-start | bytes 983048 | tf_op jit(solution)/shard_map/ppermute | solution.py:45
  31.4 9.3 %collective-permute-start.21 = (bf16[768,256]{1,0:T(8,128)(2,1)S(1)}, bf16[768,256]{1,0:T(8,128)(2,1)S(1)}, u32[]{:S(2)}, u32[]{:S(2)}) collective-permute-start(bf16[768,256]{1,0:T(8,128)(2,1)S(1)} %get-tuple-element.118), channel_id=1, source_target_pairs={{0,8},{8,0},{1,9},{9,1},{2,10},{10,2},{3,11},{11,3},{4,12},{12,4},... | collective-permute-start | bytes 1179656 | tf_op jit(solution)/shard_map/ppermute | solution.py:53
  38.2 39.8 %collective-permute-start.12 = (bf16[256,2048]{1,0:T(8,128)(2,1)S(1)}, bf16[256,2048]{1,0:T(8,128)(2,1)}, u32[]{:S(2)}, u32[]{:S(2)}) collective-permute-start(bf16[256,2048]{1,0:T(8,128)(2,1)S(1)} %normalise.1.own), channel_id=1, source_target_pairs={{0,8},{8,0},{1,9},{9,1},{2,10},{10,2},{3,11},{11,3},{4,12},{12,4},... | collective-permute-start | bytes 3145736 | tf_op jit(solution)/shard_map/ppermute | solution.py:53
  38.8 9.6 %collective-permute-start.13 = (bf16[1280,128]{1,0:T(8,128)(2,1)}, bf16[1280,128]{1,0:T(8,128)(2,1)S(1)}, u32[]{:S(2)}, u32[]{:S(2)}) collective-permute-start(bf16[1280,128]{1,0:T(8,128)(2,1)} %collective-permute-done.4.refs_2_), channel_id=1, source_target_pairs={{0,48},{16,0},{32,16},{48,32},{1,49},{17,1},{33,17},{49,33},{2,50}... | collective-permute-start | bytes 983048 | tf_op jit(solution)/shard_map/ppermute | solution.py:37
  40.7 10.3 %collective-permute-start.15 = (bf16[1280,128]{1,0:T(8,128)(2,1)S(1)}, bf16[1280,128]{1,0:T(8,128)(2,1)}, u32[]{:S(2)}, u32[]{:S(2)}) collective-permute-start(bf16[1280,128]{1,0:T(8,128)(2,1)S(1)} %copy-done.19), channel_id=1, source_target_pairs={{0,16},{16,32},{32,48},{48,0},{1,17},{17,33},{33,49},{49,1},{2,18}... | collective-permute-start | bytes 983048 | tf_op jit(solution)/shard_map/ppermute | solution.py:37
  40.8 32.5 %collective-permute-start.22 = (bf16[2,768,256]{2,1,0:T(8,128)(2,1)S(1)}, bf16[2,768,256]{2,1,0:T(8,128)(2,1)}, u32[]{:S(2)}, u32[]{:S(2)}) collective-permute-start(bf16[2,768,256]{2,1,0:T(8,128)(2,1)S(1)} %pad_maximum_fusion.cache0), channel_id=1, source_target_pairs={{0,64},{64,0},{1,65},{65,1},{2,66},{66,2},{3,67},{67,3},{4,68},{68... | collective-permute-start | bytes 2359304 | tf_op jit(solution)/shard_map/ppermute | solution.py:45
  44.3 13.2 %collective-permute-start.19 = (bf16[1280,128]{1,0:T(8,128)(2,1)}, bf16[1280,128]{1,0:T(8,128)(2,1)S(1)}, u32[]{:S(2)}, u32[]{:S(2)}) collective-permute-start(bf16[1280,128]{1,0:T(8,128)(2,1)} %collective-permute-done.4.refs_2_), channel_id=1, source_target_pairs={{0,16},{16,32},{32,48},{48,0},{1,17},{17,33},{33,49},{49,1},{2,18}... | collective-permute-start | bytes 983048 | tf_op jit(solution)/shard_map/ppermute | solution.py:37
  51.0 13.2 %collective-permute-start.16 = (bf16[1280,128]{1,0:T(8,128)(2,1)S(1)}, bf16[1280,128]{1,0:T(8,128)(2,1)}, u32[]{:S(2)}, u32[]{:S(2)}) collective-permute-start(bf16[1280,128]{1,0:T(8,128)(2,1)S(1)} %copy-done.22), channel_id=1, source_target_pairs={{0,48},{16,0},{32,16},{48,32},{1,49},{17,1},{33,17},{49,33},{2,50}... | collective-permute-start | bytes 983048 | tf_op jit(solution)/shard_map/ppermute | solution.py:37
  57.5 9.1 %collective-permute-start.20 = (bf16[1280,128]{1,0:T(8,128)(2,1)}, bf16[1280,128]{1,0:T(8,128)(2,1)}, u32[]{:S(2)}, u32[]{:S(2)}) collective-permute-start(bf16[1280,128]{1,0:T(8,128)(2,1)} %collective-permute-done.11.refs_3_), channel_id=1, source_target_pairs={{0,16},{16,32},{32,48},{48,0},{1,17},{17,33},{33,49},{49,1},{2,18}... | collective-permute-start | bytes 983048 | tf_op jit(solution)/shard_map/ppermute | solution.py:37
  64.2 9.1 %collective-permute-start.18 = (bf16[1280,128]{1,0:T(8,128)(2,1)}, bf16[1280,128]{1,0:T(8,128)(2,1)}, u32[]{:S(2)}, u32[]{:S(2)}) collective-permute-start(bf16[1280,128]{1,0:T(8,128)(2,1)} %collective-permute-done.16.refs_9_), channel_id=1, source_target_pairs={{0,64},{64,0},{1,65},{65,1},{2,66},{66,2},{3,67},{67,3},{4,68},{68... | collective-permute-start | bytes 983048 | tf_op jit(solution)/shard_map/ppermute | solution.py:45
  73.4 12.2 %collective-permute-start.23 = (bf16[2048,128]{1,0:T(8,128)(2,1)S(1)}, bf16[2048,128]{1,0:T(8,128)(2,1)}, u32[]{:S(2)}, u32[]{:S(2)}) collective-permute-start(bf16[2048,128]{1,0:T(8,128)(2,1)S(1)} %copy-done.12), channel_id=1, source_target_pairs={{0,64},{64,0},{1,65},{65,1},{2,66},{66,2},{3,67},{67,3},{4,68},{68... | collective-permute-start | bytes 1572872 | tf_op jit(solution)/shard_map/ppermute | solution.py:45
  74.9 11.7 %collective-permute-start.24 = (bf16[2048,128]{1,0:T(8,128)(2,1)S(1)}, bf16[2048,128]{1,0:T(8,128)(2,1)S(1)}, u32[]{:S(2)}, u32[]{:S(2)}) collective-permute-start(bf16[2048,128]{1,0:T(8,128)(2,1)S(1)} %copy-done.12), channel_id=1, source_target_pairs={{0,48},{16,0},{32,16},{48,32},{1,49},{17,1},{33,17},{49,33},{2,50}... | collective-permute-start | bytes 1572872 | tf_op jit(solution)/shard_map/ppermute | solution.py:37
  78.0 11.8 %collective-permute-start.25 = (bf16[2048,128]{1,0:T(8,128)(2,1)S(1)}, bf16[2048,128]{1,0:T(8,128)(2,1)S(1)}, u32[]{:S(2)}, u32[]{:S(2)}) collective-permute-start(bf16[2048,128]{1,0:T(8,128)(2,1)S(1)} %copy-done.12), channel_id=1, source_target_pairs={{0,16},{16,32},{32,48},{48,0},{1,17},{17,33},{33,49},{49,1},{2,18}... | collective-permute-start | bytes 1572872 | tf_op jit(solution)/shard_map/ppermute | solution.py:37
  89.8 9.7 %collective-permute-start.26 = (bf16[1024,128]{1,0:T(8,128)(2,1)S(1)}, bf16[1024,128]{1,0:T(8,128)(2,1)S(1)}, u32[]{:S(2)}, u32[]{:S(2)}) collective-permute-start(bf16[1024,128]{1,0:T(8,128)(2,1)S(1)} %get-tuple-element.93.q0), channel_id=1, source_target_pairs={{0,16},{16,32},{32,48},{48,0},{1,17},{17,33},{33,49},{49,1},{2,18}... | collective-permute-start | bytes 786440 | tf_op jit(solution)/shard_map/ppermute | solution.py:37
  89.8 9.8 %collective-permute-start.27 = (bf16[1024,128]{1,0:T(8,128)(2,1)S(1)}, bf16[1024,128]{1,0:T(8,128)(2,1)S(1)}, u32[]{:S(2)}, u32[]{:S(2)}) collective-permute-start(bf16[1024,128]{1,0:T(8,128)(2,1)S(1)} %get-tuple-element.93.q0), channel_id=1, source_target_pairs={{0,32},{16,48},{32,0},{48,16},{1,33},{17,49},{33,1},{49,17},{2,34}... | collective-permute-start | bytes 786440 | tf_op jit(solution)/shard_map/ppermute | solution.py:37
  91.3 9.7 %collective-permute-start.28 = (bf16[1024,128]{1,0:T(8,128)(2,1)S(1)}, bf16[1024,128]{1,0:T(8,128)(2,1)}, u32[]{:S(2)}, u32[]{:S(2)}) collective-permute-start(bf16[1024,128]{1,0:T(8,128)(2,1)S(1)} %get-tuple-element.93.q0), channel_id=1, source_target_pairs={{0,48},{16,0},{32,16},{48,32},{1,49},{17,1},{33,17},{49,33},{2,50}... | collective-permute-start | bytes 786440 | tf_op jit(solution)/shard_map/ppermute | solution.py:37
  92.6 29.8 %collective-permute-start.31 = (bf16[2048,128]{1,0:T(8,128)(2,1)}, bf16[2048,128]{1,0:T(8,128)(2,1)S(1)}, u32[]{:S(2)}, u32[]{:S(2)}) collective-permute-start(bf16[2048,128]{1,0:T(8,128)(2,1)} %collective-permute-done.23.refs_1_), channel_id=1, source_target_pairs={{0,48},{16,0},{32,16},{48,32},{1,49},{17,1},{33,17},{49,33},{2,50}... | collective-permute-start | bytes 1572872 | tf_op jit(solution)/shard_map/ppermute | solution.py:37
  93.4 29.1 %collective-permute-start.32 = (bf16[2048,128]{1,0:T(8,128)(2,1)}, bf16[2048,128]{1,0:T(8,128)(2,1)S(1)}, u32[]{:S(2)}, u32[]{:S(2)}) collective-permute-start(bf16[2048,128]{1,0:T(8,128)(2,1)} %collective-permute-done.23.refs_1_), channel_id=1, source_target_pairs={{0,16},{16,32},{32,48},{48,0},{1,17},{17,33},{33,49},{49,1},{2,18}... | collective-permute-start | bytes 1572872 | tf_op jit(solution)/shard_map/ppermute | solution.py:37
  99.4 23.0 %collective-permute-start.30 = (bf16[2048,128]{1,0:T(8,128)(2,1)S(1)}, bf16[2048,128]{1,0:T(8,128)(2,1)}, u32[]{:S(2)}, u32[]{:S(2)}) collective-permute-start(bf16[2048,128]{1,0:T(8,128)(2,1)S(1)} %copy-done.12), channel_id=1, source_target_pairs={{0,32},{16,48},{32,0},{48,16},{1,33},{17,49},{33,1},{49,17},{2,34}... | collective-permute-start | bytes 1572872 | tf_op jit(solution)/shard_map/ppermute | solution.py:37
  122.5 15.1 %collective-permute-start.33 = (bf16[144,1024]{1,0:T(8,128)(2,1)S(1)}, bf16[144,1024]{1,0:T(8,128)(2,1)S(1)}, u32[]{:S(2)}, u32[]{:S(2)}) collective-permute-start(bf16[144,1024]{1,0:T(8,128)(2,1)S(1)} %get-tuple-element.105), channel_id=1, source_target_pairs={{0,48},{16,0},{32,16},{48,32},{1,49},{17,1},{33,17},{49,33},{2,50}... | collective-permute-start | bytes 884744 | tf_op jit(solution)/shard_map/ppermute | solution.py:37
  130.8 14.0 %collective-permute-start.35 = (bf16[144,1024]{1,0:T(8,128)(2,1)S(1)}, bf16[144,1024]{1,0:T(8,128)(2,1)S(1)}, u32[]{:S(2)}, u32[]{:S(2)}) collective-permute-start(bf16[144,1024]{1,0:T(8,128)(2,1)S(1)} %get-tuple-element.107), channel_id=1, source_target_pairs={{0,16},{16,32},{32,48},{48,0},{1,17},{17,33},{33,49},{49,1},{2,18}... | collective-permute-start | bytes 884744 | tf_op jit(solution)/shard_map/ppermute | solution.py:37
  131.4 17.0 %collective-permute-start.37 = (bf16[2048,128]{1,0:T(8,128)(2,1)}, bf16[2048,128]{1,0:T(8,128)(2,1)}, u32[]{:S(2)}, u32[]{:S(2)}) collective-permute-start(bf16[2048,128]{1,0:T(8,128)(2,1)} %collective-permute-done.30.refs_4_), channel_id=1, source_target_pairs={{0,64},{64,0},{1,65},{65,1},{2,66},{66,2},{3,67},{67,3},{4,68},{68... | collective-permute-start | bytes 1572872 | tf_op jit(solution)/shard_map/ppermute | solution.py:45
  160.8 12.6 %collective-permute-start.38 = (bf16[2,512,128]{2,1,0:T(8,128)(2,1)S(1)}, bf16[2,512,128]{2,1,0:T(8,128)(2,1)S(1)}, u32[]{:S(2)}, u32[]{:S(2)}) collective-permute-start(bf16[2,512,128]{2,1,0:T(8,128)(2,1)S(1)} %get-tuple-element.114), channel_id=1, source_target_pairs={{0,2},{2,4},{4,6},{6,0},{1,3},{3,5},{5,7},{7,1},{8,10},{10,12},{12... | collective-permute-start | bytes 786440 | tf_op jit(solution)/shard_map/ppermute | solution.py:41
  (41 other events, 337.4 us)

commit v5 on v2

--- a/solution.py
+++ b/solution.py
@@ -37,35 +37,16 @@
     return lax.ppermute(x, "y", [(i, (i + k) % 4) for i in range(4)])
 
 
-def along_z(x, k):
-    return lax.ppermute(x, "z", [(i, (i + k) % 4) for i in range(4)])
-
-
 def across_x(x):
     return lax.ppermute(x, "xl", [(0, 1), (1, 0)])
 
 
-def across_far(x):
-    return lax.ppermute(x, "xh", [(0, 1), (1, 0)])
-
-
 def across_core(x):
     return lax.ppermute(x, "c", [(0, 1), (1, 0)])
 
 
 def tie(a, b):
     return lax.optimization_barrier((a, b))
-
-
-def gather_parts(w0, w1):
-    ym0, yp0, a0 = along_y(w0, 3), along_y(w0, 1), across_x(w0)
-    ym1, yp1, a1 = along_y(w1, 3), along_y(w1, 1), across_x(w1)
-    far0, far1 = along_y(yp0, 1), along_y(ym1, 3)
-    am0, ap0 = along_y(a0, 3), along_y(a0, 1)
-    am1, ap1 = along_y(a1, 3), along_y(a1, 1)
-    afar0, afar1 = across_x(far0), across_x(far1)
-    pairs = [(w0, w1), (a0, a1), (ym0, ym1), (am0, am1), (far0, far1), (afar0, afar1), (yp0, yp1), (ap0, ap1)]
-    return [part for pair in pairs for part in pair]
 
 
 def chip_order():
@@ -88,38 +69,37 @@
         c.wait()
 
 
-def norm_kernel(idx, gain, b0, b1, b2, b3, normed, held, sem):
-    refs = (b0, b1, b2, b3)
-    run([pltpu.make_async_copy(r, held.at[i], sem.at[i]) for i, r in enumerate(refs)])
+def norm_kernel(idx, gain, blocks, normed, held, sem):
+    run([pltpu.make_async_copy(blocks, held, sem.at[0])])
     total = jnp.zeros((256, 1), F32)
     for k in range(8):
-        v = held[k // 2, k % 2].astype(F32)
+        v = held[k].astype(F32)
         total = total + jnp.sum(v * v, axis=1, keepdims=True)
     scale = lax.rsqrt(total * (1.0 / 2048) + EPS)
     for k in range(8):
-        v = held[k // 2, k % 2].astype(F32) * scale * gain[idx[k]].astype(F32)
-        normed[:, pl.ds(pl.multiple_of(idx[8 + k] * 256, 256), 256)] = v.astype(BF16)
+        v = held[k].astype(F32) * scale * gain[k].astype(F32)
+        normed[:, pl.ds(pl.multiple_of(idx[k] * 256, 256), 256)] = v.astype(BF16)
 
 
 def normalise(idx, gain, blocks):
     return pl.pallas_call(
         norm_kernel,
         out_shape=jax.ShapeDtypeStruct((256, 2048), BF16),
-        in_specs=[SMEM, VMEM] + [HBM] * 4,
+        in_specs=[SMEM, VMEM, ANY],
         out_specs=VMEM,
-        scratch_shapes=[pltpu.VMEM((4, 2, 256, 256), BF16), pltpu.SemaphoreType.DMA((4,))],
+        scratch_shapes=[pltpu.VMEM((8, 256, 256), BF16), pltpu.SemaphoreType.DMA((1,))],
         compiler_params=pltpu.CompilerParams(vmem_limit_bytes=8 << 20),
         cost_estimate=pl.CostEstimate(flops=1 << 24, bytes_accessed=2 << 20, transcendentals=0),
         name="normalise",
-    )(idx, gain, *blocks)
+    )(idx, gain, blocks)
 
 
 GROUPS = ((0, 512), (512, 768))
 
 
 def project_kernel(idx, routes, router, own, other, *refs):
-    blocks = refs[:16]
-    q_out, kv_out, gates, xs, held, sel, sem = refs[16:]
+    blocks = refs[:8]
+    q_out, kv_out, gates, xs, held, sel, sem = refs[8:]
     core = idx[8]
     copies = []
     for i, r in enumerate((own, other)):
@@ -131,7 +111,7 @@
             at = pl.ds(pl.multiple_of(lane, H), H)
             copies.append(
                 pltpu.make_async_copy(
-                    blocks[k].at[pl.ds(start, rows)],
+                    blocks[k // 2].at[k % 2, pl.ds(start, rows)],
                     held.at[pl.ds(start, rows), at],
                     sem.at[16 * g + k],
                 )
@@ -186,7 +166,7 @@
             jax.ShapeDtypeStruct((512, 2 * H), BF16),
             jax.ShapeDtypeStruct((512, 2), F32),
         ),
-        in_specs=[SMEM, VMEM, VMEM] + [HBM] * 18,
+        in_specs=[SMEM, VMEM, VMEM] + [HBM] * 10,
         out_specs=(VMEM, VMEM, VMEM),
         scratch_shapes=[
             pltpu.VMEM((512, 2048), BF16),
@@ -399,8 +379,7 @@
 
 def out_kernel(idx, routes, own, other, *refs):
     blocks = refs[:8]
-    outs = refs[8:12]
-    held, padded, sem = refs[12:]
+    out, held, padded, sem = refs[8:]
     core = idx[8]
     copies = [
         pltpu.make_async_copy(r, held.at[idx[k]], sem.at[k]) for k, r in enumerate(blocks)
@@ -420,26 +399,23 @@
                 )
     for c in copies:
         c.wait()
-    for dz in range(4):
+    for k in range(0, 8, 2):
         value = jnp.zeros((512, 256), F32)
         for side in range(2):
             head = core if side == 0 else 1 - core
             rows = pl.ds(pl.multiple_of(head * 1024, 1024), 1024)
-            w = jnp.concatenate(
-                [held[idx[9 + 2 * dz], rows], held[idx[10 + 2 * dz], rows]], axis=1
-            )
+            w = jnp.concatenate([held[k, rows], held[k + 1, rows]], axis=1)
             value += jnp.dot(padded[side], w, preferred_element_type=F32)
         for s in range(2):
-            outs[dz][s] = value[:, s * H : (s + 1) * H].astype(outs[dz].dtype)
+            out[k + s] = value[:, s * H : (s + 1) * H].astype(BF16)
 
 
 def project_out(idx, routes, own, other, blocks):
     return pl.pallas_call(
         out_kernel,
-        out_shape=(jax.ShapeDtypeStruct((2, 512, H), F32),)
-        + tuple(jax.ShapeDtypeStruct((2, 512, H), BF16) for _ in range(3)),
+        out_shape=jax.ShapeDtypeStruct((8, 512, H), BF16),
         in_specs=[SMEM, VMEM, VMEM, VMEM] + [HBM] * 8,
-        out_specs=tuple([VMEM] * 4),
+        out_specs=VMEM,
         scratch_shapes=[
             pltpu.VMEM((8, 2048, H), BF16),
             pltpu.VMEM((2, 512, 1024), BF16),
@@ -464,7 +440,6 @@
     prefix_lengths,
 ):
     xl, y, c = (lax.axis_index(a) for a in WIDE)
-    z, xh = (lax.axis_index(a) for a in NARROW)
     first_core = c == 0
     chips = chip_order()
 
@@ -478,9 +453,7 @@
     def weights_of(h):
         return jnp.concatenate([head_rows(query_weight, h), head_rows(kv_weight, h)], axis=0)
 
-    gathered = gather_parts(weights_of(c), across_core(weights_of(1 - c)))
-    pair = jnp.stack([tokens, across_far(tokens)])
-    blocks = [pair] + [along_z(pair, k) for k in (1, 2, 3)]
+    w = jnp.stack([weights_of(c), across_core(weights_of(1 - c))])
     other_routes = across_core(routes)
     both_routes = jnp.where(
         first_core,
@@ -492,21 +465,27 @@
         return lax.dynamic_slice_in_dim(prefix_cache, h * 2 * H, 2 * H, 1)
 
     cache = jnp.stack([cache_of(c), across_core(cache_of(1 - c))])
-    cache_out, gathered[2] = tie(cache, gathered[2])
-    caches = [cache, across_x(cache_out)]
-
-    token_src = [lax.rem(z + 4 - dz, 4) * 2 + (xh ^ s) for dz in range(4) for s in range(2)]
-    places = [lax.rem(lax.rem(v, 4) + 4 - y, 4) * 2 + (v // 4 ^ xl) for v in token_src]
-    normed = normalise(table(token_src + places), norm_gain.reshape(8, 1, 256), blocks)
-    out_early, gathered[7] = tie(out_weight, gathered[7])
+    tokens, w = tie(tokens, w)
+    copies = jnp.broadcast_to(tokens[None], (8,) + tokens.shape)
+    blocks = lax.all_to_all(copies, NARROW, 0, 0, tiled=True)
+    far, ym, yp, a = along_y(w, 2), along_y(w, 3), along_y(w, 1), across_x(w)
+    caches = [cache, across_x(cache)]
+    far, ym, yp, a, blocks, caches = lax.optimization_barrier((far, ym, yp, a, blocks, caches))
+    am, ap, afar = along_y(a, 3), along_y(a, 1), across_x(far)
+    gathered = [w, a, ym, am, far, afar, yp, ap]
+
+    places = [(k % 4 - y + 4) % 4 * 2 + (k // 4 ^ xl) for k in range(8)]
+    normed = normalise(table(places), norm_gain.reshape(8, 1, 256), blocks)
+    out_early, am, ap = lax.optimization_barrier((out_weight, am, ap))
+    gathered[3], gathered[7] = am, ap
     o_ym, o_yp, o_a = along_y(out_early, 3), along_y(out_early, 1), across_x(out_early)
     q, kv, gates = project(
         table(chips + [c]), both_routes, router.T, normed, across_core(normed), gathered
     )
     kvs = [kv, across_x(kv)]
-    q_out, o_a, o_ym, o_yp = lax.optimization_barrier((q, o_a, o_ym, o_yp))
+    q_out, o_ym, o_yp = lax.optimization_barrier((q, o_ym, o_yp))
     qs = [q] + [along_y(q_out, k) for k in (1, 2, 3)]
-    out_late, o_a_late, qs[2] = lax.optimization_barrier((out_weight, o_a, qs[2]))
+    out_late, o_a_late, kvs[1] = lax.optimization_barrier((out_weight, o_a, kvs[1]))
     o_far, o_am, o_ap = along_y(out_late, 2), along_y(o_a_late, 3), along_y(o_a_late, 1)
 
     firsts = [(xl * 4 + lax.rem(y + 4 - k, 4)) * 512 for k in range(4)]
@@ -520,14 +499,11 @@
     gate_row = gates.reshape(2, 256, 2).transpose(0, 2, 1).reshape(1, 1024)
     attended = combine(gate_row, parts)
 
-    dests = [lax.rem(z + dz, 4) * 2 + (xh ^ s) for dz in range(4) for s in range(2)]
     sums = project_out(
-        table(chips + [c] + dests), both_routes, attended, across_core(attended), out_blocks
+        table(chips + [c]), both_routes, attended, across_core(attended), out_blocks
     )
-    total = sums[0]
-    for k in (1, 2, 3):
-        total = total + along_z(sums[k], k).astype(F32)
-    total = total[0] + across_far(total[1].astype(BF16)).astype(F32)
+    sums = lax.all_to_all(sums, NARROW, 0, 0, tiled=True)
+    total = jnp.sum(sums.astype(F32), axis=0)
     here = lax.dynamic_slice_in_dim(total, c * 256, 256, 0).astype(BF16)
     there = lax.dynamic_slice_in_dim(total, (1 - c) * 256, 256, 0).astype(BF16)
     there = across_core(there)

time: 188 us -> 184 us (0.979)
  blocking collectives: 0 us -> 22.8 us
  starting transfers between devices: 56.7 us -> 41.3 us
  Pallas kernels: 33.8 us -> 26.8 us
  waiting for transfers between devices: 88.5 us -> 85.1 us
    ppermute x21 -> x16, waiting for transfers between devices: 36 us -> 70.9 us  [along_y(): return lax.ppermute(x, 'y', [(i, (i + k) % 4) for i in range(4)])]
    ppermute x8 -> x0, waiting for transfers between devices: 23.6 us -> none  [the longest x6 16.7 us: along_z(): return lax.ppermute(x, 'z', [(i, (i + k) % 4) for i in range(4)])]
    all_to_all x0 -> x1, blocking collectives: none -> 22.8 us  [on_device(): sums = lax.all_to_all(sums, NARROW, 0, 0, tiled=True)]
    ppermute x8 -> x6, waiting for transfers between devices: 26.9 us -> 10.4 us  [across_x(): return lax.ppermute(x, 'xl', [(0, 1), (1, 0)])]
    ppermute x8 -> x0, starting transfers between devices: 13.5 us -> none  [the longest x6 9.46 us: along_z(): return lax.ppermute(x, 'z', [(i, (i + k) % 4) for i in range(4)])]
    ppermute x21 -> x16, starting transfers between devices: 28.6 us -> 18.6 us  [along_y(): return lax.ppermute(x, 'y', [(i, (i + k) % 4) for i in range(4)])]
    pallas_call x1, Pallas kernels: 17.6 us -> 10.4 us  [attend(): pl.pallas_call(attend_kernel, out_shape=tuple((jax.ShapeDtypeStruct((H +...]
    all_to_all x0 -> x1, starting transfers between devices: none -> 6.59 us  [on_device(): blocks = lax.all_to_all(copies, NARROW, 0, 0, tiled=True)]
  transfers between devices with their start and end apart: 43 -> 29, of which waited for: 24 -> 18; matrix products, arithmetic and copies ran while one was open for 2% -> 1% of each run, Pallas kernels for 14% -> 10%
where the time goes in v5:
time: 184 us; the launch traced here: 182 us
  waiting for transfers between devices  85.1 us (46%)
  starting transfers between devices  41.3 us (22%)
  Pallas kernels  26.8 us (15%)
  blocking collectives  22.8 us (12%)
  local copies, waits for them, and re-layouts  4.74 us (3%)
    ppermute x16, waiting for transfers between devices, along_y(): return lax.ppermute(x, 'y', [(i, (i + k) % 4) for i in range(4)])  70.9 us
    all_to_all x1, blocking collectives, on_device(): sums = lax.all_to_all(sums, NARROW, 0, 0, tiled=True)  22.8 us
    ppermute x16, starting transfers between devices, along_y(): return lax.ppermute(x, 'y', [(i, (i + k) % 4) for i in range(4)])  18.6 us
    ppermute x6, starting transfers between devices, across_core(): return lax.ppermute(x, 'c', [(0, 1), (1, 0)])  11.6 us
    pallas_call x1, Pallas kernels, attend(): pl.pallas_call(attend_kernel, out_shape=tuple((jax.ShapeDtypeStruct((H +...  10.4 us
    ppermute x6, waiting for transfers between devices, across_x(): return lax.ppermute(x, 'xl', [(0, 1), (1, 0)])  10.4 us
    pallas_call x1, Pallas kernels, project(): pl.pallas_call(project_kernel, out_shape=(jax.ShapeDtypeStruct((1024, H),...  7.38 us
    pallas_call x1, Pallas kernels, project_out(): pl.pallas_call(out_kernel, out_shape=jax.ShapeDtypeStruct((8, 512, H), BF...  7.35 us
  transfers between devices with their start and end apart: 29, of which 18 were waited for; matrix products, arithmetic and copies ran while one was open for 1% of the time, Pallas kernels for 10%

profile of v5, /device:TPU:3, one launch (start us, length us, event | category | flops | bytes accessed | tf_op | source)
XLA Modules:
  0.0 182.1 jit_solution(3384589401832496604)
XLA Ops:
  5.3 6.6 %all-to-all-start = ((bf16[8,256,256]{2,1,0:T(8,128)(2,1)}), bf16[8,256,256]{2,1,0:T(8,128)(2,1)S(1)}, u32[]{:S(2)}, u32[]{:S(2)}) async-start(bf16[8,256,256]{2,1,0:T(8,128)(2,1)} %broadcast_in_dim.2), calls=%async_computation | async-start | bytes 2097152 | tf_op jit(solution)/shard_map/all_to_all | solution.py:470
  12.0 1.2 collective-permute-start.7
  13.3 2.9 %collective-permute-start.2 = (bf16[2,1280,128]{2,1,0:T(8,128)(2,1)S(1)}, bf16[2,1280,128]{2,1,0:T(8,128)(2,1)}, u32[]{:S(2)}, u32[]{:S(2)}) collective-permute-start(bf16[2,1280,128]{2,1,0:T(8,128)(2,1)S(1)} %pad_maximum_fusion.1.refs_0_), channel_id=1, source_target_pairs={{0,32},{16,48},{32,0},{48,16},{1,33},{17,49},{33,1},{49,17},{2,34}... | collective-permute-start | bytes 1966088 | tf_op jit(solution)/shard_map/ppermute | solution.py:37
  18.1 12.2 %collective-permute-done.2.refs_4_ = bf16[2,1280,128]{2,1,0:T(8,128)(2,1)} collective-permute-done((bf16[2,1280,128]{2,1,0:T(8,128)(2,1)S(1)}, bf16[2,1280,128]{2,1,0:T(8,128)(2,1)}, u32[]{:S(2)}, u32[]{:S(2)}) %collective-permute-start.2) | collective-permute-done | bytes 655392 | tf_op jit(solution)/shard_map/ppermute | solution.py:37
  30.2 14.6 %collective-permute-done.3.refs_2_ = bf16[2,1280,128]{2,1,0:T(8,128)(2,1)} collective-permute-done((bf16[2,1280,128]{2,1,0:T(8,128)(2,1)S(1)}, bf16[2,1280,128]{2,1,0:T(8,128)(2,1)}, u32[]{:S(2)}, u32[]{:S(2)}) %collective-permute-start.3) | collective-permute-done | bytes 655392 | tf_op jit(solution)/shard_map/ppermute | solution.py:37
  45.6 10.4 %collective-permute-done.5.refs_1_ = bf16[2,1280,128]{2,1,0:T(8,128)(2,1)} collective-permute-done((bf16[2,1280,128]{2,1,0:T(8,128)(2,1)S(1)}, bf16[2,1280,128]{2,1,0:T(8,128)(2,1)}, u32[]{:S(2)}, u32[]{:S(2)}) %collective-permute-start.5) | collective-permute-done | bytes 655392 | tf_op jit(solution)/shard_map/ppermute | solution.py:41
  56.0 1.3 normalise.1.own
  57.3 1.3 collective-permute-start.8
  58.6 1.3 collective-permute-start.10
  59.9 1.4 collective-permute-start.9
  63.7 12.8 %collective-permute-done.10.refs_7_ = bf16[2,1280,128]{2,1,0:T(8,128)(2,1)S(1)} collective-permute-done((bf16[2,1280,128]{2,1,0:T(8,128)(2,1)}, bf16[2,1280,128]{2,1,0:T(8,128)(2,1)S(1)}, u32[]{:S(2)}, u32[]{:S(2)}) %collective-permute-start.10) | collective-permute-done | bytes 655392 | tf_op jit(solution)/shard_map/ppermute | solution.py:37
  76.7 2.5 %collective-permute-start.12 = (bf16[2048,128]{1,0:T(8,128)(2,1)}, bf16[2048,128]{1,0:T(8,128)(2,1)S(1)}, u32[]{:S(2)}, u32[]{:S(2)}) collective-permute-start(bf16[2048,128]{1,0:T(8,128)(2,1)} %refs_0_.1), channel_id=1, source_target_pairs={{0,48},{16,0},{32,16},{48,32},{1,49},{17,1},{33,17},{49,33},{2,50}... | collective-permute-start | bytes 1572872 | tf_op jit(solution)/shard_map/ppermute | solution.py:37
  79.2 7.4 %project.1 = (bf16[1024,128]{1,0:T(8,128)(2,1)S(1)}, bf16[512,256]{1,0:T(8,128)(2,1)S(1)}, f32[512,2]{1,0:T(8,128)S(1)}) custom-call(s32[9]{0:T(128)S(1)} %stack.122.idx, s32[512,2]{1,0:T(8,128)S(1)} %broadcast_select_fusion.routes, bf16[8,2048]{1,0:T(8,128)(2,1)S(1)} %bitcast.35, bf16[256,2048]{1,0:T(8,128)(2,1)} %copy-done, ...), custom_call_target="tpu_custom_call" | custom-call | flops 6442450944 | bytes 8388608 | tf_op jit(solution)/shard_map/project/pallas_call | solution.py:162
  86.7 1.3 collective-permute-start.18
  87.9 1.4 collective-permute-done.12.refs_2_
  89.3 3.0 %collective-permute-done.13.refs_6_ = bf16[2048,128]{1,0:T(8,128)(2,1)S(1)} collective-permute-done((bf16[2048,128]{1,0:T(8,128)(2,1)}, bf16[2048,128]{1,0:T(8,128)(2,1)S(1)}, u32[]{:S(2)}, u32[]{:S(2)}) %collective-permute-start.13) | collective-permute-done | bytes 524320 | tf_op jit(solution)/shard_map/ppermute | solution.py:37
  92.3 1.5 collective-permute-start.15
  93.9 1.2 collective-permute-start.16
  95.2 1.9 %collective-permute-start.20 = (bf16[2048,128]{1,0:T(8,128)(2,1)}, bf16[2048,128]{1,0:T(8,128)(2,1)S(1)}, u32[]{:S(2)}, u32[]{:S(2)}) collective-permute-start(bf16[2048,128]{1,0:T(8,128)(2,1)} %collective-permute-done.17.refs_1_), channel_id=1, source_target_pairs={{0,48},{16,0},{32,16},{48,32},{1,49},{17,1},{33,17},{49,33},{2,50}... | collective-permute-start | bytes 1572872 | tf_op jit(solution)/shard_map/ppermute | solution.py:37
  97.1 3.9 %collective-permute-done.14.q1 = bf16[1024,128]{1,0:T(8,128)(2,1)S(1)} collective-permute-done((bf16[1024,128]{1,0:T(8,128)(2,1)S(1)}, bf16[1024,128]{1,0:T(8,128)(2,1)S(1)}, u32[]{:S(2)}, u32[]{:S(2)}) %collective-permute-start.14) | collective-permute-done | bytes 262176 | tf_op jit(solution)/shard_map/ppermute | solution.py:37
  101.0 2.2 %collective-permute-done.15.q2 = bf16[1024,128]{1,0:T(8,128)(2,1)S(1)} collective-permute-done((bf16[1024,128]{1,0:T(8,128)(2,1)S(1)}, bf16[1024,128]{1,0:T(8,128)(2,1)S(1)}, u32[]{:S(2)}, u32[]{:S(2)}) %collective-permute-start.15) | collective-permute-done | bytes 262176 | tf_op jit(solution)/shard_map/ppermute | solution.py:37
  103.9 2.2 %collective-permute-done.16.q3 = bf16[1024,128]{1,0:T(8,128)(2,1)} collective-permute-done((bf16[1024,128]{1,0:T(8,128)(2,1)S(1)}, bf16[1024,128]{1,0:T(8,128)(2,1)}, u32[]{:S(2)}, u32[]{:S(2)}) %collective-permute-start.16) | collective-permute-done | bytes 262176 | tf_op jit(solution)/shard_map/ppermute | solution.py:37
  106.1 10.4 %attend.1 = (bf16[144,1024]{1,0:T(8,128)(2,1)S(1)}, bf16[144,1024]{1,0:T(8,128)(2,1)S(1)}, bf16[144,1024]{1,0:T(8,128)(2,1)S(1)}, bf16[144,1024]{1,0:T(8,128)(2,1)S(1)}) custom-call(s32[9]{0:T(128)S(1)} %stack.146.idx, s32[4]{0:T(128)S(1)} %copy-done.4, s32[4]{0:T(128)S(1)} %copy-done.5, bf16[1024,128]{1,0:T(8,128)(2,1)} %copy-done.1, ...), custom_call_target="tpu_custom_call" | custom-call | flops 12884901888 | bytes 6291456 | tf_op jit(solution)/shard_map/attend/pallas_call | solution.py:325
  116.5 9.6 %collective-permute-done.19.refs_4_ = bf16[2048,128]{1,0:T(8,128)(2,1)} collective-permute-done((bf16[2048,128]{1,0:T(8,128)(2,1)}, bf16[2048,128]{1,0:T(8,128)(2,1)}, u32[]{:S(2)}, u32[]{:S(2)}) %collective-permute-start.19) | collective-permute-done | bytes 524320 | tf_op jit(solution)/shard_map/ppermute | solution.py:37
  126.1 3.7 %collective-permute-start.22 = (bf16[144,1024]{1,0:T(8,128)(2,1)S(1)}, bf16[144,1024]{1,0:T(8,128)(2,1)S(1)}, u32[]{:S(2)}, u32[]{:S(2)}) collective-permute-start(bf16[144,1024]{1,0:T(8,128)(2,1)S(1)} %get-tuple-element.59), channel_id=1, source_target_pairs={{0,48},{16,0},{32,16},{48,32},{1,49},{17,1},{33,17},{49,33},{2,50}... | collective-permute-start | bytes 884744 | tf_op jit(solution)/shard_map/ppermute | solution.py:37
  131.8 3.0 %collective-permute-done.22.p1 = bf16[144,1024]{1,0:T(8,128)(2,1)S(1)} collective-permute-done((bf16[144,1024]{1,0:T(8,128)(2,1)S(1)}, bf16[144,1024]{1,0:T(8,128)(2,1)S(1)}, u32[]{:S(2)}, u32[]{:S(2)}) %collective-permute-start.22) | collective-permute-done | bytes 294944 | tf_op jit(solution)/shard_map/ppermute | solution.py:37
  134.8 2.2 %collective-permute-done.23.p2 = bf16[144,1024]{1,0:T(8,128)(2,1)S(1)} collective-permute-done((bf16[144,1024]{1,0:T(8,128)(2,1)S(1)}, bf16[144,1024]{1,0:T(8,128)(2,1)S(1)}, u32[]{:S(2)}, u32[]{:S(2)}) %collective-permute-start.23) | collective-permute-done | bytes 294944 | tf_op jit(solution)/shard_map/ppermute | solution.py:37
  137.0 3.2 %collective-permute-done.24.p3 = bf16[144,1024]{1,0:T(8,128)(2,1)S(1)} collective-permute-done((bf16[144,1024]{1,0:T(8,128)(2,1)S(1)}, bf16[144,1024]{1,0:T(8,128)(2,1)S(1)}, u32[]{:S(2)}, u32[]{:S(2)}) %collective-permute-start.24) | collective-permute-done | bytes 294944 | tf_op jit(solution)/shard_map/ppermute | solution.py:37
  140.5 6.7 %collective-permute-start.25 = (bf16[1024,128]{1,0:T(8,128)(2,1)S(1)}, bf16[1024,128]{1,0:T(8,128)(2,1)S(1)}, u32[]{:S(2)}, u32[]{:S(2)}) collective-permute-start(bf16[1024,128]{1,0:T(8,128)(2,1)S(1)} %combine.1.own), channel_id=1, source_target_pairs={{0,8},{8,0},{1,9},{9,1},{2,10},{10,2},{3,11},{11,3},{4,12},{12,4},... | collective-permute-start | bytes 786440 | tf_op jit(solution)/shard_map/ppermute | solution.py:45
  148.3 7.4 %project_out.1 = bf16[8,512,128]{2,1,0:T(8,128)(2,1)S(1)} custom-call(s32[9]{0:T(128)S(1)} %stack.122.idx, s32[512,2]{1,0:T(8,128)S(1)} %broadcast_select_fusion.routes, bf16[1024,128]{1,0:T(8,128)(2,1)S(1)} %combine.1.own, bf16[1024,128]{1,0:T(8,128)(2,1)S(1)} %collective-permute-done.25.other, bf16[2048,128]{1,0:T(8,128)(2,1)} %refs_0_.1, ...), custom_call_target="tpu_custom_call" | custom-call | flops 4294967296 | bytes 6291456 | tf_op jit(solution)/shard_map/project_out/pallas_call | solution.py:414
  155.7 22.8 %all_to_all.10 = bf16[8,512,128]{2,1,0:T(8,128)(2,1)S(1)} all-to-all(bf16[8,512,128]{2,1,0:T(8,128)(2,1)S(1)} %project_out.1), channel_id=1, replica_groups=mesh['xl'=2,'y'=4,'c'=2,'z'=4,'xh'=2] {'z','xh'}, dimensions={0} | all-to-all | bytes 2097152 | tf_op jit(solution)/shard_map/all_to_all | solution.py:505
  178.6 1.9 %collective-permute-start.27 = (bf16[256,128]{1,0:T(8,128)(2,1)S(1)}, bf16[256,128]{1,0:T(8,128)(2,1)S(1)}, u32[]{:S(2)}, u32[]{:S(2)}) collective-permute-start(bf16[256,128]{1,0:T(8,128)(2,1)S(1)} %get-tuple-element.72), channel_id=1, source_target_pairs={{0,8},{8,0},{1,9},{9,1},{2,10},{10,2},{3,11},{11,3},{4,12},{12,4},... | collective-permute-start | bytes 196616 | tf_op jit(solution)/shard_map/ppermute | solution.py:45
  (93 shorter events, 16.8 us)
Async XLA Ops:
  2.1 2.0 %collective-permute-start.1 = (bf16[1280,128]{1,0:T(8,128)(2,1)S(1)}, bf16[1280,128]{1,0:T(8,128)(2,1)S(1)}, u32[]{:S(2)}, u32[]{:S(2)}) collective-permute-start(bf16[1280,128]{1,0:T(8,128)(2,1)S(1)} %pad_maximum_fusion.2), channel_id=1, source_target_pairs={{0,8},{8,0},{1,9},{9,1},{2,10},{10,2},{3,11},{11,3},{4,12},{12,4},... | collective-permute-start | bytes 983048 | tf_op jit(solution)/shard_map/ppermute | solution.py:45
  2.9 9.0 %collective-permute-start.6 = (bf16[768,256]{1,0:T(8,128)(2,1)S(1)}, bf16[768,256]{1,0:T(8,128)(2,1)S(1)}, u32[]{:S(2)}, u32[]{:S(2)}) collective-permute-start(bf16[768,256]{1,0:T(8,128)(2,1)S(1)} %get-tuple-element.68), channel_id=1, source_target_pairs={{0,8},{8,0},{1,9},{9,1},{2,10},{10,2},{3,11},{11,3},{4,12},{12,4},... | collective-permute-start | bytes 1179656 | tf_op jit(solution)/shard_map/ppermute | solution.py:45
  5.3 50.7 %all-to-all-start = ((bf16[8,256,256]{2,1,0:T(8,128)(2,1)}), bf16[8,256,256]{2,1,0:T(8,128)(2,1)S(1)}, u32[]{:S(2)}, u32[]{:S(2)}) async-start(bf16[8,256,256]{2,1,0:T(8,128)(2,1)} %broadcast_in_dim.2), calls=%async_computation | async-start | bytes 2097152 | tf_op jit(solution)/shard_map/all_to_all | solution.py:470
  12.0 45.3 %copy-start.6 = (bf16[2,768,256]{2,1,0:T(8,128)(2,1)}, bf16[2,768,256]{2,1,0:T(8,128)(2,1)S(1)}, u32[]{:S(2)}) copy-start(bf16[2,768,256]{2,1,0:T(8,128)(2,1)S(1)} %pad_maximum_fusion.cache0) | copy-start | bytes 2359300
  12.0 43.9 %collective-permute-start.7 = (bf16[2,768,256]{2,1,0:T(8,128)(2,1)S(1)}, bf16[2,768,256]{2,1,0:T(8,128)(2,1)}, u32[]{:S(2)}, u32[]{:S(2)}) collective-permute-start(bf16[2,768,256]{2,1,0:T(8,128)(2,1)S(1)} %pad_maximum_fusion.cache0), channel_id=1, source_target_pairs={{0,64},{64,0},{1,65},{65,1},{2,66},{66,2},{3,67},{67,3},{4,68},{68... | collective-permute-start | bytes 2359304 | tf_op jit(solution)/shard_map/ppermute | solution.py:41
  13.3 17.0 %collective-permute-start.2 = (bf16[2,1280,128]{2,1,0:T(8,128)(2,1)S(1)}, bf16[2,1280,128]{2,1,0:T(8,128)(2,1)}, u32[]{:S(2)}, u32[]{:S(2)}) collective-permute-start(bf16[2,1280,128]{2,1,0:T(8,128)(2,1)S(1)} %pad_maximum_fusion.1.refs_0_), channel_id=1, source_target_pairs={{0,32},{16,48},{32,0},{48,16},{1,33},{17,49},{33,1},{49,17},{2,34}... | collective-permute-start | bytes 1966088 | tf_op jit(solution)/shard_map/ppermute | solution.py:37
  16.2 28.6 %collective-permute-start.3 = (bf16[2,1280,128]{2,1,0:T(8,128)(2,1)S(1)}, bf16[2,1280,128]{2,1,0:T(8,128)(2,1)}, u32[]{:S(2)}, u32[]{:S(2)}) collective-permute-start(bf16[2,1280,128]{2,1,0:T(8,128)(2,1)S(1)} %pad_maximum_fusion.1.refs_0_), channel_id=1, source_target_pairs={{0,48},{16,0},{32,16},{48,32},{1,49},{17,1},{33,17},{49,33},{2,50}... | collective-permute-start | bytes 1966088 | tf_op jit(solution)/shard_map/ppermute | solution.py:37
  17.0 28.6 %collective-permute-start.4 = (bf16[2,1280,128]{2,1,0:T(8,128)(2,1)S(1)}, bf16[2,1280,128]{2,1,0:T(8,128)(2,1)}, u32[]{:S(2)}, u32[]{:S(2)}) collective-permute-start(bf16[2,1280,128]{2,1,0:T(8,128)(2,1)S(1)} %pad_maximum_fusion.1.refs_0_), channel_id=1, source_target_pairs={{0,16},{16,32},{32,48},{48,0},{1,17},{17,33},{33,49},{49,1},{2,18}... | collective-permute-start | bytes 1966088 | tf_op jit(solution)/shard_map/ppermute | solution.py:37
  17.6 38.3 %collective-permute-start.5 = (bf16[2,1280,128]{2,1,0:T(8,128)(2,1)S(1)}, bf16[2,1280,128]{2,1,0:T(8,128)(2,1)}, u32[]{:S(2)}, u32[]{:S(2)}) collective-permute-start(bf16[2,1280,128]{2,1,0:T(8,128)(2,1)S(1)} %pad_maximum_fusion.1.refs_0_), channel_id=1, source_target_pairs={{0,64},{64,0},{1,65},{65,1},{2,66},{66,2},{3,67},{67,3},{4,68},{68... | collective-permute-start | bytes 1966088 | tf_op jit(solution)/shard_map/ppermute | solution.py:41
  18.1 43.6 %copy-start.11 = (s32[256,2]{0,1:T(2,128)S(1)}, s32[256,2]{0,1:T(2,128)}, u32[]{:S(2)}) copy-start(s32[256,2]{0,1:T(2,128)} %param.13) | copy-start | bytes 6148
  57.3 21.9 %collective-permute-start.8 = (bf16[256,2048]{1,0:T(8,128)(2,1)S(1)}, bf16[256,2048]{1,0:T(8,128)(2,1)}, u32[]{:S(2)}, u32[]{:S(2)}) collective-permute-start(bf16[256,2048]{1,0:T(8,128)(2,1)S(1)} %normalise.1.own), channel_id=1, source_target_pairs={{0,8},{8,0},{1,9},{9,1},{2,10},{10,2},{3,11},{11,3},{4,12},{12,4},... | collective-permute-start | bytes 3145736 | tf_op jit(solution)/shard_map/ppermute | solution.py:45
  58.6 17.8 %collective-permute-start.10 = (bf16[2,1280,128]{2,1,0:T(8,128)(2,1)}, bf16[2,1280,128]{2,1,0:T(8,128)(2,1)S(1)}, u32[]{:S(2)}, u32[]{:S(2)}) collective-permute-start(bf16[2,1280,128]{2,1,0:T(8,128)(2,1)} %collective-permute-done.5.refs_1_), channel_id=1, source_target_pairs={{0,16},{16,32},{32,48},{48,0},{1,17},{17,33},{33,49},{49,1},{2,18}... | collective-permute-start | bytes 1966088 | tf_op jit(solution)/shard_map/ppermute | solution.py:37
  59.9 16.5 %collective-permute-start.9 = (bf16[2,1280,128]{2,1,0:T(8,128)(2,1)}, bf16[2,1280,128]{2,1,0:T(8,128)(2,1)}, u32[]{:S(2)}, u32[]{:S(2)}) collective-permute-start(bf16[2,1280,128]{2,1,0:T(8,128)(2,1)} %collective-permute-done.5.refs_1_), channel_id=1, source_target_pairs={{0,48},{16,0},{32,16},{48,32},{1,49},{17,1},{33,17},{49,33},{2,50}... | collective-permute-start | bytes 1966088 | tf_op jit(solution)/shard_map/ppermute | solution.py:37
  61.3 17.8 %collective-permute-start.11 = (bf16[2,1280,128]{2,1,0:T(8,128)(2,1)}, bf16[2,1280,128]{2,1,0:T(8,128)(2,1)}, u32[]{:S(2)}, u32[]{:S(2)}) collective-permute-start(bf16[2,1280,128]{2,1,0:T(8,128)(2,1)} %collective-permute-done.2.refs_4_), channel_id=1, source_target_pairs={{0,64},{64,0},{1,65},{65,1},{2,66},{66,2},{3,67},{67,3},{4,68},{68... | collective-permute-start | bytes 1966088 | tf_op jit(solution)/shard_map/ppermute | solution.py:41
  61.6 1.7 collective-permute-start
  76.4 18.7 %collective-permute-start.17 = (bf16[2048,128]{1,0:T(8,128)(2,1)}, bf16[2048,128]{1,0:T(8,128)(2,1)}, u32[]{:S(2)}, u32[]{:S(2)}) collective-permute-start(bf16[2048,128]{1,0:T(8,128)(2,1)} %refs_0_.1), channel_id=1, source_target_pairs={{0,64},{64,0},{1,65},{65,1},{2,66},{66,2},{3,67},{67,3},{4,68},{68... | collective-permute-start | bytes 1572872 | tf_op jit(solution)/shard_map/ppermute | solution.py:41
  76.7 12.6 %collective-permute-start.12 = (bf16[2048,128]{1,0:T(8,128)(2,1)}, bf16[2048,128]{1,0:T(8,128)(2,1)S(1)}, u32[]{:S(2)}, u32[]{:S(2)}) collective-permute-start(bf16[2048,128]{1,0:T(8,128)(2,1)} %refs_0_.1), channel_id=1, source_target_pairs={{0,48},{16,0},{32,16},{48,32},{1,49},{17,1},{33,17},{49,33},{2,50}... | collective-permute-start | bytes 1572872 | tf_op jit(solution)/shard_map/ppermute | solution.py:37
  79.2 13.1 %collective-permute-start.13 = (bf16[2048,128]{1,0:T(8,128)(2,1)}, bf16[2048,128]{1,0:T(8,128)(2,1)S(1)}, u32[]{:S(2)}, u32[]{:S(2)}) collective-permute-start(bf16[2048,128]{1,0:T(8,128)(2,1)} %refs_0_.1), channel_id=1, source_target_pairs={{0,16},{16,32},{32,48},{48,0},{1,17},{17,33},{33,49},{49,1},{2,18}... | collective-permute-start | bytes 1572872 | tf_op jit(solution)/shard_map/ppermute | solution.py:37
  79.2 26.9 %copy-start.4 = (s32[4]{0:T(128)S(1)}, s32[4]{0:T(128)}, u32[]{:S(2)}) copy-start(s32[4]{0:T(128)} %ends_s.1) | copy-start | bytes 52
  86.7 8.5 %collective-permute-start.18 = (bf16[512,256]{1,0:T(8,128)(2,1)S(1)}, bf16[512,256]{1,0:T(8,128)(2,1)S(1)}, u32[]{:S(2)}, u32[]{:S(2)}) collective-permute-start(bf16[512,256]{1,0:T(8,128)(2,1)S(1)} %get-tuple-element.51.kv0), channel_id=1, source_target_pairs={{0,64},{64,0},{1,65},{65,1},{2,66},{66,2},{3,67},{67,3},{4,68},{68... | collective-permute-start | bytes 786440 | tf_op jit(solution)/shard_map/ppermute | solution.py:41
  92.3 8.7 %collective-permute-start.14 = (bf16[1024,128]{1,0:T(8,128)(2,1)S(1)}, bf16[1024,128]{1,0:T(8,128)(2,1)S(1)}, u32[]{:S(2)}, u32[]{:S(2)}) collective-permute-start(bf16[1024,128]{1,0:T(8,128)(2,1)S(1)} %get-tuple-element.48.q0), channel_id=1, source_target_pairs={{0,16},{16,32},{32,48},{48,0},{1,17},{17,33},{33,49},{49,1},{2,18}... | collective-permute-start | bytes 786440 | tf_op jit(solution)/shard_map/ppermute | solution.py:37
  92.3 10.9 %collective-permute-start.15 = (bf16[1024,128]{1,0:T(8,128)(2,1)S(1)}, bf16[1024,128]{1,0:T(8,128)(2,1)S(1)}, u32[]{:S(2)}, u32[]{:S(2)}) collective-permute-start(bf16[1024,128]{1,0:T(8,128)(2,1)S(1)} %get-tuple-element.48.q0), channel_id=1, source_target_pairs={{0,32},{16,48},{32,0},{48,16},{1,33},{17,49},{33,1},{49,17},{2,34}... | collective-permute-start | bytes 786440 | tf_op jit(solution)/shard_map/ppermute | solution.py:37
  93.9 12.2 %collective-permute-start.16 = (bf16[1024,128]{1,0:T(8,128)(2,1)S(1)}, bf16[1024,128]{1,0:T(8,128)(2,1)}, u32[]{:S(2)}, u32[]{:S(2)}) collective-permute-start(bf16[1024,128]{1,0:T(8,128)(2,1)S(1)} %get-tuple-element.48.q0), channel_id=1, source_target_pairs={{0,48},{16,0},{32,16},{48,32},{1,49},{17,1},{33,17},{49,33},{2,50}... | collective-permute-start | bytes 786440 | tf_op jit(solution)/shard_map/ppermute | solution.py:37
  95.2 30.9 %collective-permute-start.20 = (bf16[2048,128]{1,0:T(8,128)(2,1)}, bf16[2048,128]{1,0:T(8,128)(2,1)S(1)}, u32[]{:S(2)}, u32[]{:S(2)}) collective-permute-start(bf16[2048,128]{1,0:T(8,128)(2,1)} %collective-permute-done.17.refs_1_), channel_id=1, source_target_pairs={{0,48},{16,0},{32,16},{48,32},{1,49},{17,1},{33,17},{49,33},{2,50}... | collective-permute-start | bytes 1572872 | tf_op jit(solution)/shard_map/ppermute | solution.py:37
  97.1 29.0 %collective-permute-start.21 = (bf16[2048,128]{1,0:T(8,128)(2,1)}, bf16[2048,128]{1,0:T(8,128)(2,1)S(1)}, u32[]{:S(2)}, u32[]{:S(2)}) collective-permute-start(bf16[2048,128]{1,0:T(8,128)(2,1)} %collective-permute-done.17.refs_1_), channel_id=1, source_target_pairs={{0,16},{16,32},{32,48},{48,0},{1,17},{17,33},{33,49},{49,1},{2,18}... | collective-permute-start | bytes 1572872 | tf_op jit(solution)/shard_map/ppermute | solution.py:37
  101.0 25.1 %collective-permute-start.19 = (bf16[2048,128]{1,0:T(8,128)(2,1)}, bf16[2048,128]{1,0:T(8,128)(2,1)}, u32[]{:S(2)}, u32[]{:S(2)}) collective-permute-start(bf16[2048,128]{1,0:T(8,128)(2,1)} %refs_0_.1), channel_id=1, source_target_pairs={{0,32},{16,48},{32,0},{48,16},{1,33},{17,49},{33,1},{49,17},{2,34}... | collective-permute-start | bytes 1572872 | tf_op jit(solution)/shard_map/ppermute | solution.py:37
  126.1 8.6 %collective-permute-start.22 = (bf16[144,1024]{1,0:T(8,128)(2,1)S(1)}, bf16[144,1024]{1,0:T(8,128)(2,1)S(1)}, u32[]{:S(2)}, u32[]{:S(2)}) collective-permute-start(bf16[144,1024]{1,0:T(8,128)(2,1)S(1)} %get-tuple-element.59), channel_id=1, source_target_pairs={{0,48},{16,0},{32,16},{48,32},{1,49},{17,1},{33,17},{49,33},{2,50}... | collective-permute-start | bytes 884744 | tf_op jit(solution)/shard_map/ppermute | solution.py:37
  129.8 7.2 %collective-permute-start.23 = (bf16[144,1024]{1,0:T(8,128)(2,1)S(1)}, bf16[144,1024]{1,0:T(8,128)(2,1)S(1)}, u32[]{:S(2)}, u32[]{:S(2)}) collective-permute-start(bf16[144,1024]{1,0:T(8,128)(2,1)S(1)} %get-tuple-element.60), channel_id=1, source_target_pairs={{0,32},{16,48},{32,0},{48,16},{1,33},{17,49},{33,1},{49,17},{2,34}... | collective-permute-start | bytes 884744 | tf_op jit(solution)/shard_map/ppermute | solution.py:37
  129.8 10.4 %collective-permute-start.24 = (bf16[144,1024]{1,0:T(8,128)(2,1)S(1)}, bf16[144,1024]{1,0:T(8,128)(2,1)S(1)}, u32[]{:S(2)}, u32[]{:S(2)}) collective-permute-start(bf16[144,1024]{1,0:T(8,128)(2,1)S(1)} %get-tuple-element.61), channel_id=1, source_target_pairs={{0,16},{16,32},{32,48},{48,0},{1,17},{17,33},{33,49},{49,1},{2,18}... | collective-permute-start | bytes 884744 | tf_op jit(solution)/shard_map/ppermute | solution.py:37
  130.5 16.7 %collective-permute-start.26 = (bf16[2048,128]{1,0:T(8,128)(2,1)}, bf16[2048,128]{1,0:T(8,128)(2,1)}, u32[]{:S(2)}, u32[]{:S(2)}) collective-permute-start(bf16[2048,128]{1,0:T(8,128)(2,1)} %collective-permute-done.19.refs_4_), channel_id=1, source_target_pairs={{0,64},{64,0},{1,65},{65,1},{2,66},{66,2},{3,67},{67,3},{4,68},{68... | collective-permute-start | bytes 1572872 | tf_op jit(solution)/shard_map/ppermute | solution.py:41
  140.5 7.8 %collective-permute-start.25 = (bf16[1024,128]{1,0:T(8,128)(2,1)S(1)}, bf16[1024,128]{1,0:T(8,128)(2,1)S(1)}, u32[]{:S(2)}, u32[]{:S(2)}) collective-permute-start(bf16[1024,128]{1,0:T(8,128)(2,1)S(1)} %combine.1.own), channel_id=1, source_target_pairs={{0,8},{8,0},{1,9},{9,1},{2,10},{10,2},{3,11},{11,3},{4,12},{12,4},... | collective-permute-start | bytes 786440 | tf_op jit(solution)/shard_map/ppermute | solution.py:45
  178.6 2.8 %collective-permute-start.27 = (bf16[256,128]{1,0:T(8,128)(2,1)S(1)}, bf16[256,128]{1,0:T(8,128)(2,1)S(1)}, u32[]{:S(2)}, u32[]{:S(2)}) collective-permute-start(bf16[256,128]{1,0:T(8,128)(2,1)S(1)} %get-tuple-element.72), channel_id=1, source_target_pairs={{0,8},{8,0},{1,9},{9,1},{2,10},{10,2},{3,11},{11,3},{4,12},{12,4},... | collective-permute-start | bytes 196616 | tf_op jit(solution)/shard_map/ppermute | solution.py:45
  (17 other events, 185.0 us)

commit v6 on v5

--- a/solution.py
+++ b/solution.py
@@ -377,12 +377,11 @@
     )(gates, *parts)
 
 
-def out_kernel(idx, routes, own, other, *refs):
-    blocks = refs[:8]
-    out, held, padded, sem = refs[8:]
-    core = idx[8]
+def out_kernel(idx, routes, own, other, blocks, out, held, padded, sem):
+    core = idx[0]
     copies = [
-        pltpu.make_async_copy(r, held.at[idx[k]], sem.at[k]) for k, r in enumerate(blocks)
+        pltpu.make_async_copy(blocks.at[pl.ds(2 * k, 2)], held.at[pl.ds(2 * k, 2)], sem.at[k])
+        for k in range(4)
     ]
     for c in copies:
         c.start()
@@ -397,9 +396,8 @@
                 padded[side, half * 256 : (half + 1) * 256, e * H : (e + 1) * H] = value.astype(
                     BF16
                 )
-    for c in copies:
-        c.wait()
     for k in range(0, 8, 2):
+        copies[k // 2].wait()
         value = jnp.zeros((512, 256), F32)
         for side in range(2):
             head = core if side == 0 else 1 - core
@@ -414,17 +412,17 @@
     return pl.pallas_call(
         out_kernel,
         out_shape=jax.ShapeDtypeStruct((8, 512, H), BF16),
-        in_specs=[SMEM, VMEM, VMEM, VMEM] + [HBM] * 8,
+        in_specs=[SMEM, VMEM, VMEM, VMEM, HBM],
         out_specs=VMEM,
         scratch_shapes=[
             pltpu.VMEM((8, 2048, H), BF16),
             pltpu.VMEM((2, 512, 1024), BF16),
-            pltpu.SemaphoreType.DMA((8,)),
+            pltpu.SemaphoreType.DMA((4,)),
         ],
         compiler_params=pltpu.CompilerParams(vmem_limit_bytes=20 << 20),
         cost_estimate=pl.CostEstimate(flops=4 << 30, bytes_accessed=6 << 20, transcendentals=0),
         name="project_out",
-    )(idx, routes, own, other, *pin(blocks))
+    )(idx, routes, own, other, *pin([blocks]))
 
 
 def on_device(
@@ -442,6 +440,7 @@
     xl, y, c = (lax.axis_index(a) for a in WIDE)
     first_core = c == 0
     chips = chip_order()
+    blocks = lax.all_gather(tokens, NARROW, axis=0)
 
     def table(values):
         return jnp.stack([jnp.asarray(v, jnp.int32) for v in values])
@@ -465,42 +464,33 @@
         return lax.dynamic_slice_in_dim(prefix_cache, h * 2 * H, 2 * H, 1)
 
     cache = jnp.stack([cache_of(c), across_core(cache_of(1 - c))])
-    tokens, w = tie(tokens, w)
-    copies = jnp.broadcast_to(tokens[None], (8,) + tokens.shape)
-    blocks = lax.all_to_all(copies, NARROW, 0, 0, tiled=True)
     far, ym, yp, a = along_y(w, 2), along_y(w, 3), along_y(w, 1), across_x(w)
     caches = [cache, across_x(cache)]
-    far, ym, yp, a, blocks, caches = lax.optimization_barrier((far, ym, yp, a, blocks, caches))
+    far, ym, yp, a, caches = lax.optimization_barrier((far, ym, yp, a, caches))
     am, ap, afar = along_y(a, 3), along_y(a, 1), across_x(far)
     gathered = [w, a, ym, am, far, afar, yp, ap]
 
     places = [(k % 4 - y + 4) % 4 * 2 + (k // 4 ^ xl) for k in range(8)]
     normed = normalise(table(places), norm_gain.reshape(8, 1, 256), blocks)
-    out_early, am, ap = lax.optimization_barrier((out_weight, am, ap))
-    gathered[3], gathered[7] = am, ap
-    o_ym, o_yp, o_a = along_y(out_early, 3), along_y(out_early, 1), across_x(out_early)
     q, kv, gates = project(
         table(chips + [c]), both_routes, router.T, normed, across_core(normed), gathered
     )
+    late, q = tie(out_weight, q)
+    out_all = lax.all_gather(late, ("xl", "y"), axis=0)
     kvs = [kv, across_x(kv)]
-    q_out, o_ym, o_yp = lax.optimization_barrier((q, o_ym, o_yp))
-    qs = [q] + [along_y(q_out, k) for k in (1, 2, 3)]
-    out_late, o_a_late, kvs[1] = lax.optimization_barrier((out_weight, o_a, kvs[1]))
-    o_far, o_am, o_ap = along_y(out_late, 2), along_y(o_a_late, 3), along_y(o_a_late, 1)
+    qs = [q] + [along_y(q, k) for k in (1, 2, 3)]
 
     firsts = [(xl * 4 + lax.rem(y + 4 - k, 4)) * 512 for k in range(4)]
     mine, partner = xl * 4 + y, (1 - xl) * 4 + y
     at = [c] + firsts + [mine * 1536, partner * 1536, mine * 512, partner * 512]
     parts = list(attend(table(at), suffix_lengths, prefix_lengths, qs, caches, kvs))
-    parts[1:], o_far, o_am, o_ap = lax.optimization_barrier((parts[1:], o_far, o_am, o_ap))
     for k in range(1, 4):
         parts[k] = along_y(parts[k], 4 - k)
-    out_blocks = [out_weight, o_a, o_ym, o_am, o_far, across_x(o_far), o_yp, o_ap]
     gate_row = gates.reshape(2, 256, 2).transpose(0, 2, 1).reshape(1, 1024)
     attended = combine(gate_row, parts)
 
     sums = project_out(
-        table(chips + [c]), both_routes, attended, across_core(attended), out_blocks
+        table([c]), both_routes, attended, across_core(attended), out_all
     )
     sums = lax.all_to_all(sums, NARROW, 0, 0, tiled=True)
     total = jnp.sum(sums.astype(F32), axis=0)

time: 184 us -> 227 us (1.23); the launches traced: 182 us -> 230 us
  waiting for transfers between devices: 85.1 us -> 128 us
  starting transfers between devices: 41.3 us -> 25.9 us
  between operations: 0.32 us -> 13.7 us
  Pallas kernels: 26.8 us -> 35.3 us
  blocking collectives: 22.8 us -> 20 us
    all_gather x0 -> x2, waiting for transfers between devices: none -> 42 us  [the longest x1 42 us: on_device(): blocks = lax.all_gather(tokens, NARROW, axis=0)]
    pallas_call x1, Pallas kernels: 10.4 us -> 19.1 us  [attend(): pl.pallas_call(attend_kernel, out_shape=tuple((jax.ShapeDtypeStruct((H +...]
    all_to_all x1 -> x0, starting transfers between devices: 6.59 us -> none  [on_device(): blocks = lax.all_to_all(copies, NARROW, 0, 0, tiled=True)]
    ppermute x6, starting transfers between devices: 11.6 us -> 5.74 us  [across_core(): return lax.ppermute(x, 'c', [(0, 1), (1, 0)])]
    all_to_all x1, blocking collectives: 22.8 us -> 20 us  [on_device(): sums = lax.all_to_all(sums, NARROW, 0, 0, tiled=True)]
    ppermute x16 -> x11, starting transfers between devices: 18.6 us -> 16.9 us  [along_y(): return lax.ppermute(x, 'y', [(i, (i + k) % 4) for i in range(4)])]
    ppermute x6 -> x4, starting transfers between devices: 4.6 us -> 3.24 us  [across_x(): return lax.ppermute(x, 'xl', [(0, 1), (1, 0)])]
    ppermute x16 -> x11, waiting for transfers between devices: 70.9 us -> 70.4 us  [along_y(): return lax.ppermute(x, 'y', [(i, (i + k) % 4) for i in range(4)])]
  transfers between devices with their start and end apart: 29 -> 23, of which waited for: 18 -> 12; matrix products, arithmetic and copies ran while one was open for 1% -> 2% of each run, Pallas kernels for 10% -> 9%
where the time goes in v6:
time: 227 us; the launch traced here: 230 us
  waiting for transfers between devices  128 us (56%)
  Pallas kernels  35.3 us (16%)
  starting transfers between devices  25.9 us (11%)
  blocking collectives  20 us (9%)
  between operations  13.7 us (6%)
  local copies, waits for them, and re-layouts  5.79 us (3%)
    ppermute x11, waiting for transfers between devices, along_y(): return lax.ppermute(x, 'y', [(i, (i + k) % 4) for i in range(4)])  70.4 us
    all_gather x1, waiting for transfers between devices, on_device(): blocks = lax.all_gather(tokens, NARROW, axis=0)  42 us
    all_to_all x1, blocking collectives, on_device(): sums = lax.all_to_all(sums, NARROW, 0, 0, tiled=True)  20 us
    pallas_call x1, Pallas kernels, attend(): pl.pallas_call(attend_kernel, out_shape=tuple((jax.ShapeDtypeStruct((H +...  19.1 us
    ppermute x11, starting transfers between devices, along_y(): return lax.ppermute(x, 'y', [(i, (i + k) % 4) for i in range(4)])  16.9 us
    ppermute x4, waiting for transfers between devices, across_x(): return lax.ppermute(x, 'xl', [(0, 1), (1, 0)])  10.5 us
    pallas_call x1, Pallas kernels, project(): pl.pallas_call(project_kernel, out_shape=(jax.ShapeDtypeStruct((1024, H),...  7.38 us
    pallas_call x1, Pallas kernels, project_out(): pl.pallas_call(out_kernel, out_shape=jax.ShapeDtypeStruct((8, 512, H), BF...  7.29 us
  transfers between devices with their start and end apart: 23, of which 12 were waited for; matrix products, arithmetic and copies ran while one was open for 2% of the time, Pallas kernels for 9%

profile of v6, /device:TPU:3, one launch (start us, length us, event | category | flops | bytes accessed | tf_op | source)
XLA Modules:
  0.0 229.6 jit_solution(7531024426324504246)
XLA Ops:
  7.3 0.9 constant_dynamic-slice_fusion.3
  8.2 1.1 constant_dynamic-slice_fusion.4
  10.1 1.2 dynamic-slice_bitcast_fusion
  11.7 1.3 collective-permute-done.7
  13.4 1.4 collective-permute-start.5
  14.8 1.4 collective-permute-start.4
  16.2 1.6 collective-permute-start.3
  18.0 42.0 %all-gather.5.cloned.1.call-done = bf16[2048,256]{1,0:T(8,128)(2,1)} async-done(((bf16[256,256]{1,0:T(8,128)(2,1)}), bf16[2048,256]{1,0:T(8,128)(2,1)}) %all-gather.5.cloned.1.call-update) | async-done | bytes 1048592 | tf_op jit(solution)/shard_map/all_gather | solution.py:443
  60.0 1.2 copy-done
  61.2 1.3 normalise.1.own
  62.5 1.2 collective-permute-start.1
  63.8 1.6 collective-permute-start.10
  65.4 1.3 collective-permute-start.11
  66.7 1.4 collective-permute-start.9
  70.1 10.5 %collective-permute-done.10.refs_5_ = bf16[2,1280,128]{2,1,0:T(8,128)(2,1)} collective-permute-done((bf16[2,1280,128]{2,1,0:T(8,128)(2,1)}, bf16[2,1280,128]{2,1,0:T(8,128)(2,1)}, u32[]{:S(2)}, u32[]{:S(2)}) %collective-permute-start.10) | collective-permute-done | bytes 655392 | tf_op jit(solution)/shard_map/ppermute | solution.py:41
  80.7 2.4 %collective-permute-done.11.refs_7_ = bf16[2,1280,128]{2,1,0:T(8,128)(2,1)} collective-permute-done((bf16[2,1280,128]{2,1,0:T(8,128)(2,1)}, bf16[2,1280,128]{2,1,0:T(8,128)(2,1)}, u32[]{:S(2)}, u32[]{:S(2)}) %collective-permute-start.11) | collective-permute-done | bytes 655392 | tf_op jit(solution)/shard_map/ppermute | solution.py:37
  83.1 7.4 %project.1 = (bf16[1024,128]{1,0:T(8,128)(2,1)S(1)}, bf16[512,256]{1,0:T(8,128)(2,1)S(1)}, f32[512,2]{1,0:T(8,128)S(1)}) custom-call(s32[9]{0:T(128)S(1)} %stack.113.idx, s32[512,2]{1,0:T(8,128)S(1)} %broadcast_select_fusion.routes, bf16[8,2048]{1,0:T(8,128)(2,1)S(1)} %bitcast.38, bf16[256,2048]{1,0:T(8,128)(2,1)} %copy-done.1, ...), custom_call_target="tpu_custom_call" | custom-call | flops 6442450944 | bytes 8388608 | tf_op jit(solution)/shard_map/project/pallas_call | solution.py:162
  90.5 2.4 %collective-permute-start.14 = (bf16[1024,128]{1,0:T(8,128)(2,1)S(1)}, bf16[1024,128]{1,0:T(8,128)(2,1)S(1)}, u32[]{:S(2)}, u32[]{:S(2)}) collective-permute-start(bf16[1024,128]{1,0:T(8,128)(2,1)S(1)} %get-tuple-element.26.q0), channel_id=1, source_target_pairs={{0,48},{16,0},{32,16},{48,32},{1,49},{17,1},{33,17},{49,33},{2,50}... | collective-permute-start | bytes 786440 | tf_op jit(solution)/shard_map/ppermute | solution.py:37
  93.7 1.1 collective-permute-start.15
  95.0 2.6 %collective-permute-done.14.q3 = bf16[1024,128]{1,0:T(8,128)(2,1)S(1)} collective-permute-done((bf16[1024,128]{1,0:T(8,128)(2,1)S(1)}, bf16[1024,128]{1,0:T(8,128)(2,1)S(1)}, u32[]{:S(2)}, u32[]{:S(2)}) %collective-permute-start.14) | collective-permute-done | bytes 262176 | tf_op jit(solution)/shard_map/ppermute | solution.py:37
  97.6 3.1 %collective-permute-done.13.q2 = bf16[1024,128]{1,0:T(8,128)(2,1)S(1)} collective-permute-done((bf16[1024,128]{1,0:T(8,128)(2,1)S(1)}, bf16[1024,128]{1,0:T(8,128)(2,1)S(1)}, u32[]{:S(2)}, u32[]{:S(2)}) %collective-permute-start.13) | collective-permute-done | bytes 262176 | tf_op jit(solution)/shard_map/ppermute | solution.py:37
  100.7 46.9 %collective-permute-done.12.q1 = bf16[1024,128]{1,0:T(8,128)(2,1)S(1)} collective-permute-done((bf16[1024,128]{1,0:T(8,128)(2,1)S(1)}, bf16[1024,128]{1,0:T(8,128)(2,1)S(1)}, u32[]{:S(2)}, u32[]{:S(2)}) %collective-permute-start.12) | collective-permute-done | bytes 262176 | tf_op jit(solution)/shard_map/ppermute | solution.py:37
  148.4 19.1 %attend.1 = (bf16[144,1024]{1,0:T(8,128)(2,1)S(1)}, bf16[144,1024]{1,0:T(8,128)(2,1)S(1)}, bf16[144,1024]{1,0:T(8,128)(2,1)S(1)}, bf16[144,1024]{1,0:T(8,128)(2,1)S(1)}) custom-call(s32[9]{0:T(128)S(1)} %stack.137.idx, s32[4]{0:T(128)S(1)} %copy-done.5, s32[4]{0:T(128)S(1)} %copy-done.6, bf16[1024,128]{1,0:T(8,128)(2,1)} %copy-done.2, ...), custom_call_target="tpu_custom_call" | custom-call | flops 12884901888 | bytes 6291456 | tf_op jit(solution)/shard_map/attend/pallas_call | solution.py:325
  167.4 5.9 %collective-permute-start.16 = (bf16[144,1024]{1,0:T(8,128)(2,1)S(1)}, bf16[144,1024]{1,0:T(8,128)(2,1)S(1)}, u32[]{:S(2)}, u32[]{:S(2)}) collective-permute-start(bf16[144,1024]{1,0:T(8,128)(2,1)S(1)} %get-tuple-element.31), channel_id=1, source_target_pairs={{0,48},{16,0},{32,16},{48,32},{1,49},{17,1},{33,17},{49,33},{2,50}... | collective-permute-start | bytes 884744 | tf_op jit(solution)/shard_map/ppermute | solution.py:37
  174.1 11.0 %collective-permute-done.16.p1 = bf16[144,1024]{1,0:T(8,128)(2,1)S(1)} collective-permute-done((bf16[144,1024]{1,0:T(8,128)(2,1)S(1)}, bf16[144,1024]{1,0:T(8,128)(2,1)S(1)}, u32[]{:S(2)}, u32[]{:S(2)}) %collective-permute-start.16) | collective-permute-done | bytes 294944 | tf_op jit(solution)/shard_map/ppermute | solution.py:37
  185.2 4.3 %collective-permute-done.18.p3 = bf16[144,1024]{1,0:T(8,128)(2,1)S(1)} collective-permute-done((bf16[144,1024]{1,0:T(8,128)(2,1)S(1)}, bf16[144,1024]{1,0:T(8,128)(2,1)S(1)}, u32[]{:S(2)}, u32[]{:S(2)}) %collective-permute-start.18) | collective-permute-done | bytes 294944 | tf_op jit(solution)/shard_map/ppermute | solution.py:37
  189.7 0.9 collective-permute-start.19
  190.7 1.2 collective-permute-done.19.other
  191.8 7.3 %project_out.1 = bf16[8,512,128]{2,1,0:T(8,128)(2,1)S(1)} custom-call(s32[1]{0:T(128)} %bitcast.idx, s32[512,2]{1,0:T(8,128)S(1)} %broadcast_select_fusion.routes, bf16[1024,128]{1,0:T(8,128)(2,1)S(1)} %combine.1.own, bf16[1024,128]{1,0:T(8,128)(2,1)S(1)} %collective-permute-done.19.other, bf16[8,2048,128]{2,1,0:T(8,128)(2,1)} %bitcast.42), custom_call_target="tpu_custom_call" | custom-call | flops 4294967296 | bytes 6291456 | tf_op jit(solution)/shard_map/project_out/pallas_call | solution.py:412
  199.1 20.0 %all_to_all.5 = bf16[8,512,128]{2,1,0:T(8,128)(2,1)S(1)} all-to-all(bf16[8,512,128]{2,1,0:T(8,128)(2,1)S(1)} %project_out.1), channel_id=1, replica_groups=mesh['xl'=2,'y'=4,'c'=2,'z'=4,'xh'=2] {'z','xh'}, dimensions={0} | all-to-all | bytes 2097152 | tf_op jit(solution)/shard_map/all_to_all | solution.py:495
  219.3 1.9 collective-permute-start.20
  221.2 0.9 collective-permute-done.20
  (72 shorter events, 7.9 us)
Async XLA Ops:
  6.5 53.4 %all-gather.5.cloned.1.call-start = ((), (), s32[]{:S(2)}) async-start(), calls=%async_computation.1 | async-start | bytes 1179648 | tf_op jit(solution)/shard_map/all_gather | solution.py:443
  7.3 184.6 %all-gather.7.cloned.1.call-start = ((), (), s32[]{:S(2)}) async-start(), calls=%async_computation.2 | async-start | bytes 4718592 | tf_op jit(solution)/shard_map/all_gather | solution.py:479
  9.3 58.9 %copy-start.10 = (s32[256,2]{0,1:T(2,128)S(1)}, s32[256,2]{0,1:T(2,128)}, u32[]{:S(2)}) copy-start(s32[256,2]{0,1:T(2,128)} %param.13) | copy-start | bytes 6148
  9.3 73.8 %copy-start.4 = (bf16[2048,8]{0,1:T(8,128)(2,1)S(1)}, bf16[2048,8]{0,1:T(8,128)(2,1)}, u32[]{:S(2)}) copy-start(bf16[2048,8]{0,1:T(8,128)(2,1)} %param.12) | copy-start | bytes 98308
  9.3 2.1 collective-permute-start.2
  11.3 1.8 collective-permute-start.7
  11.5 58.5 %copy-start.8 = (bf16[2,1280,128]{2,1,0:T(8,128)(2,1)}, bf16[2,1280,128]{2,1,0:T(8,128)(2,1)S(1)}, u32[]{:S(2)}) copy-start(bf16[2,1280,128]{2,1,0:T(8,128)(2,1)S(1)} %pad_maximum_fusion.1.refs_0_) | copy-start | bytes 1966084
  11.5 51.0 %collective-permute-start.6 = (bf16[2,1280,128]{2,1,0:T(8,128)(2,1)S(1)}, bf16[2,1280,128]{2,1,0:T(8,128)(2,1)}, u32[]{:S(2)}, u32[]{:S(2)}) collective-permute-start(bf16[2,1280,128]{2,1,0:T(8,128)(2,1)S(1)} %pad_maximum_fusion.1.refs_0_), channel_id=1, source_target_pairs={{0,64},{64,0},{1,65},{65,1},{2,66},{66,2},{3,67},{67,3},{4,68},{68... | collective-permute-start | bytes 1966088 | tf_op jit(solution)/shard_map/ppermute | solution.py:41
  13.1 56.6 %copy-start.7 = (bf16[2,768,256]{2,1,0:T(8,128)(2,1)}, bf16[2,768,256]{2,1,0:T(8,128)(2,1)S(1)}, u32[]{:S(2)}) copy-start(bf16[2,768,256]{2,1,0:T(8,128)(2,1)S(1)} %pad_maximum_fusion.cache0) | copy-start | bytes 2359300
  13.2 50.6 %collective-permute-start.8 = (bf16[2,768,256]{2,1,0:T(8,128)(2,1)S(1)}, bf16[2,768,256]{2,1,0:T(8,128)(2,1)S(1)}, u32[]{:S(2)}, u32[]{:S(2)}) collective-permute-start(bf16[2,768,256]{2,1,0:T(8,128)(2,1)S(1)} %pad_maximum_fusion.cache0), channel_id=1, source_target_pairs={{0,64},{64,0},{1,65},{65,1},{2,66},{66,2},{3,67},{67,3},{4,68},{68... | collective-permute-start | bytes 2359304 | tf_op jit(solution)/shard_map/ppermute | solution.py:41
  13.4 50.4 %collective-permute-start.5 = (bf16[2,1280,128]{2,1,0:T(8,128)(2,1)S(1)}, bf16[2,1280,128]{2,1,0:T(8,128)(2,1)}, u32[]{:S(2)}, u32[]{:S(2)}) collective-permute-start(bf16[2,1280,128]{2,1,0:T(8,128)(2,1)S(1)} %pad_maximum_fusion.1.refs_0_), channel_id=1, source_target_pairs={{0,16},{16,32},{32,48},{48,0},{1,17},{17,33},{33,49},{49,1},{2,18}... | collective-permute-start | bytes 1966088 | tf_op jit(solution)/shard_map/ppermute | solution.py:37
  14.8 49.0 %collective-permute-start.4 = (bf16[2,1280,128]{2,1,0:T(8,128)(2,1)S(1)}, bf16[2,1280,128]{2,1,0:T(8,128)(2,1)}, u32[]{:S(2)}, u32[]{:S(2)}) collective-permute-start(bf16[2,1280,128]{2,1,0:T(8,128)(2,1)S(1)} %pad_maximum_fusion.1.refs_0_), channel_id=1, source_target_pairs={{0,48},{16,0},{32,16},{48,32},{1,49},{17,1},{33,17},{49,33},{2,50}... | collective-permute-start | bytes 1966088 | tf_op jit(solution)/shard_map/ppermute | solution.py:37
  16.2 47.6 %collective-permute-start.3 = (bf16[2,1280,128]{2,1,0:T(8,128)(2,1)S(1)}, bf16[2,1280,128]{2,1,0:T(8,128)(2,1)}, u32[]{:S(2)}, u32[]{:S(2)}) collective-permute-start(bf16[2,1280,128]{2,1,0:T(8,128)(2,1)S(1)} %pad_maximum_fusion.1.refs_0_), channel_id=1, source_target_pairs={{0,32},{16,48},{32,0},{48,16},{1,33},{17,49},{33,1},{49,17},{2,34}... | collective-permute-start | bytes 1966088 | tf_op jit(solution)/shard_map/ppermute | solution.py:37
  62.5 20.6 %collective-permute-start.1 = (bf16[256,2048]{1,0:T(8,128)(2,1)S(1)}, bf16[256,2048]{1,0:T(8,128)(2,1)}, u32[]{:S(2)}, u32[]{:S(2)}) collective-permute-start(bf16[256,2048]{1,0:T(8,128)(2,1)S(1)} %normalise.1.own), channel_id=1, source_target_pairs={{0,8},{8,0},{1,9},{9,1},{2,10},{10,2},{3,11},{11,3},{4,12},{12,4},... | collective-permute-start | bytes 3145736 | tf_op jit(solution)/shard_map/ppermute | solution.py:45
  63.8 16.9 %collective-permute-start.10 = (bf16[2,1280,128]{2,1,0:T(8,128)(2,1)}, bf16[2,1280,128]{2,1,0:T(8,128)(2,1)}, u32[]{:S(2)}, u32[]{:S(2)}) collective-permute-start(bf16[2,1280,128]{2,1,0:T(8,128)(2,1)} %collective-permute-done.3.refs_4_), channel_id=1, source_target_pairs={{0,64},{64,0},{1,65},{65,1},{2,66},{66,2},{3,67},{67,3},{4,68},{68... | collective-permute-start | bytes 1966088 | tf_op jit(solution)/shard_map/ppermute | solution.py:41
  65.4 17.7 %collective-permute-start.11 = (bf16[2,1280,128]{2,1,0:T(8,128)(2,1)}, bf16[2,1280,128]{2,1,0:T(8,128)(2,1)}, u32[]{:S(2)}, u32[]{:S(2)}) collective-permute-start(bf16[2,1280,128]{2,1,0:T(8,128)(2,1)} %collective-permute-done.6.refs_1_), channel_id=1, source_target_pairs={{0,16},{16,32},{32,48},{48,0},{1,17},{17,33},{33,49},{49,1},{2,18}... | collective-permute-start | bytes 1966088 | tf_op jit(solution)/shard_map/ppermute | solution.py:37
  66.7 16.4 %collective-permute-start.9 = (bf16[2,1280,128]{2,1,0:T(8,128)(2,1)}, bf16[2,1280,128]{2,1,0:T(8,128)(2,1)}, u32[]{:S(2)}, u32[]{:S(2)}) collective-permute-start(bf16[2,1280,128]{2,1,0:T(8,128)(2,1)} %collective-permute-done.6.refs_1_), channel_id=1, source_target_pairs={{0,48},{16,0},{32,16},{48,32},{1,49},{17,1},{33,17},{49,33},{2,50}... | collective-permute-start | bytes 1966088 | tf_op jit(solution)/shard_map/ppermute | solution.py:37
  68.1 1.6 collective-permute-start
  83.1 65.3 %copy-start.5 = (s32[4]{0:T(128)S(1)}, s32[4]{0:T(128)}, u32[]{:S(2)}) copy-start(s32[4]{0:T(128)} %ends_s.1) | copy-start | bytes 52
  83.1 65.3 %copy-start.6 = (s32[4]{0:T(128)S(1)}, s32[4]{0:T(128)}, u32[]{:S(2)}) copy-start(s32[4]{0:T(128)} %ends_p.1) | copy-start | bytes 52
  90.5 57.2 %copy-start.2 = (bf16[1024,128]{1,0:T(8,128)(2,1)}, bf16[1024,128]{1,0:T(8,128)(2,1)S(1)}, u32[]{:S(2)}) copy-start(bf16[1024,128]{1,0:T(8,128)(2,1)S(1)} %get-tuple-element.26.q0) | copy-start | bytes 786436
  90.5 57.1 %copy-start.3 = (bf16[512,256]{1,0:T(8,128)(2,1)}, bf16[512,256]{1,0:T(8,128)(2,1)S(1)}, u32[]{:S(2)}) copy-start(bf16[512,256]{1,0:T(8,128)(2,1)S(1)} %get-tuple-element.29.kv0) | copy-start | bytes 786436
  90.5 7.0 %collective-permute-start.14 = (bf16[1024,128]{1,0:T(8,128)(2,1)S(1)}, bf16[1024,128]{1,0:T(8,128)(2,1)S(1)}, u32[]{:S(2)}, u32[]{:S(2)}) collective-permute-start(bf16[1024,128]{1,0:T(8,128)(2,1)S(1)} %get-tuple-element.26.q0), channel_id=1, source_target_pairs={{0,48},{16,0},{32,16},{48,32},{1,49},{17,1},{33,17},{49,33},{2,50}... | collective-permute-start | bytes 786440 | tf_op jit(solution)/shard_map/ppermute | solution.py:37
  93.0 7.7 %collective-permute-start.13 = (bf16[1024,128]{1,0:T(8,128)(2,1)S(1)}, bf16[1024,128]{1,0:T(8,128)(2,1)S(1)}, u32[]{:S(2)}, u32[]{:S(2)}) collective-permute-start(bf16[1024,128]{1,0:T(8,128)(2,1)S(1)} %get-tuple-element.26.q0), channel_id=1, source_target_pairs={{0,32},{16,48},{32,0},{48,16},{1,33},{17,49},{33,1},{49,17},{2,34}... | collective-permute-start | bytes 786440 | tf_op jit(solution)/shard_map/ppermute | solution.py:37
  93.3 54.3 %collective-permute-start.12 = (bf16[1024,128]{1,0:T(8,128)(2,1)S(1)}, bf16[1024,128]{1,0:T(8,128)(2,1)S(1)}, u32[]{:S(2)}, u32[]{:S(2)}) collective-permute-start(bf16[1024,128]{1,0:T(8,128)(2,1)S(1)} %get-tuple-element.26.q0), channel_id=1, source_target_pairs={{0,16},{16,32},{32,48},{48,0},{1,17},{17,33},{33,49},{49,1},{2,18}... | collective-permute-start | bytes 786440 | tf_op jit(solution)/shard_map/ppermute | solution.py:37
  93.7 53.9 %collective-permute-start.15 = (bf16[512,256]{1,0:T(8,128)(2,1)S(1)}, bf16[512,256]{1,0:T(8,128)(2,1)}, u32[]{:S(2)}, u32[]{:S(2)}) collective-permute-start(bf16[512,256]{1,0:T(8,128)(2,1)S(1)} %get-tuple-element.29.kv0), channel_id=1, source_target_pairs={{0,64},{64,0},{1,65},{65,1},{2,66},{66,2},{3,67},{67,3},{4,68},{68... | collective-permute-start | bytes 786440 | tf_op jit(solution)/shard_map/ppermute | solution.py:41
  97.6 50.1 %copy-start.12 = (bf16[1024,128]{1,0:T(8,128)(2,1)}, bf16[1024,128]{1,0:T(8,128)(2,1)S(1)}, u32[]{:S(2)}) copy-start(bf16[1024,128]{1,0:T(8,128)(2,1)S(1)} %collective-permute-done.14.q3) | copy-start | bytes 786436
  167.4 17.7 %collective-permute-start.16 = (bf16[144,1024]{1,0:T(8,128)(2,1)S(1)}, bf16[144,1024]{1,0:T(8,128)(2,1)S(1)}, u32[]{:S(2)}, u32[]{:S(2)}) collective-permute-start(bf16[144,1024]{1,0:T(8,128)(2,1)S(1)} %get-tuple-element.31), channel_id=1, source_target_pairs={{0,48},{16,0},{32,16},{48,32},{1,49},{17,1},{33,17},{49,33},{2,50}... | collective-permute-start | bytes 884744 | tf_op jit(solution)/shard_map/ppermute | solution.py:37
  173.3 11.8 %collective-permute-start.17 = (bf16[144,1024]{1,0:T(8,128)(2,1)S(1)}, bf16[144,1024]{1,0:T(8,128)(2,1)S(1)}, u32[]{:S(2)}, u32[]{:S(2)}) collective-permute-start(bf16[144,1024]{1,0:T(8,128)(2,1)S(1)} %get-tuple-element.32), channel_id=1, source_target_pairs={{0,32},{16,48},{32,0},{48,16},{1,33},{17,49},{33,1},{49,17},{2,34}... | collective-permute-start | bytes 884744 | tf_op jit(solution)/shard_map/ppermute | solution.py:37
  173.3 16.1 %collective-permute-start.18 = (bf16[144,1024]{1,0:T(8,128)(2,1)S(1)}, bf16[144,1024]{1,0:T(8,128)(2,1)S(1)}, u32[]{:S(2)}, u32[]{:S(2)}) collective-permute-start(bf16[144,1024]{1,0:T(8,128)(2,1)S(1)} %get-tuple-element.33), channel_id=1, source_target_pairs={{0,16},{16,32},{32,48},{48,0},{1,17},{17,33},{33,49},{49,1},{2,18}... | collective-permute-start | bytes 884744 | tf_op jit(solution)/shard_map/ppermute | solution.py:37
  189.7 2.1 collective-permute-start.19
  219.3 2.8 %collective-permute-start.20 = (bf16[256,128]{1,0:T(8,128)(2,1)S(1)}, bf16[256,128]{1,0:T(8,128)(2,1)S(1)}, u32[]{:S(2)}, u32[]{:S(2)}) collective-permute-start(bf16[256,128]{1,0:T(8,128)(2,1)S(1)} %get-tuple-element.40), channel_id=1, source_target_pairs={{0,8},{8,0},{1,9},{9,1},{2,10},{10,2},{3,11},{11,3},{4,12},{12,4},... | collective-permute-start | bytes 196616 | tf_op jit(solution)/shard_map/ppermute | solution.py:45
  (6 other events, 83.8 us)
Sparse Core Ops, SparseCore 0:
  9.7 50.2 all-gather.4
  90.7 55.8 all-gather.6

commit v7 on v5

--- a/solution.py
+++ b/solution.py
@@ -41,6 +41,14 @@
     return lax.ppermute(x, "xl", [(0, 1), (1, 0)])
 
 
+def across_far(x):
+    return lax.ppermute(x, "xh", [(0, 1), (1, 0)])
+
+
+def along_z(x, k):
+    return lax.ppermute(x, "z", [(i, (i + k) % 4) for i in range(4)])
+
+
 def across_core(x):
     return lax.ppermute(x, "c", [(0, 1), (1, 0)])
 
@@ -69,29 +77,30 @@
         c.wait()
 
 
-def norm_kernel(idx, gain, blocks, normed, held, sem):
-    run([pltpu.make_async_copy(blocks, held, sem.at[0])])
+def norm_kernel(idx, gain, b0, b1, b2, b3, normed, held, sem):
+    refs = (b0, b1, b2, b3)
+    run([pltpu.make_async_copy(r, held.at[i], sem.at[i]) for i, r in enumerate(refs)])
     total = jnp.zeros((256, 1), F32)
     for k in range(8):
-        v = held[k].astype(F32)
+        v = held[k // 2, k % 2].astype(F32)
         total = total + jnp.sum(v * v, axis=1, keepdims=True)
     scale = lax.rsqrt(total * (1.0 / 2048) + EPS)
     for k in range(8):
-        v = held[k].astype(F32) * scale * gain[k].astype(F32)
-        normed[:, pl.ds(pl.multiple_of(idx[k] * 256, 256), 256)] = v.astype(BF16)
+        v = held[k // 2, k % 2].astype(F32) * scale * gain[idx[k]].astype(F32)
+        normed[:, pl.ds(pl.multiple_of(idx[8 + k] * 256, 256), 256)] = v.astype(BF16)
 
 
 def normalise(idx, gain, blocks):
     return pl.pallas_call(
         norm_kernel,
         out_shape=jax.ShapeDtypeStruct((256, 2048), BF16),
-        in_specs=[SMEM, VMEM, ANY],
+        in_specs=[SMEM, VMEM] + [ANY] * 4,
         out_specs=VMEM,
-        scratch_shapes=[pltpu.VMEM((8, 256, 256), BF16), pltpu.SemaphoreType.DMA((1,))],
+        scratch_shapes=[pltpu.VMEM((4, 2, 256, 256), BF16), pltpu.SemaphoreType.DMA((4,))],
         compiler_params=pltpu.CompilerParams(vmem_limit_bytes=8 << 20),
         cost_estimate=pl.CostEstimate(flops=1 << 24, bytes_accessed=2 << 20, transcendentals=0),
         name="normalise",
-    )(idx, gain, blocks)
+    )(idx, gain, *blocks)
 
 
 GROUPS = ((0, 512), (512, 768))
@@ -465,17 +474,19 @@
         return lax.dynamic_slice_in_dim(prefix_cache, h * 2 * H, 2 * H, 1)
 
     cache = jnp.stack([cache_of(c), across_core(cache_of(1 - c))])
-    tokens, w = tie(tokens, w)
-    copies = jnp.broadcast_to(tokens[None], (8,) + tokens.shape)
-    blocks = lax.all_to_all(copies, NARROW, 0, 0, tiled=True)
+    pair = jnp.stack([tokens, across_far(tokens)])
     far, ym, yp, a = along_y(w, 2), along_y(w, 3), along_y(w, 1), across_x(w)
     caches = [cache, across_x(cache)]
-    far, ym, yp, a, blocks, caches = lax.optimization_barrier((far, ym, yp, a, blocks, caches))
+    far, ym, yp, a, pair, caches = lax.optimization_barrier((far, ym, yp, a, pair, caches))
+    blocks = [pair] + [along_z(pair, k) for k in (1, 2, 3)]
     am, ap, afar = along_y(a, 3), along_y(a, 1), across_x(far)
+    blocks, am, ap, afar = lax.optimization_barrier((blocks, am, ap, afar))
     gathered = [w, a, ym, am, far, afar, yp, ap]
 
-    places = [(k % 4 - y + 4) % 4 * 2 + (k // 4 ^ xl) for k in range(8)]
-    normed = normalise(table(places), norm_gain.reshape(8, 1, 256), blocks)
+    z, xh = (lax.axis_index(a) for a in NARROW)
+    token_src = [lax.rem(z + 4 - dz, 4) * 2 + (xh ^ s) for dz in range(4) for s in range(2)]
+    places = [lax.rem(lax.rem(v, 4) + 4 - y, 4) * 2 + (v // 4 ^ xl) for v in token_src]
+    normed = normalise(table(token_src + places), norm_gain.reshape(8, 1, 256), blocks)
     out_early, am, ap = lax.optimization_barrier((out_weight, am, ap))
     gathered[3], gathered[7] = am, ap
     o_ym, o_yp, o_a = along_y(out_early, 3), along_y(out_early, 1), across_x(out_early)
@@ -483,8 +494,8 @@
         table(chips + [c]), both_routes, router.T, normed, across_core(normed), gathered
     )
     kvs = [kv, across_x(kv)]
-    q_out, o_ym, o_yp = lax.optimization_barrier((q, o_ym, o_yp))
-    qs = [q] + [along_y(q_out, k) for k in (1, 2, 3)]
+    qs = [q] + [along_y(q, k) for k in (1, 2, 3)]
+    qs[0], o_ym, o_yp = lax.optimization_barrier((q, o_ym, o_yp))
     out_late, o_a_late, kvs[1] = lax.optimization_barrier((out_weight, o_a, kvs[1]))
     o_far, o_am, o_ap = along_y(out_late, 2), along_y(o_a_late, 3), along_y(o_a_late, 1)
 

time: 184 us -> 175 us (0.951)
  waiting for transfers between devices: 85.1 us -> 74.5 us
  Pallas kernels: 26.8 us -> 32.8 us
  blocking collectives: 22.8 us -> 19.6 us
  starting transfers between devices: 41.3 us -> 39.2 us
    ppermute x16, waiting for transfers between devices: 70.9 us -> 58.4 us  [along_y(): return lax.ppermute(x, 'y', [(i, (i + k) % 4) for i in range(4)])]
    ppermute x0 -> x4, waiting for transfers between devices: none -> 10.5 us  [the longest x3 10.5 us: along_z(): return lax.ppermute(x, 'z', [(i, (i + k) % 4) for i in range(4)])]
    ppermute x6, waiting for transfers between devices: 10.4 us -> 1.38 us  [across_x(): return lax.ppermute(x, 'xl', [(0, 1), (1, 0)])]
    ppermute x0 -> x4, starting transfers between devices: none -> 6.88 us  [the longest x3 4.97 us: along_z(): return lax.ppermute(x, 'z', [(i, (i + k) % 4) for i in range(4)])]
    all_to_all x1 -> x0, starting transfers between devices: 6.59 us -> none  [on_device(): blocks = lax.all_to_all(copies, NARROW, 0, 0, tiled=True)]
    pallas_call x1, Pallas kernels: 10.4 us -> 16.4 us  [attend(): pl.pallas_call(attend_kernel, out_shape=tuple((jax.ShapeDtypeStruct((H +...]
    all_to_all x1, blocking collectives: 22.8 us -> 19.6 us  [on_device(): sums = lax.all_to_all(sums, NARROW, 0, 0, tiled=True)]
    unnamed x40 -> x56, local copies, waits for them, and re-layouts: 0.79 us -> 3.43 us
  transfers between devices with their start and end apart: 29 -> 32, of which waited for: 18 -> 19; matrix products, arithmetic and copies ran while one was open for 1% -> 1% of each run, Pallas kernels for 10% -> 14%
where the time goes in v7:
time: 175 us; the launch traced here: 173 us
  waiting for transfers between devices  74.5 us (43%)
  starting transfers between devices  39.2 us (22%)
  Pallas kernels  32.8 us (19%)
  blocking collectives  19.6 us (11%)
  local copies, waits for them, and re-layouts  5.43 us (3%)
    ppermute x16, waiting for transfers between devices, along_y(): return lax.ppermute(x, 'y', [(i, (i + k) % 4) for i in range(4)])  58.4 us
    all_to_all x1, blocking collectives, on_device(): sums = lax.all_to_all(sums, NARROW, 0, 0, tiled=True)  19.6 us
    ppermute x16, starting transfers between devices, along_y(): return lax.ppermute(x, 'y', [(i, (i + k) % 4) for i in range(4)])  19.1 us
    pallas_call x1, Pallas kernels, attend(): pl.pallas_call(attend_kernel, out_shape=tuple((jax.ShapeDtypeStruct((H +...  16.4 us
    ppermute x3, waiting for transfers between devices, along_z(): return lax.ppermute(x, 'z', [(i, (i + k) % 4) for i in range(4)])  10.5 us
    ppermute x6, starting transfers between devices, across_core(): return lax.ppermute(x, 'c', [(0, 1), (1, 0)])  9.41 us
    pallas_call x1, Pallas kernels, project(): pl.pallas_call(project_kernel, out_shape=(jax.ShapeDtypeStruct((1024, H),...  7.39 us
    pallas_call x1, Pallas kernels, project_out(): pl.pallas_call(out_kernel, out_shape=jax.ShapeDtypeStruct((8, 512, H), BF...  7.35 us
  transfers between devices with their start and end apart: 32, of which 19 were waited for; matrix products, arithmetic and copies ran while one was open for 1% of the time, Pallas kernels for 14%

profile of v7, /device:TPU:3, one launch (start us, length us, event | category | flops | bytes accessed | tf_op | source)
XLA Modules:
  0.0 172.9 jit_solution(17101459478427069565)
XLA Ops:
  2.2 1.9 %collective-permute-start.6 = (bf16[256,256]{1,0:T(8,128)(2,1)S(1)}, bf16[256,256]{1,0:T(8,128)(2,1)S(1)}, u32[]{:S(2)}, u32[]{:S(2)}) collective-permute-start(bf16[256,256]{1,0:T(8,128)(2,1)S(1)} %copy-done.10), channel_id=1, source_target_pairs={{0,1},{1,0},{2,3},{3,2},{4,5},{5,4},{6,7},{7,6},{8,9},{9,8},{10,11... | collective-permute-start | bytes 393224 | tf_op jit(solution)/shard_map/ppermute | solution.py:45
  4.3 1.2 collective-permute-start.8
  5.6 3.0 %collective-permute-start.2 = (bf16[2,1280,128]{2,1,0:T(8,128)(2,1)S(1)}, bf16[2,1280,128]{2,1,0:T(8,128)(2,1)S(1)}, u32[]{:S(2)}, u32[]{:S(2)}) collective-permute-start(bf16[2,1280,128]{2,1,0:T(8,128)(2,1)S(1)} %pad_maximum_fusion.1.refs_0_), channel_id=1, source_target_pairs={{0,32},{16,48},{32,0},{48,16},{1,33},{17,49},{33,1},{49,17},{2,34}... | collective-permute-start | bytes 1966088 | tf_op jit(solution)/shard_map/ppermute | solution.py:37
  10.4 11.9 %collective-permute-done.2.refs_4_ = bf16[2,1280,128]{2,1,0:T(8,128)(2,1)S(1)} collective-permute-done((bf16[2,1280,128]{2,1,0:T(8,128)(2,1)S(1)}, bf16[2,1280,128]{2,1,0:T(8,128)(2,1)S(1)}, u32[]{:S(2)}, u32[]{:S(2)}) %collective-permute-start.2) | collective-permute-done | bytes 655392 | tf_op jit(solution)/shard_map/ppermute | solution.py:37
  22.3 14.9 %collective-permute-done.3.refs_2_ = bf16[2,1280,128]{2,1,0:T(8,128)(2,1)S(1)} collective-permute-done((bf16[2,1280,128]{2,1,0:T(8,128)(2,1)S(1)}, bf16[2,1280,128]{2,1,0:T(8,128)(2,1)S(1)}, u32[]{:S(2)}, u32[]{:S(2)}) %collective-permute-start.3) | collective-permute-done | bytes 655392 | tf_op jit(solution)/shard_map/ppermute | solution.py:37
  37.9 1.4 collective-permute-done.5.refs_1_
  39.2 2.8 %collective-permute-start.12 = (bf16[2,1280,128]{2,1,0:T(8,128)(2,1)S(1)}, bf16[2,1280,128]{2,1,0:T(8,128)(2,1)S(1)}, u32[]{:S(2)}, u32[]{:S(2)}) collective-permute-start(bf16[2,1280,128]{2,1,0:T(8,128)(2,1)S(1)} %collective-permute-done.5.refs_1_), channel_id=1, source_target_pairs={{0,48},{16,0},{32,16},{48,32},{1,49},{17,1},{33,17},{49,33},{2,50}... | collective-permute-start | bytes 1966088 | tf_op jit(solution)/shard_map/ppermute | solution.py:37
  42.4 3.6 %collective-permute-start.10 = (bf16[2,256,256]{2,1,0:T(8,128)(2,1)S(1)}, bf16[2,256,256]{2,1,0:T(8,128)(2,1)S(1)}, u32[]{:S(2)}, u32[]{:S(2)}) collective-permute-start(bf16[2,256,256]{2,1,0:T(8,128)(2,1)S(1)} %pad_maximum_fusion.3.b0), channel_id=1, source_target_pairs={{0,4},{2,6},{4,0},{6,2},{1,5},{3,7},{5,1},{7,3},{8,12},{10,14},{12... | collective-permute-start | bytes 786440 | tf_op jit(solution)/shard_map/ppermute | solution.py:49
  46.4 4.2 %collective-permute-done.10.b2 = bf16[2,256,256]{2,1,0:T(8,128)(2,1)S(1)} collective-permute-done((bf16[2,256,256]{2,1,0:T(8,128)(2,1)S(1)}, bf16[2,256,256]{2,1,0:T(8,128)(2,1)S(1)}, u32[]{:S(2)}, u32[]{:S(2)}) %collective-permute-start.10) | collective-permute-done | bytes 262176 | tf_op jit(solution)/shard_map/ppermute | solution.py:49
  51.7 6.3 %collective-permute-done.11.b3 = bf16[2,256,256]{2,1,0:T(8,128)(2,1)S(1)} collective-permute-done((bf16[2,256,256]{2,1,0:T(8,128)(2,1)S(1)}, bf16[2,256,256]{2,1,0:T(8,128)(2,1)S(1)}, u32[]{:S(2)}, u32[]{:S(2)}) %collective-permute-start.11) | collective-permute-done | bytes 262176 | tf_op jit(solution)/shard_map/ppermute | solution.py:49
  58.9 1.3 normalise.1.own
  60.2 5.6 %collective-permute-start.15 = (bf16[256,2048]{1,0:T(8,128)(2,1)S(1)}, bf16[256,2048]{1,0:T(8,128)(2,1)S(1)}, u32[]{:S(2)}, u32[]{:S(2)}) collective-permute-start(bf16[256,2048]{1,0:T(8,128)(2,1)S(1)} %normalise.1.own), channel_id=1, source_target_pairs={{0,8},{8,0},{1,9},{9,1},{2,10},{10,2},{3,11},{11,3},{4,12},{12,4},... | collective-permute-start | bytes 3145736 | tf_op jit(solution)/shard_map/ppermute | solution.py:53
  66.0 2.1 %collective-permute-done = s32[256,2]{0,1:T(2,128)S(1)} collective-permute-done((s32[256,2]{0,1:T(2,128)S(1)}, s32[256,2]{0,1:T(2,128)S(1)}, u32[]{:S(2)}, u32[]{:S(2)}) %collective-permute-start) | collective-permute-done | bytes 2080 | tf_op jit(solution)/shard_map/ppermute | solution.py:53
  68.5 1.2 collective-permute-start.21
  69.7 3.0 %collective-permute-start.16 = (bf16[2048,128]{1,0:T(8,128)(2,1)}, bf16[2048,128]{1,0:T(8,128)(2,1)S(1)}, u32[]{:S(2)}, u32[]{:S(2)}) collective-permute-start(bf16[2048,128]{1,0:T(8,128)(2,1)} %refs_0_.1), channel_id=1, source_target_pairs={{0,48},{16,0},{32,16},{48,32},{1,49},{17,1},{33,17},{49,33},{2,50}... | collective-permute-start | bytes 1572872 | tf_op jit(solution)/shard_map/ppermute | solution.py:37
  73.7 7.4 %project.1 = (bf16[1024,128]{1,0:T(8,128)(2,1)S(1)}, bf16[512,256]{1,0:T(8,128)(2,1)S(1)}, f32[512,2]{1,0:T(8,128)S(1)}) custom-call(s32[9]{0:T(128)S(1)} %stack.155.idx, s32[512,2]{1,0:T(8,128)S(1)} %broadcast_select_fusion.routes, bf16[8,2048]{1,0:T(8,128)(2,1)S(1)} %bitcast.45, bf16[256,2048]{1,0:T(8,128)(2,1)} %copy-done, bf16[256,2048]{1,0:T(8,128)(2,1)} %copy-done.13, ...), custom_call_target="tpu_custom_call" | custom-call | flops 6442450944 | bytes 8388608 | tf_op jit(solution)/shard_map/project/pallas_call | solution.py:171
  81.5 2.1 %collective-permute-done.16.refs_2_ = bf16[2048,128]{1,0:T(8,128)(2,1)S(1)} collective-permute-done((bf16[2048,128]{1,0:T(8,128)(2,1)}, bf16[2048,128]{1,0:T(8,128)(2,1)S(1)}, u32[]{:S(2)}, u32[]{:S(2)}) %collective-permute-start.16) | collective-permute-done | bytes 524320 | tf_op jit(solution)/shard_map/ppermute | solution.py:37
  83.6 2.2 %collective-permute-start.19 = (bf16[1024,128]{1,0:T(8,128)(2,1)S(1)}, bf16[1024,128]{1,0:T(8,128)(2,1)S(1)}, u32[]{:S(2)}, u32[]{:S(2)}) collective-permute-start(bf16[1024,128]{1,0:T(8,128)(2,1)S(1)} %get-tuple-element.58.q0), channel_id=1, source_target_pairs={{0,32},{16,48},{32,0},{48,16},{1,33},{17,49},{33,1},{49,17},{2,34}... | collective-permute-start | bytes 786440 | tf_op jit(solution)/shard_map/ppermute | solution.py:37
  88.6 1.8 %collective-permute-start.24 = (bf16[2048,128]{1,0:T(8,128)(2,1)}, bf16[2048,128]{1,0:T(8,128)(2,1)S(1)}, u32[]{:S(2)}, u32[]{:S(2)}) collective-permute-start(bf16[2048,128]{1,0:T(8,128)(2,1)} %collective-permute-done.21.refs_1_), channel_id=1, source_target_pairs={{0,48},{16,0},{32,16},{48,32},{1,49},{17,1},{33,17},{49,33},{2,50}... | collective-permute-start | bytes 1572872 | tf_op jit(solution)/shard_map/ppermute | solution.py:37
  90.4 3.8 %collective-permute-done.18.q1 = bf16[1024,128]{1,0:T(8,128)(2,1)S(1)} collective-permute-done((bf16[1024,128]{1,0:T(8,128)(2,1)S(1)}, bf16[1024,128]{1,0:T(8,128)(2,1)S(1)}, u32[]{:S(2)}, u32[]{:S(2)}) %collective-permute-start.18) | collective-permute-done | bytes 262176 | tf_op jit(solution)/shard_map/ppermute | solution.py:37
  94.2 1.7 collective-permute-done.19.q2
  96.6 2.3 %collective-permute-done.20.q3 = bf16[1024,128]{1,0:T(8,128)(2,1)} collective-permute-done((bf16[1024,128]{1,0:T(8,128)(2,1)S(1)}, bf16[1024,128]{1,0:T(8,128)(2,1)}, u32[]{:S(2)}, u32[]{:S(2)}) %collective-permute-start.20) | collective-permute-done | bytes 262176 | tf_op jit(solution)/shard_map/ppermute | solution.py:37
  98.9 16.4 %attend.1 = (bf16[144,1024]{1,0:T(8,128)(2,1)S(1)}, bf16[144,1024]{1,0:T(8,128)(2,1)S(1)}, bf16[144,1024]{1,0:T(8,128)(2,1)S(1)}, bf16[144,1024]{1,0:T(8,128)(2,1)S(1)}) custom-call(s32[9]{0:T(128)S(1)} %stack.190.idx, s32[4]{0:T(128)S(1)} %copy-done.4, s32[4]{0:T(128)S(1)} %copy-done.5, bf16[1024,128]{1,0:T(8,128)(2,1)} %copy-done.1, ...), custom_call_target="tpu_custom_call" | custom-call | flops 12884901888 | bytes 6291456 | tf_op jit(solution)/shard_map/attend/pallas_call | solution.py:334
  115.3 3.2 %collective-permute-done.23.refs_4_ = bf16[2048,128]{1,0:T(8,128)(2,1)} collective-permute-done((bf16[2048,128]{1,0:T(8,128)(2,1)}, bf16[2048,128]{1,0:T(8,128)(2,1)}, u32[]{:S(2)}, u32[]{:S(2)}) %collective-permute-start.23) | collective-permute-done | bytes 524320 | tf_op jit(solution)/shard_map/ppermute | solution.py:37
  118.5 2.0 %collective-permute-done.25.refs_7_ = bf16[2048,128]{1,0:T(8,128)(2,1)S(1)} collective-permute-done((bf16[2048,128]{1,0:T(8,128)(2,1)}, bf16[2048,128]{1,0:T(8,128)(2,1)S(1)}, u32[]{:S(2)}, u32[]{:S(2)}) %collective-permute-start.25) | collective-permute-done | bytes 524320 | tf_op jit(solution)/shard_map/ppermute | solution.py:37
  120.5 3.2 %collective-permute-start.26 = (bf16[144,1024]{1,0:T(8,128)(2,1)S(1)}, bf16[144,1024]{1,0:T(8,128)(2,1)S(1)}, u32[]{:S(2)}, u32[]{:S(2)}) collective-permute-start(bf16[144,1024]{1,0:T(8,128)(2,1)S(1)} %get-tuple-element.69), channel_id=1, source_target_pairs={{0,48},{16,0},{32,16},{48,32},{1,49},{17,1},{33,17},{49,33},{2,50}... | collective-permute-start | bytes 884744 | tf_op jit(solution)/shard_map/ppermute | solution.py:37
  124.8 4.4 %collective-permute-done.26.p1 = bf16[144,1024]{1,0:T(8,128)(2,1)S(1)} collective-permute-done((bf16[144,1024]{1,0:T(8,128)(2,1)S(1)}, bf16[144,1024]{1,0:T(8,128)(2,1)S(1)}, u32[]{:S(2)}, u32[]{:S(2)}) %collective-permute-start.26) | collective-permute-done | bytes 294944 | tf_op jit(solution)/shard_map/ppermute | solution.py:37
  129.2 1.8 %collective-permute-done.27.p2 = bf16[144,1024]{1,0:T(8,128)(2,1)S(1)} collective-permute-done((bf16[144,1024]{1,0:T(8,128)(2,1)S(1)}, bf16[144,1024]{1,0:T(8,128)(2,1)S(1)}, u32[]{:S(2)}, u32[]{:S(2)}) %collective-permute-start.27) | collective-permute-done | bytes 294944 | tf_op jit(solution)/shard_map/ppermute | solution.py:37
  130.9 8.9 %collective-permute-done.28.p3 = bf16[144,1024]{1,0:T(8,128)(2,1)S(1)} collective-permute-done((bf16[144,1024]{1,0:T(8,128)(2,1)S(1)}, bf16[144,1024]{1,0:T(8,128)(2,1)S(1)}, u32[]{:S(2)}, u32[]{:S(2)}) %collective-permute-start.28) | collective-permute-done | bytes 294944 | tf_op jit(solution)/shard_map/ppermute | solution.py:37
  142.3 7.4 %project_out.1 = bf16[8,512,128]{2,1,0:T(8,128)(2,1)S(1)} custom-call(s32[9]{0:T(128)S(1)} %stack.155.idx, s32[512,2]{1,0:T(8,128)S(1)} %broadcast_select_fusion.routes, bf16[1024,128]{1,0:T(8,128)(2,1)S(1)} %combine.1.own, bf16[1024,128]{1,0:T(8,128)(2,1)S(1)} %collective-permute-done.29.other, bf16[2048,128]{1,0:T(8,128)(2,1)} %refs_0_.1, ...), custom_call_target="tpu_custom_call" | custom-call | flops 4294967296 | bytes 6291456 | tf_op jit(solution)/shard_map/project_out/pallas_call | solution.py:423
  149.6 19.6 %all_to_all.5 = bf16[8,512,128]{2,1,0:T(8,128)(2,1)S(1)} all-to-all(bf16[8,512,128]{2,1,0:T(8,128)(2,1)S(1)} %project_out.1), channel_id=1, replica_groups=mesh['xl'=2,'y'=4,'c'=2,'z'=4,'xh'=2] {'z','xh'}, dimensions={0} | all-to-all | bytes 2097152 | tf_op jit(solution)/shard_map/all_to_all | solution.py:516
  169.4 1.9 %collective-permute-start.31 = (bf16[256,128]{1,0:T(8,128)(2,1)S(1)}, bf16[256,128]{1,0:T(8,128)(2,1)S(1)}, u32[]{:S(2)}, u32[]{:S(2)}) collective-permute-start(bf16[256,128]{1,0:T(8,128)(2,1)S(1)} %get-tuple-element.82), channel_id=1, source_target_pairs={{0,8},{8,0},{1,9},{9,1},{2,10},{10,2},{3,11},{11,3},{4,12},{12,4},... | collective-permute-start | bytes 196616 | tf_op jit(solution)/shard_map/ppermute | solution.py:53
  (115 shorter events, 18.2 us)
Async XLA Ops:
  1.3 2.9 %collective-permute-start.7 = (bf16[768,256]{1,0:T(8,128)(2,1)S(1)}, bf16[768,256]{1,0:T(8,128)(2,1)S(1)}, u32[]{:S(2)}, u32[]{:S(2)}) collective-permute-start(bf16[768,256]{1,0:T(8,128)(2,1)S(1)} %get-tuple-element.78), channel_id=1, source_target_pairs={{0,8},{8,0},{1,9},{9,1},{2,10},{10,2},{3,11},{11,3},{4,12},{12,4},... | collective-permute-start | bytes 1179656 | tf_op jit(solution)/shard_map/ppermute | solution.py:53
  2.1 3.4 %collective-permute-start.1 = (bf16[1280,128]{1,0:T(8,128)(2,1)S(1)}, bf16[1280,128]{1,0:T(8,128)(2,1)S(1)}, u32[]{:S(2)}, u32[]{:S(2)}) collective-permute-start(bf16[1280,128]{1,0:T(8,128)(2,1)S(1)} %pad_maximum_fusion.2), channel_id=1, source_target_pairs={{0,8},{8,0},{1,9},{9,1},{2,10},{10,2},{3,11},{11,3},{4,12},{12,4},... | collective-permute-start | bytes 983048 | tf_op jit(solution)/shard_map/ppermute | solution.py:53
  2.2 7.8 %collective-permute-start.6 = (bf16[256,256]{1,0:T(8,128)(2,1)S(1)}, bf16[256,256]{1,0:T(8,128)(2,1)S(1)}, u32[]{:S(2)}, u32[]{:S(2)}) collective-permute-start(bf16[256,256]{1,0:T(8,128)(2,1)S(1)} %copy-done.10), channel_id=1, source_target_pairs={{0,1},{1,0},{2,3},{3,2},{4,5},{5,4},{6,7},{7,6},{8,9},{9,8},{10,11... | collective-permute-start | bytes 393224 | tf_op jit(solution)/shard_map/ppermute | solution.py:45
  4.3 35.0 %collective-permute-start.8 = (bf16[2,768,256]{2,1,0:T(8,128)(2,1)S(1)}, bf16[2,768,256]{2,1,0:T(8,128)(2,1)S(1)}, u32[]{:S(2)}, u32[]{:S(2)}) collective-permute-start(bf16[2,768,256]{2,1,0:T(8,128)(2,1)S(1)} %pad_maximum_fusion.cache0), channel_id=1, source_target_pairs={{0,64},{64,0},{1,65},{65,1},{2,66},{66,2},{3,67},{67,3},{4,68},{68... | collective-permute-start | bytes 2359304 | tf_op jit(solution)/shard_map/ppermute | solution.py:41
  5.6 16.7 %collective-permute-start.2 = (bf16[2,1280,128]{2,1,0:T(8,128)(2,1)S(1)}, bf16[2,1280,128]{2,1,0:T(8,128)(2,1)S(1)}, u32[]{:S(2)}, u32[]{:S(2)}) collective-permute-start(bf16[2,1280,128]{2,1,0:T(8,128)(2,1)S(1)} %pad_maximum_fusion.1.refs_0_), channel_id=1, source_target_pairs={{0,32},{16,48},{32,0},{48,16},{1,33},{17,49},{33,1},{49,17},{2,34}... | collective-permute-start | bytes 1966088 | tf_op jit(solution)/shard_map/ppermute | solution.py:37
  8.6 28.6 %collective-permute-start.3 = (bf16[2,1280,128]{2,1,0:T(8,128)(2,1)S(1)}, bf16[2,1280,128]{2,1,0:T(8,128)(2,1)S(1)}, u32[]{:S(2)}, u32[]{:S(2)}) collective-permute-start(bf16[2,1280,128]{2,1,0:T(8,128)(2,1)S(1)} %pad_maximum_fusion.1.refs_0_), channel_id=1, source_target_pairs={{0,48},{16,0},{32,16},{48,32},{1,49},{17,1},{33,17},{49,33},{2,50}... | collective-permute-start | bytes 1966088 | tf_op jit(solution)/shard_map/ppermute | solution.py:37
  9.4 28.5 %collective-permute-start.4 = (bf16[2,1280,128]{2,1,0:T(8,128)(2,1)S(1)}, bf16[2,1280,128]{2,1,0:T(8,128)(2,1)S(1)}, u32[]{:S(2)}, u32[]{:S(2)}) collective-permute-start(bf16[2,1280,128]{2,1,0:T(8,128)(2,1)S(1)} %pad_maximum_fusion.1.refs_0_), channel_id=1, source_target_pairs={{0,16},{16,32},{32,48},{48,0},{1,17},{17,33},{33,49},{49,1},{2,18}... | collective-permute-start | bytes 1966088 | tf_op jit(solution)/shard_map/ppermute | solution.py:37
  10.1 29.2 %collective-permute-start.5 = (bf16[2,1280,128]{2,1,0:T(8,128)(2,1)S(1)}, bf16[2,1280,128]{2,1,0:T(8,128)(2,1)S(1)}, u32[]{:S(2)}, u32[]{:S(2)}) collective-permute-start(bf16[2,1280,128]{2,1,0:T(8,128)(2,1)S(1)} %pad_maximum_fusion.1.refs_0_), channel_id=1, source_target_pairs={{0,64},{64,0},{1,65},{65,1},{2,66},{66,2},{3,67},{67,3},{4,68},{68... | collective-permute-start | bytes 1966088 | tf_op jit(solution)/shard_map/ppermute | solution.py:41
  39.2 18.8 %collective-permute-start.12 = (bf16[2,1280,128]{2,1,0:T(8,128)(2,1)S(1)}, bf16[2,1280,128]{2,1,0:T(8,128)(2,1)S(1)}, u32[]{:S(2)}, u32[]{:S(2)}) collective-permute-start(bf16[2,1280,128]{2,1,0:T(8,128)(2,1)S(1)} %collective-permute-done.5.refs_1_), channel_id=1, source_target_pairs={{0,48},{16,0},{32,16},{48,32},{1,49},{17,1},{33,17},{49,33},{2,50}... | collective-permute-start | bytes 1966088 | tf_op jit(solution)/shard_map/ppermute | solution.py:37
  42.0 16.0 %collective-permute-start.13 = (bf16[2,1280,128]{2,1,0:T(8,128)(2,1)S(1)}, bf16[2,1280,128]{2,1,0:T(8,128)(2,1)}, u32[]{:S(2)}, u32[]{:S(2)}) collective-permute-start(bf16[2,1280,128]{2,1,0:T(8,128)(2,1)S(1)} %collective-permute-done.5.refs_1_), channel_id=1, source_target_pairs={{0,16},{16,32},{32,48},{48,0},{1,17},{17,33},{33,49},{49,1},{2,18}... | collective-permute-start | bytes 1966088 | tf_op jit(solution)/shard_map/ppermute | solution.py:37
  42.0 16.0 %collective-permute-start.14 = (bf16[2,1280,128]{2,1,0:T(8,128)(2,1)S(1)}, bf16[2,1280,128]{2,1,0:T(8,128)(2,1)}, u32[]{:S(2)}, u32[]{:S(2)}) collective-permute-start(bf16[2,1280,128]{2,1,0:T(8,128)(2,1)S(1)} %collective-permute-done.2.refs_4_), channel_id=1, source_target_pairs={{0,64},{64,0},{1,65},{65,1},{2,66},{66,2},{3,67},{67,3},{4,68},{68... | collective-permute-start | bytes 1966088 | tf_op jit(solution)/shard_map/ppermute | solution.py:41
  42.4 8.2 %collective-permute-start.10 = (bf16[2,256,256]{2,1,0:T(8,128)(2,1)S(1)}, bf16[2,256,256]{2,1,0:T(8,128)(2,1)S(1)}, u32[]{:S(2)}, u32[]{:S(2)}) collective-permute-start(bf16[2,256,256]{2,1,0:T(8,128)(2,1)S(1)} %pad_maximum_fusion.3.b0), channel_id=1, source_target_pairs={{0,4},{2,6},{4,0},{6,2},{1,5},{3,7},{5,1},{7,3},{8,12},{10,14},{12... | collective-permute-start | bytes 786440 | tf_op jit(solution)/shard_map/ppermute | solution.py:49
  46.0 12.1 %collective-permute-start.11 = (bf16[2,256,256]{2,1,0:T(8,128)(2,1)S(1)}, bf16[2,256,256]{2,1,0:T(8,128)(2,1)S(1)}, u32[]{:S(2)}, u32[]{:S(2)}) collective-permute-start(bf16[2,256,256]{2,1,0:T(8,128)(2,1)S(1)} %pad_maximum_fusion.3.b0), channel_id=1, source_target_pairs={{0,6},{2,0},{4,2},{6,4},{1,7},{3,1},{5,3},{7,5},{8,14},{10,8},{12,... | collective-permute-start | bytes 786440 | tf_op jit(solution)/shard_map/ppermute | solution.py:49
  50.6 7.4 %collective-permute-start.9 = (bf16[2,256,256]{2,1,0:T(8,128)(2,1)S(1)}, bf16[2,256,256]{2,1,0:T(8,128)(2,1)S(1)}, u32[]{:S(2)}, u32[]{:S(2)}) collective-permute-start(bf16[2,256,256]{2,1,0:T(8,128)(2,1)S(1)} %pad_maximum_fusion.3.b0), channel_id=1, source_target_pairs={{0,2},{2,4},{4,6},{6,0},{1,3},{3,5},{5,7},{7,1},{8,10},{10,12},{12... | collective-permute-start | bytes 786440 | tf_op jit(solution)/shard_map/ppermute | solution.py:49
  60.2 12.5 %collective-permute-start.15 = (bf16[256,2048]{1,0:T(8,128)(2,1)S(1)}, bf16[256,2048]{1,0:T(8,128)(2,1)S(1)}, u32[]{:S(2)}, u32[]{:S(2)}) collective-permute-start(bf16[256,2048]{1,0:T(8,128)(2,1)S(1)} %normalise.1.own), channel_id=1, source_target_pairs={{0,8},{8,0},{1,9},{9,1},{2,10},{10,2},{3,11},{11,3},{4,12},{12,4},... | collective-permute-start | bytes 3145736 | tf_op jit(solution)/shard_map/ppermute | solution.py:53
  65.8 2.3 %collective-permute-start = (s32[256,2]{0,1:T(2,128)S(1)}, s32[256,2]{0,1:T(2,128)S(1)}, u32[]{:S(2)}, u32[]{:S(2)}) collective-permute-start(s32[256,2]{0,1:T(2,128)S(1)} %copy-done.12), channel_id=1, source_target_pairs={{0,8},{8,0},{1,9},{9,1},{2,10},{10,2},{3,11},{11,3},{4,12},{12,4},... | collective-permute-start | bytes 6152 | tf_op jit(solution)/shard_map/ppermute | solution.py:53
  68.5 20.1 %collective-permute-start.21 = (bf16[2048,128]{1,0:T(8,128)(2,1)}, bf16[2048,128]{1,0:T(8,128)(2,1)}, u32[]{:S(2)}, u32[]{:S(2)}) collective-permute-start(bf16[2048,128]{1,0:T(8,128)(2,1)} %refs_0_.1), channel_id=1, source_target_pairs={{0,64},{64,0},{1,65},{65,1},{2,66},{66,2},{3,67},{67,3},{4,68},{68... | collective-permute-start | bytes 1572872 | tf_op jit(solution)/shard_map/ppermute | solution.py:41
  69.7 13.9 %collective-permute-start.16 = (bf16[2048,128]{1,0:T(8,128)(2,1)}, bf16[2048,128]{1,0:T(8,128)(2,1)S(1)}, u32[]{:S(2)}, u32[]{:S(2)}) collective-permute-start(bf16[2048,128]{1,0:T(8,128)(2,1)} %refs_0_.1), channel_id=1, source_target_pairs={{0,48},{16,0},{32,16},{48,32},{1,49},{17,1},{33,17},{49,33},{2,50}... | collective-permute-start | bytes 1572872 | tf_op jit(solution)/shard_map/ppermute | solution.py:37
  72.7 13.9 %collective-permute-start.17 = (bf16[2048,128]{1,0:T(8,128)(2,1)}, bf16[2048,128]{1,0:T(8,128)(2,1)S(1)}, u32[]{:S(2)}, u32[]{:S(2)}) collective-permute-start(bf16[2048,128]{1,0:T(8,128)(2,1)} %refs_0_.1), channel_id=1, source_target_pairs={{0,16},{16,32},{32,48},{48,0},{1,17},{17,33},{33,49},{49,1},{2,18}... | collective-permute-start | bytes 1572872 | tf_op jit(solution)/shard_map/ppermute | solution.py:37
  81.1 7.5 %collective-permute-start.22 = (bf16[512,256]{1,0:T(8,128)(2,1)S(1)}, bf16[512,256]{1,0:T(8,128)(2,1)S(1)}, u32[]{:S(2)}, u32[]{:S(2)}) collective-permute-start(bf16[512,256]{1,0:T(8,128)(2,1)S(1)} %get-tuple-element.61.kv0), channel_id=1, source_target_pairs={{0,64},{64,0},{1,65},{65,1},{2,66},{66,2},{3,67},{67,3},{4,68},{68... | collective-permute-start | bytes 786440 | tf_op jit(solution)/shard_map/ppermute | solution.py:41
  81.5 12.7 %collective-permute-start.18 = (bf16[1024,128]{1,0:T(8,128)(2,1)S(1)}, bf16[1024,128]{1,0:T(8,128)(2,1)S(1)}, u32[]{:S(2)}, u32[]{:S(2)}) collective-permute-start(bf16[1024,128]{1,0:T(8,128)(2,1)S(1)} %get-tuple-element.58.q0), channel_id=1, source_target_pairs={{0,16},{16,32},{32,48},{48,0},{1,17},{17,33},{33,49},{49,1},{2,18}... | collective-permute-start | bytes 786440 | tf_op jit(solution)/shard_map/ppermute | solution.py:37
  83.6 12.3 %collective-permute-start.19 = (bf16[1024,128]{1,0:T(8,128)(2,1)S(1)}, bf16[1024,128]{1,0:T(8,128)(2,1)S(1)}, u32[]{:S(2)}, u32[]{:S(2)}) collective-permute-start(bf16[1024,128]{1,0:T(8,128)(2,1)S(1)} %get-tuple-element.58.q0), channel_id=1, source_target_pairs={{0,32},{16,48},{32,0},{48,16},{1,33},{17,49},{33,1},{49,17},{2,34}... | collective-permute-start | bytes 786440 | tf_op jit(solution)/shard_map/ppermute | solution.py:37
  87.4 11.5 %collective-permute-start.20 = (bf16[1024,128]{1,0:T(8,128)(2,1)S(1)}, bf16[1024,128]{1,0:T(8,128)(2,1)}, u32[]{:S(2)}, u32[]{:S(2)}) collective-permute-start(bf16[1024,128]{1,0:T(8,128)(2,1)S(1)} %get-tuple-element.58.q0), channel_id=1, source_target_pairs={{0,48},{16,0},{32,16},{48,32},{1,49},{17,1},{33,17},{49,33},{2,50}... | collective-permute-start | bytes 786440 | tf_op jit(solution)/shard_map/ppermute | solution.py:37
  88.6 29.8 %collective-permute-start.24 = (bf16[2048,128]{1,0:T(8,128)(2,1)}, bf16[2048,128]{1,0:T(8,128)(2,1)S(1)}, u32[]{:S(2)}, u32[]{:S(2)}) collective-permute-start(bf16[2048,128]{1,0:T(8,128)(2,1)} %collective-permute-done.21.refs_1_), channel_id=1, source_target_pairs={{0,48},{16,0},{32,16},{48,32},{1,49},{17,1},{33,17},{49,33},{2,50}... | collective-permute-start | bytes 1572872 | tf_op jit(solution)/shard_map/ppermute | solution.py:37
  90.4 30.1 %collective-permute-start.25 = (bf16[2048,128]{1,0:T(8,128)(2,1)}, bf16[2048,128]{1,0:T(8,128)(2,1)S(1)}, u32[]{:S(2)}, u32[]{:S(2)}) collective-permute-start(bf16[2048,128]{1,0:T(8,128)(2,1)} %collective-permute-done.21.refs_1_), channel_id=1, source_target_pairs={{0,16},{16,32},{32,48},{48,0},{1,17},{17,33},{33,49},{49,1},{2,18}... | collective-permute-start | bytes 1572872 | tf_op jit(solution)/shard_map/ppermute | solution.py:37
  94.2 24.3 %collective-permute-start.23 = (bf16[2048,128]{1,0:T(8,128)(2,1)}, bf16[2048,128]{1,0:T(8,128)(2,1)}, u32[]{:S(2)}, u32[]{:S(2)}) collective-permute-start(bf16[2048,128]{1,0:T(8,128)(2,1)} %refs_0_.1), channel_id=1, source_target_pairs={{0,32},{16,48},{32,0},{48,16},{1,33},{17,49},{33,1},{49,17},{2,34}... | collective-permute-start | bytes 1572872 | tf_op jit(solution)/shard_map/ppermute | solution.py:37
  120.5 8.7 %collective-permute-start.26 = (bf16[144,1024]{1,0:T(8,128)(2,1)S(1)}, bf16[144,1024]{1,0:T(8,128)(2,1)S(1)}, u32[]{:S(2)}, u32[]{:S(2)}) collective-permute-start(bf16[144,1024]{1,0:T(8,128)(2,1)S(1)} %get-tuple-element.69), channel_id=1, source_target_pairs={{0,48},{16,0},{32,16},{48,32},{1,49},{17,1},{33,17},{49,33},{2,50}... | collective-permute-start | bytes 884744 | tf_op jit(solution)/shard_map/ppermute | solution.py:37
  123.7 7.2 %collective-permute-start.27 = (bf16[144,1024]{1,0:T(8,128)(2,1)S(1)}, bf16[144,1024]{1,0:T(8,128)(2,1)S(1)}, u32[]{:S(2)}, u32[]{:S(2)}) collective-permute-start(bf16[144,1024]{1,0:T(8,128)(2,1)S(1)} %get-tuple-element.70), channel_id=1, source_target_pairs={{0,32},{16,48},{32,0},{48,16},{1,33},{17,49},{33,1},{49,17},{2,34}... | collective-permute-start | bytes 884744 | tf_op jit(solution)/shard_map/ppermute | solution.py:37
  123.8 16.1 %collective-permute-start.28 = (bf16[144,1024]{1,0:T(8,128)(2,1)S(1)}, bf16[144,1024]{1,0:T(8,128)(2,1)S(1)}, u32[]{:S(2)}, u32[]{:S(2)}) collective-permute-start(bf16[144,1024]{1,0:T(8,128)(2,1)S(1)} %get-tuple-element.71), channel_id=1, source_target_pairs={{0,16},{16,32},{32,48},{48,0},{1,17},{17,33},{33,49},{49,1},{2,18}... | collective-permute-start | bytes 884744 | tf_op jit(solution)/shard_map/ppermute | solution.py:37
  124.3 16.8 %collective-permute-start.30 = (bf16[2048,128]{1,0:T(8,128)(2,1)}, bf16[2048,128]{1,0:T(8,128)(2,1)S(1)}, u32[]{:S(2)}, u32[]{:S(2)}) collective-permute-start(bf16[2048,128]{1,0:T(8,128)(2,1)} %collective-permute-done.23.refs_4_), channel_id=1, source_target_pairs={{0,64},{64,0},{1,65},{65,1},{2,66},{66,2},{3,67},{67,3},{4,68},{68... | collective-permute-start | bytes 1572872 | tf_op jit(solution)/shard_map/ppermute | solution.py:41
  140.2 2.1 %collective-permute-start.29 = (bf16[1024,128]{1,0:T(8,128)(2,1)S(1)}, bf16[1024,128]{1,0:T(8,128)(2,1)S(1)}, u32[]{:S(2)}, u32[]{:S(2)}) collective-permute-start(bf16[1024,128]{1,0:T(8,128)(2,1)S(1)} %combine.1.own), channel_id=1, source_target_pairs={{0,8},{8,0},{1,9},{9,1},{2,10},{10,2},{3,11},{11,3},{4,12},{12,4},... | collective-permute-start | bytes 786440 | tf_op jit(solution)/shard_map/ppermute | solution.py:53
  169.4 2.8 %collective-permute-start.31 = (bf16[256,128]{1,0:T(8,128)(2,1)S(1)}, bf16[256,128]{1,0:T(8,128)(2,1)S(1)}, u32[]{:S(2)}, u32[]{:S(2)}) collective-permute-start(bf16[256,128]{1,0:T(8,128)(2,1)S(1)} %get-tuple-element.82), channel_id=1, source_target_pairs={{0,8},{8,0},{1,9},{9,1},{2,10},{10,2},{3,11},{11,3},{4,12},{12,4},... | collective-permute-start | bytes 196616 | tf_op jit(solution)/shard_map/ppermute | solution.py:53
  (28 other events, 377.8 us)

commit v8 on v7

--- a/solution.py
+++ b/solution.py
@@ -23,8 +23,6 @@
 CK = 512
 R = 512
 CHUNKS = 8
-TILES = 8
-DUMMY = 8
 UNROLL = 4
 
 SMEM = pl.BlockSpec(memory_space=pltpu.SMEM)
@@ -45,10 +43,6 @@
     return lax.ppermute(x, "xh", [(0, 1), (1, 0)])
 
 
-def along_z(x, k):
-    return lax.ppermute(x, "z", [(i, (i + k) % 4) for i in range(4)])
-
-
 def across_core(x):
     return lax.ppermute(x, "c", [(0, 1), (1, 0)])
 
@@ -77,9 +71,8 @@
         c.wait()
 
 
-def norm_kernel(idx, gain, b0, b1, b2, b3, normed, held, sem):
-    refs = (b0, b1, b2, b3)
-    run([pltpu.make_async_copy(r, held.at[i], sem.at[i]) for i, r in enumerate(refs)])
+def norm_kernel(idx, gain, blocks, normed, held, sem):
+    run([pltpu.make_async_copy(blocks, held, sem.at[0])])
     total = jnp.zeros((256, 1), F32)
     for k in range(8):
         v = held[k // 2, k % 2].astype(F32)
@@ -94,13 +87,13 @@
     return pl.pallas_call(
         norm_kernel,
         out_shape=jax.ShapeDtypeStruct((256, 2048), BF16),
-        in_specs=[SMEM, VMEM] + [ANY] * 4,
+        in_specs=[SMEM, VMEM, ANY],
         out_specs=VMEM,
-        scratch_shapes=[pltpu.VMEM((4, 2, 256, 256), BF16), pltpu.SemaphoreType.DMA((4,))],
+        scratch_shapes=[pltpu.VMEM((4, 2, 256, 256), BF16), pltpu.SemaphoreType.DMA((1,))],
         compiler_params=pltpu.CompilerParams(vmem_limit_bytes=8 << 20),
         cost_estimate=pl.CostEstimate(flops=1 << 24, bytes_accessed=2 << 20, transcendentals=0),
         name="normalise",
-    )(idx, gain, *blocks)
+    )(idx, gain, blocks)
 
 
 GROUPS = ((0, 512), (512, 768))
@@ -143,6 +136,7 @@
     gates[:, 0:1] = e0 / (e0 + e1)
     gates[:, 1:2] = e1 / (e0 + e1)
 
+    wanted = [jnp.broadcast_to(routes[:, j : j + 1], (512, H)) for j in range(2)]
     for r in range(5):
         if r == 0:
             for c in copies[2:18]:
@@ -157,8 +151,7 @@
         for j in range(2):
             value = jnp.zeros((512, H), F32) if r == 0 else sel[j]
             for e in range(2):
-                hit = routes[:, j : j + 1] == 2 * r + e
-                value = jnp.where(hit, acc[:, e * H : (e + 1) * H], value)
+                value = jnp.where(wanted[j] == 2 * r + e, acc[:, e * H : (e + 1) * H], value)
             if r < 3:
                 sel[j] = value
             else:
@@ -189,23 +182,25 @@
     )(idx, routes, router, *pin([own, other, *blocks]))
 
 
-def attend_kernel(idx, ends_s, ends_p, q0, q1, q2, q3, cache0, cache1, kv0, kv1, *refs):
-    outs = refs[:4]
-    q, keep, limits, top, tot, acc, sa, sb, chunk_of, tile_of, sem = refs[4:]
+def attend_kernel(count, idx, ends_s, ends_p, *refs):
+    queries, (cache0, cache1, kv0, kv1) = refs[:count], refs[count : count + 4]
+    outs = refs[count + 4 : 2 * count + 4]
+    q, keep, limits, top, tot, acc, sa, sb, chunk_of, tile_of, sem = refs[2 * count + 4 :]
+    tiles = 2 * count
     core = idx[0]
     copies = [
         pltpu.make_async_copy(r, q.at[pl.ds(1024 * b, 1024)], sem.at[b])
-        for b, r in enumerate((q0, q1, q2, q3))
+        for b, r in enumerate(queries)
     ]
     for i, r in enumerate((cache0, cache1)):
         for side in range(2):
             at = pl.multiple_of(i * 1536 + 768 * (core if side == 0 else 1 - core), 256)
             copies.append(
-                pltpu.make_async_copy(r.at[side], keep.at[pl.ds(at, 768)], sem.at[4 + 2 * i + side])
+                pltpu.make_async_copy(r.at[side], keep.at[pl.ds(at, 768)], sem.at[count + 2 * i + side])
             )
     for i, r in enumerate((kv0, kv1)):
         copies.append(
-            pltpu.make_async_copy(r, keep.at[pl.ds(3072 + 512 * i, 512)], sem.at[8 + i])
+            pltpu.make_async_copy(r, keep.at[pl.ds(3072 + 512 * i, 512)], sem.at[count + 4 + i])
         )
     for c in copies:
         c.start()
@@ -224,28 +219,28 @@
             own = jnp.where(later, se[k], own)
         return lo, hi, own
 
-    for t in range(TILES):
-        first = idx[1 + t // 2] + (t % 2) * 256
+    for t in range(tiles):
+        first = idx[5 + t // 2] + (t % 2) * 256
         token = first + lax.rem(lax.broadcasted_iota(jnp.int32, (1, R), 1), 256)
         lo, hi, own = allowed_of(token)
         limits[t, 0:1] = lo
         limits[t, 1:2] = hi
         limits[t, 2:3] = own
         limits[t, 3:4] = token + 1
-    limits[DUMMY] = jnp.zeros((4, R), jnp.int32)
+    limits[tiles] = jnp.zeros((4, R), jnp.int32)
     top[...] = jnp.full(top.shape, FLOOR, F32)
     tot[...] = jnp.zeros(tot.shape, F32)
     acc[...] = jnp.zeros(acc.shape, F32)
 
     def base_of(i):
-        slot = jnp.where(i < 3, idx[5] + i * CK, idx[6] + (i - 3) * CK)
-        return jnp.where(i < 6, slot, jnp.where(i == 6, idx[7], idx[8]))
+        slot = jnp.where(i < 3, idx[1] + i * CK, idx[2] + (i - 3) * CK)
+        return jnp.where(i < 6, slot, jnp.where(i == 6, idx[3], idx[4]))
 
     def collect(want_full, start):
         def visit(n, count):
-            i, t = n // TILES, lax.rem(n, TILES)
+            i, t = n // tiles, lax.rem(n, tiles)
             base = base_of(i)
-            first = idx[1 + t // 2] + lax.rem(t, 2) * 256
+            first = idx[5 + t // 2] + lax.rem(t, 2) * 256
             last = first + 255
             lo_a, hi_a, own_a = allowed_of(first)
             lo_b, hi_b, own_b = allowed_of(last)
@@ -263,18 +258,18 @@
 
             return count + hit.astype(jnp.int32)
 
-        count = lax.fori_loop(0, CHUNKS * TILES, visit, start)
+        count = lax.fori_loop(0, CHUNKS * tiles, visit, start)
         rounds = (count + UNROLL - 1) // UNROLL
         for k in range(UNROLL):
             chunk_of[count + k] = 0
-            tile_of[count + k] = DUMMY
+            tile_of[count + k] = tiles
         return rounds
 
     full_rounds = collect(True, 0)
     all_rounds = collect(False, full_rounds * UNROLL)
     for c in copies:
         c.wait()
-    q[4096:4608] = jnp.zeros((R, H), BF16)
+    q[tiles * R : (tiles + 1) * R] = jnp.zeros((R, H), BF16)
 
     def scores(n, out):
         keys = keep[pl.ds(pl.multiple_of(chunk_of[n] * CK, CK), CK), :H]
@@ -310,12 +305,12 @@
         return body
 
     chunk_of[all_rounds * UNROLL] = 0
-    tile_of[all_rounds * UNROLL] = DUMMY
+    tile_of[all_rounds * UNROLL] = tiles
     scores(0, sa)
     lax.fori_loop(0, full_rounds, rounds(False), 0)
     lax.fori_loop(full_rounds, all_rounds, rounds(True), 0)
 
-    for t in range(TILES):
+    for t in range(tiles):
         total = tot[t]
         safe = jnp.where(total > 0.0, total, 1.0)
         cols = slice((t % 2) * R, (t % 2 + 1) * R)
@@ -331,27 +326,28 @@
 
 
 def attend(idx, suffix_lengths, prefix_lengths, qs, caches, kvs):
+    count, tiles = len(qs), 2 * len(qs)
     return pl.pallas_call(
-        attend_kernel,
-        out_shape=tuple(jax.ShapeDtypeStruct((H + 16, 1024), BF16) for _ in range(4)),
-        in_specs=[SMEM] * 3 + [HBM] * 8,
-        out_specs=tuple([VMEM] * 4),
+        functools.partial(attend_kernel, count),
+        out_shape=tuple(jax.ShapeDtypeStruct((H + 16, 1024), BF16) for _ in range(count)),
+        in_specs=[SMEM] * 3 + [HBM] * (count + 4),
+        out_specs=tuple([VMEM] * count),
         scratch_shapes=[
-            pltpu.VMEM((9 * R, H), BF16),
+            pltpu.VMEM(((tiles + 1) * R, H), BF16),
             pltpu.VMEM((CHUNKS * CK, 2 * H), BF16),
-            pltpu.VMEM((TILES + 1, 4, R), jnp.int32),
-            pltpu.VMEM((TILES + 1, 1, R), F32),
-            pltpu.VMEM((TILES + 1, 1, R), F32),
-            pltpu.VMEM((TILES + 1, H, R), F32),
+            pltpu.VMEM((tiles + 1, 4, R), jnp.int32),
+            pltpu.VMEM((tiles + 1, 1, R), F32),
+            pltpu.VMEM((tiles + 1, 1, R), F32),
+            pltpu.VMEM((tiles + 1, H, R), F32),
             pltpu.VMEM((CK, R), F32),
             pltpu.VMEM((CK, R), F32),
-            pltpu.SMEM((CHUNKS * TILES + 4 * UNROLL,), jnp.int32),
-            pltpu.SMEM((CHUNKS * TILES + 4 * UNROLL,), jnp.int32),
-            pltpu.SemaphoreType.DMA((10,)),
+            pltpu.SMEM((CHUNKS * tiles + 4 * UNROLL,), jnp.int32),
+            pltpu.SMEM((CHUNKS * tiles + 4 * UNROLL,), jnp.int32),
+            pltpu.SemaphoreType.DMA((count + 6,)),
         ],
         compiler_params=pltpu.CompilerParams(vmem_limit_bytes=20 << 20),
         cost_estimate=pl.CostEstimate(
-            flops=12 << 30, bytes_accessed=6 << 20, transcendentals=10 << 20
+            flops=count * (3 << 30), bytes_accessed=4 << 20, transcendentals=count << 21
         ),
         name="attend",
     )(idx, suffix_lengths, prefix_lengths, *pin([*qs, *caches, *kvs]))
@@ -395,26 +391,22 @@
     ]
     for c in copies:
         c.start()
-    for side, source in enumerate((own, other)):
-        for half in range(2):
+    for half in range(2):
+        rows = slice(half * 256, (half + 1) * 256)
+        wanted = [jnp.broadcast_to(routes[rows, j : j + 1], (256, H)) for j in range(2)]
+        for side, source in enumerate((own, other)):
+            head = core if side == 0 else 1 - core
+            first = source[half * 512 : half * 512 + 256].astype(F32)
+            second = source[half * 512 + 256 : half * 512 + 512].astype(F32)
             for e in range(E):
-                value = jnp.zeros((256, H), F32)
-                for j in range(2):
-                    hit = routes[half * 256 : (half + 1) * 256, j : j + 1] == e
-                    at = (half * 2 + j) * 256
-                    value = jnp.where(hit, source[at : at + 256].astype(F32), value)
-                padded[side, half * 256 : (half + 1) * 256, e * H : (e + 1) * H] = value.astype(
-                    BF16
-                )
+                value = jnp.where(wanted[1] == e, second, 0.0)
+                value = jnp.where(wanted[0] == e, first, value).astype(BF16)
+                padded[rows, pl.ds(pl.multiple_of((head * E + e) * H, H), H)] = value
     for c in copies:
         c.wait()
     for k in range(0, 8, 2):
-        value = jnp.zeros((512, 256), F32)
-        for side in range(2):
-            head = core if side == 0 else 1 - core
-            rows = pl.ds(pl.multiple_of(head * 1024, 1024), 1024)
-            w = jnp.concatenate([held[k, rows], held[k + 1, rows]], axis=1)
-            value += jnp.dot(padded[side], w, preferred_element_type=F32)
+        w = jnp.concatenate([held[k], held[k + 1]], axis=1)
+        value = jnp.dot(padded[...], w, preferred_element_type=F32)
         for s in range(2):
             out[k + s] = value[:, s * H : (s + 1) * H].astype(BF16)
 
@@ -427,7 +419,7 @@
         out_specs=VMEM,
         scratch_shapes=[
             pltpu.VMEM((8, 2048, H), BF16),
-            pltpu.VMEM((2, 512, 1024), BF16),
+            pltpu.VMEM((512, 2048), BF16),
             pltpu.SemaphoreType.DMA((8,)),
         ],
         compiler_params=pltpu.CompilerParams(vmem_limit_bytes=20 << 20),
@@ -477,14 +469,15 @@
     pair = jnp.stack([tokens, across_far(tokens)])
     far, ym, yp, a = along_y(w, 2), along_y(w, 3), along_y(w, 1), across_x(w)
     caches = [cache, across_x(cache)]
-    far, ym, yp, a, pair, caches = lax.optimization_barrier((far, ym, yp, a, pair, caches))
-    blocks = [pair] + [along_z(pair, k) for k in (1, 2, 3)]
+    copies = jnp.broadcast_to(pair[None], (4,) + pair.shape)
+    far, ym, yp, a, copies, caches = lax.optimization_barrier((far, ym, yp, a, copies, caches))
+    blocks = lax.all_to_all(copies, "z", 0, 0, tiled=True)
     am, ap, afar = along_y(a, 3), along_y(a, 1), across_x(far)
     blocks, am, ap, afar = lax.optimization_barrier((blocks, am, ap, afar))
     gathered = [w, a, ym, am, far, afar, yp, ap]
 
-    z, xh = (lax.axis_index(a) for a in NARROW)
-    token_src = [lax.rem(z + 4 - dz, 4) * 2 + (xh ^ s) for dz in range(4) for s in range(2)]
+    xh = lax.axis_index("xh")
+    token_src = [k * 2 + (xh ^ s) for k in range(4) for s in range(2)]
     places = [lax.rem(lax.rem(v, 4) + 4 - y, 4) * 2 + (v // 4 ^ xl) for v in token_src]
     normed = normalise(table(token_src + places), norm_gain.reshape(8, 1, 256), blocks)
     out_early, am, ap = lax.optimization_barrier((out_weight, am, ap))
@@ -501,8 +494,10 @@
 
     firsts = [(xl * 4 + lax.rem(y + 4 - k, 4)) * 512 for k in range(4)]
     mine, partner = xl * 4 + y, (1 - xl) * 4 + y
-    at = [c] + firsts + [mine * 1536, partner * 1536, mine * 512, partner * 512]
-    parts = list(attend(table(at), suffix_lengths, prefix_lengths, qs, caches, kvs))
+    at = [c, mine * 1536, partner * 1536, mine * 512, partner * 512]
+    lengths = (suffix_lengths, prefix_lengths)
+    parts = list(attend(table(at + firsts[:1]), *lengths, qs[:1], caches, kvs))
+    parts += list(attend(table(at + firsts[1:]), *lengths, qs[1:], caches, kvs))
     parts[1:], o_far, o_am, o_ap = lax.optimization_barrier((parts[1:], o_far, o_am, o_ap))
     for k in range(1, 4):
         parts[k] = along_y(parts[k], 4 - k)

time: 175 us -> 174 us (level)
  starting transfers between devices: 39.2 us -> 34.9 us
  Pallas kernels: 32.8 us -> 34.6 us
    ppermute x3 -> x0, waiting for transfers between devices: 10.5 us -> none  [along_z(): return lax.ppermute(x, 'z', [(i, (i + k) % 4) for i in range(4)])]
    ppermute x16, waiting for transfers between devices: 58.4 us -> 67.6 us  [along_y(): return lax.ppermute(x, 'y', [(i, (i + k) % 4) for i in range(4)])]
    all_to_all x0 -> x1, starting transfers between devices: none -> 5.03 us  [on_device(): blocks = lax.all_to_all(copies, 'z', 0, 0, tiled=True)]
    ppermute x3 -> x0, starting transfers between devices: 4.97 us -> none  [along_z(): return lax.ppermute(x, 'z', [(i, (i + k) % 4) for i in range(4)])]
    pallas_call x1 -> x2, Pallas kernels: 16.4 us -> 19.9 us  [attend(): pl.pallas_call(functools.partial(attend_kernel, count), out_shape=tuple((...]
    ppermute x6, starting transfers between devices: 9.41 us -> 6.65 us  [across_core(): return lax.ppermute(x, 'c', [(0, 1), (1, 0)])]
    unnamed x56 -> x58, local copies, waits for them, and re-layouts: 3.43 us -> 3.6 us
  transfers between devices with their start and end apart: 32 -> 30, of which waited for: 19 -> 16; matrix products, arithmetic and copies ran while one was open for 1% -> 1% of each run, Pallas kernels for 14% -> 16%
where the time goes in v8:
time: 174 us; the launch traced here: 171 us
  waiting for transfers between devices  73.3 us (42%)
  starting transfers between devices  34.9 us (20%)
  Pallas kernels  34.6 us (20%)
  blocking collectives  20.4 us (12%)
  local copies, waits for them, and re-layouts  6.84 us (4%)
    ppermute x16, waiting for transfers between devices, along_y(): return lax.ppermute(x, 'y', [(i, (i + k) % 4) for i in range(4)])  67.6 us
    all_to_all x1, blocking collectives, on_device(): sums = lax.all_to_all(sums, NARROW, 0, 0, tiled=True)  20.4 us
    pallas_call x2, Pallas kernels, attend(): pl.pallas_call(functools.partial(attend_kernel, count), out_shape=tuple((...  19.9 us
    ppermute x16, starting transfers between devices, along_y(): return lax.ppermute(x, 'y', [(i, (i + k) % 4) for i in range(4)])  17.9 us
    pallas_call x1, Pallas kernels, project(): pl.pallas_call(project_kernel, out_shape=(jax.ShapeDtypeStruct((1024, H),...  7.37 us
    ppermute x6, starting transfers between devices, across_core(): return lax.ppermute(x, 'c', [(0, 1), (1, 0)])  6.65 us
    pallas_call x1, Pallas kernels, project_out(): pl.pallas_call(out_kernel, out_shape=jax.ShapeDtypeStruct((8, 512, H), BF...  5.72 us
    all_to_all x1, starting transfers between devices, on_device(): blocks = lax.all_to_all(copies, 'z', 0, 0, tiled=True)  5.03 us
  transfers between devices with their start and end apart: 30, of which 16 were waited for; matrix products, arithmetic and copies ran while one was open for 1% of the time, Pallas kernels for 16%

profile of v8, /device:TPU:3, one launch (start us, length us, event | category | flops | bytes accessed | tf_op | source)
XLA Modules:
  0.0 171.5 jit_solution(35275293277493045)
XLA Ops:
  0.0 1.2 dynamic-slice_bitcast_fusion
  2.2 1.9 %collective-permute-start.6 = (bf16[256,256]{1,0:T(8,128)(2,1)S(1)}, bf16[256,256]{1,0:T(8,128)(2,1)S(1)}, u32[]{:S(2)}, u32[]{:S(2)}) collective-permute-start(bf16[256,256]{1,0:T(8,128)(2,1)S(1)} %copy-done.10), channel_id=1, source_target_pairs={{0,1},{1,0},{2,3},{3,2},{4,5},{5,4},{6,7},{7,6},{8,9},{9,8},{10,11... | collective-permute-start | bytes 393224 | tf_op jit(solution)/shard_map/ppermute | solution.py:43
  4.3 1.2 collective-permute-start.8
  5.6 3.0 %collective-permute-start.2 = (bf16[2,1280,128]{2,1,0:T(8,128)(2,1)S(1)}, bf16[2,1280,128]{2,1,0:T(8,128)(2,1)S(1)}, u32[]{:S(2)}, u32[]{:S(2)}) collective-permute-start(bf16[2,1280,128]{2,1,0:T(8,128)(2,1)S(1)} %pad_maximum_fusion.1.refs_0_), channel_id=1, source_target_pairs={{0,32},{16,48},{32,0},{48,16},{1,33},{17,49},{33,1},{49,17},{2,34}... | collective-permute-start | bytes 1966088 | tf_op jit(solution)/shard_map/ppermute | solution.py:35
  10.4 11.9 %collective-permute-done.2.refs_4_ = bf16[2,1280,128]{2,1,0:T(8,128)(2,1)S(1)} collective-permute-done((bf16[2,1280,128]{2,1,0:T(8,128)(2,1)S(1)}, bf16[2,1280,128]{2,1,0:T(8,128)(2,1)S(1)}, u32[]{:S(2)}, u32[]{:S(2)}) %collective-permute-start.2) | collective-permute-done | bytes 655392 | tf_op jit(solution)/shard_map/ppermute | solution.py:35
  22.3 14.9 %collective-permute-done.3.refs_2_ = bf16[2,1280,128]{2,1,0:T(8,128)(2,1)S(1)} collective-permute-done((bf16[2,1280,128]{2,1,0:T(8,128)(2,1)S(1)}, bf16[2,1280,128]{2,1,0:T(8,128)(2,1)S(1)}, u32[]{:S(2)}, u32[]{:S(2)}) %collective-permute-start.3) | collective-permute-done | bytes 655392 | tf_op jit(solution)/shard_map/ppermute | solution.py:35
  37.9 1.5 collective-permute-done.5.refs_1_
  39.4 1.2 broadcast_in_dim.2
  40.7 5.0 %all-to-all-start = ((bf16[4,2,256,256]{3,2,1,0:T(8,128)(2,1)}), bf16[4,2,256,256]{3,2,1,0:T(8,128)(2,1)S(1)}, u32[]{:S(2)}, u32[]{:S(2)}) async-start(bf16[4,2,256,256]{3,2,1,0:T(8,128)(2,1)} %broadcast_in_dim.2), calls=%async_computation | async-start | bytes 2097152 | tf_op jit(solution)/shard_map/all_to_all | solution.py:474
  45.7 1.3 collective-permute-start.10
  47.3 1.4 collective-permute-start.9
  48.9 12.9 %collective-permute-done.10.refs_7_ = bf16[2,1280,128]{2,1,0:T(8,128)(2,1)S(1)} collective-permute-done((bf16[2,1280,128]{2,1,0:T(8,128)(2,1)}, bf16[2,1280,128]{2,1,0:T(8,128)(2,1)S(1)}, u32[]{:S(2)}, u32[]{:S(2)}) %collective-permute-start.10) | collective-permute-done | bytes 655392 | tf_op jit(solution)/shard_map/ppermute | solution.py:35
  62.6 1.3 normalise.1.own
  63.9 2.6 %collective-permute-start.12 = (bf16[256,2048]{1,0:T(8,128)(2,1)S(1)}, bf16[256,2048]{1,0:T(8,128)(2,1)S(1)}, u32[]{:S(2)}, u32[]{:S(2)}) collective-permute-start(bf16[256,2048]{1,0:T(8,128)(2,1)S(1)} %normalise.1.own), channel_id=1, source_target_pairs={{0,8},{8,0},{1,9},{9,1},{2,10},{10,2},{3,11},{11,3},{4,12},{12,4},... | collective-permute-start | bytes 3145736 | tf_op jit(solution)/shard_map/ppermute | solution.py:47
  66.8 2.1 %collective-permute-done = s32[256,2]{0,1:T(2,128)S(1)} collective-permute-done((s32[256,2]{0,1:T(2,128)S(1)}, s32[256,2]{0,1:T(2,128)S(1)}, u32[]{:S(2)}, u32[]{:S(2)}) %collective-permute-start) | collective-permute-done | bytes 2080 | tf_op jit(solution)/shard_map/ppermute | solution.py:47
  70.1 2.6 %collective-permute-start.13 = (bf16[2048,128]{1,0:T(8,128)(2,1)}, bf16[2048,128]{1,0:T(8,128)(2,1)S(1)}, u32[]{:S(2)}, u32[]{:S(2)}) collective-permute-start(bf16[2048,128]{1,0:T(8,128)(2,1)} %refs_0_.1), channel_id=1, source_target_pairs={{0,48},{16,0},{32,16},{48,32},{1,49},{17,1},{33,17},{49,33},{2,50}... | collective-permute-start | bytes 1572872 | tf_op jit(solution)/shard_map/ppermute | solution.py:35
  73.7 7.4 %project.1 = (bf16[1024,128]{1,0:T(8,128)(2,1)S(1)}, bf16[512,256]{1,0:T(8,128)(2,1)S(1)}, f32[512,2]{1,0:T(8,128)S(1)}) custom-call(s32[9]{0:T(128)S(1)} %stack.163.idx, s32[512,2]{1,0:T(8,128)S(1)} %broadcast_select_fusion.routes, bf16[8,2048]{1,0:T(8,128)(2,1)S(1)} %bitcast.45, bf16[256,2048]{1,0:T(8,128)(2,1)} %copy-done, bf16[256,2048]{1,0:T(8,128)(2,1)} %copy-done.13, ...), custom_call_target="tpu_custom_call" | custom-call | flops 6442450944 | bytes 8388608 | tf_op jit(solution)/shard_map/project/pallas_call | solution.py:164
  81.6 2.0 %collective-permute-done.13.refs_2_ = bf16[2048,128]{1,0:T(8,128)(2,1)S(1)} collective-permute-done((bf16[2048,128]{1,0:T(8,128)(2,1)}, bf16[2048,128]{1,0:T(8,128)(2,1)S(1)}, u32[]{:S(2)}, u32[]{:S(2)}) %collective-permute-start.13) | collective-permute-done | bytes 524320 | tf_op jit(solution)/shard_map/ppermute | solution.py:35
  83.6 2.2 %collective-permute-start.18 = (bf16[1024,128]{1,0:T(8,128)(2,1)S(1)}, bf16[1024,128]{1,0:T(8,128)(2,1)S(1)}, u32[]{:S(2)}, u32[]{:S(2)}) collective-permute-start(bf16[1024,128]{1,0:T(8,128)(2,1)S(1)} %get-tuple-element.51.refs_0_), channel_id=1, source_target_pairs={{0,32},{16,48},{32,0},{48,16},{1,33},{17,49},{33,1},{49,17},{2,34}... | collective-permute-start | bytes 786440 | tf_op jit(solution)/shard_map/ppermute | solution.py:35
  88.9 1.6 collective-permute-start.21
  90.6 3.2 %collective-permute-done.17.refs_0_ = bf16[1024,128]{1,0:T(8,128)(2,1)S(1)} collective-permute-done((bf16[1024,128]{1,0:T(8,128)(2,1)S(1)}, bf16[1024,128]{1,0:T(8,128)(2,1)S(1)}, u32[]{:S(2)}, u32[]{:S(2)}) %collective-permute-start.17) | collective-permute-done | bytes 262176 | tf_op jit(solution)/shard_map/ppermute | solution.py:35
  93.8 2.5 %collective-permute-done.18.refs_1_ = bf16[1024,128]{1,0:T(8,128)(2,1)S(1)} collective-permute-done((bf16[1024,128]{1,0:T(8,128)(2,1)S(1)}, bf16[1024,128]{1,0:T(8,128)(2,1)S(1)}, u32[]{:S(2)}, u32[]{:S(2)}) %collective-permute-start.18) | collective-permute-done | bytes 262176 | tf_op jit(solution)/shard_map/ppermute | solution.py:35
  96.3 2.6 %collective-permute-done.19.refs_2_ = bf16[1024,128]{1,0:T(8,128)(2,1)S(1)} collective-permute-done((bf16[1024,128]{1,0:T(8,128)(2,1)S(1)}, bf16[1024,128]{1,0:T(8,128)(2,1)S(1)}, u32[]{:S(2)}, u32[]{:S(2)}) %collective-permute-start.19) | collective-permute-done | bytes 262176 | tf_op jit(solution)/shard_map/ppermute | solution.py:35
  99.7 12.8 %attend.3 = (bf16[144,1024]{1,0:T(8,128)(2,1)S(1)}, bf16[144,1024]{1,0:T(8,128)(2,1)S(1)}, bf16[144,1024]{1,0:T(8,128)(2,1)S(1)}) custom-call(s32[8]{0:T(128)S(1)} %stack.199.idx, s32[4]{0:T(128)S(1)} %copy-done.4, s32[4]{0:T(128)S(1)} %copy-done.5, bf16[1024,128]{1,0:T(8,128)(2,1)} %copy-done.26, bf16[1024,128]{1,0:T(8,128)(2,1)} %copy-done.27, ...), custom_call_target="tpu_custom_call" | custom-call | flops 9663676416 | bytes 4194304 | tf_op jit(solution)/shard_map/attend/pallas_call | solution.py:330
  112.4 6.4 %collective-permute-done.20.refs_4_ = bf16[2048,128]{1,0:T(8,128)(2,1)S(1)} collective-permute-done((bf16[2048,128]{1,0:T(8,128)(2,1)}, bf16[2048,128]{1,0:T(8,128)(2,1)S(1)}, u32[]{:S(2)}, u32[]{:S(2)}) %collective-permute-start.20) | collective-permute-done | bytes 524320 | tf_op jit(solution)/shard_map/ppermute | solution.py:35
  118.8 1.9 %collective-permute-done.22.refs_7_ = bf16[2048,128]{1,0:T(8,128)(2,1)S(1)} collective-permute-done((bf16[2048,128]{1,0:T(8,128)(2,1)}, bf16[2048,128]{1,0:T(8,128)(2,1)S(1)}, u32[]{:S(2)}, u32[]{:S(2)}) %collective-permute-start.22) | collective-permute-done | bytes 524320 | tf_op jit(solution)/shard_map/ppermute | solution.py:35
  120.7 2.3 %collective-permute-start.23 = (bf16[144,1024]{1,0:T(8,128)(2,1)S(1)}, bf16[144,1024]{1,0:T(8,128)(2,1)S(1)}, u32[]{:S(2)}, u32[]{:S(2)}) collective-permute-start(bf16[144,1024]{1,0:T(8,128)(2,1)S(1)} %get-tuple-element.61), channel_id=1, source_target_pairs={{0,48},{16,0},{32,16},{48,32},{1,49},{17,1},{33,17},{49,33},{2,50}... | collective-permute-start | bytes 884744 | tf_op jit(solution)/shard_map/ppermute | solution.py:35
  123.9 7.2 %attend.2.p0 = bf16[144,1024]{1,0:T(8,128)(2,1)S(1)} custom-call(s32[6]{0:T(128)S(1)} %stack.195.idx, s32[4]{0:T(128)S(1)} %copy-done.4, s32[4]{0:T(128)S(1)} %copy-done.5, bf16[1024,128]{1,0:T(8,128)(2,1)} %copy-done.1, bf16[2,768,256]{2,1,0:T(8,128)(2,1)} %copy-done.6, bf16[2,768,256]{2,1,0:T(8,128)(2,1)} %copy-done.14, bf16[512,256]{1,0:T(8,128)(2,1)} %copy-done.2, ...), custom_call_target="tpu_custom_call" | custom-call | flops 3221225472 | bytes 4194304 | tf_op jit(solution)/shard_map/attend/pallas_call | solution.py:330
  131.2 7.9 %collective-permute-done.25.p3 = bf16[144,1024]{1,0:T(8,128)(2,1)S(1)} collective-permute-done((bf16[144,1024]{1,0:T(8,128)(2,1)S(1)}, bf16[144,1024]{1,0:T(8,128)(2,1)S(1)}, u32[]{:S(2)}, u32[]{:S(2)}) %collective-permute-start.25) | collective-permute-done | bytes 294944 | tf_op jit(solution)/shard_map/ppermute | solution.py:35
  141.7 5.7 %project_out.1 = bf16[8,512,128]{2,1,0:T(8,128)(2,1)S(1)} custom-call(s32[9]{0:T(128)S(1)} %stack.163.idx, s32[512,2]{1,0:T(8,128)S(1)} %broadcast_select_fusion.routes, bf16[1024,128]{1,0:T(8,128)(2,1)S(1)} %combine.1.own, bf16[1024,128]{1,0:T(8,128)(2,1)S(1)} %collective-permute-done.26.other, bf16[2048,128]{1,0:T(8,128)(2,1)} %refs_0_.1, ...), custom_call_target="tpu_custom_call" | custom-call | flops 4294967296 | bytes 6291456 | tf_op jit(solution)/shard_map/project_out/pallas_call | solution.py:415
  147.5 20.4 %all_to_all.10 = bf16[8,512,128]{2,1,0:T(8,128)(2,1)S(1)} all-to-all(bf16[8,512,128]{2,1,0:T(8,128)(2,1)S(1)} %project_out.1), channel_id=1, replica_groups=mesh['xl'=2,'y'=4,'c'=2,'z'=4,'xh'=2] {'z','xh'}, dimensions={0} | all-to-all | bytes 2097152 | tf_op jit(solution)/shard_map/all_to_all | solution.py:511
  168.0 1.9 %collective-permute-start.28 = (bf16[256,128]{1,0:T(8,128)(2,1)S(1)}, bf16[256,128]{1,0:T(8,128)(2,1)S(1)}, u32[]{:S(2)}, u32[]{:S(2)}) collective-permute-start(bf16[256,128]{1,0:T(8,128)(2,1)S(1)} %get-tuple-element.74), channel_id=1, source_target_pairs={{0,8},{8,0},{1,9},{9,1},{2,10},{10,2},{3,11},{11,3},{4,12},{12,4},... | collective-permute-start | bytes 196616 | tf_op jit(solution)/shard_map/ppermute | solution.py:47
  (116 shorter events, 17.3 us)
Async XLA Ops:
  1.3 2.9 %collective-permute-start.7 = (bf16[768,256]{1,0:T(8,128)(2,1)S(1)}, bf16[768,256]{1,0:T(8,128)(2,1)S(1)}, u32[]{:S(2)}, u32[]{:S(2)}) collective-permute-start(bf16[768,256]{1,0:T(8,128)(2,1)S(1)} %get-tuple-element.70), channel_id=1, source_target_pairs={{0,8},{8,0},{1,9},{9,1},{2,10},{10,2},{3,11},{11,3},{4,12},{12,4},... | collective-permute-start | bytes 1179656 | tf_op jit(solution)/shard_map/ppermute | solution.py:47
  2.1 3.4 %collective-permute-start.1 = (bf16[1280,128]{1,0:T(8,128)(2,1)S(1)}, bf16[1280,128]{1,0:T(8,128)(2,1)S(1)}, u32[]{:S(2)}, u32[]{:S(2)}) collective-permute-start(bf16[1280,128]{1,0:T(8,128)(2,1)S(1)} %pad_maximum_fusion.2), channel_id=1, source_target_pairs={{0,8},{8,0},{1,9},{9,1},{2,10},{10,2},{3,11},{11,3},{4,12},{12,4},... | collective-permute-start | bytes 983048 | tf_op jit(solution)/shard_map/ppermute | solution.py:47
  2.2 7.8 %collective-permute-start.6 = (bf16[256,256]{1,0:T(8,128)(2,1)S(1)}, bf16[256,256]{1,0:T(8,128)(2,1)S(1)}, u32[]{:S(2)}, u32[]{:S(2)}) collective-permute-start(bf16[256,256]{1,0:T(8,128)(2,1)S(1)} %copy-done.10), channel_id=1, source_target_pairs={{0,1},{1,0},{2,3},{3,2},{4,5},{5,4},{6,7},{7,6},{8,9},{9,8},{10,11... | collective-permute-start | bytes 393224 | tf_op jit(solution)/shard_map/ppermute | solution.py:43
  4.3 36.3 %copy-start.6 = (bf16[2,768,256]{2,1,0:T(8,128)(2,1)}, bf16[2,768,256]{2,1,0:T(8,128)(2,1)S(1)}, u32[]{:S(2)}) copy-start(bf16[2,768,256]{2,1,0:T(8,128)(2,1)S(1)} %pad_maximum_fusion.refs_1_.refs_3_) | copy-start | bytes 2359300
  4.3 35.1 %collective-permute-start.8 = (bf16[2,768,256]{2,1,0:T(8,128)(2,1)S(1)}, bf16[2,768,256]{2,1,0:T(8,128)(2,1)S(1)}, u32[]{:S(2)}, u32[]{:S(2)}) collective-permute-start(bf16[2,768,256]{2,1,0:T(8,128)(2,1)S(1)} %pad_maximum_fusion.refs_1_.refs_3_), channel_id=1, source_target_pairs={{0,64},{64,0},{1,65},{65,1},{2,66},{66,2},{3,67},{67,3},{4,68},{68... | collective-permute-start | bytes 2359304 | tf_op jit(solution)/shard_map/ppermute | solution.py:39
  5.6 16.7 %collective-permute-start.2 = (bf16[2,1280,128]{2,1,0:T(8,128)(2,1)S(1)}, bf16[2,1280,128]{2,1,0:T(8,128)(2,1)S(1)}, u32[]{:S(2)}, u32[]{:S(2)}) collective-permute-start(bf16[2,1280,128]{2,1,0:T(8,128)(2,1)S(1)} %pad_maximum_fusion.1.refs_0_), channel_id=1, source_target_pairs={{0,32},{16,48},{32,0},{48,16},{1,33},{17,49},{33,1},{49,17},{2,34}... | collective-permute-start | bytes 1966088 | tf_op jit(solution)/shard_map/ppermute | solution.py:35
  8.6 28.6 %collective-permute-start.3 = (bf16[2,1280,128]{2,1,0:T(8,128)(2,1)S(1)}, bf16[2,1280,128]{2,1,0:T(8,128)(2,1)S(1)}, u32[]{:S(2)}, u32[]{:S(2)}) collective-permute-start(bf16[2,1280,128]{2,1,0:T(8,128)(2,1)S(1)} %pad_maximum_fusion.1.refs_0_), channel_id=1, source_target_pairs={{0,48},{16,0},{32,16},{48,32},{1,49},{17,1},{33,17},{49,33},{2,50}... | collective-permute-start | bytes 1966088 | tf_op jit(solution)/shard_map/ppermute | solution.py:35
  9.4 28.5 %collective-permute-start.4 = (bf16[2,1280,128]{2,1,0:T(8,128)(2,1)S(1)}, bf16[2,1280,128]{2,1,0:T(8,128)(2,1)S(1)}, u32[]{:S(2)}, u32[]{:S(2)}) collective-permute-start(bf16[2,1280,128]{2,1,0:T(8,128)(2,1)S(1)} %pad_maximum_fusion.1.refs_0_), channel_id=1, source_target_pairs={{0,16},{16,32},{32,48},{48,0},{1,17},{17,33},{33,49},{49,1},{2,18}... | collective-permute-start | bytes 1966088 | tf_op jit(solution)/shard_map/ppermute | solution.py:35
  10.1 29.3 %collective-permute-start.5 = (bf16[2,1280,128]{2,1,0:T(8,128)(2,1)S(1)}, bf16[2,1280,128]{2,1,0:T(8,128)(2,1)}, u32[]{:S(2)}, u32[]{:S(2)}) collective-permute-start(bf16[2,1280,128]{2,1,0:T(8,128)(2,1)S(1)} %pad_maximum_fusion.1.refs_0_), channel_id=1, source_target_pairs={{0,64},{64,0},{1,65},{65,1},{2,66},{66,2},{3,67},{67,3},{4,68},{68... | collective-permute-start | bytes 1966088 | tf_op jit(solution)/shard_map/ppermute | solution.py:39
  22.3 40.3 %copy-start.15 = (bf16[2,1280,128]{2,1,0:T(8,128)(2,1)}, bf16[2,1280,128]{2,1,0:T(8,128)(2,1)S(1)}, u32[]{:S(2)}) copy-start(bf16[2,1280,128]{2,1,0:T(8,128)(2,1)S(1)} %collective-permute-done.2.refs_4_) | copy-start | bytes 1966084
  40.7 22.0 %all-to-all-start = ((bf16[4,2,256,256]{3,2,1,0:T(8,128)(2,1)}), bf16[4,2,256,256]{3,2,1,0:T(8,128)(2,1)S(1)}, u32[]{:S(2)}, u32[]{:S(2)}) async-start(bf16[4,2,256,256]{3,2,1,0:T(8,128)(2,1)} %broadcast_in_dim.2), calls=%async_computation | async-start | bytes 2097152 | tf_op jit(solution)/shard_map/all_to_all | solution.py:474
  45.7 16.1 %collective-permute-start.10 = (bf16[2,1280,128]{2,1,0:T(8,128)(2,1)}, bf16[2,1280,128]{2,1,0:T(8,128)(2,1)S(1)}, u32[]{:S(2)}, u32[]{:S(2)}) collective-permute-start(bf16[2,1280,128]{2,1,0:T(8,128)(2,1)} %collective-permute-done.5.refs_1_), channel_id=1, source_target_pairs={{0,16},{16,32},{32,48},{48,0},{1,17},{17,33},{33,49},{49,1},{2,18}... | collective-permute-start | bytes 1966088 | tf_op jit(solution)/shard_map/ppermute | solution.py:35
  47.0 14.8 %collective-permute-start.11 = (bf16[2,1280,128]{2,1,0:T(8,128)(2,1)S(1)}, bf16[2,1280,128]{2,1,0:T(8,128)(2,1)}, u32[]{:S(2)}, u32[]{:S(2)}) collective-permute-start(bf16[2,1280,128]{2,1,0:T(8,128)(2,1)S(1)} %collective-permute-done.2.refs_4_), channel_id=1, source_target_pairs={{0,64},{64,0},{1,65},{65,1},{2,66},{66,2},{3,67},{67,3},{4,68},{68... | collective-permute-start | bytes 1966088 | tf_op jit(solution)/shard_map/ppermute | solution.py:39
  47.3 14.5 %collective-permute-start.9 = (bf16[2,1280,128]{2,1,0:T(8,128)(2,1)}, bf16[2,1280,128]{2,1,0:T(8,128)(2,1)}, u32[]{:S(2)}, u32[]{:S(2)}) collective-permute-start(bf16[2,1280,128]{2,1,0:T(8,128)(2,1)} %collective-permute-done.5.refs_1_), channel_id=1, source_target_pairs={{0,48},{16,0},{32,16},{48,32},{1,49},{17,1},{33,17},{49,33},{2,50}... | collective-permute-start | bytes 1966088 | tf_op jit(solution)/shard_map/ppermute | solution.py:35
  63.9 8.8 %collective-permute-start.12 = (bf16[256,2048]{1,0:T(8,128)(2,1)S(1)}, bf16[256,2048]{1,0:T(8,128)(2,1)S(1)}, u32[]{:S(2)}, u32[]{:S(2)}) collective-permute-start(bf16[256,2048]{1,0:T(8,128)(2,1)S(1)} %normalise.1.own), channel_id=1, source_target_pairs={{0,8},{8,0},{1,9},{9,1},{2,10},{10,2},{3,11},{11,3},{4,12},{12,4},... | collective-permute-start | bytes 3145736 | tf_op jit(solution)/shard_map/ppermute | solution.py:47
  66.6 2.3 %collective-permute-start = (s32[256,2]{0,1:T(2,128)S(1)}, s32[256,2]{0,1:T(2,128)S(1)}, u32[]{:S(2)}, u32[]{:S(2)}) collective-permute-start(s32[256,2]{0,1:T(2,128)S(1)} %copy-done.12), channel_id=1, source_target_pairs={{0,8},{8,0},{1,9},{9,1},{2,10},{10,2},{3,11},{11,3},{4,12},{12,4},... | collective-permute-start | bytes 6152 | tf_op jit(solution)/shard_map/ppermute | solution.py:47
  69.2 19.7 %collective-permute-start.15 = (bf16[2048,128]{1,0:T(8,128)(2,1)}, bf16[2048,128]{1,0:T(8,128)(2,1)}, u32[]{:S(2)}, u32[]{:S(2)}) collective-permute-start(bf16[2048,128]{1,0:T(8,128)(2,1)} %refs_0_.1), channel_id=1, source_target_pairs={{0,64},{64,0},{1,65},{65,1},{2,66},{66,2},{3,67},{67,3},{4,68},{68... | collective-permute-start | bytes 1572872 | tf_op jit(solution)/shard_map/ppermute | solution.py:39
  70.1 13.6 %collective-permute-start.13 = (bf16[2048,128]{1,0:T(8,128)(2,1)}, bf16[2048,128]{1,0:T(8,128)(2,1)S(1)}, u32[]{:S(2)}, u32[]{:S(2)}) collective-permute-start(bf16[2048,128]{1,0:T(8,128)(2,1)} %refs_0_.1), channel_id=1, source_target_pairs={{0,48},{16,0},{32,16},{48,32},{1,49},{17,1},{33,17},{49,33},{2,50}... | collective-permute-start | bytes 1572872 | tf_op jit(solution)/shard_map/ppermute | solution.py:35
  72.7 13.9 %collective-permute-start.14 = (bf16[2048,128]{1,0:T(8,128)(2,1)}, bf16[2048,128]{1,0:T(8,128)(2,1)S(1)}, u32[]{:S(2)}, u32[]{:S(2)}) collective-permute-start(bf16[2048,128]{1,0:T(8,128)(2,1)} %refs_0_.1), channel_id=1, source_target_pairs={{0,16},{16,32},{32,48},{48,0},{1,17},{17,33},{33,49},{49,1},{2,18}... | collective-permute-start | bytes 1572872 | tf_op jit(solution)/shard_map/ppermute | solution.py:35
  81.1 7.8 %collective-permute-start.16 = (bf16[512,256]{1,0:T(8,128)(2,1)S(1)}, bf16[512,256]{1,0:T(8,128)(2,1)S(1)}, u32[]{:S(2)}, u32[]{:S(2)}) collective-permute-start(bf16[512,256]{1,0:T(8,128)(2,1)S(1)} %get-tuple-element.54.refs_3_.refs_5_), channel_id=1, source_target_pairs={{0,64},{64,0},{1,65},{65,1},{2,66},{66,2},{3,67},{67,3},{4,68},{68... | collective-permute-start | bytes 786440 | tf_op jit(solution)/shard_map/ppermute | solution.py:39
  81.5 12.3 %collective-permute-start.17 = (bf16[1024,128]{1,0:T(8,128)(2,1)S(1)}, bf16[1024,128]{1,0:T(8,128)(2,1)S(1)}, u32[]{:S(2)}, u32[]{:S(2)}) collective-permute-start(bf16[1024,128]{1,0:T(8,128)(2,1)S(1)} %get-tuple-element.51.refs_0_), channel_id=1, source_target_pairs={{0,16},{16,32},{32,48},{48,0},{1,17},{17,33},{33,49},{49,1},{2,18}... | collective-permute-start | bytes 786440 | tf_op jit(solution)/shard_map/ppermute | solution.py:35
  83.6 12.7 %collective-permute-start.18 = (bf16[1024,128]{1,0:T(8,128)(2,1)S(1)}, bf16[1024,128]{1,0:T(8,128)(2,1)S(1)}, u32[]{:S(2)}, u32[]{:S(2)}) collective-permute-start(bf16[1024,128]{1,0:T(8,128)(2,1)S(1)} %get-tuple-element.51.refs_0_), channel_id=1, source_target_pairs={{0,32},{16,48},{32,0},{48,16},{1,33},{17,49},{33,1},{49,17},{2,34}... | collective-permute-start | bytes 786440 | tf_op jit(solution)/shard_map/ppermute | solution.py:35
  87.4 11.5 %collective-permute-start.19 = (bf16[1024,128]{1,0:T(8,128)(2,1)S(1)}, bf16[1024,128]{1,0:T(8,128)(2,1)S(1)}, u32[]{:S(2)}, u32[]{:S(2)}) collective-permute-start(bf16[1024,128]{1,0:T(8,128)(2,1)S(1)} %get-tuple-element.51.refs_0_), channel_id=1, source_target_pairs={{0,48},{16,0},{32,16},{48,32},{1,49},{17,1},{33,17},{49,33},{2,50}... | collective-permute-start | bytes 786440 | tf_op jit(solution)/shard_map/ppermute | solution.py:35
  88.9 29.9 %collective-permute-start.21 = (bf16[2048,128]{1,0:T(8,128)(2,1)}, bf16[2048,128]{1,0:T(8,128)(2,1)S(1)}, u32[]{:S(2)}, u32[]{:S(2)}) collective-permute-start(bf16[2048,128]{1,0:T(8,128)(2,1)} %collective-permute-done.15.refs_1_), channel_id=1, source_target_pairs={{0,48},{16,0},{32,16},{48,32},{1,49},{17,1},{33,17},{49,33},{2,50}... | collective-permute-start | bytes 1572872 | tf_op jit(solution)/shard_map/ppermute | solution.py:35
  90.5 30.2 %collective-permute-start.22 = (bf16[2048,128]{1,0:T(8,128)(2,1)}, bf16[2048,128]{1,0:T(8,128)(2,1)S(1)}, u32[]{:S(2)}, u32[]{:S(2)}) collective-permute-start(bf16[2048,128]{1,0:T(8,128)(2,1)} %collective-permute-done.15.refs_1_), channel_id=1, source_target_pairs={{0,16},{16,32},{32,48},{48,0},{1,17},{17,33},{33,49},{49,1},{2,18}... | collective-permute-start | bytes 1572872 | tf_op jit(solution)/shard_map/ppermute | solution.py:35
  93.8 25.0 %collective-permute-start.20 = (bf16[2048,128]{1,0:T(8,128)(2,1)}, bf16[2048,128]{1,0:T(8,128)(2,1)S(1)}, u32[]{:S(2)}, u32[]{:S(2)}) collective-permute-start(bf16[2048,128]{1,0:T(8,128)(2,1)} %refs_0_.1), channel_id=1, source_target_pairs={{0,32},{16,48},{32,0},{48,16},{1,33},{17,49},{33,1},{49,17},{2,34}... | collective-permute-start | bytes 1572872 | tf_op jit(solution)/shard_map/ppermute | solution.py:35
  120.7 10.4 %collective-permute-start.23 = (bf16[144,1024]{1,0:T(8,128)(2,1)S(1)}, bf16[144,1024]{1,0:T(8,128)(2,1)S(1)}, u32[]{:S(2)}, u32[]{:S(2)}) collective-permute-start(bf16[144,1024]{1,0:T(8,128)(2,1)S(1)} %get-tuple-element.61), channel_id=1, source_target_pairs={{0,48},{16,0},{32,16},{48,32},{1,49},{17,1},{33,17},{49,33},{2,50}... | collective-permute-start | bytes 884744 | tf_op jit(solution)/shard_map/ppermute | solution.py:35
  123.0 8.2 %collective-permute-start.24 = (bf16[144,1024]{1,0:T(8,128)(2,1)S(1)}, bf16[144,1024]{1,0:T(8,128)(2,1)S(1)}, u32[]{:S(2)}, u32[]{:S(2)}) collective-permute-start(bf16[144,1024]{1,0:T(8,128)(2,1)S(1)} %get-tuple-element.62), channel_id=1, source_target_pairs={{0,32},{16,48},{32,0},{48,16},{1,33},{17,49},{33,1},{49,17},{2,34}... | collective-permute-start | bytes 884744 | tf_op jit(solution)/shard_map/ppermute | solution.py:35
  123.0 16.1 %collective-permute-start.25 = (bf16[144,1024]{1,0:T(8,128)(2,1)S(1)}, bf16[144,1024]{1,0:T(8,128)(2,1)S(1)}, u32[]{:S(2)}, u32[]{:S(2)}) collective-permute-start(bf16[144,1024]{1,0:T(8,128)(2,1)S(1)} %get-tuple-element.63), channel_id=1, source_target_pairs={{0,16},{16,32},{32,48},{48,0},{1,17},{17,33},{33,49},{49,1},{2,18}... | collective-permute-start | bytes 884744 | tf_op jit(solution)/shard_map/ppermute | solution.py:35
  123.6 16.9 %collective-permute-start.27 = (bf16[2048,128]{1,0:T(8,128)(2,1)S(1)}, bf16[2048,128]{1,0:T(8,128)(2,1)S(1)}, u32[]{:S(2)}, u32[]{:S(2)}) collective-permute-start(bf16[2048,128]{1,0:T(8,128)(2,1)S(1)} %collective-permute-done.20.refs_4_), channel_id=1, source_target_pairs={{0,64},{64,0},{1,65},{65,1},{2,66},{66,2},{3,67},{67,3},{4,68},{68... | collective-permute-start | bytes 1572872 | tf_op jit(solution)/shard_map/ppermute | solution.py:39
  139.4 2.3 %collective-permute-start.26 = (bf16[1024,128]{1,0:T(8,128)(2,1)S(1)}, bf16[1024,128]{1,0:T(8,128)(2,1)S(1)}, u32[]{:S(2)}, u32[]{:S(2)}) collective-permute-start(bf16[1024,128]{1,0:T(8,128)(2,1)S(1)} %combine.1.own), channel_id=1, source_target_pairs={{0,8},{8,0},{1,9},{9,1},{2,10},{10,2},{3,11},{11,3},{4,12},{12,4},... | collective-permute-start | bytes 786440 | tf_op jit(solution)/shard_map/ppermute | solution.py:47
  168.0 2.8 %collective-permute-start.28 = (bf16[256,128]{1,0:T(8,128)(2,1)S(1)}, bf16[256,128]{1,0:T(8,128)(2,1)S(1)}, u32[]{:S(2)}, u32[]{:S(2)}) collective-permute-start(bf16[256,128]{1,0:T(8,128)(2,1)S(1)} %get-tuple-element.74), channel_id=1, source_target_pairs={{0,8},{8,0},{1,9},{9,1},{2,10},{10,2},{3,11},{11,3},{4,12},{12,4},... | collective-permute-start | bytes 196616 | tf_op jit(solution)/shard_map/ppermute | solution.py:47
  (27 other events, 219.6 us)

commit v9 on v8

--- a/solution.py
+++ b/solution.py
@@ -71,15 +71,15 @@
         c.wait()
 
 
-def norm_kernel(idx, gain, blocks, normed, held, sem):
-    run([pltpu.make_async_copy(blocks, held, sem.at[0])])
+def norm_kernel(idx, gain, b0, b1, normed, held, sem):
+    run([pltpu.make_async_copy(r, held.at[i], sem.at[i]) for i, r in enumerate((b0, b1))])
     total = jnp.zeros((256, 1), F32)
     for k in range(8):
-        v = held[k // 2, k % 2].astype(F32)
+        v = held[k // 4, k % 4].astype(F32)
         total = total + jnp.sum(v * v, axis=1, keepdims=True)
     scale = lax.rsqrt(total * (1.0 / 2048) + EPS)
     for k in range(8):
-        v = held[k // 2, k % 2].astype(F32) * scale * gain[idx[k]].astype(F32)
+        v = held[k // 4, k % 4].astype(F32) * scale * gain[idx[k]].astype(F32)
         normed[:, pl.ds(pl.multiple_of(idx[8 + k] * 256, 256), 256)] = v.astype(BF16)
 
 
@@ -87,13 +87,13 @@
     return pl.pallas_call(
         norm_kernel,
         out_shape=jax.ShapeDtypeStruct((256, 2048), BF16),
-        in_specs=[SMEM, VMEM, ANY],
+        in_specs=[SMEM, VMEM, ANY, ANY],
         out_specs=VMEM,
-        scratch_shapes=[pltpu.VMEM((4, 2, 256, 256), BF16), pltpu.SemaphoreType.DMA((1,))],
+        scratch_shapes=[pltpu.VMEM((2, 4, 256, 256), BF16), pltpu.SemaphoreType.DMA((2,))],
         compiler_params=pltpu.CompilerParams(vmem_limit_bytes=8 << 20),
         cost_estimate=pl.CostEstimate(flops=1 << 24, bytes_accessed=2 << 20, transcendentals=0),
         name="normalise",
-    )(idx, gain, blocks)
+    )(idx, gain, *blocks)
 
 
 GROUPS = ((0, 512), (512, 768))
@@ -383,12 +383,15 @@
 
 
 def out_kernel(idx, routes, own, other, *refs):
-    blocks = refs[:8]
-    out, held, padded, sem = refs[8:]
+    blocks = refs[:10]
+    out, held, padded, sem = refs[10:]
     core = idx[8]
-    copies = [
-        pltpu.make_async_copy(r, held.at[idx[k]], sem.at[k]) for k, r in enumerate(blocks)
-    ]
+    copies = []
+    for k, slot in enumerate((0, 1, 2, 3, 6, 7)):
+        copies.append(pltpu.make_async_copy(blocks[k], held.at[idx[slot]], sem.at[k]))
+    for k in range(6, 10):
+        target = held.at[idx[4 + (k - 6) // 2], pl.ds((k % 2) * 1024, 1024)]
+        copies.append(pltpu.make_async_copy(blocks[k], target, sem.at[k]))
     for c in copies:
         c.start()
     for half in range(2):
@@ -415,12 +418,12 @@
     return pl.pallas_call(
         out_kernel,
         out_shape=jax.ShapeDtypeStruct((8, 512, H), BF16),
-        in_specs=[SMEM, VMEM, VMEM, VMEM] + [HBM] * 8,
+        in_specs=[SMEM, VMEM, VMEM, VMEM] + [HBM] * 10,
         out_specs=VMEM,
         scratch_shapes=[
             pltpu.VMEM((8, 2048, H), BF16),
             pltpu.VMEM((512, 2048), BF16),
-            pltpu.SemaphoreType.DMA((8,)),
+            pltpu.SemaphoreType.DMA((10,)),
         ],
         compiler_params=pltpu.CompilerParams(vmem_limit_bytes=20 << 20),
         cost_estimate=pl.CostEstimate(flops=4 << 30, bytes_accessed=6 << 20, transcendentals=0),
@@ -466,31 +469,33 @@
         return lax.dynamic_slice_in_dim(prefix_cache, h * 2 * H, 2 * H, 1)
 
     cache = jnp.stack([cache_of(c), across_core(cache_of(1 - c))])
-    pair = jnp.stack([tokens, across_far(tokens)])
+    half_row = across_far(tokens)
     far, ym, yp, a = along_y(w, 2), along_y(w, 3), along_y(w, 1), across_x(w)
     caches = [cache, across_x(cache)]
-    copies = jnp.broadcast_to(pair[None], (4,) + pair.shape)
-    far, ym, yp, a, copies, caches = lax.optimization_barrier((far, ym, yp, a, copies, caches))
-    blocks = lax.all_to_all(copies, "z", 0, 0, tiled=True)
-    am, ap, afar = along_y(a, 3), along_y(a, 1), across_x(far)
-    blocks, am, ap, afar = lax.optimization_barrier((blocks, am, ap, afar))
-    gathered = [w, a, ym, am, far, afar, yp, ap]
-
+    blocks = [lax.all_gather(v, "z", axis=0) for v in (tokens, half_row)]
     xh = lax.axis_index("xh")
-    token_src = [k * 2 + (xh ^ s) for k in range(4) for s in range(2)]
+    token_src = [k * 2 + (xh ^ s) for s in range(2) for k in range(4)]
     places = [lax.rem(lax.rem(v, 4) + 4 - y, 4) * 2 + (v // 4 ^ xl) for v in token_src]
     normed = normalise(table(token_src + places), norm_gain.reshape(8, 1, 256), blocks)
+    far, ym, yp, a, normed, caches, both_routes = lax.optimization_barrier(
+        (far, ym, yp, a, normed, caches, both_routes)
+    )
+    am, ap, afar = along_y(a, 3), along_y(a, 1), across_x(far)
+    other_normed = across_core(normed)
+    gathered = [w, a, ym, am, far, afar, yp, ap]
+
     out_early, am, ap = lax.optimization_barrier((out_weight, am, ap))
     gathered[3], gathered[7] = am, ap
     o_ym, o_yp, o_a = along_y(out_early, 3), along_y(out_early, 1), across_x(out_early)
     q, kv, gates = project(
-        table(chips + [c]), both_routes, router.T, normed, across_core(normed), gathered
+        table(chips + [c]), both_routes, router.T, normed, other_normed, gathered
     )
     kvs = [kv, across_x(kv)]
     qs = [q] + [along_y(q, k) for k in (1, 2, 3)]
     qs[0], o_ym, o_yp = lax.optimization_barrier((q, o_ym, o_yp))
-    out_late, o_a_late, kvs[1] = lax.optimization_barrier((out_weight, o_a, kvs[1]))
-    o_far, o_am, o_ap = along_y(out_late, 2), along_y(o_a_late, 3), along_y(o_a_late, 1)
+    o_a_late, up, down, kvs[1] = lax.optimization_barrier((o_a, o_yp[:1024], o_ym[1024:], kvs[1]))
+    far0, far1 = along_y(up, 1), along_y(down, 3)
+    o_am, o_ap = along_y(o_a_late, 3), along_y(o_a_late, 1)
 
     firsts = [(xl * 4 + lax.rem(y + 4 - k, 4)) * 512 for k in range(4)]
     mine, partner = xl * 4 + y, (1 - xl) * 4 + y
@@ -498,10 +503,13 @@
     lengths = (suffix_lengths, prefix_lengths)
     parts = list(attend(table(at + firsts[:1]), *lengths, qs[:1], caches, kvs))
     parts += list(attend(table(at + firsts[1:]), *lengths, qs[1:], caches, kvs))
-    parts[1:], o_far, o_am, o_ap = lax.optimization_barrier((parts[1:], o_far, o_am, o_ap))
+    parts[1:], far0, far1, o_am, o_ap = lax.optimization_barrier(
+        (parts[1:], far0, far1, o_am, o_ap)
+    )
     for k in range(1, 4):
         parts[k] = along_y(parts[k], 4 - k)
-    out_blocks = [out_weight, o_a, o_ym, o_am, o_far, across_x(o_far), o_yp, o_ap]
+    out_blocks = [out_weight, o_a, o_ym, o_am, o_yp, o_ap]
+    out_blocks += [far0, far1, across_x(far0), across_x(far1)]
     gate_row = gates.reshape(2, 256, 2).transpose(0, 2, 1).reshape(1, 1024)
     attended = combine(gate_row, parts)
 

time: 174 us -> 162 us (0.931)
  waiting for transfers between devices: 73.3 us -> 47.9 us
  blocking collectives: 20.4 us -> 41.6 us
  Pallas kernels: 34.6 us -> 27 us
  starting transfers between devices: 34.9 us -> 38.4 us
  local copies, waits for them, and re-layouts: 6.84 us -> 3.71 us
    ppermute x16 -> x17, waiting for transfers between devices: 67.6 us -> 39.1 us  [along_y(): return lax.ppermute(x, 'y', [(i, (i + k) % 4) for i in range(4)])]
    all_gather x0 -> x2, blocking collectives: none -> 23.6 us  [on_device(): blocks = [lax.all_gather(v, 'z', axis=0) for v in (tokens, half_row)]]
    pallas_call x2, Pallas kernels: 19.9 us -> 12.3 us  [attend(): pl.pallas_call(functools.partial(attend_kernel, count), out_shape=tuple((...]
    ppermute x6 -> x7, starting transfers between devices: 3.41 us -> 9.58 us  [across_x(): return lax.ppermute(x, 'xl', [(0, 1), (1, 0)])]
    ppermute x6 -> x7, waiting for transfers between devices: 1.49 us -> 7.4 us  [across_x(): return lax.ppermute(x, 'xl', [(0, 1), (1, 0)])]
    all_to_all x1 -> x0, starting transfers between devices: 5.03 us -> none  [on_device(): blocks = lax.all_to_all(copies, 'z', 0, 0, tiled=True)]
    ppermute x6, waiting for transfers between devices: 4.17 us -> 1.41 us  [across_core(): return lax.ppermute(x, 'c', [(0, 1), (1, 0)])]
    ppermute x6, starting transfers between devices: 6.65 us -> 9.29 us  [across_core(): return lax.ppermute(x, 'c', [(0, 1), (1, 0)])]
  transfers between devices with their start and end apart: 30 -> 31, of which waited for: 16 -> 17; matrix products, arithmetic and copies ran while one was open for 1% -> 2% of each run, Pallas kernels for 16% -> 13%
where the time goes in v9:
time: 162 us; the launch traced here: 161 us
  waiting for transfers between devices  47.9 us (30%)
  blocking collectives  41.6 us (26%)
  starting transfers between devices  38.4 us (24%)
  Pallas kernels  27 us (17%)
  local copies, waits for them, and re-layouts  3.71 us (2%)
  other arithmetic  1.9 us (1%)
    ppermute x17, waiting for transfers between devices, along_y(): return lax.ppermute(x, 'y', [(i, (i + k) % 4) for i in range(4)])  39.1 us
    all_gather x2, blocking collectives, on_device(): blocks = [lax.all_gather(v, 'z', axis=0) for v in (tokens, half_row)]  23.6 us
    all_to_all x1, blocking collectives, on_device(): sums = lax.all_to_all(sums, NARROW, 0, 0, tiled=True)  18 us
    ppermute x17, starting transfers between devices, along_y(): return lax.ppermute(x, 'y', [(i, (i + k) % 4) for i in range(4)])  17.7 us
    pallas_call x2, Pallas kernels, attend(): pl.pallas_call(functools.partial(attend_kernel, count), out_shape=tuple((...  12.3 us
    ppermute x7, starting transfers between devices, across_x(): return lax.ppermute(x, 'xl', [(0, 1), (1, 0)])  9.58 us
    ppermute x6, starting transfers between devices, across_core(): return lax.ppermute(x, 'c', [(0, 1), (1, 0)])  9.29 us
    ppermute x7, waiting for transfers between devices, across_x(): return lax.ppermute(x, 'xl', [(0, 1), (1, 0)])  7.4 us
  transfers between devices with their start and end apart: 31, of which 17 were waited for; matrix products, arithmetic and copies ran while one was open for 2% of the time, Pallas kernels for 13%

profile of v9, /device:TPU:3, one launch (start us, length us, event | category | flops | bytes accessed | tf_op | source)
XLA Modules:
  0.0 161.0 jit_solution(15041882875560683112)
XLA Ops:
  0.0 1.8 %collective-permute-start.5 = (bf16[256,256]{1,0:T(8,128)(2,1)}, bf16[256,256]{1,0:T(8,128)(2,1)S(1)}, u32[]{:S(2)}, u32[]{:S(2)}) collective-permute-start(bf16[256,256]{1,0:T(8,128)(2,1)} %param.10), channel_id=1, source_target_pairs={{0,1},{1,0},{2,3},{3,2},{4,5},{5,4},{6,7},{7,6},{8,9},{9,8},{10,11... | collective-permute-start | bytes 393224 | tf_op jit(solution)/shard_map/ppermute | solution.py:43
  1.9 1.2 dynamic-slice_bitcast_fusion
  5.5 1.2 collective-permute-start.7
  7.7 2.9 %collective-permute-start.1 = (bf16[2,1280,128]{2,1,0:T(8,128)(2,1)}, bf16[2,1280,128]{2,1,0:T(8,128)(2,1)}, u32[]{:S(2)}, u32[]{:S(2)}) collective-permute-start(bf16[2,1280,128]{2,1,0:T(8,128)(2,1)} %pad_maximum_fusion.1.refs_0_), channel_id=1, source_target_pairs={{0,32},{16,48},{32,0},{48,16},{1,33},{17,49},{33,1},{49,17},{2,34}... | collective-permute-start | bytes 1966088 | tf_op jit(solution)/shard_map/ppermute | solution.py:35
  12.4 12.5 %all-gather = bf16[1024,256]{1,0:T(8,128)(2,1)S(1)} all-gather(bf16[256,256]{1,0:T(8,128)(2,1)S(1)} %copy-done.8), channel_id=2, replica_groups=mesh['xl'=2,'y'=4,'c'=2,'z'=4,'xh'=2] {'z'}, dimensions={0}, use_global_device_ids=true | all-gather | bytes 655360 | tf_op jit(solution)/shard_map/all_gather | solution.py:475
  25.2 11.1 %all-gather.1 = bf16[1024,256]{1,0:T(8,128)(2,1)S(1)} all-gather(bf16[256,256]{1,0:T(8,128)(2,1)S(1)} %collective-permute-done.5), channel_id=3, replica_groups=mesh['xl'=2,'y'=4,'c'=2,'z'=4,'xh'=2] {'z'}, dimensions={0}, use_global_device_ids=true | all-gather | bytes 655360 | tf_op jit(solution)/shard_map/all_gather | solution.py:475
  36.3 1.3 normalise.1.own
  37.7 1.9 %collective-permute-done.2.refs_2_ = bf16[2,1280,128]{2,1,0:T(8,128)(2,1)} collective-permute-done((bf16[2,1280,128]{2,1,0:T(8,128)(2,1)}, bf16[2,1280,128]{2,1,0:T(8,128)(2,1)}, u32[]{:S(2)}, u32[]{:S(2)}) %collective-permute-start.2) | collective-permute-done | bytes 655392 | tf_op jit(solution)/shard_map/ppermute | solution.py:35
  40.2 3.1 %collective-permute-start.9 = (bf16[256,2048]{1,0:T(8,128)(2,1)S(1)}, bf16[256,2048]{1,0:T(8,128)(2,1)}, u32[]{:S(2)}, u32[]{:S(2)}) collective-permute-start(bf16[256,2048]{1,0:T(8,128)(2,1)S(1)} %normalise.1.own), channel_id=1, source_target_pairs={{0,8},{8,0},{1,9},{9,1},{2,10},{10,2},{3,11},{11,3},{4,12},{12,4},... | collective-permute-start | bytes 3145736 | tf_op jit(solution)/shard_map/ppermute | solution.py:47
  43.3 2.0 %collective-permute-start.10 = (bf16[2,1280,128]{2,1,0:T(8,128)(2,1)}, bf16[2,1280,128]{2,1,0:T(8,128)(2,1)S(1)}, u32[]{:S(2)}, u32[]{:S(2)}) collective-permute-start(bf16[2,1280,128]{2,1,0:T(8,128)(2,1)} %collective-permute-done.4.refs_1_), channel_id=1, source_target_pairs={{0,48},{16,0},{32,16},{48,32},{1,49},{17,1},{33,17},{49,33},{2,50}... | collective-permute-start | bytes 1966088 | tf_op jit(solution)/shard_map/ppermute | solution.py:35
  45.3 1.2 collective-permute-start.12
  46.5 13.4 %collective-permute-done.10.refs_3_ = bf16[2,1280,128]{2,1,0:T(8,128)(2,1)S(1)} collective-permute-done((bf16[2,1280,128]{2,1,0:T(8,128)(2,1)}, bf16[2,1280,128]{2,1,0:T(8,128)(2,1)S(1)}, u32[]{:S(2)}, u32[]{:S(2)}) %collective-permute-start.10) | collective-permute-done | bytes 655392 | tf_op jit(solution)/shard_map/ppermute | solution.py:35
  60.8 2.0 %collective-permute-done.11.refs_7_ = bf16[2,1280,128]{2,1,0:T(8,128)(2,1)} collective-permute-done((bf16[2,1280,128]{2,1,0:T(8,128)(2,1)}, bf16[2,1280,128]{2,1,0:T(8,128)(2,1)}, u32[]{:S(2)}, u32[]{:S(2)}) %collective-permute-start.11) | collective-permute-done | bytes 655392 | tf_op jit(solution)/shard_map/ppermute | solution.py:35
  65.4 7.4 %project.1 = (bf16[1024,128]{1,0:T(8,128)(2,1)S(1)}, bf16[512,256]{1,0:T(8,128)(2,1)S(1)}, f32[512,2]{1,0:T(8,128)S(1)}) custom-call(s32[9]{0:T(128)S(1)} %stack.154.idx, s32[512,2]{1,0:T(8,128)S(1)} %broadcast_select_fusion.routes, bf16[8,2048]{1,0:T(8,128)(2,1)S(1)} %bitcast.47, bf16[256,2048]{1,0:T(8,128)(2,1)} %copy-done, ...), custom_call_target="tpu_custom_call" | custom-call | flops 6442450944 | bytes 8388608 | tf_op jit(solution)/shard_map/project/pallas_call | solution.py:164
  73.3 2.1 %collective-permute-done.13.refs_2_ = bf16[2048,128]{1,0:T(8,128)(2,1)S(1)} collective-permute-done((bf16[2048,128]{1,0:T(8,128)(2,1)}, bf16[2048,128]{1,0:T(8,128)(2,1)S(1)}, u32[]{:S(2)}, u32[]{:S(2)}) %collective-permute-start.13) | collective-permute-done | bytes 524320 | tf_op jit(solution)/shard_map/ppermute | solution.py:35
  75.3 1.5 collective-permute-start.18
  78.3 3.4 %collective-permute-done.16.refs_4_.refs_6_ = bf16[512,256]{1,0:T(8,128)(2,1)S(1)} collective-permute-done((bf16[512,256]{1,0:T(8,128)(2,1)S(1)}, bf16[512,256]{1,0:T(8,128)(2,1)S(1)}, u32[]{:S(2)}, u32[]{:S(2)}) %collective-permute-start.16) | collective-permute-done | bytes 262176 | tf_op jit(solution)/shard_map/ppermute | solution.py:39
  81.8 2.6 %collective-permute-start.22 = (bf16[2048,128]{1,0:T(8,128)(2,1)}, bf16[2048,128]{1,0:T(8,128)(2,1)S(1)}, u32[]{:S(2)}, u32[]{:S(2)}) collective-permute-start(bf16[2048,128]{1,0:T(8,128)(2,1)} %collective-permute-done.15.refs_1_), channel_id=1, source_target_pairs={{0,48},{16,0},{32,16},{48,32},{1,49},{17,1},{33,17},{49,33},{2,50}... | collective-permute-start | bytes 1572872 | tf_op jit(solution)/shard_map/ppermute | solution.py:35
  85.3 1.4 collective-permute-done.18.refs_1_
  86.7 1.3 collective-permute-start.21
  88.0 1.4 collective-permute-done.19.refs_2_
  89.4 7.7 %attend.3 = (bf16[144,1024]{1,0:T(8,128)(2,1)S(1)}, bf16[144,1024]{1,0:T(8,128)(2,1)S(1)}, bf16[144,1024]{1,0:T(8,128)(2,1)S(1)}) custom-call(s32[8]{0:T(128)S(1)} %stack.187.idx, s32[4]{0:T(128)S(1)} %copy-done.4, s32[4]{0:T(128)S(1)} %copy-done.5, bf16[1024,128]{1,0:T(8,128)(2,1)} %copy-done.18, bf16[1024,128]{1,0:T(8,128)(2,1)} %copy-done.19, ...), custom_call_target="tpu_custom_call" | custom-call | flops 9663676416 | bytes 4194304 | tf_op jit(solution)/shard_map/attend/pallas_call | solution.py:330
  97.1 9.0 %collective-permute-done.20.refs_6_ = bf16[1024,128]{1,0:T(8,128)(2,1)S(1)} collective-permute-done((bf16[1024,128]{1,0:T(8,128)(2,1)S(1)}, bf16[1024,128]{1,0:T(8,128)(2,1)S(1)}, u32[]{:S(2)}, u32[]{:S(2)}) %collective-permute-start.20) | collective-permute-done | bytes 262176 | tf_op jit(solution)/shard_map/ppermute | solution.py:35
  106.3 3.5 %collective-permute-start.24 = (bf16[144,1024]{1,0:T(8,128)(2,1)S(1)}, bf16[144,1024]{1,0:T(8,128)(2,1)S(1)}, u32[]{:S(2)}, u32[]{:S(2)}) collective-permute-start(bf16[144,1024]{1,0:T(8,128)(2,1)S(1)} %get-tuple-element.60), channel_id=1, source_target_pairs={{0,48},{16,0},{32,16},{48,32},{1,49},{17,1},{33,17},{49,33},{2,50}... | collective-permute-start | bytes 884744 | tf_op jit(solution)/shard_map/ppermute | solution.py:35
  110.4 4.6 %attend.2.p0 = bf16[144,1024]{1,0:T(8,128)(2,1)S(1)} custom-call(s32[6]{0:T(128)S(1)} %stack.183.idx, s32[4]{0:T(128)S(1)} %copy-done.4, s32[4]{0:T(128)S(1)} %copy-done.5, bf16[1024,128]{1,0:T(8,128)(2,1)} %copy-done.1, bf16[2,768,256]{2,1,0:T(8,128)(2,1)} %copy-done.6, bf16[2,768,256]{2,1,0:T(8,128)(2,1)} %collective-permute-done.7.refs_2_.refs_4_, ...), custom_call_target="tpu_custom_call" | custom-call | flops 3221225472 | bytes 4194304 | tf_op jit(solution)/shard_map/attend/pallas_call | solution.py:330
  115.0 5.2 %collective-permute-start.28 = (bf16[1024,128]{1,0:T(8,128)(2,1)S(1)}, bf16[1024,128]{1,0:T(8,128)(2,1)S(1)}, u32[]{:S(2)}, u32[]{:S(2)}) collective-permute-start(bf16[1024,128]{1,0:T(8,128)(2,1)S(1)} %collective-permute-done.20.refs_6_), channel_id=1, source_target_pairs={{0,64},{64,0},{1,65},{65,1},{2,66},{66,2},{3,67},{67,3},{4,68},{68... | collective-permute-start | bytes 786440 | tf_op jit(solution)/shard_map/ppermute | solution.py:39
  120.4 1.2 collective-permute-done.24.p1
  121.6 4.3 %collective-permute-done.26.p3 = bf16[144,1024]{1,0:T(8,128)(2,1)S(1)} collective-permute-done((bf16[144,1024]{1,0:T(8,128)(2,1)S(1)}, bf16[144,1024]{1,0:T(8,128)(2,1)S(1)}, u32[]{:S(2)}, u32[]{:S(2)}) %collective-permute-start.26) | collective-permute-done | bytes 294944 | tf_op jit(solution)/shard_map/ppermute | solution.py:35
  127.3 3.9 %collective-permute-done.29.refs_9_ = bf16[1024,128]{1,0:T(8,128)(2,1)S(1)} collective-permute-done((bf16[1024,128]{1,0:T(8,128)(2,1)S(1)}, bf16[1024,128]{1,0:T(8,128)(2,1)S(1)}, u32[]{:S(2)}, u32[]{:S(2)}) %collective-permute-start.29) | collective-permute-done | bytes 262176 | tf_op jit(solution)/shard_map/ppermute | solution.py:39
  132.0 5.7 %project_out.1 = bf16[8,512,128]{2,1,0:T(8,128)(2,1)S(1)} custom-call(s32[9]{0:T(128)S(1)} %stack.154.idx, s32[512,2]{1,0:T(8,128)S(1)} %broadcast_select_fusion.routes, bf16[1024,128]{1,0:T(8,128)(2,1)S(1)} %combine.1.own, bf16[1024,128]{1,0:T(8,128)(2,1)S(1)} %collective-permute-done.27.other, bf16[2048,128]{1,0:T(8,128)(2,1)} %refs_0_.1, ...), custom_call_target="tpu_custom_call" | custom-call | flops 4294967296 | bytes 6291456 | tf_op jit(solution)/shard_map/project_out/pallas_call | solution.py:418
  137.7 18.0 %all_to_all.5 = bf16[8,512,128]{2,1,0:T(8,128)(2,1)S(1)} all-to-all(bf16[8,512,128]{2,1,0:T(8,128)(2,1)S(1)} %project_out.1), channel_id=1, replica_groups=mesh['xl'=2,'y'=4,'c'=2,'z'=4,'xh'=2] {'z','xh'}, dimensions={0} | all-to-all | bytes 2097152 | tf_op jit(solution)/shard_map/all_to_all | solution.py:519
  155.9 3.4 %collective-permute-start.30 = (bf16[256,128]{1,0:T(8,128)(2,1)S(1)}, bf16[256,128]{1,0:T(8,128)(2,1)S(1)}, u32[]{:S(2)}, u32[]{:S(2)}) collective-permute-start(bf16[256,128]{1,0:T(8,128)(2,1)S(1)} %get-tuple-element.72), channel_id=1, source_target_pairs={{0,8},{8,0},{1,9},{9,1},{2,10},{10,2},{3,11},{11,3},{4,12},{12,4},... | collective-permute-start | bytes 196616 | tf_op jit(solution)/shard_map/ppermute | solution.py:47
  (110 shorter events, 17.4 us)
Async XLA Ops:
  0.0 12.0 %collective-permute-start.5 = (bf16[256,256]{1,0:T(8,128)(2,1)}, bf16[256,256]{1,0:T(8,128)(2,1)S(1)}, u32[]{:S(2)}, u32[]{:S(2)}) collective-permute-start(bf16[256,256]{1,0:T(8,128)(2,1)} %param.10), channel_id=1, source_target_pairs={{0,1},{1,0},{2,3},{3,2},{4,5},{5,4},{6,7},{7,6},{8,9},{9,8},{10,11... | collective-permute-start | bytes 393224 | tf_op jit(solution)/shard_map/ppermute | solution.py:43
  3.0 2.4 %collective-permute-start.6 = (bf16[768,256]{1,0:T(8,128)(2,1)S(1)}, bf16[768,256]{1,0:T(8,128)(2,1)S(1)}, u32[]{:S(2)}, u32[]{:S(2)}) collective-permute-start(bf16[768,256]{1,0:T(8,128)(2,1)S(1)} %get-tuple-element.68), channel_id=1, source_target_pairs={{0,8},{8,0},{1,9},{9,1},{2,10},{10,2},{3,11},{11,3},{4,12},{12,4},... | collective-permute-start | bytes 1179656 | tf_op jit(solution)/shard_map/ppermute | solution.py:47
  4.2 2.6 %collective-permute-start = (bf16[1280,128]{1,0:T(8,128)(2,1)S(1)}, bf16[1280,128]{1,0:T(8,128)(2,1)S(1)}, u32[]{:S(2)}, u32[]{:S(2)}) collective-permute-start(bf16[1280,128]{1,0:T(8,128)(2,1)S(1)} %pad_maximum_fusion.2), channel_id=1, source_target_pairs={{0,8},{8,0},{1,9},{9,1},{2,10},{10,2},{3,11},{11,3},{4,12},{12,4},... | collective-permute-start | bytes 983048 | tf_op jit(solution)/shard_map/ppermute | solution.py:47
  4.3 7.0 %collective-permute-start.8 = (s32[256,2]{0,1:T(2,128)S(1)}, s32[256,2]{0,1:T(2,128)S(1)}, u32[]{:S(2)}, u32[]{:S(2)}) collective-permute-start(s32[256,2]{0,1:T(2,128)S(1)} %copy-done.13), channel_id=1, source_target_pairs={{0,8},{8,0},{1,9},{9,1},{2,10},{10,2},{3,11},{11,3},{4,12},{12,4},... | collective-permute-start | bytes 6152 | tf_op jit(solution)/shard_map/ppermute | solution.py:47
  5.5 34.7 %collective-permute-start.7 = (bf16[2,768,256]{2,1,0:T(8,128)(2,1)S(1)}, bf16[2,768,256]{2,1,0:T(8,128)(2,1)}, u32[]{:S(2)}, u32[]{:S(2)}) collective-permute-start(bf16[2,768,256]{2,1,0:T(8,128)(2,1)S(1)} %pad_maximum_fusion.refs_1_.refs_3_), channel_id=1, source_target_pairs={{0,64},{64,0},{1,65},{65,1},{2,66},{66,2},{3,67},{67,3},{4,68},{68... | collective-permute-start | bytes 2359304 | tf_op jit(solution)/shard_map/ppermute | solution.py:39
  7.7 30.0 %collective-permute-start.1 = (bf16[2,1280,128]{2,1,0:T(8,128)(2,1)}, bf16[2,1280,128]{2,1,0:T(8,128)(2,1)}, u32[]{:S(2)}, u32[]{:S(2)}) collective-permute-start(bf16[2,1280,128]{2,1,0:T(8,128)(2,1)} %pad_maximum_fusion.1.refs_0_), channel_id=1, source_target_pairs={{0,32},{16,48},{32,0},{48,16},{1,33},{17,49},{33,1},{49,17},{2,34}... | collective-permute-start | bytes 1966088 | tf_op jit(solution)/shard_map/ppermute | solution.py:35
  10.6 29.0 %collective-permute-start.2 = (bf16[2,1280,128]{2,1,0:T(8,128)(2,1)}, bf16[2,1280,128]{2,1,0:T(8,128)(2,1)}, u32[]{:S(2)}, u32[]{:S(2)}) collective-permute-start(bf16[2,1280,128]{2,1,0:T(8,128)(2,1)} %pad_maximum_fusion.1.refs_0_), channel_id=1, source_target_pairs={{0,48},{16,0},{32,16},{48,32},{1,49},{17,1},{33,17},{49,33},{2,50}... | collective-permute-start | bytes 1966088 | tf_op jit(solution)/shard_map/ppermute | solution.py:35
  11.4 28.8 %collective-permute-start.3 = (bf16[2,1280,128]{2,1,0:T(8,128)(2,1)}, bf16[2,1280,128]{2,1,0:T(8,128)(2,1)}, u32[]{:S(2)}, u32[]{:S(2)}) collective-permute-start(bf16[2,1280,128]{2,1,0:T(8,128)(2,1)} %pad_maximum_fusion.1.refs_0_), channel_id=1, source_target_pairs={{0,16},{16,32},{32,48},{48,0},{1,17},{17,33},{33,49},{49,1},{2,18}... | collective-permute-start | bytes 1966088 | tf_op jit(solution)/shard_map/ppermute | solution.py:35
  12.1 28.1 %collective-permute-start.4 = (bf16[2,1280,128]{2,1,0:T(8,128)(2,1)}, bf16[2,1280,128]{2,1,0:T(8,128)(2,1)}, u32[]{:S(2)}, u32[]{:S(2)}) collective-permute-start(bf16[2,1280,128]{2,1,0:T(8,128)(2,1)} %pad_maximum_fusion.1.refs_0_), channel_id=1, source_target_pairs={{0,64},{64,0},{1,65},{65,1},{2,66},{66,2},{3,67},{67,3},{4,68},{68... | collective-permute-start | bytes 1966088 | tf_op jit(solution)/shard_map/ppermute | solution.py:39
  36.3 29.1 %copy-start.3 = (bf16[2048,8]{0,1:T(8,128)(2,1)S(1)}, bf16[2048,8]{0,1:T(8,128)(2,1)}, u32[]{:S(2)}) copy-start(bf16[2048,8]{0,1:T(8,128)(2,1)} %param.12) | copy-start | bytes 98308
  40.2 25.2 %collective-permute-start.9 = (bf16[256,2048]{1,0:T(8,128)(2,1)S(1)}, bf16[256,2048]{1,0:T(8,128)(2,1)}, u32[]{:S(2)}, u32[]{:S(2)}) collective-permute-start(bf16[256,2048]{1,0:T(8,128)(2,1)S(1)} %normalise.1.own), channel_id=1, source_target_pairs={{0,8},{8,0},{1,9},{9,1},{2,10},{10,2},{3,11},{11,3},{4,12},{12,4},... | collective-permute-start | bytes 3145736 | tf_op jit(solution)/shard_map/ppermute | solution.py:47
  43.3 16.6 %collective-permute-start.10 = (bf16[2,1280,128]{2,1,0:T(8,128)(2,1)}, bf16[2,1280,128]{2,1,0:T(8,128)(2,1)S(1)}, u32[]{:S(2)}, u32[]{:S(2)}) collective-permute-start(bf16[2,1280,128]{2,1,0:T(8,128)(2,1)} %collective-permute-done.4.refs_1_), channel_id=1, source_target_pairs={{0,48},{16,0},{32,16},{48,32},{1,49},{17,1},{33,17},{49,33},{2,50}... | collective-permute-start | bytes 1966088 | tf_op jit(solution)/shard_map/ppermute | solution.py:35
  45.3 17.5 %collective-permute-start.11 = (bf16[2,1280,128]{2,1,0:T(8,128)(2,1)}, bf16[2,1280,128]{2,1,0:T(8,128)(2,1)}, u32[]{:S(2)}, u32[]{:S(2)}) collective-permute-start(bf16[2,1280,128]{2,1,0:T(8,128)(2,1)} %collective-permute-done.4.refs_1_), channel_id=1, source_target_pairs={{0,16},{16,32},{32,48},{48,0},{1,17},{17,33},{33,49},{49,1},{2,18}... | collective-permute-start | bytes 1966088 | tf_op jit(solution)/shard_map/ppermute | solution.py:35
  45.3 20.1 %collective-permute-start.12 = (bf16[2,1280,128]{2,1,0:T(8,128)(2,1)}, bf16[2,1280,128]{2,1,0:T(8,128)(2,1)}, u32[]{:S(2)}, u32[]{:S(2)}) collective-permute-start(bf16[2,1280,128]{2,1,0:T(8,128)(2,1)} %collective-permute-done.1.refs_4_), channel_id=1, source_target_pairs={{0,64},{64,0},{1,65},{65,1},{2,66},{66,2},{3,67},{67,3},{4,68},{68... | collective-permute-start | bytes 1966088 | tf_op jit(solution)/shard_map/ppermute | solution.py:39
  62.8 12.6 %collective-permute-start.13 = (bf16[2048,128]{1,0:T(8,128)(2,1)}, bf16[2048,128]{1,0:T(8,128)(2,1)S(1)}, u32[]{:S(2)}, u32[]{:S(2)}) collective-permute-start(bf16[2048,128]{1,0:T(8,128)(2,1)} %refs_0_.1), channel_id=1, source_target_pairs={{0,48},{16,0},{32,16},{48,32},{1,49},{17,1},{33,17},{49,33},{2,50}... | collective-permute-start | bytes 1572872 | tf_op jit(solution)/shard_map/ppermute | solution.py:35
  63.9 13.7 %collective-permute-start.14 = (bf16[2048,128]{1,0:T(8,128)(2,1)}, bf16[2048,128]{1,0:T(8,128)(2,1)S(1)}, u32[]{:S(2)}, u32[]{:S(2)}) collective-permute-start(bf16[2048,128]{1,0:T(8,128)(2,1)} %refs_0_.1), channel_id=1, source_target_pairs={{0,16},{16,32},{32,48},{48,0},{1,17},{17,33},{33,49},{49,1},{2,18}... | collective-permute-start | bytes 1572872 | tf_op jit(solution)/shard_map/ppermute | solution.py:35
  64.2 14.1 %collective-permute-start.15 = (bf16[2048,128]{1,0:T(8,128)(2,1)}, bf16[2048,128]{1,0:T(8,128)(2,1)}, u32[]{:S(2)}, u32[]{:S(2)}) collective-permute-start(bf16[2048,128]{1,0:T(8,128)(2,1)} %refs_0_.1), channel_id=1, source_target_pairs={{0,64},{64,0},{1,65},{65,1},{2,66},{66,2},{3,67},{67,3},{4,68},{68... | collective-permute-start | bytes 1572872 | tf_op jit(solution)/shard_map/ppermute | solution.py:39
  72.9 8.9 %collective-permute-start.16 = (bf16[512,256]{1,0:T(8,128)(2,1)S(1)}, bf16[512,256]{1,0:T(8,128)(2,1)S(1)}, u32[]{:S(2)}, u32[]{:S(2)}) collective-permute-start(bf16[512,256]{1,0:T(8,128)(2,1)S(1)} %get-tuple-element.50.refs_3_.refs_5_), channel_id=1, source_target_pairs={{0,64},{64,0},{1,65},{65,1},{2,66},{66,2},{3,67},{67,3},{4,68},{68... | collective-permute-start | bytes 786440 | tf_op jit(solution)/shard_map/ppermute | solution.py:39
  73.3 12.0 %collective-permute-start.17 = (bf16[1024,128]{1,0:T(8,128)(2,1)S(1)}, bf16[1024,128]{1,0:T(8,128)(2,1)S(1)}, u32[]{:S(2)}, u32[]{:S(2)}) collective-permute-start(bf16[1024,128]{1,0:T(8,128)(2,1)S(1)} %get-tuple-element.47.refs_0_), channel_id=1, source_target_pairs={{0,16},{16,32},{32,48},{48,0},{1,17},{17,33},{33,49},{49,1},{2,18}... | collective-permute-start | bytes 786440 | tf_op jit(solution)/shard_map/ppermute | solution.py:35
  75.3 11.3 %collective-permute-start.18 = (bf16[1024,128]{1,0:T(8,128)(2,1)S(1)}, bf16[1024,128]{1,0:T(8,128)(2,1)S(1)}, u32[]{:S(2)}, u32[]{:S(2)}) collective-permute-start(bf16[1024,128]{1,0:T(8,128)(2,1)S(1)} %get-tuple-element.47.refs_0_), channel_id=1, source_target_pairs={{0,32},{16,48},{32,0},{48,16},{1,33},{17,49},{33,1},{49,17},{2,34}... | collective-permute-start | bytes 786440 | tf_op jit(solution)/shard_map/ppermute | solution.py:35
  77.6 11.8 %collective-permute-start.19 = (bf16[1024,128]{1,0:T(8,128)(2,1)S(1)}, bf16[1024,128]{1,0:T(8,128)(2,1)}, u32[]{:S(2)}, u32[]{:S(2)}) collective-permute-start(bf16[1024,128]{1,0:T(8,128)(2,1)S(1)} %get-tuple-element.47.refs_0_), channel_id=1, source_target_pairs={{0,48},{16,0},{32,16},{48,32},{1,49},{17,1},{33,17},{49,33},{2,50}... | collective-permute-start | bytes 786440 | tf_op jit(solution)/shard_map/ppermute | solution.py:35
  81.8 24.5 %collective-permute-start.22 = (bf16[2048,128]{1,0:T(8,128)(2,1)}, bf16[2048,128]{1,0:T(8,128)(2,1)S(1)}, u32[]{:S(2)}, u32[]{:S(2)}) collective-permute-start(bf16[2048,128]{1,0:T(8,128)(2,1)} %collective-permute-done.15.refs_1_), channel_id=1, source_target_pairs={{0,48},{16,0},{32,16},{48,32},{1,49},{17,1},{33,17},{49,33},{2,50}... | collective-permute-start | bytes 1572872 | tf_op jit(solution)/shard_map/ppermute | solution.py:35
  84.4 21.9 %collective-permute-start.23 = (bf16[2048,128]{1,0:T(8,128)(2,1)}, bf16[2048,128]{1,0:T(8,128)(2,1)S(1)}, u32[]{:S(2)}, u32[]{:S(2)}) collective-permute-start(bf16[2048,128]{1,0:T(8,128)(2,1)} %collective-permute-done.15.refs_1_), channel_id=1, source_target_pairs={{0,16},{16,32},{32,48},{48,0},{1,17},{17,33},{33,49},{49,1},{2,18}... | collective-permute-start | bytes 1572872 | tf_op jit(solution)/shard_map/ppermute | solution.py:35
  85.3 20.9 %collective-permute-start.20 = (bf16[1024,128]{1,0:T(8,128)(2,1)S(1)}, bf16[1024,128]{1,0:T(8,128)(2,1)S(1)}, u32[]{:S(2)}, u32[]{:S(2)}) collective-permute-start(bf16[1024,128]{1,0:T(8,128)(2,1)S(1)} %slice.6), channel_id=1, source_target_pairs={{0,16},{16,32},{32,48},{48,0},{1,17},{17,33},{33,49},{49,1},{2,18}... | collective-permute-start | bytes 786440 | tf_op jit(solution)/shard_map/ppermute | solution.py:35
  86.7 19.5 %collective-permute-start.21 = (bf16[1024,128]{1,0:T(8,128)(2,1)S(1)}, bf16[1024,128]{1,0:T(8,128)(2,1)S(1)}, u32[]{:S(2)}, u32[]{:S(2)}) collective-permute-start(bf16[1024,128]{1,0:T(8,128)(2,1)S(1)} %slice.7), channel_id=1, source_target_pairs={{0,48},{16,0},{32,16},{48,32},{1,49},{17,1},{33,17},{49,33},{2,50}... | collective-permute-start | bytes 786440 | tf_op jit(solution)/shard_map/ppermute | solution.py:35
  106.3 15.3 %collective-permute-start.24 = (bf16[144,1024]{1,0:T(8,128)(2,1)S(1)}, bf16[144,1024]{1,0:T(8,128)(2,1)S(1)}, u32[]{:S(2)}, u32[]{:S(2)}) collective-permute-start(bf16[144,1024]{1,0:T(8,128)(2,1)S(1)} %get-tuple-element.60), channel_id=1, source_target_pairs={{0,48},{16,0},{32,16},{48,32},{1,49},{17,1},{33,17},{49,33},{2,50}... | collective-permute-start | bytes 884744 | tf_op jit(solution)/shard_map/ppermute | solution.py:35
  109.7 11.8 %collective-permute-start.25 = (bf16[144,1024]{1,0:T(8,128)(2,1)S(1)}, bf16[144,1024]{1,0:T(8,128)(2,1)S(1)}, u32[]{:S(2)}, u32[]{:S(2)}) collective-permute-start(bf16[144,1024]{1,0:T(8,128)(2,1)S(1)} %get-tuple-element.61), channel_id=1, source_target_pairs={{0,32},{16,48},{32,0},{48,16},{1,33},{17,49},{33,1},{49,17},{2,34}... | collective-permute-start | bytes 884744 | tf_op jit(solution)/shard_map/ppermute | solution.py:35
  109.7 16.1 %collective-permute-start.26 = (bf16[144,1024]{1,0:T(8,128)(2,1)S(1)}, bf16[144,1024]{1,0:T(8,128)(2,1)S(1)}, u32[]{:S(2)}, u32[]{:S(2)}) collective-permute-start(bf16[144,1024]{1,0:T(8,128)(2,1)S(1)} %get-tuple-element.62), channel_id=1, source_target_pairs={{0,16},{16,32},{32,48},{48,0},{1,17},{17,33},{33,49},{49,1},{2,18}... | collective-permute-start | bytes 884744 | tf_op jit(solution)/shard_map/ppermute | solution.py:35
  115.0 12.3 %collective-permute-start.28 = (bf16[1024,128]{1,0:T(8,128)(2,1)S(1)}, bf16[1024,128]{1,0:T(8,128)(2,1)S(1)}, u32[]{:S(2)}, u32[]{:S(2)}) collective-permute-start(bf16[1024,128]{1,0:T(8,128)(2,1)S(1)} %collective-permute-done.20.refs_6_), channel_id=1, source_target_pairs={{0,64},{64,0},{1,65},{65,1},{2,66},{66,2},{3,67},{67,3},{4,68},{68... | collective-permute-start | bytes 786440 | tf_op jit(solution)/shard_map/ppermute | solution.py:39
  120.3 11.0 %collective-permute-start.29 = (bf16[1024,128]{1,0:T(8,128)(2,1)S(1)}, bf16[1024,128]{1,0:T(8,128)(2,1)S(1)}, u32[]{:S(2)}, u32[]{:S(2)}) collective-permute-start(bf16[1024,128]{1,0:T(8,128)(2,1)S(1)} %collective-permute-done.21.refs_7_), channel_id=1, source_target_pairs={{0,64},{64,0},{1,65},{65,1},{2,66},{66,2},{3,67},{67,3},{4,68},{68... | collective-permute-start | bytes 786440 | tf_op jit(solution)/shard_map/ppermute | solution.py:39
  126.2 5.1 %collective-permute-start.27 = (bf16[1024,128]{1,0:T(8,128)(2,1)S(1)}, bf16[1024,128]{1,0:T(8,128)(2,1)S(1)}, u32[]{:S(2)}, u32[]{:S(2)}) collective-permute-start(bf16[1024,128]{1,0:T(8,128)(2,1)S(1)} %combine.1.own), channel_id=1, source_target_pairs={{0,8},{8,0},{1,9},{9,1},{2,10},{10,2},{3,11},{11,3},{4,12},{12,4},... | collective-permute-start | bytes 786440 | tf_op jit(solution)/shard_map/ppermute | solution.py:47
  155.9 4.3 %collective-permute-start.30 = (bf16[256,128]{1,0:T(8,128)(2,1)S(1)}, bf16[256,128]{1,0:T(8,128)(2,1)S(1)}, u32[]{:S(2)}, u32[]{:S(2)}) collective-permute-start(bf16[256,128]{1,0:T(8,128)(2,1)S(1)} %get-tuple-element.72), channel_id=1, source_target_pairs={{0,8},{8,0},{1,9},{9,1},{2,10},{10,2},{3,11},{11,3},{4,12},{12,4},... | collective-permute-start | bytes 196616 | tf_op jit(solution)/shard_map/ppermute | solution.py:47
  (23 other events, 235.7 us)

commit v10 on v9

--- a/solution.py
+++ b/solution.py
@@ -493,9 +493,9 @@
     kvs = [kv, across_x(kv)]
     qs = [q] + [along_y(q, k) for k in (1, 2, 3)]
     qs[0], o_ym, o_yp = lax.optimization_barrier((q, o_ym, o_yp))
-    o_a_late, up, down, kvs[1] = lax.optimization_barrier((o_a, o_yp[:1024], o_ym[1024:], kvs[1]))
+    o_a, up, down, kvs[1] = lax.optimization_barrier((o_a, o_yp[:1024], o_ym[1024:], kvs[1]))
     far0, far1 = along_y(up, 1), along_y(down, 3)
-    o_am, o_ap = along_y(o_a_late, 3), along_y(o_a_late, 1)
+    o_am, o_ap = across_x(o_ym), across_x(o_yp)
 
     firsts = [(xl * 4 + lax.rem(y + 4 - k, 4)) * 512 for k in range(4)]
     mine, partner = xl * 4 + y, (1 - xl) * 4 + y
@@ -508,8 +508,9 @@
     )
     for k in range(1, 4):
         parts[k] = along_y(parts[k], 4 - k)
-    out_blocks = [out_weight, o_a, o_ym, o_am, o_yp, o_ap]
-    out_blocks += [far0, far1, across_x(far0), across_x(far1)]
+    afar0, afar1 = across_x(far0), across_x(far1)
+    parts, afar0, afar1 = lax.optimization_barrier((parts, afar0, afar1))
+    out_blocks = [out_weight, o_a, o_ym, o_am, o_yp, o_ap, far0, far1, afar0, afar1]
     gate_row = gates.reshape(2, 256, 2).transpose(0, 2, 1).reshape(1, 1024)
     attended = combine(gate_row, parts)
 

time: 162 us -> 158 us (0.975)
  waiting for transfers between devices: 47.9 us -> 41.7 us
  blocking collectives: 41.6 us -> 43.9 us
  Pallas kernels: 27 us -> 29 us
    ppermute x17 -> x15, waiting for transfers between devices: 39.1 us -> 28 us  [along_y(): return lax.ppermute(x, 'y', [(i, (i + k) % 4) for i in range(4)])]
    ppermute x7 -> x9, waiting for transfers between devices: 7.4 us -> 11.1 us  [across_x(): return lax.ppermute(x, 'xl', [(0, 1), (1, 0)])]
    all_to_all x1, blocking collectives: 18 us -> 20.4 us  [on_device(): sums = lax.all_to_all(sums, NARROW, 0, 0, tiled=True)]
    pallas_call x2, Pallas kernels: 12.3 us -> 14.3 us  [attend(): pl.pallas_call(functools.partial(attend_kernel, count), out_shape=tuple((...]
    ppermute x7 -> x9, starting transfers between devices: 9.58 us -> 8.27 us  [across_x(): return lax.ppermute(x, 'xl', [(0, 1), (1, 0)])]
    ppermute x17 -> x15, starting transfers between devices: 17.7 us -> 17.7 us  [along_y(): return lax.ppermute(x, 'y', [(i, (i + k) % 4) for i in range(4)])]
  transfers between devices with their start and end apart: 31 -> 31, of which waited for: 17 -> 16; matrix products, arithmetic and copies ran while one was open for 2% -> 2% of each run, Pallas kernels for 13% -> 15%
where the time goes in v10:
time: 158 us; the launch traced here: 157 us
  blocking collectives  43.9 us (28%)
  waiting for transfers between devices  41.7 us (26%)
  starting transfers between devices  36.9 us (23%)
  Pallas kernels  29 us (18%)
  local copies, waits for them, and re-layouts  3.02 us (2%)
  other arithmetic  1.9 us (1%)
    ppermute x15, waiting for transfers between devices, along_y(): return lax.ppermute(x, 'y', [(i, (i + k) % 4) for i in range(4)])  28 us
    all_gather x2, blocking collectives, on_device(): blocks = [lax.all_gather(v, 'z', axis=0) for v in (tokens, half_row)]  23.6 us
    all_to_all x1, blocking collectives, on_device(): sums = lax.all_to_all(sums, NARROW, 0, 0, tiled=True)  20.4 us
    ppermute x15, starting transfers between devices, along_y(): return lax.ppermute(x, 'y', [(i, (i + k) % 4) for i in range(4)])  17.7 us
    pallas_call x2, Pallas kernels, attend(): pl.pallas_call(functools.partial(attend_kernel, count), out_shape=tuple((...  14.3 us
    ppermute x9, waiting for transfers between devices, across_x(): return lax.ppermute(x, 'xl', [(0, 1), (1, 0)])  11.1 us
    ppermute x6, starting transfers between devices, across_core(): return lax.ppermute(x, 'c', [(0, 1), (1, 0)])  9.11 us
    ppermute x9, starting transfers between devices, across_x(): return lax.ppermute(x, 'xl', [(0, 1), (1, 0)])  8.27 us
  transfers between devices with their start and end apart: 31, of which 16 were waited for; matrix products, arithmetic and copies ran while one was open for 2% of the time, Pallas kernels for 15%

profile of v10, /device:TPU:3, one launch (start us, length us, event | category | flops | bytes accessed | tf_op | source)
XLA Modules:
  0.0 156.9 jit_solution(16883216227390784441)
XLA Ops:
  0.0 1.8 %collective-permute-start.5 = (bf16[256,256]{1,0:T(8,128)(2,1)}, bf16[256,256]{1,0:T(8,128)(2,1)S(1)}, u32[]{:S(2)}, u32[]{:S(2)}) collective-permute-start(bf16[256,256]{1,0:T(8,128)(2,1)} %param.10), channel_id=1, source_target_pairs={{0,1},{1,0},{2,3},{3,2},{4,5},{5,4},{6,7},{7,6},{8,9},{9,8},{10,11... | collective-permute-start | bytes 393224 | tf_op jit(solution)/shard_map/ppermute | solution.py:43
  5.5 1.2 collective-permute-start.7
  7.7 2.9 %collective-permute-start.1 = (bf16[2,1280,128]{2,1,0:T(8,128)(2,1)}, bf16[2,1280,128]{2,1,0:T(8,128)(2,1)}, u32[]{:S(2)}, u32[]{:S(2)}) collective-permute-start(bf16[2,1280,128]{2,1,0:T(8,128)(2,1)} %pad_maximum_fusion.1.refs_0_), channel_id=1, source_target_pairs={{0,32},{16,48},{32,0},{48,16},{1,33},{17,49},{33,1},{49,17},{2,34}... | collective-permute-start | bytes 1966088 | tf_op jit(solution)/shard_map/ppermute | solution.py:35
  12.4 12.5 %all-gather = bf16[1024,256]{1,0:T(8,128)(2,1)S(1)} all-gather(bf16[256,256]{1,0:T(8,128)(2,1)S(1)} %copy-done.8), channel_id=2, replica_groups=mesh['xl'=2,'y'=4,'c'=2,'z'=4,'xh'=2] {'z'}, dimensions={0}, use_global_device_ids=true | all-gather | bytes 655360 | tf_op jit(solution)/shard_map/all_gather | solution.py:475
  25.2 11.1 %all-gather.1 = bf16[1024,256]{1,0:T(8,128)(2,1)S(1)} all-gather(bf16[256,256]{1,0:T(8,128)(2,1)S(1)} %collective-permute-done.5), channel_id=3, replica_groups=mesh['xl'=2,'y'=4,'c'=2,'z'=4,'xh'=2] {'z'}, dimensions={0}, use_global_device_ids=true | all-gather | bytes 655360 | tf_op jit(solution)/shard_map/all_gather | solution.py:475
  36.3 1.3 normalise.1.own
  37.7 1.9 %collective-permute-done.2.refs_2_ = bf16[2,1280,128]{2,1,0:T(8,128)(2,1)} collective-permute-done((bf16[2,1280,128]{2,1,0:T(8,128)(2,1)}, bf16[2,1280,128]{2,1,0:T(8,128)(2,1)}, u32[]{:S(2)}, u32[]{:S(2)}) %collective-permute-start.2) | collective-permute-done | bytes 655392 | tf_op jit(solution)/shard_map/ppermute | solution.py:35
  40.2 3.1 %collective-permute-start.9 = (bf16[256,2048]{1,0:T(8,128)(2,1)S(1)}, bf16[256,2048]{1,0:T(8,128)(2,1)}, u32[]{:S(2)}, u32[]{:S(2)}) collective-permute-start(bf16[256,2048]{1,0:T(8,128)(2,1)S(1)} %normalise.1.own), channel_id=1, source_target_pairs={{0,8},{8,0},{1,9},{9,1},{2,10},{10,2},{3,11},{11,3},{4,12},{12,4},... | collective-permute-start | bytes 3145736 | tf_op jit(solution)/shard_map/ppermute | solution.py:47
  43.3 2.0 %collective-permute-start.10 = (bf16[2,1280,128]{2,1,0:T(8,128)(2,1)}, bf16[2,1280,128]{2,1,0:T(8,128)(2,1)S(1)}, u32[]{:S(2)}, u32[]{:S(2)}) collective-permute-start(bf16[2,1280,128]{2,1,0:T(8,128)(2,1)} %collective-permute-done.4.refs_1_), channel_id=1, source_target_pairs={{0,48},{16,0},{32,16},{48,32},{1,49},{17,1},{33,17},{49,33},{2,50}... | collective-permute-start | bytes 1966088 | tf_op jit(solution)/shard_map/ppermute | solution.py:35
  46.5 13.4 %collective-permute-done.10.refs_3_ = bf16[2,1280,128]{2,1,0:T(8,128)(2,1)S(1)} collective-permute-done((bf16[2,1280,128]{2,1,0:T(8,128)(2,1)}, bf16[2,1280,128]{2,1,0:T(8,128)(2,1)S(1)}, u32[]{:S(2)}, u32[]{:S(2)}) %collective-permute-start.10) | collective-permute-done | bytes 655392 | tf_op jit(solution)/shard_map/ppermute | solution.py:35
  60.8 2.0 %collective-permute-done.11.refs_7_ = bf16[2,1280,128]{2,1,0:T(8,128)(2,1)} collective-permute-done((bf16[2,1280,128]{2,1,0:T(8,128)(2,1)}, bf16[2,1280,128]{2,1,0:T(8,128)(2,1)}, u32[]{:S(2)}, u32[]{:S(2)}) %collective-permute-start.11) | collective-permute-done | bytes 655392 | tf_op jit(solution)/shard_map/ppermute | solution.py:35
  65.4 7.4 %project.1 = (bf16[1024,128]{1,0:T(8,128)(2,1)S(1)}, bf16[512,256]{1,0:T(8,128)(2,1)S(1)}, f32[512,2]{1,0:T(8,128)S(1)}) custom-call(s32[9]{0:T(128)S(1)} %stack.154.idx, s32[512,2]{1,0:T(8,128)S(1)} %broadcast_select_fusion.routes, bf16[8,2048]{1,0:T(8,128)(2,1)S(1)} %bitcast.47, bf16[256,2048]{1,0:T(8,128)(2,1)} %copy-done, ...), custom_call_target="tpu_custom_call" | custom-call | flops 6442450944 | bytes 8388608 | tf_op jit(solution)/shard_map/project/pallas_call | solution.py:164
  73.3 2.1 %collective-permute-done.13.refs_2_ = bf16[2048,128]{1,0:T(8,128)(2,1)S(1)} collective-permute-done((bf16[2048,128]{1,0:T(8,128)(2,1)}, bf16[2048,128]{1,0:T(8,128)(2,1)S(1)}, u32[]{:S(2)}, u32[]{:S(2)}) %collective-permute-start.13) | collective-permute-done | bytes 524320 | tf_op jit(solution)/shard_map/ppermute | solution.py:35
  75.3 1.5 collective-permute-start.18
  78.3 1.4 collective-permute-start.22
  79.7 2.0 %collective-permute-done.16.refs_4_.refs_6_ = bf16[512,256]{1,0:T(8,128)(2,1)S(1)} collective-permute-done((bf16[512,256]{1,0:T(8,128)(2,1)S(1)}, bf16[512,256]{1,0:T(8,128)(2,1)S(1)}, u32[]{:S(2)}, u32[]{:S(2)}) %collective-permute-start.16) | collective-permute-done | bytes 262176 | tf_op jit(solution)/shard_map/ppermute | solution.py:39
  82.9 2.3 %collective-permute-done.17.refs_0_ = bf16[1024,128]{1,0:T(8,128)(2,1)S(1)} collective-permute-done((bf16[1024,128]{1,0:T(8,128)(2,1)S(1)}, bf16[1024,128]{1,0:T(8,128)(2,1)S(1)}, u32[]{:S(2)}, u32[]{:S(2)}) %collective-permute-start.17) | collective-permute-done | bytes 262176 | tf_op jit(solution)/shard_map/ppermute | solution.py:35
  85.3 1.4 collective-permute-done.18.refs_1_
  86.7 1.3 collective-permute-start.21
  88.0 1.4 collective-permute-done.19.refs_2_
  89.4 9.7 %attend.3 = (bf16[144,1024]{1,0:T(8,128)(2,1)S(1)}, bf16[144,1024]{1,0:T(8,128)(2,1)S(1)}, bf16[144,1024]{1,0:T(8,128)(2,1)S(1)}) custom-call(s32[8]{0:T(128)S(1)} %stack.187.idx, s32[4]{0:T(128)S(1)} %copy-done.4, s32[4]{0:T(128)S(1)} %copy-done.5, bf16[1024,128]{1,0:T(8,128)(2,1)} %copy-done.18, bf16[1024,128]{1,0:T(8,128)(2,1)} %copy-done.19, ...), custom_call_target="tpu_custom_call" | custom-call | flops 9663676416 | bytes 4194304 | tf_op jit(solution)/shard_map/attend/pallas_call | solution.py:330
  99.2 5.1 %collective-permute-done.23.refs_5_ = bf16[2048,128]{1,0:T(8,128)(2,1)S(1)} collective-permute-done((bf16[2048,128]{1,0:T(8,128)(2,1)S(1)}, bf16[2048,128]{1,0:T(8,128)(2,1)S(1)}, u32[]{:S(2)}, u32[]{:S(2)}) %collective-permute-start.23) | collective-permute-done | bytes 524320 | tf_op jit(solution)/shard_map/ppermute | solution.py:39
  104.2 2.6 %collective-permute-start.24 = (bf16[144,1024]{1,0:T(8,128)(2,1)S(1)}, bf16[144,1024]{1,0:T(8,128)(2,1)S(1)}, u32[]{:S(2)}, u32[]{:S(2)}) collective-permute-start(bf16[144,1024]{1,0:T(8,128)(2,1)S(1)} %get-tuple-element.65), channel_id=1, source_target_pairs={{0,48},{16,0},{32,16},{48,32},{1,49},{17,1},{33,17},{49,33},{2,50}... | collective-permute-start | bytes 884744 | tf_op jit(solution)/shard_map/ppermute | solution.py:35
  106.8 4.1 %collective-permute-start.25 = (bf16[144,1024]{1,0:T(8,128)(2,1)S(1)}, bf16[144,1024]{1,0:T(8,128)(2,1)S(1)}, u32[]{:S(2)}, u32[]{:S(2)}) collective-permute-start(bf16[144,1024]{1,0:T(8,128)(2,1)S(1)} %get-tuple-element.66), channel_id=1, source_target_pairs={{0,32},{16,48},{32,0},{48,16},{1,33},{17,49},{33,1},{49,17},{2,34}... | collective-permute-start | bytes 884744 | tf_op jit(solution)/shard_map/ppermute | solution.py:35
  111.0 1.5 collective-permute-start.28
  112.4 4.6 %attend.2.p0 = bf16[144,1024]{1,0:T(8,128)(2,1)S(1)} custom-call(s32[6]{0:T(128)S(1)} %stack.183.idx, s32[4]{0:T(128)S(1)} %copy-done.4, s32[4]{0:T(128)S(1)} %copy-done.5, bf16[1024,128]{1,0:T(8,128)(2,1)} %copy-done.1, bf16[2,768,256]{2,1,0:T(8,128)(2,1)} %copy-done.6, bf16[2,768,256]{2,1,0:T(8,128)(2,1)} %collective-permute-done.7.refs_2_.refs_4_, ...), custom_call_target="tpu_custom_call" | custom-call | flops 3221225472 | bytes 4194304 | tf_op jit(solution)/shard_map/attend/pallas_call | solution.py:330
  117.1 4.0 %collective-permute-done.28.refs_9_ = bf16[1024,128]{1,0:T(8,128)(2,1)S(1)} collective-permute-done((bf16[1024,128]{1,0:T(8,128)(2,1)S(1)}, bf16[1024,128]{1,0:T(8,128)(2,1)S(1)}, u32[]{:S(2)}, u32[]{:S(2)}) %collective-permute-start.28) | collective-permute-done | bytes 262176 | tf_op jit(solution)/shard_map/ppermute | solution.py:39
  121.2 2.0 %collective-permute-done.26.p3 = bf16[144,1024]{1,0:T(8,128)(2,1)S(1)} collective-permute-done((bf16[144,1024]{1,0:T(8,128)(2,1)S(1)}, bf16[144,1024]{1,0:T(8,128)(2,1)S(1)}, u32[]{:S(2)}, u32[]{:S(2)}) %collective-permute-start.26) | collective-permute-done | bytes 294944 | tf_op jit(solution)/shard_map/ppermute | solution.py:35
  123.5 2.5 %collective-permute-start.29 = (bf16[1024,128]{1,0:T(8,128)(2,1)S(1)}, bf16[1024,128]{1,0:T(8,128)(2,1)S(1)}, u32[]{:S(2)}, u32[]{:S(2)}) collective-permute-start(bf16[1024,128]{1,0:T(8,128)(2,1)S(1)} %combine.1.own), channel_id=1, source_target_pairs={{0,8},{8,0},{1,9},{9,1},{2,10},{10,2},{3,11},{11,3},{4,12},{12,4},... | collective-permute-start | bytes 786440 | tf_op jit(solution)/shard_map/ppermute | solution.py:47
  127.1 5.7 %project_out.1 = bf16[8,512,128]{2,1,0:T(8,128)(2,1)S(1)} custom-call(s32[9]{0:T(128)S(1)} %stack.154.idx, s32[512,2]{1,0:T(8,128)S(1)} %broadcast_select_fusion.routes, bf16[1024,128]{1,0:T(8,128)(2,1)S(1)} %combine.1.own, bf16[1024,128]{1,0:T(8,128)(2,1)S(1)} %collective-permute-done.29.other, bf16[2048,128]{1,0:T(8,128)(2,1)} %refs_0_.1, ...), custom_call_target="tpu_custom_call" | custom-call | flops 4294967296 | bytes 6291456 | tf_op jit(solution)/shard_map/project_out/pallas_call | solution.py:418
  132.9 20.4 %all_to_all.5 = bf16[8,512,128]{2,1,0:T(8,128)(2,1)S(1)} all-to-all(bf16[8,512,128]{2,1,0:T(8,128)(2,1)S(1)} %project_out.1), channel_id=1, replica_groups=mesh['xl'=2,'y'=4,'c'=2,'z'=4,'xh'=2] {'z','xh'}, dimensions={0} | all-to-all | bytes 2097152 | tf_op jit(solution)/shard_map/all_to_all | solution.py:520
  153.4 1.9 %collective-permute-start.30 = (bf16[256,128]{1,0:T(8,128)(2,1)S(1)}, bf16[256,128]{1,0:T(8,128)(2,1)S(1)}, u32[]{:S(2)}, u32[]{:S(2)}) collective-permute-start(bf16[256,128]{1,0:T(8,128)(2,1)S(1)} %get-tuple-element.84), channel_id=1, source_target_pairs={{0,8},{8,0},{1,9},{9,1},{2,10},{10,2},{3,11},{11,3},{4,12},{12,4},... | collective-permute-start | bytes 196616 | tf_op jit(solution)/shard_map/ppermute | solution.py:47
  (110 shorter events, 18.4 us)
Async XLA Ops:
  0.0 12.0 %collective-permute-start.5 = (bf16[256,256]{1,0:T(8,128)(2,1)}, bf16[256,256]{1,0:T(8,128)(2,1)S(1)}, u32[]{:S(2)}, u32[]{:S(2)}) collective-permute-start(bf16[256,256]{1,0:T(8,128)(2,1)} %param.10), channel_id=1, source_target_pairs={{0,1},{1,0},{2,3},{3,2},{4,5},{5,4},{6,7},{7,6},{8,9},{9,8},{10,11... | collective-permute-start | bytes 393224 | tf_op jit(solution)/shard_map/ppermute | solution.py:43
  3.0 2.4 %collective-permute-start.6 = (bf16[768,256]{1,0:T(8,128)(2,1)S(1)}, bf16[768,256]{1,0:T(8,128)(2,1)S(1)}, u32[]{:S(2)}, u32[]{:S(2)}) collective-permute-start(bf16[768,256]{1,0:T(8,128)(2,1)S(1)} %get-tuple-element.80), channel_id=1, source_target_pairs={{0,8},{8,0},{1,9},{9,1},{2,10},{10,2},{3,11},{11,3},{4,12},{12,4},... | collective-permute-start | bytes 1179656 | tf_op jit(solution)/shard_map/ppermute | solution.py:47
  4.2 2.6 %collective-permute-start = (bf16[1280,128]{1,0:T(8,128)(2,1)S(1)}, bf16[1280,128]{1,0:T(8,128)(2,1)S(1)}, u32[]{:S(2)}, u32[]{:S(2)}) collective-permute-start(bf16[1280,128]{1,0:T(8,128)(2,1)S(1)} %pad_maximum_fusion.2), channel_id=1, source_target_pairs={{0,8},{8,0},{1,9},{9,1},{2,10},{10,2},{3,11},{11,3},{4,12},{12,4},... | collective-permute-start | bytes 983048 | tf_op jit(solution)/shard_map/ppermute | solution.py:47
  4.3 7.0 %collective-permute-start.8 = (s32[256,2]{0,1:T(2,128)S(1)}, s32[256,2]{0,1:T(2,128)S(1)}, u32[]{:S(2)}, u32[]{:S(2)}) collective-permute-start(s32[256,2]{0,1:T(2,128)S(1)} %copy-done.13), channel_id=1, source_target_pairs={{0,8},{8,0},{1,9},{9,1},{2,10},{10,2},{3,11},{11,3},{4,12},{12,4},... | collective-permute-start | bytes 6152 | tf_op jit(solution)/shard_map/ppermute | solution.py:47
  5.5 34.7 %collective-permute-start.7 = (bf16[2,768,256]{2,1,0:T(8,128)(2,1)S(1)}, bf16[2,768,256]{2,1,0:T(8,128)(2,1)}, u32[]{:S(2)}, u32[]{:S(2)}) collective-permute-start(bf16[2,768,256]{2,1,0:T(8,128)(2,1)S(1)} %pad_maximum_fusion.refs_1_.refs_3_), channel_id=1, source_target_pairs={{0,64},{64,0},{1,65},{65,1},{2,66},{66,2},{3,67},{67,3},{4,68},{68... | collective-permute-start | bytes 2359304 | tf_op jit(solution)/shard_map/ppermute | solution.py:39
  7.7 30.0 %collective-permute-start.1 = (bf16[2,1280,128]{2,1,0:T(8,128)(2,1)}, bf16[2,1280,128]{2,1,0:T(8,128)(2,1)}, u32[]{:S(2)}, u32[]{:S(2)}) collective-permute-start(bf16[2,1280,128]{2,1,0:T(8,128)(2,1)} %pad_maximum_fusion.1.refs_0_), channel_id=1, source_target_pairs={{0,32},{16,48},{32,0},{48,16},{1,33},{17,49},{33,1},{49,17},{2,34}... | collective-permute-start | bytes 1966088 | tf_op jit(solution)/shard_map/ppermute | solution.py:35
  10.6 29.0 %collective-permute-start.2 = (bf16[2,1280,128]{2,1,0:T(8,128)(2,1)}, bf16[2,1280,128]{2,1,0:T(8,128)(2,1)}, u32[]{:S(2)}, u32[]{:S(2)}) collective-permute-start(bf16[2,1280,128]{2,1,0:T(8,128)(2,1)} %pad_maximum_fusion.1.refs_0_), channel_id=1, source_target_pairs={{0,48},{16,0},{32,16},{48,32},{1,49},{17,1},{33,17},{49,33},{2,50}... | collective-permute-start | bytes 1966088 | tf_op jit(solution)/shard_map/ppermute | solution.py:35
  11.4 28.8 %collective-permute-start.3 = (bf16[2,1280,128]{2,1,0:T(8,128)(2,1)}, bf16[2,1280,128]{2,1,0:T(8,128)(2,1)}, u32[]{:S(2)}, u32[]{:S(2)}) collective-permute-start(bf16[2,1280,128]{2,1,0:T(8,128)(2,1)} %pad_maximum_fusion.1.refs_0_), channel_id=1, source_target_pairs={{0,16},{16,32},{32,48},{48,0},{1,17},{17,33},{33,49},{49,1},{2,18}... | collective-permute-start | bytes 1966088 | tf_op jit(solution)/shard_map/ppermute | solution.py:35
  12.1 28.1 %collective-permute-start.4 = (bf16[2,1280,128]{2,1,0:T(8,128)(2,1)}, bf16[2,1280,128]{2,1,0:T(8,128)(2,1)}, u32[]{:S(2)}, u32[]{:S(2)}) collective-permute-start(bf16[2,1280,128]{2,1,0:T(8,128)(2,1)} %pad_maximum_fusion.1.refs_0_), channel_id=1, source_target_pairs={{0,64},{64,0},{1,65},{65,1},{2,66},{66,2},{3,67},{67,3},{4,68},{68... | collective-permute-start | bytes 1966088 | tf_op jit(solution)/shard_map/ppermute | solution.py:39
  36.3 29.1 %copy-start.3 = (bf16[2048,8]{0,1:T(8,128)(2,1)S(1)}, bf16[2048,8]{0,1:T(8,128)(2,1)}, u32[]{:S(2)}) copy-start(bf16[2048,8]{0,1:T(8,128)(2,1)} %param.12) | copy-start | bytes 98308
  40.2 25.2 %collective-permute-start.9 = (bf16[256,2048]{1,0:T(8,128)(2,1)S(1)}, bf16[256,2048]{1,0:T(8,128)(2,1)}, u32[]{:S(2)}, u32[]{:S(2)}) collective-permute-start(bf16[256,2048]{1,0:T(8,128)(2,1)S(1)} %normalise.1.own), channel_id=1, source_target_pairs={{0,8},{8,0},{1,9},{9,1},{2,10},{10,2},{3,11},{11,3},{4,12},{12,4},... | collective-permute-start | bytes 3145736 | tf_op jit(solution)/shard_map/ppermute | solution.py:47
  43.3 16.6 %collective-permute-start.10 = (bf16[2,1280,128]{2,1,0:T(8,128)(2,1)}, bf16[2,1280,128]{2,1,0:T(8,128)(2,1)S(1)}, u32[]{:S(2)}, u32[]{:S(2)}) collective-permute-start(bf16[2,1280,128]{2,1,0:T(8,128)(2,1)} %collective-permute-done.4.refs_1_), channel_id=1, source_target_pairs={{0,48},{16,0},{32,16},{48,32},{1,49},{17,1},{33,17},{49,33},{2,50}... | collective-permute-start | bytes 1966088 | tf_op jit(solution)/shard_map/ppermute | solution.py:35
  45.3 17.5 %collective-permute-start.11 = (bf16[2,1280,128]{2,1,0:T(8,128)(2,1)}, bf16[2,1280,128]{2,1,0:T(8,128)(2,1)}, u32[]{:S(2)}, u32[]{:S(2)}) collective-permute-start(bf16[2,1280,128]{2,1,0:T(8,128)(2,1)} %collective-permute-done.4.refs_1_), channel_id=1, source_target_pairs={{0,16},{16,32},{32,48},{48,0},{1,17},{17,33},{33,49},{49,1},{2,18}... | collective-permute-start | bytes 1966088 | tf_op jit(solution)/shard_map/ppermute | solution.py:35
  45.3 20.1 %collective-permute-start.12 = (bf16[2,1280,128]{2,1,0:T(8,128)(2,1)}, bf16[2,1280,128]{2,1,0:T(8,128)(2,1)}, u32[]{:S(2)}, u32[]{:S(2)}) collective-permute-start(bf16[2,1280,128]{2,1,0:T(8,128)(2,1)} %collective-permute-done.1.refs_4_), channel_id=1, source_target_pairs={{0,64},{64,0},{1,65},{65,1},{2,66},{66,2},{3,67},{67,3},{4,68},{68... | collective-permute-start | bytes 1966088 | tf_op jit(solution)/shard_map/ppermute | solution.py:39
  62.8 12.6 %collective-permute-start.13 = (bf16[2048,128]{1,0:T(8,128)(2,1)}, bf16[2048,128]{1,0:T(8,128)(2,1)S(1)}, u32[]{:S(2)}, u32[]{:S(2)}) collective-permute-start(bf16[2048,128]{1,0:T(8,128)(2,1)} %refs_0_.1), channel_id=1, source_target_pairs={{0,48},{16,0},{32,16},{48,32},{1,49},{17,1},{33,17},{49,33},{2,50}... | collective-permute-start | bytes 1572872 | tf_op jit(solution)/shard_map/ppermute | solution.py:35
  63.9 13.7 %collective-permute-start.14 = (bf16[2048,128]{1,0:T(8,128)(2,1)}, bf16[2048,128]{1,0:T(8,128)(2,1)S(1)}, u32[]{:S(2)}, u32[]{:S(2)}) collective-permute-start(bf16[2048,128]{1,0:T(8,128)(2,1)} %refs_0_.1), channel_id=1, source_target_pairs={{0,16},{16,32},{32,48},{48,0},{1,17},{17,33},{33,49},{49,1},{2,18}... | collective-permute-start | bytes 1572872 | tf_op jit(solution)/shard_map/ppermute | solution.py:35
  64.2 14.1 %collective-permute-start.15 = (bf16[2048,128]{1,0:T(8,128)(2,1)}, bf16[2048,128]{1,0:T(8,128)(2,1)}, u32[]{:S(2)}, u32[]{:S(2)}) collective-permute-start(bf16[2048,128]{1,0:T(8,128)(2,1)} %refs_0_.1), channel_id=1, source_target_pairs={{0,64},{64,0},{1,65},{65,1},{2,66},{66,2},{3,67},{67,3},{4,68},{68... | collective-permute-start | bytes 1572872 | tf_op jit(solution)/shard_map/ppermute | solution.py:39
  72.9 8.9 %collective-permute-start.16 = (bf16[512,256]{1,0:T(8,128)(2,1)S(1)}, bf16[512,256]{1,0:T(8,128)(2,1)S(1)}, u32[]{:S(2)}, u32[]{:S(2)}) collective-permute-start(bf16[512,256]{1,0:T(8,128)(2,1)S(1)} %get-tuple-element.56.refs_3_.refs_5_), channel_id=1, source_target_pairs={{0,64},{64,0},{1,65},{65,1},{2,66},{66,2},{3,67},{67,3},{4,68},{68... | collective-permute-start | bytes 786440 | tf_op jit(solution)/shard_map/ppermute | solution.py:39
  73.3 12.0 %collective-permute-start.17 = (bf16[1024,128]{1,0:T(8,128)(2,1)S(1)}, bf16[1024,128]{1,0:T(8,128)(2,1)S(1)}, u32[]{:S(2)}, u32[]{:S(2)}) collective-permute-start(bf16[1024,128]{1,0:T(8,128)(2,1)S(1)} %get-tuple-element.53.refs_0_), channel_id=1, source_target_pairs={{0,16},{16,32},{32,48},{48,0},{1,17},{17,33},{33,49},{49,1},{2,18}... | collective-permute-start | bytes 786440 | tf_op jit(solution)/shard_map/ppermute | solution.py:35
  75.3 11.3 %collective-permute-start.18 = (bf16[1024,128]{1,0:T(8,128)(2,1)S(1)}, bf16[1024,128]{1,0:T(8,128)(2,1)S(1)}, u32[]{:S(2)}, u32[]{:S(2)}) collective-permute-start(bf16[1024,128]{1,0:T(8,128)(2,1)S(1)} %get-tuple-element.53.refs_0_), channel_id=1, source_target_pairs={{0,32},{16,48},{32,0},{48,16},{1,33},{17,49},{33,1},{49,17},{2,34}... | collective-permute-start | bytes 786440 | tf_op jit(solution)/shard_map/ppermute | solution.py:35
  77.6 11.8 %collective-permute-start.19 = (bf16[1024,128]{1,0:T(8,128)(2,1)S(1)}, bf16[1024,128]{1,0:T(8,128)(2,1)}, u32[]{:S(2)}, u32[]{:S(2)}) collective-permute-start(bf16[1024,128]{1,0:T(8,128)(2,1)S(1)} %get-tuple-element.53.refs_0_), channel_id=1, source_target_pairs={{0,48},{16,0},{32,16},{48,32},{1,49},{17,1},{33,17},{49,33},{2,50}... | collective-permute-start | bytes 786440 | tf_op jit(solution)/shard_map/ppermute | solution.py:35
  78.3 20.8 %collective-permute-start.22 = (bf16[2048,128]{1,0:T(8,128)(2,1)S(1)}, bf16[2048,128]{1,0:T(8,128)(2,1)S(1)}, u32[]{:S(2)}, u32[]{:S(2)}) collective-permute-start(bf16[2048,128]{1,0:T(8,128)(2,1)S(1)} %collective-permute-done.13.refs_2_), channel_id=1, source_target_pairs={{0,64},{64,0},{1,65},{65,1},{2,66},{66,2},{3,67},{67,3},{4,68},{68... | collective-permute-start | bytes 1572872 | tf_op jit(solution)/shard_map/ppermute | solution.py:39
  81.8 22.5 %collective-permute-start.23 = (bf16[2048,128]{1,0:T(8,128)(2,1)S(1)}, bf16[2048,128]{1,0:T(8,128)(2,1)S(1)}, u32[]{:S(2)}, u32[]{:S(2)}) collective-permute-start(bf16[2048,128]{1,0:T(8,128)(2,1)S(1)} %collective-permute-done.14.refs_4_), channel_id=1, source_target_pairs={{0,64},{64,0},{1,65},{65,1},{2,66},{66,2},{3,67},{67,3},{4,68},{68... | collective-permute-start | bytes 1572872 | tf_op jit(solution)/shard_map/ppermute | solution.py:39
  85.3 13.8 %collective-permute-start.20 = (bf16[1024,128]{1,0:T(8,128)(2,1)S(1)}, bf16[1024,128]{1,0:T(8,128)(2,1)S(1)}, u32[]{:S(2)}, u32[]{:S(2)}) collective-permute-start(bf16[1024,128]{1,0:T(8,128)(2,1)S(1)} %slice.6), channel_id=1, source_target_pairs={{0,16},{16,32},{32,48},{48,0},{1,17},{17,33},{33,49},{49,1},{2,18}... | collective-permute-start | bytes 786440 | tf_op jit(solution)/shard_map/ppermute | solution.py:35
  86.7 12.4 %collective-permute-start.21 = (bf16[1024,128]{1,0:T(8,128)(2,1)S(1)}, bf16[1024,128]{1,0:T(8,128)(2,1)S(1)}, u32[]{:S(2)}, u32[]{:S(2)}) collective-permute-start(bf16[1024,128]{1,0:T(8,128)(2,1)S(1)} %slice.7), channel_id=1, source_target_pairs={{0,48},{16,0},{32,16},{48,32},{1,49},{17,1},{33,17},{49,33},{2,50}... | collective-permute-start | bytes 786440 | tf_op jit(solution)/shard_map/ppermute | solution.py:35
  104.2 16.9 %collective-permute-start.24 = (bf16[144,1024]{1,0:T(8,128)(2,1)S(1)}, bf16[144,1024]{1,0:T(8,128)(2,1)S(1)}, u32[]{:S(2)}, u32[]{:S(2)}) collective-permute-start(bf16[144,1024]{1,0:T(8,128)(2,1)S(1)} %get-tuple-element.65), channel_id=1, source_target_pairs={{0,48},{16,0},{32,16},{48,32},{1,49},{17,1},{33,17},{49,33},{2,50}... | collective-permute-start | bytes 884744 | tf_op jit(solution)/shard_map/ppermute | solution.py:35
  106.8 14.3 %collective-permute-start.25 = (bf16[144,1024]{1,0:T(8,128)(2,1)S(1)}, bf16[144,1024]{1,0:T(8,128)(2,1)S(1)}, u32[]{:S(2)}, u32[]{:S(2)}) collective-permute-start(bf16[144,1024]{1,0:T(8,128)(2,1)S(1)} %get-tuple-element.66), channel_id=1, source_target_pairs={{0,32},{16,48},{32,0},{48,16},{1,33},{17,49},{33,1},{49,17},{2,34}... | collective-permute-start | bytes 884744 | tf_op jit(solution)/shard_map/ppermute | solution.py:35
  111.0 12.2 %collective-permute-start.26 = (bf16[144,1024]{1,0:T(8,128)(2,1)S(1)}, bf16[144,1024]{1,0:T(8,128)(2,1)S(1)}, u32[]{:S(2)}, u32[]{:S(2)}) collective-permute-start(bf16[144,1024]{1,0:T(8,128)(2,1)S(1)} %get-tuple-element.67), channel_id=1, source_target_pairs={{0,16},{16,32},{32,48},{48,0},{1,17},{17,33},{33,49},{49,1},{2,18}... | collective-permute-start | bytes 884744 | tf_op jit(solution)/shard_map/ppermute | solution.py:35
  111.0 6.1 %collective-permute-start.27 = (bf16[1024,128]{1,0:T(8,128)(2,1)S(1)}, bf16[1024,128]{1,0:T(8,128)(2,1)S(1)}, u32[]{:S(2)}, u32[]{:S(2)}) collective-permute-start(bf16[1024,128]{1,0:T(8,128)(2,1)S(1)} %collective-permute-done.20.refs_6_), channel_id=1, source_target_pairs={{0,64},{64,0},{1,65},{65,1},{2,66},{66,2},{3,67},{67,3},{4,68},{68... | collective-permute-start | bytes 786440 | tf_op jit(solution)/shard_map/ppermute | solution.py:39
  111.0 10.2 %collective-permute-start.28 = (bf16[1024,128]{1,0:T(8,128)(2,1)S(1)}, bf16[1024,128]{1,0:T(8,128)(2,1)S(1)}, u32[]{:S(2)}, u32[]{:S(2)}) collective-permute-start(bf16[1024,128]{1,0:T(8,128)(2,1)S(1)} %collective-permute-done.21.refs_7_), channel_id=1, source_target_pairs={{0,64},{64,0},{1,65},{65,1},{2,66},{66,2},{3,67},{67,3},{4,68},{68... | collective-permute-start | bytes 786440 | tf_op jit(solution)/shard_map/ppermute | solution.py:39
  123.5 3.6 %collective-permute-start.29 = (bf16[1024,128]{1,0:T(8,128)(2,1)S(1)}, bf16[1024,128]{1,0:T(8,128)(2,1)S(1)}, u32[]{:S(2)}, u32[]{:S(2)}) collective-permute-start(bf16[1024,128]{1,0:T(8,128)(2,1)S(1)} %combine.1.own), channel_id=1, source_target_pairs={{0,8},{8,0},{1,9},{9,1},{2,10},{10,2},{3,11},{11,3},{4,12},{12,4},... | collective-permute-start | bytes 786440 | tf_op jit(solution)/shard_map/ppermute | solution.py:47
  153.4 2.8 %collective-permute-start.30 = (bf16[256,128]{1,0:T(8,128)(2,1)S(1)}, bf16[256,128]{1,0:T(8,128)(2,1)S(1)}, u32[]{:S(2)}, u32[]{:S(2)}) collective-permute-start(bf16[256,128]{1,0:T(8,128)(2,1)S(1)} %get-tuple-element.84), channel_id=1, source_target_pairs={{0,8},{8,0},{1,9},{9,1},{2,10},{10,2},{3,11},{11,3},{4,12},{12,4},... | collective-permute-start | bytes 196616 | tf_op jit(solution)/shard_map/ppermute | solution.py:47
  (23 other events, 279.1 us)

commit v11 on v10

--- a/solution.py
+++ b/solution.py
@@ -182,14 +182,14 @@
     )(idx, routes, router, *pin([own, other, *blocks]))
 
 
-def attend_kernel(count, idx, ends_s, ends_p, *refs):
+def attend_kernel(count, half, idx, ends_s, ends_p, *refs):
     queries, (cache0, cache1, kv0, kv1) = refs[:count], refs[count : count + 4]
     outs = refs[count + 4 : 2 * count + 4]
     q, keep, limits, top, tot, acc, sa, sb, chunk_of, tile_of, sem = refs[2 * count + 4 :]
-    tiles = 2 * count
+    tiles = count
     core = idx[0]
     copies = [
-        pltpu.make_async_copy(r, q.at[pl.ds(1024 * b, 1024)], sem.at[b])
+        pltpu.make_async_copy(r.at[pl.ds(half * R, R)], q.at[pl.ds(R * b, R)], sem.at[b])
         for b, r in enumerate(queries)
     ]
     for i, r in enumerate((cache0, cache1)):
@@ -220,7 +220,7 @@
         return lo, hi, own
 
     for t in range(tiles):
-        first = idx[5 + t // 2] + (t % 2) * 256
+        first = idx[5 + t] + half * 256
         token = first + lax.rem(lax.broadcasted_iota(jnp.int32, (1, R), 1), 256)
         lo, hi, own = allowed_of(token)
         limits[t, 0:1] = lo
@@ -240,7 +240,7 @@
         def visit(n, count):
             i, t = n // tiles, lax.rem(n, tiles)
             base = base_of(i)
-            first = idx[5 + t // 2] + lax.rem(t, 2) * 256
+            first = idx[5 + t] + half * 256
             last = first + 255
             lo_a, hi_a, own_a = allowed_of(first)
             lo_b, hi_b, own_b = allowed_of(last)
@@ -313,23 +313,22 @@
     for t in range(tiles):
         total = tot[t]
         safe = jnp.where(total > 0.0, total, 1.0)
-        cols = slice((t % 2) * R, (t % 2 + 1) * R)
-        out = outs[t // 2]
-        out[0:H, cols] = (acc[t] / safe).astype(BF16)
+        out = outs[t]
+        out[0:H] = (acc[t] / safe).astype(BF16)
         lse = jnp.where(total > 0.0, top[t] * SCALE2 + jnp.log2(safe), FLOOR)
         high = lse.astype(BF16).astype(F32)
         mid = (lse - high).astype(BF16).astype(F32)
         low = lse - high - mid
         row = lax.broadcasted_iota(jnp.int32, (16, R), 0)
         packed = jnp.where(row == 0, high, jnp.where(row == 1, mid, jnp.where(row == 2, low, 0.0)))
-        out[H : H + 16, cols] = packed.astype(BF16)
-
-
-def attend(idx, suffix_lengths, prefix_lengths, qs, caches, kvs):
-    count, tiles = len(qs), 2 * len(qs)
+        out[H : H + 16] = packed.astype(BF16)
+
+
+def attend(half, idx, suffix_lengths, prefix_lengths, qs, caches, kvs):
+    count = tiles = len(qs)
     return pl.pallas_call(
-        functools.partial(attend_kernel, count),
-        out_shape=tuple(jax.ShapeDtypeStruct((H + 16, 1024), BF16) for _ in range(count)),
+        functools.partial(attend_kernel, count, half),
+        out_shape=tuple(jax.ShapeDtypeStruct((H + 16, R), BF16) for _ in range(count)),
         in_specs=[SMEM] * 3 + [HBM] * (count + 4),
         out_specs=tuple([VMEM] * count),
         scratch_shapes=[
@@ -347,7 +346,7 @@
         ],
         compiler_params=pltpu.CompilerParams(vmem_limit_bytes=20 << 20),
         cost_estimate=pl.CostEstimate(
-            flops=count * (3 << 30), bytes_accessed=4 << 20, transcendentals=count << 21
+            flops=count * (3 << 29), bytes_accessed=4 << 20, transcendentals=count << 20
         ),
         name="attend",
     )(idx, suffix_lengths, prefix_lengths, *pin([*qs, *caches, *kvs]))
@@ -362,7 +361,7 @@
     high = jnp.maximum(jnp.maximum(lses[0], lses[1]), jnp.maximum(lses[2], lses[3]))
     share = [jnp.exp2(v - high) for v in lses]
     norm = gates[...] / (share[0] + share[1] + share[2] + share[3])
-    for at in range(0, 1024, 256):
+    for at in range(0, R, 256):
         cols = slice(at, at + 256)
         total = jnp.zeros((H, 256), F32)
         for p, s in zip(parts, share):
@@ -373,7 +372,7 @@
 def combine(gates, parts):
     return pl.pallas_call(
         combine_kernel,
-        out_shape=jax.ShapeDtypeStruct((1024, H), BF16),
+        out_shape=jax.ShapeDtypeStruct((R, H), BF16),
         in_specs=[VMEM] * 5,
         out_specs=VMEM,
         compiler_params=pltpu.CompilerParams(vmem_limit_bytes=8 << 20),
@@ -394,17 +393,14 @@
         copies.append(pltpu.make_async_copy(blocks[k], target, sem.at[k]))
     for c in copies:
         c.start()
-    for half in range(2):
-        rows = slice(half * 256, (half + 1) * 256)
-        wanted = [jnp.broadcast_to(routes[rows, j : j + 1], (256, H)) for j in range(2)]
-        for side, source in enumerate((own, other)):
-            head = core if side == 0 else 1 - core
-            first = source[half * 512 : half * 512 + 256].astype(F32)
-            second = source[half * 512 + 256 : half * 512 + 512].astype(F32)
-            for e in range(E):
-                value = jnp.where(wanted[1] == e, second, 0.0)
-                value = jnp.where(wanted[0] == e, first, value).astype(BF16)
-                padded[rows, pl.ds(pl.multiple_of((head * E + e) * H, H), H)] = value
+    wanted = [jnp.broadcast_to(routes[:, j : j + 1], (256, H)) for j in range(2)]
+    for side, source in enumerate((own, other)):
+        head = core if side == 0 else 1 - core
+        first, second = source[0:256].astype(F32), source[256:512].astype(F32)
+        for e in range(E):
+            value = jnp.where(wanted[1] == e, second, 0.0)
+            value = jnp.where(wanted[0] == e, first, value).astype(BF16)
+            padded[:, pl.ds(pl.multiple_of((head * E + e) * H, H), H)] = value
     for c in copies:
         c.wait()
     for k in range(0, 8, 2):
@@ -417,16 +413,16 @@
 def project_out(idx, routes, own, other, blocks):
     return pl.pallas_call(
         out_kernel,
-        out_shape=jax.ShapeDtypeStruct((8, 512, H), BF16),
+        out_shape=jax.ShapeDtypeStruct((8, 256, H), BF16),
         in_specs=[SMEM, VMEM, VMEM, VMEM] + [HBM] * 10,
         out_specs=VMEM,
         scratch_shapes=[
             pltpu.VMEM((8, 2048, H), BF16),
-            pltpu.VMEM((512, 2048), BF16),
+            pltpu.VMEM((256, 2048), BF16),
             pltpu.SemaphoreType.DMA((10,)),
         ],
         compiler_params=pltpu.CompilerParams(vmem_limit_bytes=20 << 20),
-        cost_estimate=pl.CostEstimate(flops=4 << 30, bytes_accessed=6 << 20, transcendentals=0),
+        cost_estimate=pl.CostEstimate(flops=2 << 30, bytes_accessed=6 << 20, transcendentals=0),
         name="project_out",
     )(idx, routes, own, other, *pin(blocks))
 
@@ -492,7 +488,6 @@
     )
     kvs = [kv, across_x(kv)]
     qs = [q] + [along_y(q, k) for k in (1, 2, 3)]
-    qs[0], o_ym, o_yp = lax.optimization_barrier((q, o_ym, o_yp))
     o_a, up, down, kvs[1] = lax.optimization_barrier((o_a, o_yp[:1024], o_ym[1024:], kvs[1]))
     far0, far1 = along_y(up, 1), along_y(down, 3)
     o_am, o_ap = across_x(o_ym), across_x(o_yp)
@@ -501,27 +496,34 @@
     mine, partner = xl * 4 + y, (1 - xl) * 4 + y
     at = [c, mine * 1536, partner * 1536, mine * 512, partner * 512]
     lengths = (suffix_lengths, prefix_lengths)
-    parts = list(attend(table(at + firsts[:1]), *lengths, qs[:1], caches, kvs))
-    parts += list(attend(table(at + firsts[1:]), *lengths, qs[1:], caches, kvs))
-    parts[1:], far0, far1, o_am, o_ap = lax.optimization_barrier(
-        (parts[1:], far0, far1, o_am, o_ap)
-    )
+    at = table(at + firsts)
+    gate_rows = gates.reshape(2, 256, 2).transpose(0, 2, 1).reshape(2, 1, R)
+    parts = [list(attend(0, at, *lengths, qs, caches, kvs))]
+    parts[0][1:], far0, far1 = lax.optimization_barrier((parts[0][1:], far0, far1))
+    qs, o_am, o_ap = lax.optimization_barrier((qs, o_am, o_ap))
+    parts.append(list(attend(1, at, *lengths, qs, caches, kvs)))
     for k in range(1, 4):
-        parts[k] = along_y(parts[k], 4 - k)
+        parts[0][k] = along_y(parts[0][k], 4 - k)
+    parts = lax.optimization_barrier(parts)
+    for k in range(1, 4):
+        parts[1][k] = along_y(parts[1][k], 4 - k)
     afar0, afar1 = across_x(far0), across_x(far1)
-    parts, afar0, afar1 = lax.optimization_barrier((parts, afar0, afar1))
+    parts[0], afar0, afar1 = lax.optimization_barrier((parts[0], afar0, afar1))
     out_blocks = [out_weight, o_a, o_ym, o_am, o_yp, o_ap, far0, far1, afar0, afar1]
-    gate_row = gates.reshape(2, 256, 2).transpose(0, 2, 1).reshape(1, 1024)
-    attended = combine(gate_row, parts)
-
-    sums = project_out(
-        table(chips + [c]), both_routes, attended, across_core(attended), out_blocks
-    )
-    sums = lax.all_to_all(sums, NARROW, 0, 0, tiled=True)
-    total = jnp.sum(sums.astype(F32), axis=0)
-    here = lax.dynamic_slice_in_dim(total, c * 256, 256, 0).astype(BF16)
-    there = lax.dynamic_slice_in_dim(total, (1 - c) * 256, 256, 0).astype(BF16)
-    there = across_core(there)
+    totals = []
+    for half in range(2):
+        attended = combine(gate_rows[half], parts[half])
+        sums = project_out(
+            table(chips + [c]),
+            both_routes[half * 256 : (half + 1) * 256],
+            attended,
+            across_core(attended),
+            out_blocks,
+        )
+        sums = lax.all_to_all(sums, NARROW, 0, 0, tiled=True)
+        totals.append(jnp.sum(sums.astype(F32), axis=0).astype(BF16))
+    here = jnp.where(first_core, totals[0], totals[1])
+    there = across_core(jnp.where(first_core, totals[1], totals[0]))
     return jnp.where(
         first_core,
         jnp.concatenate([here, there], axis=1),

time: 158 us -> 166 us (1.051); the launches traced: 157 us -> 163 us
  blocking collectives: 43.9 us -> 23.5 us
  starting transfers between devices: 36.9 us -> 49 us
  Pallas kernels: 29 us -> 38.5 us
  waiting for transfers between devices: 41.7 us -> 44.9 us
  local copies, waits for them, and re-layouts: 3.02 us -> 4.72 us
    all_to_all x1 -> x0, blocking collectives: 20.4 us -> none  [on_device(): sums = lax.all_to_all(sums, NARROW, 0, 0, tiled=True)]
    all_to_all x0 -> x2, waiting for transfers between devices: none -> 13.2 us  [on_device(): sums = lax.all_to_all(sums, NARROW, 0, 0, tiled=True)]
    pallas_call x4 -> x6, Pallas kernels: 20.3 us -> 29.8 us  [the longest x2 19.7 us: attend(): pl.pallas_call(functools.partial(attend_kernel, count, half), out_shape=t...]
    ppermute x9, waiting for transfers between devices: 11.1 us -> 3.62 us  [across_x(): return lax.ppermute(x, 'xl', [(0, 1), (1, 0)])]
    all_to_all x0 -> x2, starting transfers between devices: none -> 7 us  [on_device(): sums = lax.all_to_all(sums, NARROW, 0, 0, tiled=True)]
    ppermute x6 -> x7, starting transfers between devices: 9.11 us -> 13.5 us  [across_core(): return lax.ppermute(x, 'c', [(0, 1), (1, 0)])]
    ppermute x15 -> x18, waiting for transfers between devices: 28 us -> 26.2 us  [along_y(): return lax.ppermute(x, 'y', [(i, (i + k) % 4) for i in range(4)])]
    unnamed x48 -> x49, local copies, waits for them, and re-layouts: 0.96 us -> 2.69 us
  transfers between devices with their start and end apart: 31 -> 37, of which waited for: 16 -> 15; matrix products, arithmetic and copies ran while one was open for 2% -> 2% of each run, Pallas kernels for 15% -> 23%
where the time goes in v11:
time: 166 us; the launch traced here: 163 us
  starting transfers between devices  49 us (30%)
  waiting for transfers between devices  44.9 us (27%)
  Pallas kernels  38.5 us (23%)
  blocking collectives  23.5 us (14%)
  local copies, waits for them, and re-layouts  4.72 us (3%)
  other arithmetic  1.92 us (1%)
    ppermute x18, waiting for transfers between devices, along_y(): return lax.ppermute(x, 'y', [(i, (i + k) % 4) for i in range(4)])  26.2 us
    all_gather x2, blocking collectives, on_device(): blocks = [lax.all_gather(v, 'z', axis=0) for v in (tokens, half_row)]  23.5 us
    pallas_call x2, Pallas kernels, attend(): pl.pallas_call(functools.partial(attend_kernel, count, half), out_shape=t...  19.7 us
    ppermute x18, starting transfers between devices, along_y(): return lax.ppermute(x, 'y', [(i, (i + k) % 4) for i in range(4)])  18.5 us
    ppermute x7, starting transfers between devices, across_core(): return lax.ppermute(x, 'c', [(0, 1), (1, 0)])  13.5 us
    all_to_all x2, waiting for transfers between devices, on_device(): sums = lax.all_to_all(sums, NARROW, 0, 0, tiled=True)  13.2 us
    pallas_call x2, Pallas kernels, project_out(): pl.pallas_call(out_kernel, out_shape=jax.ShapeDtypeStruct((8, 256, H), BF...  9.63 us
    ppermute x9, starting transfers between devices, across_x(): return lax.ppermute(x, 'xl', [(0, 1), (1, 0)])  8.06 us
  transfers between devices with their start and end apart: 37, of which 15 were waited for; matrix products, arithmetic and copies ran while one was open for 2% of the time, Pallas kernels for 23%

profile of v11, /device:TPU:3, one launch (start us, length us, event | category | flops | bytes accessed | tf_op | source)
XLA Modules:
  0.0 163.0 jit_solution(10261225876823603515)
XLA Ops:
  0.0 1.8 %collective-permute-start.5 = (bf16[256,256]{1,0:T(8,128)(2,1)}, bf16[256,256]{1,0:T(8,128)(2,1)S(1)}, u32[]{:S(2)}, u32[]{:S(2)}) collective-permute-start(bf16[256,256]{1,0:T(8,128)(2,1)} %param.10), channel_id=1, source_target_pairs={{0,1},{1,0},{2,3},{3,2},{4,5},{5,4},{6,7},{7,6},{8,9},{9,8},{10,11... | collective-permute-start | bytes 393224 | tf_op jit(solution)/shard_map/ppermute | solution.py:43
  8.0 2.9 %collective-permute-start.1 = (bf16[2,1280,128]{2,1,0:T(8,128)(2,1)}, bf16[2,1280,128]{2,1,0:T(8,128)(2,1)}, u32[]{:S(2)}, u32[]{:S(2)}) collective-permute-start(bf16[2,1280,128]{2,1,0:T(8,128)(2,1)} %pad_maximum_fusion.1.refs_0_), channel_id=1, source_target_pairs={{0,32},{16,48},{32,0},{48,16},{1,33},{17,49},{33,1},{49,17},{2,34}... | collective-permute-start | bytes 1966088 | tf_op jit(solution)/shard_map/ppermute | solution.py:35
  12.7 12.4 %all-gather = bf16[1024,256]{1,0:T(8,128)(2,1)S(1)} all-gather(bf16[256,256]{1,0:T(8,128)(2,1)S(1)} %copy-done.8), channel_id=2, replica_groups=mesh['xl'=2,'y'=4,'c'=2,'z'=4,'xh'=2] {'z'}, dimensions={0}, use_global_device_ids=true | all-gather | bytes 655360 | tf_op jit(solution)/shard_map/all_gather | solution.py:471
  25.4 11.1 %all-gather.1 = bf16[1024,256]{1,0:T(8,128)(2,1)S(1)} all-gather(bf16[256,256]{1,0:T(8,128)(2,1)S(1)} %collective-permute-done.5), channel_id=3, replica_groups=mesh['xl'=2,'y'=4,'c'=2,'z'=4,'xh'=2] {'z'}, dimensions={0}, use_global_device_ids=true | all-gather | bytes 655360 | tf_op jit(solution)/shard_map/all_gather | solution.py:471
  37.9 2.0 %collective-permute-done.2.refs_2_ = bf16[2,1280,128]{2,1,0:T(8,128)(2,1)} collective-permute-done((bf16[2,1280,128]{2,1,0:T(8,128)(2,1)}, bf16[2,1280,128]{2,1,0:T(8,128)(2,1)}, u32[]{:S(2)}, u32[]{:S(2)}) %collective-permute-start.2) | collective-permute-done | bytes 655392 | tf_op jit(solution)/shard_map/ppermute | solution.py:35
  40.5 3.3 %collective-permute-start.9 = (bf16[256,2048]{1,0:T(8,128)(2,1)S(1)}, bf16[256,2048]{1,0:T(8,128)(2,1)}, u32[]{:S(2)}, u32[]{:S(2)}) collective-permute-start(bf16[256,2048]{1,0:T(8,128)(2,1)S(1)} %normalise.1.own), channel_id=1, source_target_pairs={{0,8},{8,0},{1,9},{9,1},{2,10},{10,2},{3,11},{11,3},{4,12},{12,4},... | collective-permute-start | bytes 3145736 | tf_op jit(solution)/shard_map/ppermute | solution.py:47
  43.8 2.0 %collective-permute-start.10 = (bf16[2,1280,128]{2,1,0:T(8,128)(2,1)}, bf16[2,1280,128]{2,1,0:T(8,128)(2,1)S(1)}, u32[]{:S(2)}, u32[]{:S(2)}) collective-permute-start(bf16[2,1280,128]{2,1,0:T(8,128)(2,1)} %collective-permute-done.4.refs_1_), channel_id=1, source_target_pairs={{0,48},{16,0},{32,16},{48,32},{1,49},{17,1},{33,17},{49,33},{2,50}... | collective-permute-start | bytes 1966088 | tf_op jit(solution)/shard_map/ppermute | solution.py:35
  47.0 13.4 %collective-permute-done.10.refs_3_ = bf16[2,1280,128]{2,1,0:T(8,128)(2,1)S(1)} collective-permute-done((bf16[2,1280,128]{2,1,0:T(8,128)(2,1)}, bf16[2,1280,128]{2,1,0:T(8,128)(2,1)S(1)}, u32[]{:S(2)}, u32[]{:S(2)}) %collective-permute-start.10) | collective-permute-done | bytes 655392 | tf_op jit(solution)/shard_map/ppermute | solution.py:35
  61.2 2.0 %collective-permute-done.11.refs_7_ = bf16[2,1280,128]{2,1,0:T(8,128)(2,1)} collective-permute-done((bf16[2,1280,128]{2,1,0:T(8,128)(2,1)}, bf16[2,1280,128]{2,1,0:T(8,128)(2,1)}, u32[]{:S(2)}, u32[]{:S(2)}) %collective-permute-start.11) | collective-permute-done | bytes 655392 | tf_op jit(solution)/shard_map/ppermute | solution.py:35
  65.9 7.4 %project.1 = (bf16[1024,128]{1,0:T(8,128)(2,1)S(1)}, bf16[512,256]{1,0:T(8,128)(2,1)S(1)}, f32[512,2]{1,0:T(8,128)S(1)}) custom-call(s32[9]{0:T(128)S(1)} %stack.156.idx, s32[512,2]{1,0:T(8,128)S(1)} %broadcast_select_fusion.routes, bf16[8,2048]{1,0:T(8,128)(2,1)S(1)} %bitcast.55, bf16[256,2048]{1,0:T(8,128)(2,1)} %copy-done, ...), custom_call_target="tpu_custom_call" | custom-call | flops 6442450944 | bytes 8388608 | tf_op jit(solution)/shard_map/project/pallas_call | solution.py:164
  73.7 2.1 %collective-permute-done.18.refs_2_ = bf16[2048,128]{1,0:T(8,128)(2,1)S(1)} collective-permute-done((bf16[2048,128]{1,0:T(8,128)(2,1)}, bf16[2048,128]{1,0:T(8,128)(2,1)S(1)}, u32[]{:S(2)}, u32[]{:S(2)}) %collective-permute-start.18) | collective-permute-done | bytes 524320 | tf_op jit(solution)/shard_map/ppermute | solution.py:35
  75.8 1.4 collective-permute-start.14
  78.8 1.4 collective-permute-start.25
  80.2 2.1 %collective-permute-done.19.refs_7_ = bf16[512,256]{1,0:T(8,128)(2,1)S(1)} collective-permute-done((bf16[512,256]{1,0:T(8,128)(2,1)S(1)}, bf16[512,256]{1,0:T(8,128)(2,1)S(1)}, u32[]{:S(2)}, u32[]{:S(2)}) %collective-permute-start.19) | collective-permute-done | bytes 262176 | tf_op jit(solution)/shard_map/ppermute | solution.py:39
  83.4 2.3 %collective-permute-done.13.refs_1_ = bf16[1024,128]{1,0:T(8,128)(2,1)S(1)} collective-permute-done((bf16[1024,128]{1,0:T(8,128)(2,1)S(1)}, bf16[1024,128]{1,0:T(8,128)(2,1)S(1)}, u32[]{:S(2)}, u32[]{:S(2)}) %collective-permute-start.13) | collective-permute-done | bytes 262176 | tf_op jit(solution)/shard_map/ppermute | solution.py:35
  85.8 1.5 collective-permute-done.14.refs_2_
  88.5 1.4 collective-permute-done.15.refs_3_
  89.9 9.5 %attend.2 = (bf16[144,512]{1,0:T(8,128)(2,1)S(1)}, bf16[144,512]{1,0:T(8,128)(2,1)S(1)}, bf16[144,512]{1,0:T(8,128)(2,1)S(1)}, bf16[144,512]{1,0:T(8,128)(2,1)S(1)}) custom-call(s32[9]{0:T(128)S(1)} %stack.188.idx, s32[4]{0:T(128)S(1)} %copy-done.4, s32[4]{0:T(128)S(1)} %copy-done.5, bf16[1024,128]{1,0:T(8,128)(2,1)} %copy-done.1, ...), custom_call_target="tpu_custom_call" | custom-call | flops 6442450944 | bytes 4194304 | tf_op jit(solution)/shard_map/attend/pallas_call | solution.py:329
  99.4 1.6 collective-permute-start.22
  101.0 2.1 %collective-permute-start.23 = (bf16[144,512]{1,0:T(8,128)(2,1)S(1)}, bf16[144,512]{1,0:T(8,128)(2,1)S(1)}, u32[]{:S(2)}, u32[]{:S(2)}) collective-permute-start(bf16[144,512]{1,0:T(8,128)(2,1)S(1)} %get-tuple-element.78), channel_id=1, source_target_pairs={{0,32},{16,48},{32,0},{48,16},{1,33},{17,49},{33,1},{49,17},{2,34}... | collective-permute-start | bytes 442376 | tf_op jit(solution)/shard_map/ppermute | solution.py:35
  103.2 1.5 collective-permute-done.26.refs_5_
  105.9 10.2 %attend.3 = (bf16[144,512]{1,0:T(8,128)(2,1)S(1)}, bf16[144,512]{1,0:T(8,128)(2,1)S(1)}, bf16[144,512]{1,0:T(8,128)(2,1)S(1)}, bf16[144,512]{1,0:T(8,128)(2,1)S(1)}) custom-call(s32[9]{0:T(128)S(1)} %stack.188.idx, s32[4]{0:T(128)S(1)} %copy-done.4, s32[4]{0:T(128)S(1)} %copy-done.5, bf16[1024,128]{1,0:T(8,128)(2,1)} %copy-done.1, ...), custom_call_target="tpu_custom_call" | custom-call | flops 6442450944 | bytes 4194304 | tf_op jit(solution)/shard_map/attend/pallas_call | solution.py:329
  117.0 5.1 %collective-permute-start.29 = (bf16[512,128]{1,0:T(8,128)(2,1)S(1)}, bf16[512,128]{1,0:T(8,128)(2,1)S(1)}, u32[]{:S(2)}, u32[]{:S(2)}) collective-permute-start(bf16[512,128]{1,0:T(8,128)(2,1)S(1)} %combine.2.own), channel_id=1, source_target_pairs={{0,8},{8,0},{1,9},{9,1},{2,10},{10,2},{3,11},{11,3},{4,12},{12,4},... | collective-permute-start | bytes 393224 | tf_op jit(solution)/shard_map/ppermute | solution.py:47
  122.1 1.3 collective-permute-start.30
  123.5 2.6 %collective-permute-start.31 = (bf16[144,512]{1,0:T(8,128)(2,1)S(1)}, bf16[144,512]{1,0:T(8,128)(2,1)S(1)}, u32[]{:S(2)}, u32[]{:S(2)}) collective-permute-start(bf16[144,512]{1,0:T(8,128)(2,1)S(1)} %get-tuple-element.105), channel_id=1, source_target_pairs={{0,32},{16,48},{32,0},{48,16},{1,33},{17,49},{33,1},{49,17},{2,34}... | collective-permute-start | bytes 442376 | tf_op jit(solution)/shard_map/ppermute | solution.py:35
  126.1 4.8 %project_out.2 = bf16[8,256,128]{2,1,0:T(8,128)(2,1)} custom-call(s32[9]{0:T(128)S(1)} %stack.156.idx, s32[256,2]{1,0:T(8,128)S(1)} %get-tuple-element.111.routes, bf16[512,128]{1,0:T(8,128)(2,1)S(1)} %combine.2.own, bf16[512,128]{1,0:T(8,128)(2,1)S(1)} %collective-permute-done.29.other, bf16[2048,128]{1,0:T(8,128)(2,1)} %refs_0_.3, ...), custom_call_target="tpu_custom_call" | custom-call | flops 2147483648 | bytes 6291456 | tf_op jit(solution)/shard_map/project_out/pallas_call | solution.py:414
  130.9 3.5 %all-to-all-start = ((bf16[8,256,128]{2,1,0:T(8,128)(2,1)}), bf16[8,256,128]{2,1,0:T(8,128)(2,1)S(1)}, u32[]{:S(2)}, u32[]{:S(2)}) async-start(bf16[8,256,128]{2,1,0:T(8,128)(2,1)} %project_out.2), calls=%async_computation | async-start | bytes 1048576 | tf_op jit(solution)/shard_map/all_to_all | solution.py:523
  136.6 4.8 %project_out.3 = bf16[8,256,128]{2,1,0:T(8,128)(2,1)} custom-call(s32[9]{0:T(128)S(1)} %stack.156.idx, s32[256,2]{1,0:T(8,128)S(1)} %get-tuple-element.112.routes, bf16[512,128]{1,0:T(8,128)(2,1)S(1)} %combine.3.own, bf16[512,128]{1,0:T(8,128)(2,1)S(1)} %collective-permute-done.33.other, bf16[2048,128]{1,0:T(8,128)(2,1)} %refs_0_.3, ...), custom_call_target="tpu_custom_call" | custom-call | flops 2147483648 | bytes 6291456 | tf_op jit(solution)/shard_map/project_out/pallas_call | solution.py:414
  141.4 3.8 %all-to-all-done = bf16[8,256,128]{2,1,0:T(8,128)(2,1)S(1)} async-done(((bf16[8,256,128]{2,1,0:T(8,128)(2,1)}), bf16[8,256,128]{2,1,0:T(8,128)(2,1)S(1)}, u32[]{:S(2)}, u32[]{:S(2)}) %all-to-all-start) | async-done | bytes 524320 | tf_op jit(solution)/shard_map/all_to_all | solution.py:523
  145.2 3.5 %all-to-all-start.1 = ((bf16[8,256,128]{2,1,0:T(8,128)(2,1)}), bf16[8,256,128]{2,1,0:T(8,128)(2,1)S(1)}, u32[]{:S(2)}, u32[]{:S(2)}) async-start(bf16[8,256,128]{2,1,0:T(8,128)(2,1)} %project_out.3), calls=%async_computation.1 | async-start | bytes 1048576 | tf_op jit(solution)/shard_map/all_to_all | solution.py:523
  148.7 9.5 %all-to-all-done.1 = bf16[8,256,128]{2,1,0:T(8,128)(2,1)S(1)} async-done(((bf16[8,256,128]{2,1,0:T(8,128)(2,1)}), bf16[8,256,128]{2,1,0:T(8,128)(2,1)S(1)}, u32[]{:S(2)}, u32[]{:S(2)}) %all-to-all-start.1) | async-done | bytes 524320 | tf_op jit(solution)/shard_map/all_to_all | solution.py:523
  158.3 3.1 %collective-permute-start.34 = (bf16[256,128]{1,0:T(8,128)(2,1)S(1)}, bf16[256,128]{1,0:T(8,128)(2,1)S(1)}, u32[]{:S(2)}, u32[]{:S(2)}) collective-permute-start(bf16[256,128]{1,0:T(8,128)(2,1)S(1)} %get-tuple-element.114), channel_id=1, source_target_pairs={{0,8},{8,0},{1,9},{9,1},{2,10},{10,2},{3,11},{11,3},{4,12},{12,4},... | collective-permute-start | bytes 196616 | tf_op jit(solution)/shard_map/ppermute | solution.py:47
  (124 shorter events, 25.0 us)
Async XLA Ops:
  0.0 12.4 %collective-permute-start.5 = (bf16[256,256]{1,0:T(8,128)(2,1)}, bf16[256,256]{1,0:T(8,128)(2,1)S(1)}, u32[]{:S(2)}, u32[]{:S(2)}) collective-permute-start(bf16[256,256]{1,0:T(8,128)(2,1)} %param.10), channel_id=1, source_target_pairs={{0,1},{1,0},{2,3},{3,2},{4,5},{5,4},{6,7},{7,6},{8,9},{9,8},{10,11... | collective-permute-start | bytes 393224 | tf_op jit(solution)/shard_map/ppermute | solution.py:43
  5.9 34.7 %collective-permute-start.7 = (bf16[2,768,256]{2,1,0:T(8,128)(2,1)S(1)}, bf16[2,768,256]{2,1,0:T(8,128)(2,1)}, u32[]{:S(2)}, u32[]{:S(2)}) collective-permute-start(bf16[2,768,256]{2,1,0:T(8,128)(2,1)S(1)} %pad_maximum_fusion.refs_4_), channel_id=1, source_target_pairs={{0,64},{64,0},{1,65},{65,1},{2,66},{66,2},{3,67},{67,3},{4,68},{68... | collective-permute-start | bytes 2359304 | tf_op jit(solution)/shard_map/ppermute | solution.py:39
  8.0 29.9 %collective-permute-start.1 = (bf16[2,1280,128]{2,1,0:T(8,128)(2,1)}, bf16[2,1280,128]{2,1,0:T(8,128)(2,1)}, u32[]{:S(2)}, u32[]{:S(2)}) collective-permute-start(bf16[2,1280,128]{2,1,0:T(8,128)(2,1)} %pad_maximum_fusion.1.refs_0_), channel_id=1, source_target_pairs={{0,32},{16,48},{32,0},{48,16},{1,33},{17,49},{33,1},{49,17},{2,34}... | collective-permute-start | bytes 1966088 | tf_op jit(solution)/shard_map/ppermute | solution.py:35
  10.9 28.9 %collective-permute-start.2 = (bf16[2,1280,128]{2,1,0:T(8,128)(2,1)}, bf16[2,1280,128]{2,1,0:T(8,128)(2,1)}, u32[]{:S(2)}, u32[]{:S(2)}) collective-permute-start(bf16[2,1280,128]{2,1,0:T(8,128)(2,1)} %pad_maximum_fusion.1.refs_0_), channel_id=1, source_target_pairs={{0,48},{16,0},{32,16},{48,32},{1,49},{17,1},{33,17},{49,33},{2,50}... | collective-permute-start | bytes 1966088 | tf_op jit(solution)/shard_map/ppermute | solution.py:35
  11.7 28.8 %collective-permute-start.3 = (bf16[2,1280,128]{2,1,0:T(8,128)(2,1)}, bf16[2,1280,128]{2,1,0:T(8,128)(2,1)}, u32[]{:S(2)}, u32[]{:S(2)}) collective-permute-start(bf16[2,1280,128]{2,1,0:T(8,128)(2,1)} %pad_maximum_fusion.1.refs_0_), channel_id=1, source_target_pairs={{0,16},{16,32},{32,48},{48,0},{1,17},{17,33},{33,49},{49,1},{2,18}... | collective-permute-start | bytes 1966088 | tf_op jit(solution)/shard_map/ppermute | solution.py:35
  12.4 28.1 %collective-permute-start.4 = (bf16[2,1280,128]{2,1,0:T(8,128)(2,1)}, bf16[2,1280,128]{2,1,0:T(8,128)(2,1)}, u32[]{:S(2)}, u32[]{:S(2)}) collective-permute-start(bf16[2,1280,128]{2,1,0:T(8,128)(2,1)} %pad_maximum_fusion.1.refs_0_), channel_id=1, source_target_pairs={{0,64},{64,0},{1,65},{65,1},{2,66},{66,2},{3,67},{67,3},{4,68},{68... | collective-permute-start | bytes 1966088 | tf_op jit(solution)/shard_map/ppermute | solution.py:39
  40.5 25.4 %collective-permute-start.9 = (bf16[256,2048]{1,0:T(8,128)(2,1)S(1)}, bf16[256,2048]{1,0:T(8,128)(2,1)}, u32[]{:S(2)}, u32[]{:S(2)}) collective-permute-start(bf16[256,2048]{1,0:T(8,128)(2,1)S(1)} %normalise.1.own), channel_id=1, source_target_pairs={{0,8},{8,0},{1,9},{9,1},{2,10},{10,2},{3,11},{11,3},{4,12},{12,4},... | collective-permute-start | bytes 3145736 | tf_op jit(solution)/shard_map/ppermute | solution.py:47
  43.8 16.6 %collective-permute-start.10 = (bf16[2,1280,128]{2,1,0:T(8,128)(2,1)}, bf16[2,1280,128]{2,1,0:T(8,128)(2,1)S(1)}, u32[]{:S(2)}, u32[]{:S(2)}) collective-permute-start(bf16[2,1280,128]{2,1,0:T(8,128)(2,1)} %collective-permute-done.4.refs_1_), channel_id=1, source_target_pairs={{0,48},{16,0},{32,16},{48,32},{1,49},{17,1},{33,17},{49,33},{2,50}... | collective-permute-start | bytes 1966088 | tf_op jit(solution)/shard_map/ppermute | solution.py:35
  45.8 17.5 %collective-permute-start.11 = (bf16[2,1280,128]{2,1,0:T(8,128)(2,1)}, bf16[2,1280,128]{2,1,0:T(8,128)(2,1)}, u32[]{:S(2)}, u32[]{:S(2)}) collective-permute-start(bf16[2,1280,128]{2,1,0:T(8,128)(2,1)} %collective-permute-done.4.refs_1_), channel_id=1, source_target_pairs={{0,16},{16,32},{32,48},{48,0},{1,17},{17,33},{33,49},{49,1},{2,18}... | collective-permute-start | bytes 1966088 | tf_op jit(solution)/shard_map/ppermute | solution.py:35
  45.8 20.1 %collective-permute-start.12 = (bf16[2,1280,128]{2,1,0:T(8,128)(2,1)}, bf16[2,1280,128]{2,1,0:T(8,128)(2,1)}, u32[]{:S(2)}, u32[]{:S(2)}) collective-permute-start(bf16[2,1280,128]{2,1,0:T(8,128)(2,1)} %collective-permute-done.1.refs_4_), channel_id=1, source_target_pairs={{0,64},{64,0},{1,65},{65,1},{2,66},{66,2},{3,67},{67,3},{4,68},{68... | collective-permute-start | bytes 1966088 | tf_op jit(solution)/shard_map/ppermute | solution.py:39
  63.3 12.6 %collective-permute-start.18 = (bf16[2048,128]{1,0:T(8,128)(2,1)}, bf16[2048,128]{1,0:T(8,128)(2,1)S(1)}, u32[]{:S(2)}, u32[]{:S(2)}) collective-permute-start(bf16[2048,128]{1,0:T(8,128)(2,1)} %refs_0_.3), channel_id=1, source_target_pairs={{0,48},{16,0},{32,16},{48,32},{1,49},{17,1},{33,17},{49,33},{2,50}... | collective-permute-start | bytes 1572872 | tf_op jit(solution)/shard_map/ppermute | solution.py:35
  64.3 13.7 %collective-permute-start.17 = (bf16[2048,128]{1,0:T(8,128)(2,1)}, bf16[2048,128]{1,0:T(8,128)(2,1)S(1)}, u32[]{:S(2)}, u32[]{:S(2)}) collective-permute-start(bf16[2048,128]{1,0:T(8,128)(2,1)} %refs_0_.3), channel_id=1, source_target_pairs={{0,16},{16,32},{32,48},{48,0},{1,17},{17,33},{33,49},{49,1},{2,18}... | collective-permute-start | bytes 1572872 | tf_op jit(solution)/shard_map/ppermute | solution.py:35
  64.8 14.0 %collective-permute-start.16 = (bf16[2048,128]{1,0:T(8,128)(2,1)}, bf16[2048,128]{1,0:T(8,128)(2,1)}, u32[]{:S(2)}, u32[]{:S(2)}) collective-permute-start(bf16[2048,128]{1,0:T(8,128)(2,1)} %refs_0_.3), channel_id=1, source_target_pairs={{0,64},{64,0},{1,65},{65,1},{2,66},{66,2},{3,67},{67,3},{4,68},{68... | collective-permute-start | bytes 1572872 | tf_op jit(solution)/shard_map/ppermute | solution.py:39
  73.3 8.9 %collective-permute-start.19 = (bf16[512,256]{1,0:T(8,128)(2,1)S(1)}, bf16[512,256]{1,0:T(8,128)(2,1)S(1)}, u32[]{:S(2)}, u32[]{:S(2)}) collective-permute-start(bf16[512,256]{1,0:T(8,128)(2,1)S(1)} %get-tuple-element.68.refs_6_), channel_id=1, source_target_pairs={{0,64},{64,0},{1,65},{65,1},{2,66},{66,2},{3,67},{67,3},{4,68},{68... | collective-permute-start | bytes 786440 | tf_op jit(solution)/shard_map/ppermute | solution.py:39
  73.7 12.0 %collective-permute-start.13 = (bf16[1024,128]{1,0:T(8,128)(2,1)S(1)}, bf16[1024,128]{1,0:T(8,128)(2,1)S(1)}, u32[]{:S(2)}, u32[]{:S(2)}) collective-permute-start(bf16[1024,128]{1,0:T(8,128)(2,1)S(1)} %get-tuple-element.80.refs_0_), channel_id=1, source_target_pairs={{0,16},{16,32},{32,48},{48,0},{1,17},{17,33},{33,49},{49,1},{2,18}... | collective-permute-start | bytes 786440 | tf_op jit(solution)/shard_map/ppermute | solution.py:35
  75.8 11.4 %collective-permute-start.14 = (bf16[1024,128]{1,0:T(8,128)(2,1)S(1)}, bf16[1024,128]{1,0:T(8,128)(2,1)}, u32[]{:S(2)}, u32[]{:S(2)}) collective-permute-start(bf16[1024,128]{1,0:T(8,128)(2,1)S(1)} %get-tuple-element.80.refs_0_), channel_id=1, source_target_pairs={{0,32},{16,48},{32,0},{48,16},{1,33},{17,49},{33,1},{49,17},{2,34}... | collective-permute-start | bytes 786440 | tf_op jit(solution)/shard_map/ppermute | solution.py:35
  78.0 11.8 %collective-permute-start.15 = (bf16[1024,128]{1,0:T(8,128)(2,1)S(1)}, bf16[1024,128]{1,0:T(8,128)(2,1)}, u32[]{:S(2)}, u32[]{:S(2)}) collective-permute-start(bf16[1024,128]{1,0:T(8,128)(2,1)S(1)} %get-tuple-element.80.refs_0_), channel_id=1, source_target_pairs={{0,48},{16,0},{32,16},{48,32},{1,49},{17,1},{33,17},{49,33},{2,50}... | collective-permute-start | bytes 786440 | tf_op jit(solution)/shard_map/ppermute | solution.py:35
  78.8 24.4 %collective-permute-start.25 = (bf16[2048,128]{1,0:T(8,128)(2,1)S(1)}, bf16[2048,128]{1,0:T(8,128)(2,1)S(1)}, u32[]{:S(2)}, u32[]{:S(2)}) collective-permute-start(bf16[2048,128]{1,0:T(8,128)(2,1)S(1)} %collective-permute-done.18.refs_2_), channel_id=1, source_target_pairs={{0,64},{64,0},{1,65},{65,1},{2,66},{66,2},{3,67},{67,3},{4,68},{68... | collective-permute-start | bytes 1572872 | tf_op jit(solution)/shard_map/ppermute | solution.py:39
  82.3 22.5 %collective-permute-start.26 = (bf16[2048,128]{1,0:T(8,128)(2,1)S(1)}, bf16[2048,128]{1,0:T(8,128)(2,1)S(1)}, u32[]{:S(2)}, u32[]{:S(2)}) collective-permute-start(bf16[2048,128]{1,0:T(8,128)(2,1)S(1)} %collective-permute-done.17.refs_4_), channel_id=1, source_target_pairs={{0,64},{64,0},{1,65},{65,1},{2,66},{66,2},{3,67},{67,3},{4,68},{68... | collective-permute-start | bytes 1572872 | tf_op jit(solution)/shard_map/ppermute | solution.py:39
  85.8 13.6 %collective-permute-start.20 = (bf16[1024,128]{1,0:T(8,128)(2,1)S(1)}, bf16[1024,128]{1,0:T(8,128)(2,1)S(1)}, u32[]{:S(2)}, u32[]{:S(2)}) collective-permute-start(bf16[1024,128]{1,0:T(8,128)(2,1)S(1)} %slice.27), channel_id=1, source_target_pairs={{0,16},{16,32},{32,48},{48,0},{1,17},{17,33},{33,49},{49,1},{2,18}... | collective-permute-start | bytes 786440 | tf_op jit(solution)/shard_map/ppermute | solution.py:35
  87.3 12.2 %collective-permute-start.21 = (bf16[1024,128]{1,0:T(8,128)(2,1)S(1)}, bf16[1024,128]{1,0:T(8,128)(2,1)S(1)}, u32[]{:S(2)}, u32[]{:S(2)}) collective-permute-start(bf16[1024,128]{1,0:T(8,128)(2,1)S(1)} %slice.28), channel_id=1, source_target_pairs={{0,48},{16,0},{32,16},{48,32},{1,49},{17,1},{33,17},{49,33},{2,50}... | collective-permute-start | bytes 786440 | tf_op jit(solution)/shard_map/ppermute | solution.py:35
  99.4 16.7 %collective-permute-start.22 = (bf16[144,512]{1,0:T(8,128)(2,1)S(1)}, bf16[144,512]{1,0:T(8,128)(2,1)S(1)}, u32[]{:S(2)}, u32[]{:S(2)}) collective-permute-start(bf16[144,512]{1,0:T(8,128)(2,1)S(1)} %get-tuple-element.77), channel_id=1, source_target_pairs={{0,48},{16,0},{32,16},{48,32},{1,49},{17,1},{33,17},{49,33},{2,50}... | collective-permute-start | bytes 442376 | tf_op jit(solution)/shard_map/ppermute | solution.py:35
  101.0 15.1 %collective-permute-start.23 = (bf16[144,512]{1,0:T(8,128)(2,1)S(1)}, bf16[144,512]{1,0:T(8,128)(2,1)S(1)}, u32[]{:S(2)}, u32[]{:S(2)}) collective-permute-start(bf16[144,512]{1,0:T(8,128)(2,1)S(1)} %get-tuple-element.78), channel_id=1, source_target_pairs={{0,32},{16,48},{32,0},{48,16},{1,33},{17,49},{33,1},{49,17},{2,34}... | collective-permute-start | bytes 442376 | tf_op jit(solution)/shard_map/ppermute | solution.py:35
  103.1 13.1 %collective-permute-start.24 = (bf16[144,512]{1,0:T(8,128)(2,1)S(1)}, bf16[144,512]{1,0:T(8,128)(2,1)S(1)}, u32[]{:S(2)}, u32[]{:S(2)}) collective-permute-start(bf16[144,512]{1,0:T(8,128)(2,1)S(1)} %get-tuple-element.79), channel_id=1, source_target_pairs={{0,16},{16,32},{32,48},{48,0},{1,17},{17,33},{33,49},{49,1},{2,18}... | collective-permute-start | bytes 442376 | tf_op jit(solution)/shard_map/ppermute | solution.py:35
  103.1 13.1 %collective-permute-start.27 = (bf16[1024,128]{1,0:T(8,128)(2,1)S(1)}, bf16[1024,128]{1,0:T(8,128)(2,1)S(1)}, u32[]{:S(2)}, u32[]{:S(2)}) collective-permute-start(bf16[1024,128]{1,0:T(8,128)(2,1)S(1)} %collective-permute-done.20.refs_6_), channel_id=1, source_target_pairs={{0,64},{64,0},{1,65},{65,1},{2,66},{66,2},{3,67},{67,3},{4,68},{68... | collective-permute-start | bytes 786440 | tf_op jit(solution)/shard_map/ppermute | solution.py:39
  104.7 11.5 %collective-permute-start.28 = (bf16[1024,128]{1,0:T(8,128)(2,1)S(1)}, bf16[1024,128]{1,0:T(8,128)(2,1)S(1)}, u32[]{:S(2)}, u32[]{:S(2)}) collective-permute-start(bf16[1024,128]{1,0:T(8,128)(2,1)S(1)} %collective-permute-done.21.refs_7_), channel_id=1, source_target_pairs={{0,64},{64,0},{1,65},{65,1},{2,66},{66,2},{3,67},{67,3},{4,68},{68... | collective-permute-start | bytes 786440 | tf_op jit(solution)/shard_map/ppermute | solution.py:39
  117.0 9.1 %collective-permute-start.29 = (bf16[512,128]{1,0:T(8,128)(2,1)S(1)}, bf16[512,128]{1,0:T(8,128)(2,1)S(1)}, u32[]{:S(2)}, u32[]{:S(2)}) collective-permute-start(bf16[512,128]{1,0:T(8,128)(2,1)S(1)} %combine.2.own), channel_id=1, source_target_pairs={{0,8},{8,0},{1,9},{9,1},{2,10},{10,2},{3,11},{11,3},{4,12},{12,4},... | collective-permute-start | bytes 393224 | tf_op jit(solution)/shard_map/ppermute | solution.py:47
  122.1 12.3 %collective-permute-start.30 = (bf16[144,512]{1,0:T(8,128)(2,1)S(1)}, bf16[144,512]{1,0:T(8,128)(2,1)S(1)}, u32[]{:S(2)}, u32[]{:S(2)}) collective-permute-start(bf16[144,512]{1,0:T(8,128)(2,1)S(1)} %get-tuple-element.104), channel_id=1, source_target_pairs={{0,48},{16,0},{32,16},{48,32},{1,49},{17,1},{33,17},{49,33},{2,50}... | collective-permute-start | bytes 442376 | tf_op jit(solution)/shard_map/ppermute | solution.py:35
  123.5 11.0 %collective-permute-start.31 = (bf16[144,512]{1,0:T(8,128)(2,1)S(1)}, bf16[144,512]{1,0:T(8,128)(2,1)S(1)}, u32[]{:S(2)}, u32[]{:S(2)}) collective-permute-start(bf16[144,512]{1,0:T(8,128)(2,1)S(1)} %get-tuple-element.105), channel_id=1, source_target_pairs={{0,32},{16,48},{32,0},{48,16},{1,33},{17,49},{33,1},{49,17},{2,34}... | collective-permute-start | bytes 442376 | tf_op jit(solution)/shard_map/ppermute | solution.py:35
  126.1 8.4 %collective-permute-start.32 = (bf16[144,512]{1,0:T(8,128)(2,1)S(1)}, bf16[144,512]{1,0:T(8,128)(2,1)S(1)}, u32[]{:S(2)}, u32[]{:S(2)}) collective-permute-start(bf16[144,512]{1,0:T(8,128)(2,1)S(1)} %get-tuple-element.106), channel_id=1, source_target_pairs={{0,16},{16,32},{32,48},{48,0},{1,17},{17,33},{33,49},{49,1},{2,18}... | collective-permute-start | bytes 442376 | tf_op jit(solution)/shard_map/ppermute | solution.py:35
  130.9 14.2 %all-to-all-start = ((bf16[8,256,128]{2,1,0:T(8,128)(2,1)}), bf16[8,256,128]{2,1,0:T(8,128)(2,1)S(1)}, u32[]{:S(2)}, u32[]{:S(2)}) async-start(bf16[8,256,128]{2,1,0:T(8,128)(2,1)} %project_out.2), calls=%async_computation | async-start | bytes 1048576 | tf_op jit(solution)/shard_map/all_to_all | solution.py:523
  145.2 13.0 %all-to-all-start.1 = ((bf16[8,256,128]{2,1,0:T(8,128)(2,1)}), bf16[8,256,128]{2,1,0:T(8,128)(2,1)S(1)}, u32[]{:S(2)}, u32[]{:S(2)}) async-start(bf16[8,256,128]{2,1,0:T(8,128)(2,1)} %project_out.3), calls=%async_computation.1 | async-start | bytes 1048576 | tf_op jit(solution)/shard_map/all_to_all | solution.py:523
  (28 other events, 223.7 us)

commit v12 on v10

--- a/solution.py
+++ b/solution.py
@@ -388,9 +388,9 @@
     core = idx[8]
     copies = []
     for k, slot in enumerate((0, 1, 2, 3, 6, 7)):
-        copies.append(pltpu.make_async_copy(blocks[k], held.at[idx[slot]], sem.at[k]))
+        copies.append(pltpu.make_async_copy(blocks[k], held.at[slot], sem.at[k]))
     for k in range(6, 10):
-        target = held.at[idx[4 + (k - 6) // 2], pl.ds((k % 2) * 1024, 1024)]
+        target = held.at[4 + (k - 6) // 2, pl.ds((k % 2) * 1024, 1024)]
         copies.append(pltpu.make_async_copy(blocks[k], target, sem.at[k]))
     for c in copies:
         c.start()
@@ -405,13 +405,13 @@
                 value = jnp.where(wanted[1] == e, second, 0.0)
                 value = jnp.where(wanted[0] == e, first, value).astype(BF16)
                 padded[rows, pl.ds(pl.multiple_of((head * E + e) * H, H), H)] = value
-    for c in copies:
-        c.wait()
-    for k in range(0, 8, 2):
+    for k, arrived in ((0, copies[0:2]), (2, copies[2:4]), (6, copies[4:6]), (4, copies[6:])):
+        for c in arrived:
+            c.wait()
         w = jnp.concatenate([held[k], held[k + 1]], axis=1)
         value = jnp.dot(padded[...], w, preferred_element_type=F32)
         for s in range(2):
-            out[k + s] = value[:, s * H : (s + 1) * H].astype(BF16)
+            out[idx[k + s]] = value[:, s * H : (s + 1) * H].astype(BF16)
 
 
 def project_out(idx, routes, own, other, blocks):
@@ -501,13 +501,16 @@
     mine, partner = xl * 4 + y, (1 - xl) * 4 + y
     at = [c, mine * 1536, partner * 1536, mine * 512, partner * 512]
     lengths = (suffix_lengths, prefix_lengths)
-    parts = list(attend(table(at + firsts[:1]), *lengths, qs[:1], caches, kvs))
-    parts += list(attend(table(at + firsts[1:]), *lengths, qs[1:], caches, kvs))
-    parts[1:], far0, far1, o_am, o_ap = lax.optimization_barrier(
-        (parts[1:], far0, far1, o_am, o_ap)
-    )
-    for k in range(1, 4):
-        parts[k] = along_y(parts[k], 4 - k)
+    (part2,) = attend(table(at + firsts[2:3]), *lengths, qs[2:3], caches, kvs)
+    part2, qs[1], qs[3] = lax.optimization_barrier((part2, qs[1], qs[3]))
+    part1, part3 = attend(table(at + firsts[1::2]), *lengths, qs[1::2], caches, kvs)
+    part2 = along_y(part2, 2)
+    part2, qs[0] = tie(part2, qs[0])
+    (own,) = attend(table(at + firsts[:1]), *lengths, qs[:1], caches, kvs)
+    part1, part3, far0, far1, o_am, o_ap = lax.optimization_barrier(
+        (part1, part3, far0, far1, o_am, o_ap)
+    )
+    parts = [own, along_y(part1, 3), part2, along_y(part3, 1)]
     afar0, afar1 = across_x(far0), across_x(far1)
     parts, afar0, afar1 = lax.optimization_barrier((parts, afar0, afar1))
     out_blocks = [out_weight, o_a, o_ym, o_am, o_yp, o_ap, far0, far1, afar0, afar1]

time: 158 us -> 157 us (level)
  waiting for transfers between devices: 41.7 us -> 24.7 us
  Pallas kernels: 29 us -> 39.7 us
  starting transfers between devices: 36.9 us -> 41 us
    pallas_call x2 -> x3, Pallas kernels: 14.3 us -> 23.2 us  [attend(): pl.pallas_call(functools.partial(attend_kernel, count), out_shape=tuple((...]
    ppermute x9, waiting for transfers between devices: 11.1 us -> 2.28 us  [across_x(): return lax.ppermute(x, 'xl', [(0, 1), (1, 0)])]
    ppermute x15, waiting for transfers between devices: 28 us -> 19.8 us  [along_y(): return lax.ppermute(x, 'y', [(i, (i + k) % 4) for i in range(4)])]
    ppermute x6, starting transfers between devices: 9.11 us -> 14.4 us  [across_core(): return lax.ppermute(x, 'c', [(0, 1), (1, 0)])]
    pallas_call x1, Pallas kernels: 5.73 us -> 7.42 us  [project_out(): pl.pallas_call(out_kernel, out_shape=jax.ShapeDtypeStruct((8, 512, H), BF...]
  transfers between devices with their start and end apart: 31 -> 31, of which waited for: 16 -> 10; matrix products, arithmetic and copies ran while one was open for 2% -> 2% of each run, Pallas kernels for 15% -> 20%
where the time goes in v12:
time: 157 us; the launch traced here: 156 us
  blocking collectives  44.2 us (28%)
  starting transfers between devices  41 us (26%)
  Pallas kernels  39.7 us (25%)
  waiting for transfers between devices  24.7 us (16%)
  local copies, waits for them, and re-layouts  3.82 us (2%)
  other arithmetic  1.9 us (1%)
    all_gather x2, blocking collectives, on_device(): blocks = [lax.all_gather(v, 'z', axis=0) for v in (tokens, half_row)]  23.6 us
    pallas_call x3, Pallas kernels, attend(): pl.pallas_call(functools.partial(attend_kernel, count), out_shape=tuple((...  23.2 us
    all_to_all x1, blocking collectives, on_device(): sums = lax.all_to_all(sums, NARROW, 0, 0, tiled=True)  20.6 us
    ppermute x15, waiting for transfers between devices, along_y(): return lax.ppermute(x, 'y', [(i, (i + k) % 4) for i in range(4)])  19.8 us
    ppermute x15, starting transfers between devices, along_y(): return lax.ppermute(x, 'y', [(i, (i + k) % 4) for i in range(4)])  16.5 us
    ppermute x6, starting transfers between devices, across_core(): return lax.ppermute(x, 'c', [(0, 1), (1, 0)])  14.4 us
    ppermute x9, starting transfers between devices, across_x(): return lax.ppermute(x, 'xl', [(0, 1), (1, 0)])  8.27 us
    pallas_call x1, Pallas kernels, project_out(): pl.pallas_call(out_kernel, out_shape=jax.ShapeDtypeStruct((8, 512, H), BF...  7.42 us
  transfers between devices with their start and end apart: 31, of which 10 were waited for; matrix products, arithmetic and copies ran while one was open for 2% of the time, Pallas kernels for 20%

profile of v12, /device:TPU:3, one launch (start us, length us, event | category | flops | bytes accessed | tf_op | source)
XLA Modules:
  0.0 155.8 jit_solution(17997402527857194058)
XLA Ops:
  0.0 1.8 %collective-permute-start.5 = (bf16[256,256]{1,0:T(8,128)(2,1)}, bf16[256,256]{1,0:T(8,128)(2,1)S(1)}, u32[]{:S(2)}, u32[]{:S(2)}) collective-permute-start(bf16[256,256]{1,0:T(8,128)(2,1)} %param.10), channel_id=1, source_target_pairs={{0,1},{1,0},{2,3},{3,2},{4,5},{5,4},{6,7},{7,6},{8,9},{9,8},{10,11... | collective-permute-start | bytes 393224 | tf_op jit(solution)/shard_map/ppermute | solution.py:43
  1.9 1.2 dynamic-slice_bitcast_fusion
  5.5 1.2 collective-permute-start.7
  7.7 2.9 %collective-permute-start.1 = (bf16[2,1280,128]{2,1,0:T(8,128)(2,1)}, bf16[2,1280,128]{2,1,0:T(8,128)(2,1)}, u32[]{:S(2)}, u32[]{:S(2)}) collective-permute-start(bf16[2,1280,128]{2,1,0:T(8,128)(2,1)} %pad_maximum_fusion.1.refs_0_), channel_id=1, source_target_pairs={{0,32},{16,48},{32,0},{48,16},{1,33},{17,49},{33,1},{49,17},{2,34}... | collective-permute-start | bytes 1966088 | tf_op jit(solution)/shard_map/ppermute | solution.py:35
  12.4 12.5 %all-gather = bf16[1024,256]{1,0:T(8,128)(2,1)S(1)} all-gather(bf16[256,256]{1,0:T(8,128)(2,1)S(1)} %copy-done.8), channel_id=2, replica_groups=mesh['xl'=2,'y'=4,'c'=2,'z'=4,'xh'=2] {'z'}, dimensions={0}, use_global_device_ids=true | all-gather | bytes 655360 | tf_op jit(solution)/shard_map/all_gather | solution.py:475
  25.2 11.1 %all-gather.1 = bf16[1024,256]{1,0:T(8,128)(2,1)S(1)} all-gather(bf16[256,256]{1,0:T(8,128)(2,1)S(1)} %collective-permute-done.5), channel_id=3, replica_groups=mesh['xl'=2,'y'=4,'c'=2,'z'=4,'xh'=2] {'z'}, dimensions={0}, use_global_device_ids=true | all-gather | bytes 655360 | tf_op jit(solution)/shard_map/all_gather | solution.py:475
  36.3 1.3 normalise.1.own
  37.7 1.9 %collective-permute-done.2.refs_2_ = bf16[2,1280,128]{2,1,0:T(8,128)(2,1)} collective-permute-done((bf16[2,1280,128]{2,1,0:T(8,128)(2,1)}, bf16[2,1280,128]{2,1,0:T(8,128)(2,1)}, u32[]{:S(2)}, u32[]{:S(2)}) %collective-permute-start.2) | collective-permute-done | bytes 655392 | tf_op jit(solution)/shard_map/ppermute | solution.py:35
  40.2 3.1 %collective-permute-start.9 = (bf16[256,2048]{1,0:T(8,128)(2,1)S(1)}, bf16[256,2048]{1,0:T(8,128)(2,1)}, u32[]{:S(2)}, u32[]{:S(2)}) collective-permute-start(bf16[256,2048]{1,0:T(8,128)(2,1)S(1)} %normalise.1.own), channel_id=1, source_target_pairs={{0,8},{8,0},{1,9},{9,1},{2,10},{10,2},{3,11},{11,3},{4,12},{12,4},... | collective-permute-start | bytes 3145736 | tf_op jit(solution)/shard_map/ppermute | solution.py:47
  43.3 2.0 %collective-permute-start.10 = (bf16[2,1280,128]{2,1,0:T(8,128)(2,1)}, bf16[2,1280,128]{2,1,0:T(8,128)(2,1)S(1)}, u32[]{:S(2)}, u32[]{:S(2)}) collective-permute-start(bf16[2,1280,128]{2,1,0:T(8,128)(2,1)} %collective-permute-done.4.refs_1_), channel_id=1, source_target_pairs={{0,48},{16,0},{32,16},{48,32},{1,49},{17,1},{33,17},{49,33},{2,50}... | collective-permute-start | bytes 1966088 | tf_op jit(solution)/shard_map/ppermute | solution.py:35
  45.3 1.2 collective-permute-start.12
  46.5 13.4 %collective-permute-done.10.refs_3_ = bf16[2,1280,128]{2,1,0:T(8,128)(2,1)S(1)} collective-permute-done((bf16[2,1280,128]{2,1,0:T(8,128)(2,1)}, bf16[2,1280,128]{2,1,0:T(8,128)(2,1)S(1)}, u32[]{:S(2)}, u32[]{:S(2)}) %collective-permute-start.10) | collective-permute-done | bytes 655392 | tf_op jit(solution)/shard_map/ppermute | solution.py:35
  60.8 2.0 %collective-permute-done.11.refs_7_ = bf16[2,1280,128]{2,1,0:T(8,128)(2,1)} collective-permute-done((bf16[2,1280,128]{2,1,0:T(8,128)(2,1)}, bf16[2,1280,128]{2,1,0:T(8,128)(2,1)}, u32[]{:S(2)}, u32[]{:S(2)}) %collective-permute-start.11) | collective-permute-done | bytes 655392 | tf_op jit(solution)/shard_map/ppermute | solution.py:35
  62.8 1.1 collective-permute-start.15
  64.2 1.2 collective-permute-start.14
  65.4 7.4 %project.1 = (bf16[1024,128]{1,0:T(8,128)(2,1)S(1)}, bf16[512,256]{1,0:T(8,128)(2,1)S(1)}, f32[512,2]{1,0:T(8,128)S(1)}) custom-call(s32[9]{0:T(128)S(1)} %stack.162.idx, s32[512,2]{1,0:T(8,128)S(1)} %broadcast_select_fusion.routes, bf16[8,2048]{1,0:T(8,128)(2,1)S(1)} %bitcast.47, bf16[256,2048]{1,0:T(8,128)(2,1)} %copy-done, ...), custom_call_target="tpu_custom_call" | custom-call | flops 6442450944 | bytes 8388608 | tf_op jit(solution)/shard_map/project/pallas_call | solution.py:164
  75.3 1.2 collective-permute-start.18
  78.1 1.4 collective-permute-start.23
  79.5 2.3 %collective-permute-done.17.refs_4_.refs_5_ = bf16[512,256]{1,0:T(8,128)(2,1)S(1)} collective-permute-done((bf16[512,256]{1,0:T(8,128)(2,1)S(1)}, bf16[512,256]{1,0:T(8,128)(2,1)S(1)}, u32[]{:S(2)}, u32[]{:S(2)}) %collective-permute-start.17) | collective-permute-done | bytes 262176 | tf_op jit(solution)/shard_map/ppermute | solution.py:39
  81.8 1.2 collective-permute-start.24
  83.7 5.9 %attend.3 = bf16[144,1024]{1,0:T(8,128)(2,1)S(1)} custom-call(s32[6]{0:T(128)S(1)} %stack.193.idx, s32[4]{0:T(128)S(1)} %copy-done.4, s32[4]{0:T(128)S(1)} %copy-done.5, bf16[1024,128]{1,0:T(8,128)(2,1)} %copy-done.18, bf16[2,768,256]{2,1,0:T(8,128)(2,1)} %copy-done.6, bf16[2,768,256]{2,1,0:T(8,128)(2,1)} %collective-permute-done.7.refs_2_.refs_3_, ...), custom_call_target="tpu_custom_call" | custom-call | flops 3221225472 | bytes 4194304 | tf_op jit(solution)/shard_map/attend/pallas_call | solution.py:330
  89.6 1.0 collective-permute-start.21
  90.6 1.7 %collective-permute-start.22 = (bf16[1024,128]{1,0:T(8,128)(2,1)S(1)}, bf16[1024,128]{1,0:T(8,128)(2,1)S(1)}, u32[]{:S(2)}, u32[]{:S(2)}) collective-permute-start(bf16[1024,128]{1,0:T(8,128)(2,1)S(1)} %slice.7), channel_id=1, source_target_pairs={{0,48},{16,0},{32,16},{48,32},{1,49},{17,1},{33,17},{49,33},{2,50}... | collective-permute-start | bytes 786440 | tf_op jit(solution)/shard_map/ppermute | solution.py:35
  92.5 10.0 %attend.5 = (bf16[144,1024]{1,0:T(8,128)(2,1)S(1)}, bf16[144,1024]{1,0:T(8,128)(2,1)S(1)}) custom-call(s32[7]{0:T(128)S(1)} %stack.196.idx, s32[4]{0:T(128)S(1)} %copy-done.4, s32[4]{0:T(128)S(1)} %copy-done.5, bf16[1024,128]{1,0:T(8,128)(2,1)} %copy-done.21, bf16[1024,128]{1,0:T(8,128)(2,1)} %copy-done.23, bf16[2,768,256]{2,1,0:T(8,128)(2,1)} %copy-done.6, ...), custom_call_target="tpu_custom_call" | custom-call | flops 6442450944 | bytes 4194304 | tf_op jit(solution)/shard_map/attend/pallas_call | solution.py:330
  102.6 3.3 %collective-permute-start.25 = (bf16[144,1024]{1,0:T(8,128)(2,1)S(1)}, bf16[144,1024]{1,0:T(8,128)(2,1)S(1)}, u32[]{:S(2)}, u32[]{:S(2)}) collective-permute-start(bf16[144,1024]{1,0:T(8,128)(2,1)S(1)} %get-tuple-element.71), channel_id=1, source_target_pairs={{0,48},{16,0},{32,16},{48,32},{1,49},{17,1},{33,17},{49,33},{2,50}... | collective-permute-start | bytes 884744 | tf_op jit(solution)/shard_map/ppermute | solution.py:35
  105.8 1.2 collective-permute-start.27
  107.3 7.4 %attend.4.p0 = bf16[144,1024]{1,0:T(8,128)(2,1)S(1)} custom-call(s32[6]{0:T(128)S(1)} %stack.191.idx, s32[4]{0:T(128)S(1)} %copy-done.4, s32[4]{0:T(128)S(1)} %copy-done.5, bf16[1024,128]{1,0:T(8,128)(2,1)} %copy-done.1, bf16[2,768,256]{2,1,0:T(8,128)(2,1)} %copy-done.6, bf16[2,768,256]{2,1,0:T(8,128)(2,1)} %collective-permute-done.7.refs_2_.refs_3_, ...), custom_call_target="tpu_custom_call" | custom-call | flops 3221225472 | bytes 4194304 | tf_op jit(solution)/shard_map/attend/pallas_call | solution.py:330
  115.1 7.8 %collective-permute-start.29 = (bf16[1024,128]{1,0:T(8,128)(2,1)S(1)}, bf16[1024,128]{1,0:T(8,128)(2,1)S(1)}, u32[]{:S(2)}, u32[]{:S(2)}) collective-permute-start(bf16[1024,128]{1,0:T(8,128)(2,1)S(1)} %combine.1.own), channel_id=1, source_target_pairs={{0,8},{8,0},{1,9},{9,1},{2,10},{10,2},{3,11},{11,3},{4,12},{12,4},... | collective-permute-start | bytes 786440 | tf_op jit(solution)/shard_map/ppermute | solution.py:47
  122.9 1.2 collective-permute-done.29.other
  124.1 7.4 %project_out.1 = bf16[8,512,128]{2,1,0:T(8,128)(2,1)S(1)} custom-call(s32[9]{0:T(128)S(1)} %stack.162.idx, s32[512,2]{1,0:T(8,128)S(1)} %broadcast_select_fusion.routes, bf16[1024,128]{1,0:T(8,128)(2,1)S(1)} %combine.1.own, bf16[1024,128]{1,0:T(8,128)(2,1)S(1)} %collective-permute-done.29.other, bf16[2048,128]{1,0:T(8,128)(2,1)} %refs_0_.1, ...), custom_call_target="tpu_custom_call" | custom-call | flops 4294967296 | bytes 6291456 | tf_op jit(solution)/shard_map/project_out/pallas_call | solution.py:418
  131.5 20.6 %all_to_all.5 = bf16[8,512,128]{2,1,0:T(8,128)(2,1)S(1)} all-to-all(bf16[8,512,128]{2,1,0:T(8,128)(2,1)S(1)} %project_out.1), channel_id=1, replica_groups=mesh['xl'=2,'y'=4,'c'=2,'z'=4,'xh'=2] {'z','xh'}, dimensions={0} | all-to-all | bytes 2097152 | tf_op jit(solution)/shard_map/all_to_all | solution.py:523
  152.3 1.9 %collective-permute-start.30 = (bf16[256,128]{1,0:T(8,128)(2,1)S(1)}, bf16[256,128]{1,0:T(8,128)(2,1)S(1)}, u32[]{:S(2)}, u32[]{:S(2)}) collective-permute-start(bf16[256,128]{1,0:T(8,128)(2,1)S(1)} %get-tuple-element.90), channel_id=1, source_target_pairs={{0,8},{8,0},{1,9},{9,1},{2,10},{10,2},{3,11},{11,3},{4,12},{12,4},... | collective-permute-start | bytes 196616 | tf_op jit(solution)/shard_map/ppermute | solution.py:47
  (114 shorter events, 14.8 us)
Async XLA Ops:
  0.0 12.0 %collective-permute-start.5 = (bf16[256,256]{1,0:T(8,128)(2,1)}, bf16[256,256]{1,0:T(8,128)(2,1)S(1)}, u32[]{:S(2)}, u32[]{:S(2)}) collective-permute-start(bf16[256,256]{1,0:T(8,128)(2,1)} %param.10), channel_id=1, source_target_pairs={{0,1},{1,0},{2,3},{3,2},{4,5},{5,4},{6,7},{7,6},{8,9},{9,8},{10,11... | collective-permute-start | bytes 393224 | tf_op jit(solution)/shard_map/ppermute | solution.py:43
  3.0 2.4 %collective-permute-start.6 = (bf16[768,256]{1,0:T(8,128)(2,1)S(1)}, bf16[768,256]{1,0:T(8,128)(2,1)S(1)}, u32[]{:S(2)}, u32[]{:S(2)}) collective-permute-start(bf16[768,256]{1,0:T(8,128)(2,1)S(1)} %get-tuple-element.86), channel_id=1, source_target_pairs={{0,8},{8,0},{1,9},{9,1},{2,10},{10,2},{3,11},{11,3},{4,12},{12,4},... | collective-permute-start | bytes 1179656 | tf_op jit(solution)/shard_map/ppermute | solution.py:47
  4.2 2.6 %collective-permute-start = (bf16[1280,128]{1,0:T(8,128)(2,1)S(1)}, bf16[1280,128]{1,0:T(8,128)(2,1)S(1)}, u32[]{:S(2)}, u32[]{:S(2)}) collective-permute-start(bf16[1280,128]{1,0:T(8,128)(2,1)S(1)} %pad_maximum_fusion.2), channel_id=1, source_target_pairs={{0,8},{8,0},{1,9},{9,1},{2,10},{10,2},{3,11},{11,3},{4,12},{12,4},... | collective-permute-start | bytes 983048 | tf_op jit(solution)/shard_map/ppermute | solution.py:47
  4.3 7.0 %collective-permute-start.8 = (s32[256,2]{0,1:T(2,128)S(1)}, s32[256,2]{0,1:T(2,128)S(1)}, u32[]{:S(2)}, u32[]{:S(2)}) collective-permute-start(s32[256,2]{0,1:T(2,128)S(1)} %copy-done.13), channel_id=1, source_target_pairs={{0,8},{8,0},{1,9},{9,1},{2,10},{10,2},{3,11},{11,3},{4,12},{12,4},... | collective-permute-start | bytes 6152 | tf_op jit(solution)/shard_map/ppermute | solution.py:47
  5.5 34.7 %collective-permute-start.7 = (bf16[2,768,256]{2,1,0:T(8,128)(2,1)S(1)}, bf16[2,768,256]{2,1,0:T(8,128)(2,1)}, u32[]{:S(2)}, u32[]{:S(2)}) collective-permute-start(bf16[2,768,256]{2,1,0:T(8,128)(2,1)S(1)} %pad_maximum_fusion.refs_1_.refs_2_), channel_id=1, source_target_pairs={{0,64},{64,0},{1,65},{65,1},{2,66},{66,2},{3,67},{67,3},{4,68},{68... | collective-permute-start | bytes 2359304 | tf_op jit(solution)/shard_map/ppermute | solution.py:39
  7.7 30.0 %collective-permute-start.1 = (bf16[2,1280,128]{2,1,0:T(8,128)(2,1)}, bf16[2,1280,128]{2,1,0:T(8,128)(2,1)}, u32[]{:S(2)}, u32[]{:S(2)}) collective-permute-start(bf16[2,1280,128]{2,1,0:T(8,128)(2,1)} %pad_maximum_fusion.1.refs_0_), channel_id=1, source_target_pairs={{0,32},{16,48},{32,0},{48,16},{1,33},{17,49},{33,1},{49,17},{2,34}... | collective-permute-start | bytes 1966088 | tf_op jit(solution)/shard_map/ppermute | solution.py:35
  10.6 29.0 %collective-permute-start.2 = (bf16[2,1280,128]{2,1,0:T(8,128)(2,1)}, bf16[2,1280,128]{2,1,0:T(8,128)(2,1)}, u32[]{:S(2)}, u32[]{:S(2)}) collective-permute-start(bf16[2,1280,128]{2,1,0:T(8,128)(2,1)} %pad_maximum_fusion.1.refs_0_), channel_id=1, source_target_pairs={{0,48},{16,0},{32,16},{48,32},{1,49},{17,1},{33,17},{49,33},{2,50}... | collective-permute-start | bytes 1966088 | tf_op jit(solution)/shard_map/ppermute | solution.py:35
  11.4 28.8 %collective-permute-start.3 = (bf16[2,1280,128]{2,1,0:T(8,128)(2,1)}, bf16[2,1280,128]{2,1,0:T(8,128)(2,1)}, u32[]{:S(2)}, u32[]{:S(2)}) collective-permute-start(bf16[2,1280,128]{2,1,0:T(8,128)(2,1)} %pad_maximum_fusion.1.refs_0_), channel_id=1, source_target_pairs={{0,16},{16,32},{32,48},{48,0},{1,17},{17,33},{33,49},{49,1},{2,18}... | collective-permute-start | bytes 1966088 | tf_op jit(solution)/shard_map/ppermute | solution.py:35
  12.1 28.1 %collective-permute-start.4 = (bf16[2,1280,128]{2,1,0:T(8,128)(2,1)}, bf16[2,1280,128]{2,1,0:T(8,128)(2,1)}, u32[]{:S(2)}, u32[]{:S(2)}) collective-permute-start(bf16[2,1280,128]{2,1,0:T(8,128)(2,1)} %pad_maximum_fusion.1.refs_0_), channel_id=1, source_target_pairs={{0,64},{64,0},{1,65},{65,1},{2,66},{66,2},{3,67},{67,3},{4,68},{68... | collective-permute-start | bytes 1966088 | tf_op jit(solution)/shard_map/ppermute | solution.py:39
  36.3 29.1 %copy-start.3 = (bf16[2048,8]{0,1:T(8,128)(2,1)S(1)}, bf16[2048,8]{0,1:T(8,128)(2,1)}, u32[]{:S(2)}) copy-start(bf16[2048,8]{0,1:T(8,128)(2,1)} %param.12) | copy-start | bytes 98308
  40.2 25.2 %collective-permute-start.9 = (bf16[256,2048]{1,0:T(8,128)(2,1)S(1)}, bf16[256,2048]{1,0:T(8,128)(2,1)}, u32[]{:S(2)}, u32[]{:S(2)}) collective-permute-start(bf16[256,2048]{1,0:T(8,128)(2,1)S(1)} %normalise.1.own), channel_id=1, source_target_pairs={{0,8},{8,0},{1,9},{9,1},{2,10},{10,2},{3,11},{11,3},{4,12},{12,4},... | collective-permute-start | bytes 3145736 | tf_op jit(solution)/shard_map/ppermute | solution.py:47
  43.3 16.6 %collective-permute-start.10 = (bf16[2,1280,128]{2,1,0:T(8,128)(2,1)}, bf16[2,1280,128]{2,1,0:T(8,128)(2,1)S(1)}, u32[]{:S(2)}, u32[]{:S(2)}) collective-permute-start(bf16[2,1280,128]{2,1,0:T(8,128)(2,1)} %collective-permute-done.4.refs_1_), channel_id=1, source_target_pairs={{0,48},{16,0},{32,16},{48,32},{1,49},{17,1},{33,17},{49,33},{2,50}... | collective-permute-start | bytes 1966088 | tf_op jit(solution)/shard_map/ppermute | solution.py:35
  45.3 17.5 %collective-permute-start.11 = (bf16[2,1280,128]{2,1,0:T(8,128)(2,1)}, bf16[2,1280,128]{2,1,0:T(8,128)(2,1)}, u32[]{:S(2)}, u32[]{:S(2)}) collective-permute-start(bf16[2,1280,128]{2,1,0:T(8,128)(2,1)} %collective-permute-done.4.refs_1_), channel_id=1, source_target_pairs={{0,16},{16,32},{32,48},{48,0},{1,17},{17,33},{33,49},{49,1},{2,18}... | collective-permute-start | bytes 1966088 | tf_op jit(solution)/shard_map/ppermute | solution.py:35
  45.3 20.1 %collective-permute-start.12 = (bf16[2,1280,128]{2,1,0:T(8,128)(2,1)}, bf16[2,1280,128]{2,1,0:T(8,128)(2,1)}, u32[]{:S(2)}, u32[]{:S(2)}) collective-permute-start(bf16[2,1280,128]{2,1,0:T(8,128)(2,1)} %collective-permute-done.1.refs_4_), channel_id=1, source_target_pairs={{0,64},{64,0},{1,65},{65,1},{2,66},{66,2},{3,67},{67,3},{4,68},{68... | collective-permute-start | bytes 1966088 | tf_op jit(solution)/shard_map/ppermute | solution.py:39
  62.8 12.6 %collective-permute-start.15 = (bf16[2048,128]{1,0:T(8,128)(2,1)}, bf16[2048,128]{1,0:T(8,128)(2,1)S(1)}, u32[]{:S(2)}, u32[]{:S(2)}) collective-permute-start(bf16[2048,128]{1,0:T(8,128)(2,1)} %refs_0_.1), channel_id=1, source_target_pairs={{0,48},{16,0},{32,16},{48,32},{1,49},{17,1},{33,17},{49,33},{2,50}... | collective-permute-start | bytes 1572872 | tf_op jit(solution)/shard_map/ppermute | solution.py:35
  63.9 13.7 %collective-permute-start.16 = (bf16[2048,128]{1,0:T(8,128)(2,1)}, bf16[2048,128]{1,0:T(8,128)(2,1)S(1)}, u32[]{:S(2)}, u32[]{:S(2)}) collective-permute-start(bf16[2048,128]{1,0:T(8,128)(2,1)} %refs_0_.1), channel_id=1, source_target_pairs={{0,16},{16,32},{32,48},{48,0},{1,17},{17,33},{33,49},{49,1},{2,18}... | collective-permute-start | bytes 1572872 | tf_op jit(solution)/shard_map/ppermute | solution.py:35
  64.2 13.8 %collective-permute-start.14 = (bf16[2048,128]{1,0:T(8,128)(2,1)}, bf16[2048,128]{1,0:T(8,128)(2,1)}, u32[]{:S(2)}, u32[]{:S(2)}) collective-permute-start(bf16[2048,128]{1,0:T(8,128)(2,1)} %refs_0_.1), channel_id=1, source_target_pairs={{0,64},{64,0},{1,65},{65,1},{2,66},{66,2},{3,67},{67,3},{4,68},{68... | collective-permute-start | bytes 1572872 | tf_op jit(solution)/shard_map/ppermute | solution.py:39
  72.9 8.9 %collective-permute-start.17 = (bf16[512,256]{1,0:T(8,128)(2,1)S(1)}, bf16[512,256]{1,0:T(8,128)(2,1)S(1)}, u32[]{:S(2)}, u32[]{:S(2)}) collective-permute-start(bf16[512,256]{1,0:T(8,128)(2,1)S(1)} %get-tuple-element.57.refs_3_.refs_4_), channel_id=1, source_target_pairs={{0,64},{64,0},{1,65},{65,1},{2,66},{66,2},{3,67},{67,3},{4,68},{68... | collective-permute-start | bytes 786440 | tf_op jit(solution)/shard_map/ppermute | solution.py:39
  73.3 9.7 %collective-permute-start.13 = (bf16[1024,128]{1,0:T(8,128)(2,1)S(1)}, bf16[1024,128]{1,0:T(8,128)(2,1)S(1)}, u32[]{:S(2)}, u32[]{:S(2)}) collective-permute-start(bf16[1024,128]{1,0:T(8,128)(2,1)S(1)} %get-tuple-element.64.refs_0_), channel_id=1, source_target_pairs={{0,32},{16,48},{32,0},{48,16},{1,33},{17,49},{33,1},{49,17},{2,34}... | collective-permute-start | bytes 786440 | tf_op jit(solution)/shard_map/ppermute | solution.py:35
  75.3 14.2 %collective-permute-start.18 = (bf16[1024,128]{1,0:T(8,128)(2,1)S(1)}, bf16[1024,128]{1,0:T(8,128)(2,1)S(1)}, u32[]{:S(2)}, u32[]{:S(2)}) collective-permute-start(bf16[1024,128]{1,0:T(8,128)(2,1)S(1)} %get-tuple-element.64.refs_0_), channel_id=1, source_target_pairs={{0,16},{16,32},{32,48},{48,0},{1,17},{17,33},{33,49},{49,1},{2,18}... | collective-permute-start | bytes 786440 | tf_op jit(solution)/shard_map/ppermute | solution.py:35
  77.6 12.0 %collective-permute-start.19 = (bf16[1024,128]{1,0:T(8,128)(2,1)S(1)}, bf16[1024,128]{1,0:T(8,128)(2,1)S(1)}, u32[]{:S(2)}, u32[]{:S(2)}) collective-permute-start(bf16[1024,128]{1,0:T(8,128)(2,1)S(1)} %get-tuple-element.64.refs_0_), channel_id=1, source_target_pairs={{0,48},{16,0},{32,16},{48,32},{1,49},{17,1},{33,17},{49,33},{2,50}... | collective-permute-start | bytes 786440 | tf_op jit(solution)/shard_map/ppermute | solution.py:35
  78.1 24.5 %collective-permute-start.23 = (bf16[2048,128]{1,0:T(8,128)(2,1)S(1)}, bf16[2048,128]{1,0:T(8,128)(2,1)S(1)}, u32[]{:S(2)}, u32[]{:S(2)}) collective-permute-start(bf16[2048,128]{1,0:T(8,128)(2,1)S(1)} %collective-permute-done.15.refs_2_), channel_id=1, source_target_pairs={{0,64},{64,0},{1,65},{65,1},{2,66},{66,2},{3,67},{67,3},{4,68},{68... | collective-permute-start | bytes 1572872 | tf_op jit(solution)/shard_map/ppermute | solution.py:39
  81.8 20.8 %collective-permute-start.24 = (bf16[2048,128]{1,0:T(8,128)(2,1)S(1)}, bf16[2048,128]{1,0:T(8,128)(2,1)S(1)}, u32[]{:S(2)}, u32[]{:S(2)}) collective-permute-start(bf16[2048,128]{1,0:T(8,128)(2,1)S(1)} %collective-permute-done.16.refs_4_), channel_id=1, source_target_pairs={{0,64},{64,0},{1,65},{65,1},{2,66},{66,2},{3,67},{67,3},{4,68},{68... | collective-permute-start | bytes 1572872 | tf_op jit(solution)/shard_map/ppermute | solution.py:39
  89.6 12.9 %collective-permute-start.21 = (bf16[1024,128]{1,0:T(8,128)(2,1)S(1)}, bf16[1024,128]{1,0:T(8,128)(2,1)S(1)}, u32[]{:S(2)}, u32[]{:S(2)}) collective-permute-start(bf16[1024,128]{1,0:T(8,128)(2,1)S(1)} %slice.6), channel_id=1, source_target_pairs={{0,16},{16,32},{32,48},{48,0},{1,17},{17,33},{33,49},{49,1},{2,18}... | collective-permute-start | bytes 786440 | tf_op jit(solution)/shard_map/ppermute | solution.py:35
  90.6 11.9 %collective-permute-start.22 = (bf16[1024,128]{1,0:T(8,128)(2,1)S(1)}, bf16[1024,128]{1,0:T(8,128)(2,1)S(1)}, u32[]{:S(2)}, u32[]{:S(2)}) collective-permute-start(bf16[1024,128]{1,0:T(8,128)(2,1)S(1)} %slice.7), channel_id=1, source_target_pairs={{0,48},{16,0},{32,16},{48,32},{1,49},{17,1},{33,17},{49,33},{2,50}... | collective-permute-start | bytes 786440 | tf_op jit(solution)/shard_map/ppermute | solution.py:35
  92.3 10.1 %collective-permute-start.20 = (bf16[144,1024]{1,0:T(8,128)(2,1)S(1)}, bf16[144,1024]{1,0:T(8,128)(2,1)S(1)}, u32[]{:S(2)}, u32[]{:S(2)}) collective-permute-start(bf16[144,1024]{1,0:T(8,128)(2,1)S(1)} %attend.3), channel_id=1, source_target_pairs={{0,32},{16,48},{32,0},{48,16},{1,33},{17,49},{33,1},{49,17},{2,34}... | collective-permute-start | bytes 884744 | tf_op jit(solution)/shard_map/ppermute | solution.py:35
  102.6 12.2 %collective-permute-start.25 = (bf16[144,1024]{1,0:T(8,128)(2,1)S(1)}, bf16[144,1024]{1,0:T(8,128)(2,1)S(1)}, u32[]{:S(2)}, u32[]{:S(2)}) collective-permute-start(bf16[144,1024]{1,0:T(8,128)(2,1)S(1)} %get-tuple-element.71), channel_id=1, source_target_pairs={{0,48},{16,0},{32,16},{48,32},{1,49},{17,1},{33,17},{49,33},{2,50}... | collective-permute-start | bytes 884744 | tf_op jit(solution)/shard_map/ppermute | solution.py:35
  105.8 9.0 %collective-permute-start.26 = (bf16[144,1024]{1,0:T(8,128)(2,1)S(1)}, bf16[144,1024]{1,0:T(8,128)(2,1)S(1)}, u32[]{:S(2)}, u32[]{:S(2)}) collective-permute-start(bf16[144,1024]{1,0:T(8,128)(2,1)S(1)} %get-tuple-element.73), channel_id=1, source_target_pairs={{0,16},{16,32},{32,48},{48,0},{1,17},{17,33},{33,49},{49,1},{2,18}... | collective-permute-start | bytes 884744 | tf_op jit(solution)/shard_map/ppermute | solution.py:35
  105.8 8.9 %collective-permute-start.27 = (bf16[1024,128]{1,0:T(8,128)(2,1)S(1)}, bf16[1024,128]{1,0:T(8,128)(2,1)S(1)}, u32[]{:S(2)}, u32[]{:S(2)}) collective-permute-start(bf16[1024,128]{1,0:T(8,128)(2,1)S(1)} %collective-permute-done.21.refs_6_), channel_id=1, source_target_pairs={{0,64},{64,0},{1,65},{65,1},{2,66},{66,2},{3,67},{67,3},{4,68},{68... | collective-permute-start | bytes 786440 | tf_op jit(solution)/shard_map/ppermute | solution.py:39
  107.0 7.8 %collective-permute-start.28 = (bf16[1024,128]{1,0:T(8,128)(2,1)S(1)}, bf16[1024,128]{1,0:T(8,128)(2,1)S(1)}, u32[]{:S(2)}, u32[]{:S(2)}) collective-permute-start(bf16[1024,128]{1,0:T(8,128)(2,1)S(1)} %collective-permute-done.22.refs_7_), channel_id=1, source_target_pairs={{0,64},{64,0},{1,65},{65,1},{2,66},{66,2},{3,67},{67,3},{4,68},{68... | collective-permute-start | bytes 786440 | tf_op jit(solution)/shard_map/ppermute | solution.py:39
  115.1 8.9 %collective-permute-start.29 = (bf16[1024,128]{1,0:T(8,128)(2,1)S(1)}, bf16[1024,128]{1,0:T(8,128)(2,1)S(1)}, u32[]{:S(2)}, u32[]{:S(2)}) collective-permute-start(bf16[1024,128]{1,0:T(8,128)(2,1)S(1)} %combine.1.own), channel_id=1, source_target_pairs={{0,8},{8,0},{1,9},{9,1},{2,10},{10,2},{3,11},{11,3},{4,12},{12,4},... | collective-permute-start | bytes 786440 | tf_op jit(solution)/shard_map/ppermute | solution.py:47
  152.3 2.8 %collective-permute-start.30 = (bf16[256,128]{1,0:T(8,128)(2,1)S(1)}, bf16[256,128]{1,0:T(8,128)(2,1)S(1)}, u32[]{:S(2)}, u32[]{:S(2)}) collective-permute-start(bf16[256,128]{1,0:T(8,128)(2,1)S(1)} %get-tuple-element.90), channel_id=1, source_target_pairs={{0,8},{8,0},{1,9},{9,1},{2,10},{10,2},{3,11},{11,3},{4,12},{12,4},... | collective-permute-start | bytes 196616 | tf_op jit(solution)/shard_map/ppermute | solution.py:47
  (24 other events, 214.9 us)

commit v13 on v10

--- a/solution.py
+++ b/solution.py
@@ -96,7 +96,7 @@
     )(idx, gain, *blocks)
 
 
-GROUPS = ((0, 512), (512, 768))
+GROUPS = ((0, 256), (256, 512), (768, 512))
 
 
 def project_kernel(idx, routes, router, own, other, *refs):
@@ -106,7 +106,7 @@
     copies = []
     for i, r in enumerate((own, other)):
         at = pl.multiple_of((core if i == 0 else 1 - core) * 256, 256)
-        copies.append(pltpu.make_async_copy(r, xs.at[pl.ds(at, 256)], sem.at[32 + i]))
+        copies.append(pltpu.make_async_copy(r, xs.at[pl.ds(at, 256)], sem.at[48 + i]))
     for g, (start, rows) in enumerate(GROUPS):
         for k in range(16):
             lane = (k // 2) * 256 + H * (core if k % 2 == 0 else 1 - core)
@@ -138,12 +138,10 @@
 
     wanted = [jnp.broadcast_to(routes[:, j : j + 1], (512, H)) for j in range(2)]
     for r in range(5):
-        if r == 0:
-            for c in copies[2:18]:
-                c.wait()
-        if r == 2:
-            for c in copies[18:]:
-                c.wait()
+        for g, (start, rows) in enumerate(GROUPS):
+            if start == r * 256:
+                for c in copies[2 + 16 * g : 18 + 16 * g]:
+                    c.wait()
         acc = nt_dot(xs[...], held[r * 256 : (r + 1) * 256])
         if r == 4:
             kv_out[...] = acc.astype(BF16)
@@ -174,7 +172,7 @@
             pltpu.VMEM((512, 2048), BF16),
             pltpu.VMEM((1280, 2048), BF16),
             pltpu.VMEM((2, 512, H), F32),
-            pltpu.SemaphoreType.DMA((34,)),
+            pltpu.SemaphoreType.DMA((50,)),
         ],
         compiler_params=pltpu.CompilerParams(vmem_limit_bytes=20 << 20),
         cost_estimate=pl.CostEstimate(flops=6 << 30, bytes_accessed=8 << 20, transcendentals=0),
@@ -185,7 +183,7 @@
 def attend_kernel(count, idx, ends_s, ends_p, *refs):
     queries, (cache0, cache1, kv0, kv1) = refs[:count], refs[count : count + 4]
     outs = refs[count + 4 : 2 * count + 4]
-    q, keep, limits, top, tot, acc, sa, sb, chunk_of, tile_of, sem = refs[2 * count + 4 :]
+    q, keep, limits, top, tot, acc, sa, sb, chunk_of, tile_of, part_of, sem = refs[2 * count + 4 :]
     tiles = 2 * count
     core = idx[0]
     copies = [
@@ -236,37 +234,50 @@
         slot = jnp.where(i < 3, idx[1] + i * CK, idx[2] + (i - 3) * CK)
         return jnp.where(i < 6, slot, jnp.where(i == 6, idx[3], idx[4]))
 
-    def collect(want_full, start):
-        def visit(n, count):
-            i, t = n // tiles, lax.rem(n, tiles)
-            base = base_of(i)
-            first = idx[5 + t // 2] + lax.rem(t, 2) * 256
-            last = first + 255
-            lo_a, hi_a, own_a = allowed_of(first)
-            lo_b, hi_b, own_b = allowed_of(last)
-            pre = i < 6
-            lo_first, lo_last = jnp.where(pre, lo_a, own_a), jnp.where(pre, lo_b, own_b)
-            hi_first, hi_last = jnp.where(pre, hi_a, first + 1), jnp.where(pre, hi_b, last + 1)
-            some = (base + CK > lo_first) & (base < hi_last)
-            full = (base >= lo_last) & (base + CK <= hi_first)
-            hit = full if want_full else (some & jnp.logical_not(full))
-
-            @pl.when(hit)
-            def _():
-                chunk_of[count] = i
-                tile_of[count] = t
-
-            return count + hit.astype(jnp.int32)
-
-        count = lax.fori_loop(0, CHUNKS * tiles, visit, start)
-        rounds = (count + UNROLL - 1) // UNROLL
+    def visit(n, counts):
+        whole, partial = counts
+        i, t = n // tiles, lax.rem(n, tiles)
+        base = base_of(i)
+        first = idx[5 + t // 2] + lax.rem(t, 2) * 256
+        last = first + 255
+        lo_a, hi_a, own_a = allowed_of(first)
+        lo_b, hi_b, own_b = allowed_of(last)
+        pre = i < 6
+        lo_first, lo_last = jnp.where(pre, lo_a, own_a), jnp.where(pre, lo_b, own_b)
+        hi_first, hi_last = jnp.where(pre, hi_a, first + 1), jnp.where(pre, hi_b, last + 1)
+        some = (base + CK > lo_first) & (base < hi_last)
+        full = (base >= lo_last) & (base + CK <= hi_first)
+        part = some & jnp.logical_not(full)
+
+        @pl.when(full)
+        def _():
+            chunk_of[whole] = i
+            tile_of[whole] = t
+
+        @pl.when(part)
+        def _():
+            part_of[partial] = n
+
+        return whole + full.astype(jnp.int32), partial + part.astype(jnp.int32)
+
+    def pad(count):
         for k in range(UNROLL):
             chunk_of[count + k] = 0
             tile_of[count + k] = tiles
-        return rounds
-
-    full_rounds = collect(True, 0)
-    all_rounds = collect(False, full_rounds * UNROLL)
+        return (count + UNROLL - 1) // UNROLL
+
+    whole, partial = lax.fori_loop(0, CHUNKS * tiles, visit, (0, 0))
+    full_rounds = pad(whole)
+    start = full_rounds * UNROLL
+
+    def move(k, _):
+        n = part_of[k]
+        chunk_of[start + k] = n // tiles
+        tile_of[start + k] = lax.rem(n, tiles)
+        return 0
+
+    lax.fori_loop(0, partial, move, 0)
+    all_rounds = pad(start + partial)
     for c in copies:
         c.wait()
     q[tiles * R : (tiles + 1) * R] = jnp.zeros((R, H), BF16)
@@ -343,6 +354,7 @@
             pltpu.VMEM((CK, R), F32),
             pltpu.SMEM((CHUNKS * tiles + 4 * UNROLL,), jnp.int32),
             pltpu.SMEM((CHUNKS * tiles + 4 * UNROLL,), jnp.int32),
+            pltpu.SMEM((CHUNKS * tiles,), jnp.int32),
             pltpu.SemaphoreType.DMA((count + 6,)),
         ],
         compiler_params=pltpu.CompilerParams(vmem_limit_bytes=20 << 20),

time: 158 us -> 157 us (level)
  Pallas kernels: 29 us -> 36.7 us
  starting transfers between devices: 36.9 us -> 31.7 us
  waiting for transfers between devices: 41.7 us -> 37.6 us
    pallas_call x2, Pallas kernels: 14.3 us -> 21.5 us  [attend(): pl.pallas_call(functools.partial(attend_kernel, count), out_shape=tuple((...]
    ppermute x9, waiting for transfers between devices: 11.1 us -> 4.17 us  [across_x(): return lax.ppermute(x, 'xl', [(0, 1), (1, 0)])]
    ppermute x15, starting transfers between devices: 17.7 us -> 13.8 us  [along_y(): return lax.ppermute(x, 'y', [(i, (i + k) % 4) for i in range(4)])]
    ppermute x15, waiting for transfers between devices: 28 us -> 30.9 us  [along_y(): return lax.ppermute(x, 'y', [(i, (i + k) % 4) for i in range(4)])]
  transfers between devices with their start and end apart: 31 -> 31, of which waited for: 16 -> 16; matrix products, arithmetic and copies ran while one was open for 2% -> 2% of each run, Pallas kernels for 15% -> 20%
where the time goes in v13:
time: 157 us; the launch traced here: 155 us
  blocking collectives  43.9 us (28%)
  waiting for transfers between devices  37.6 us (24%)
  Pallas kernels  36.7 us (23%)
  starting transfers between devices  31.7 us (20%)
  local copies, waits for them, and re-layouts  3.08 us (2%)
  other arithmetic  1.9 us (1%)
    ppermute x15, waiting for transfers between devices, along_y(): return lax.ppermute(x, 'y', [(i, (i + k) % 4) for i in range(4)])  30.9 us
    all_gather x2, blocking collectives, on_device(): blocks = [lax.all_gather(v, 'z', axis=0) for v in (tokens, half_row)]  23.6 us
    pallas_call x2, Pallas kernels, attend(): pl.pallas_call(functools.partial(attend_kernel, count), out_shape=tuple((...  21.5 us
    all_to_all x1, blocking collectives, on_device(): sums = lax.all_to_all(sums, NARROW, 0, 0, tiled=True)  20.4 us
    ppermute x15, starting transfers between devices, along_y(): return lax.ppermute(x, 'y', [(i, (i + k) % 4) for i in range(4)])  13.8 us
    ppermute x9, starting transfers between devices, across_x(): return lax.ppermute(x, 'xl', [(0, 1), (1, 0)])  8.29 us
    ppermute x6, starting transfers between devices, across_core(): return lax.ppermute(x, 'c', [(0, 1), (1, 0)])  7.78 us
    pallas_call x1, Pallas kernels, project(): pl.pallas_call(project_kernel, out_shape=(jax.ShapeDtypeStruct((1024, H),...  7.78 us
  transfers between devices with their start and end apart: 31, of which 16 were waited for; matrix products, arithmetic and copies ran while one was open for 2% of the time, Pallas kernels for 20%

profile of v13, /device:TPU:3, one launch (start us, length us, event | category | flops | bytes accessed | tf_op | source)
XLA Modules:
  0.0 155.3 jit_solution(12851807550744772836)
XLA Ops:
  0.0 1.8 %collective-permute-start.5 = (bf16[256,256]{1,0:T(8,128)(2,1)}, bf16[256,256]{1,0:T(8,128)(2,1)S(1)}, u32[]{:S(2)}, u32[]{:S(2)}) collective-permute-start(bf16[256,256]{1,0:T(8,128)(2,1)} %param.10), channel_id=1, source_target_pairs={{0,1},{1,0},{2,3},{3,2},{4,5},{5,4},{6,7},{7,6},{8,9},{9,8},{10,11... | collective-permute-start | bytes 393224 | tf_op jit(solution)/shard_map/ppermute | solution.py:43
  1.9 1.2 dynamic-slice_bitcast_fusion
  5.5 1.2 collective-permute-start.7
  7.7 2.9 %collective-permute-start.1 = (bf16[2,1280,128]{2,1,0:T(8,128)(2,1)}, bf16[2,1280,128]{2,1,0:T(8,128)(2,1)}, u32[]{:S(2)}, u32[]{:S(2)}) collective-permute-start(bf16[2,1280,128]{2,1,0:T(8,128)(2,1)} %pad_maximum_fusion.1.refs_0_), channel_id=1, source_target_pairs={{0,32},{16,48},{32,0},{48,16},{1,33},{17,49},{33,1},{49,17},{2,34}... | collective-permute-start | bytes 1966088 | tf_op jit(solution)/shard_map/ppermute | solution.py:35
  12.4 12.5 %all-gather = bf16[1024,256]{1,0:T(8,128)(2,1)S(1)} all-gather(bf16[256,256]{1,0:T(8,128)(2,1)S(1)} %copy-done.8), channel_id=2, replica_groups=mesh['xl'=2,'y'=4,'c'=2,'z'=4,'xh'=2] {'z'}, dimensions={0}, use_global_device_ids=true | all-gather | bytes 655360 | tf_op jit(solution)/shard_map/all_gather | solution.py:487
  25.2 11.1 %all-gather.1 = bf16[1024,256]{1,0:T(8,128)(2,1)S(1)} all-gather(bf16[256,256]{1,0:T(8,128)(2,1)S(1)} %collective-permute-done.5), channel_id=3, replica_groups=mesh['xl'=2,'y'=4,'c'=2,'z'=4,'xh'=2] {'z'}, dimensions={0}, use_global_device_ids=true | all-gather | bytes 655360 | tf_op jit(solution)/shard_map/all_gather | solution.py:487
  36.3 1.3 normalise.1.own
  37.7 1.9 %collective-permute-done.2.refs_2_ = bf16[2,1280,128]{2,1,0:T(8,128)(2,1)} collective-permute-done((bf16[2,1280,128]{2,1,0:T(8,128)(2,1)}, bf16[2,1280,128]{2,1,0:T(8,128)(2,1)}, u32[]{:S(2)}, u32[]{:S(2)}) %collective-permute-start.2) | collective-permute-done | bytes 655392 | tf_op jit(solution)/shard_map/ppermute | solution.py:35
  40.2 3.1 %collective-permute-start.9 = (bf16[256,2048]{1,0:T(8,128)(2,1)S(1)}, bf16[256,2048]{1,0:T(8,128)(2,1)}, u32[]{:S(2)}, u32[]{:S(2)}) collective-permute-start(bf16[256,2048]{1,0:T(8,128)(2,1)S(1)} %normalise.1.own), channel_id=1, source_target_pairs={{0,8},{8,0},{1,9},{9,1},{2,10},{10,2},{3,11},{11,3},{4,12},{12,4},... | collective-permute-start | bytes 3145736 | tf_op jit(solution)/shard_map/ppermute | solution.py:47
  43.3 2.0 %collective-permute-start.10 = (bf16[2,1280,128]{2,1,0:T(8,128)(2,1)}, bf16[2,1280,128]{2,1,0:T(8,128)(2,1)S(1)}, u32[]{:S(2)}, u32[]{:S(2)}) collective-permute-start(bf16[2,1280,128]{2,1,0:T(8,128)(2,1)} %collective-permute-done.4.refs_1_), channel_id=1, source_target_pairs={{0,48},{16,0},{32,16},{48,32},{1,49},{17,1},{33,17},{49,33},{2,50}... | collective-permute-start | bytes 1966088 | tf_op jit(solution)/shard_map/ppermute | solution.py:35
  45.3 1.2 collective-permute-start.12
  46.5 13.4 %collective-permute-done.10.refs_3_ = bf16[2,1280,128]{2,1,0:T(8,128)(2,1)S(1)} collective-permute-done((bf16[2,1280,128]{2,1,0:T(8,128)(2,1)}, bf16[2,1280,128]{2,1,0:T(8,128)(2,1)S(1)}, u32[]{:S(2)}, u32[]{:S(2)}) %collective-permute-start.10) | collective-permute-done | bytes 655392 | tf_op jit(solution)/shard_map/ppermute | solution.py:35
  60.8 2.0 %collective-permute-done.11.refs_7_ = bf16[2,1280,128]{2,1,0:T(8,128)(2,1)} collective-permute-done((bf16[2,1280,128]{2,1,0:T(8,128)(2,1)}, bf16[2,1280,128]{2,1,0:T(8,128)(2,1)}, u32[]{:S(2)}, u32[]{:S(2)}) %collective-permute-start.11) | collective-permute-done | bytes 655392 | tf_op jit(solution)/shard_map/ppermute | solution.py:35
  64.2 1.2 collective-permute-start.15
  65.4 7.8 %project.1 = (bf16[1024,128]{1,0:T(8,128)(2,1)S(1)}, bf16[512,256]{1,0:T(8,128)(2,1)S(1)}, f32[512,2]{1,0:T(8,128)S(1)}) custom-call(s32[9]{0:T(128)S(1)} %stack.154.idx, s32[512,2]{1,0:T(8,128)S(1)} %broadcast_select_fusion.routes, bf16[8,2048]{1,0:T(8,128)(2,1)S(1)} %bitcast.47, bf16[256,2048]{1,0:T(8,128)(2,1)} %copy-done, ...), custom_call_target="tpu_custom_call" | custom-call | flops 6442450944 | bytes 8388608 | tf_op jit(solution)/shard_map/project/pallas_call | solution.py:162
  73.7 1.7 %collective-permute-done.13.refs_2_ = bf16[2048,128]{1,0:T(8,128)(2,1)S(1)} collective-permute-done((bf16[2048,128]{1,0:T(8,128)(2,1)}, bf16[2048,128]{1,0:T(8,128)(2,1)S(1)}, u32[]{:S(2)}, u32[]{:S(2)}) %collective-permute-start.13) | collective-permute-done | bytes 524320 | tf_op jit(solution)/shard_map/ppermute | solution.py:35
  75.3 1.8 %collective-permute-start.18 = (bf16[1024,128]{1,0:T(8,128)(2,1)S(1)}, bf16[1024,128]{1,0:T(8,128)(2,1)S(1)}, u32[]{:S(2)}, u32[]{:S(2)}) collective-permute-start(bf16[1024,128]{1,0:T(8,128)(2,1)S(1)} %get-tuple-element.53.refs_0_), channel_id=1, source_target_pairs={{0,32},{16,48},{32,0},{48,16},{1,33},{17,49},{33,1},{49,17},{2,34}... | collective-permute-start | bytes 786440 | tf_op jit(solution)/shard_map/ppermute | solution.py:35
  78.3 1.4 collective-permute-start.22
  79.7 2.0 %collective-permute-done.16.refs_4_.refs_6_ = bf16[512,256]{1,0:T(8,128)(2,1)S(1)} collective-permute-done((bf16[512,256]{1,0:T(8,128)(2,1)S(1)}, bf16[512,256]{1,0:T(8,128)(2,1)S(1)}, u32[]{:S(2)}, u32[]{:S(2)}) %collective-permute-start.16) | collective-permute-done | bytes 262176 | tf_op jit(solution)/shard_map/ppermute | solution.py:39
  81.8 1.2 collective-permute-start.23
  82.9 2.1 %collective-permute-done.17.refs_0_ = bf16[1024,128]{1,0:T(8,128)(2,1)S(1)} collective-permute-done((bf16[1024,128]{1,0:T(8,128)(2,1)S(1)}, bf16[1024,128]{1,0:T(8,128)(2,1)S(1)}, u32[]{:S(2)}, u32[]{:S(2)}) %collective-permute-start.17) | collective-permute-done | bytes 262176 | tf_op jit(solution)/shard_map/ppermute | solution.py:35
  85.0 2.1 %collective-permute-done.18.refs_1_ = bf16[1024,128]{1,0:T(8,128)(2,1)S(1)} collective-permute-done((bf16[1024,128]{1,0:T(8,128)(2,1)S(1)}, bf16[1024,128]{1,0:T(8,128)(2,1)S(1)}, u32[]{:S(2)}, u32[]{:S(2)}) %collective-permute-start.18) | collective-permute-done | bytes 262176 | tf_op jit(solution)/shard_map/ppermute | solution.py:35
  87.8 1.6 %collective-permute-done.19.refs_2_ = bf16[1024,128]{1,0:T(8,128)(2,1)} collective-permute-done((bf16[1024,128]{1,0:T(8,128)(2,1)S(1)}, bf16[1024,128]{1,0:T(8,128)(2,1)}, u32[]{:S(2)}, u32[]{:S(2)}) %collective-permute-start.19) | collective-permute-done | bytes 262176 | tf_op jit(solution)/shard_map/ppermute | solution.py:35
  89.4 14.2 %attend.3 = (bf16[144,1024]{1,0:T(8,128)(2,1)S(1)}, bf16[144,1024]{1,0:T(8,128)(2,1)S(1)}, bf16[144,1024]{1,0:T(8,128)(2,1)S(1)}) custom-call(s32[8]{0:T(128)S(1)} %stack.187.idx, s32[4]{0:T(128)S(1)} %copy-done.4, s32[4]{0:T(128)S(1)} %copy-done.5, bf16[1024,128]{1,0:T(8,128)(2,1)} %copy-done.18, bf16[1024,128]{1,0:T(8,128)(2,1)} %copy-done.19, ...), custom_call_target="tpu_custom_call" | custom-call | flops 9663676416 | bytes 4194304 | tf_op jit(solution)/shard_map/attend/pallas_call | solution.py:341
  104.2 2.6 %collective-permute-start.24 = (bf16[144,1024]{1,0:T(8,128)(2,1)S(1)}, bf16[144,1024]{1,0:T(8,128)(2,1)S(1)}, u32[]{:S(2)}, u32[]{:S(2)}) collective-permute-start(bf16[144,1024]{1,0:T(8,128)(2,1)S(1)} %get-tuple-element.65), channel_id=1, source_target_pairs={{0,48},{16,0},{32,16},{48,32},{1,49},{17,1},{33,17},{49,33},{2,50}... | collective-permute-start | bytes 884744 | tf_op jit(solution)/shard_map/ppermute | solution.py:35
  108.9 7.3 %attend.2.p0 = bf16[144,1024]{1,0:T(8,128)(2,1)S(1)} custom-call(s32[6]{0:T(128)S(1)} %stack.183.idx, s32[4]{0:T(128)S(1)} %copy-done.4, s32[4]{0:T(128)S(1)} %copy-done.5, bf16[1024,128]{1,0:T(8,128)(2,1)} %copy-done.1, bf16[2,768,256]{2,1,0:T(8,128)(2,1)} %copy-done.6, bf16[2,768,256]{2,1,0:T(8,128)(2,1)} %collective-permute-done.7.refs_2_.refs_4_, ...), custom_call_target="tpu_custom_call" | custom-call | flops 3221225472 | bytes 4194304 | tf_op jit(solution)/shard_map/attend/pallas_call | solution.py:341
  116.2 1.6 %collective-permute-done.28.refs_9_ = bf16[1024,128]{1,0:T(8,128)(2,1)S(1)} collective-permute-done((bf16[1024,128]{1,0:T(8,128)(2,1)S(1)}, bf16[1024,128]{1,0:T(8,128)(2,1)S(1)}, u32[]{:S(2)}, u32[]{:S(2)}) %collective-permute-start.28) | collective-permute-done | bytes 262176 | tf_op jit(solution)/shard_map/ppermute | solution.py:39
  117.9 5.1 %collective-permute-done.26.p3 = bf16[144,1024]{1,0:T(8,128)(2,1)S(1)} collective-permute-done((bf16[144,1024]{1,0:T(8,128)(2,1)S(1)}, bf16[144,1024]{1,0:T(8,128)(2,1)S(1)}, u32[]{:S(2)}, u32[]{:S(2)}) %collective-permute-start.26) | collective-permute-done | bytes 294944 | tf_op jit(solution)/shard_map/ppermute | solution.py:35
  124.4 1.2 collective-permute-done.29.other
  125.6 5.7 %project_out.1 = bf16[8,512,128]{2,1,0:T(8,128)(2,1)S(1)} custom-call(s32[9]{0:T(128)S(1)} %stack.154.idx, s32[512,2]{1,0:T(8,128)S(1)} %broadcast_select_fusion.routes, bf16[1024,128]{1,0:T(8,128)(2,1)S(1)} %combine.1.own, bf16[1024,128]{1,0:T(8,128)(2,1)S(1)} %collective-permute-done.29.other, bf16[2048,128]{1,0:T(8,128)(2,1)} %refs_0_.1, ...), custom_call_target="tpu_custom_call" | custom-call | flops 4294967296 | bytes 6291456 | tf_op jit(solution)/shard_map/project_out/pallas_call | solution.py:430
  131.3 20.4 %all_to_all.5 = bf16[8,512,128]{2,1,0:T(8,128)(2,1)S(1)} all-to-all(bf16[8,512,128]{2,1,0:T(8,128)(2,1)S(1)} %project_out.1), channel_id=1, replica_groups=mesh['xl'=2,'y'=4,'c'=2,'z'=4,'xh'=2] {'z','xh'}, dimensions={0} | all-to-all | bytes 2097152 | tf_op jit(solution)/shard_map/all_to_all | solution.py:532
  151.8 1.9 %collective-permute-start.30 = (bf16[256,128]{1,0:T(8,128)(2,1)S(1)}, bf16[256,128]{1,0:T(8,128)(2,1)S(1)}, u32[]{:S(2)}, u32[]{:S(2)}) collective-permute-start(bf16[256,128]{1,0:T(8,128)(2,1)S(1)} %get-tuple-element.84), channel_id=1, source_target_pairs={{0,8},{8,0},{1,9},{9,1},{2,10},{10,2},{3,11},{11,3},{4,12},{12,4},... | collective-permute-start | bytes 196616 | tf_op jit(solution)/shard_map/ppermute | solution.py:47
  (110 shorter events, 16.6 us)
Async XLA Ops:
  0.0 12.0 %collective-permute-start.5 = (bf16[256,256]{1,0:T(8,128)(2,1)}, bf16[256,256]{1,0:T(8,128)(2,1)S(1)}, u32[]{:S(2)}, u32[]{:S(2)}) collective-permute-start(bf16[256,256]{1,0:T(8,128)(2,1)} %param.10), channel_id=1, source_target_pairs={{0,1},{1,0},{2,3},{3,2},{4,5},{5,4},{6,7},{7,6},{8,9},{9,8},{10,11... | collective-permute-start | bytes 393224 | tf_op jit(solution)/shard_map/ppermute | solution.py:43
  3.0 2.4 %collective-permute-start.6 = (bf16[768,256]{1,0:T(8,128)(2,1)S(1)}, bf16[768,256]{1,0:T(8,128)(2,1)S(1)}, u32[]{:S(2)}, u32[]{:S(2)}) collective-permute-start(bf16[768,256]{1,0:T(8,128)(2,1)S(1)} %get-tuple-element.80), channel_id=1, source_target_pairs={{0,8},{8,0},{1,9},{9,1},{2,10},{10,2},{3,11},{11,3},{4,12},{12,4},... | collective-permute-start | bytes 1179656 | tf_op jit(solution)/shard_map/ppermute | solution.py:47
  4.2 2.6 %collective-permute-start = (bf16[1280,128]{1,0:T(8,128)(2,1)S(1)}, bf16[1280,128]{1,0:T(8,128)(2,1)S(1)}, u32[]{:S(2)}, u32[]{:S(2)}) collective-permute-start(bf16[1280,128]{1,0:T(8,128)(2,1)S(1)} %pad_maximum_fusion.2), channel_id=1, source_target_pairs={{0,8},{8,0},{1,9},{9,1},{2,10},{10,2},{3,11},{11,3},{4,12},{12,4},... | collective-permute-start | bytes 983048 | tf_op jit(solution)/shard_map/ppermute | solution.py:47
  4.3 7.0 %collective-permute-start.8 = (s32[256,2]{0,1:T(2,128)S(1)}, s32[256,2]{0,1:T(2,128)S(1)}, u32[]{:S(2)}, u32[]{:S(2)}) collective-permute-start(s32[256,2]{0,1:T(2,128)S(1)} %copy-done.13), channel_id=1, source_target_pairs={{0,8},{8,0},{1,9},{9,1},{2,10},{10,2},{3,11},{11,3},{4,12},{12,4},... | collective-permute-start | bytes 6152 | tf_op jit(solution)/shard_map/ppermute | solution.py:47
  5.5 34.7 %collective-permute-start.7 = (bf16[2,768,256]{2,1,0:T(8,128)(2,1)S(1)}, bf16[2,768,256]{2,1,0:T(8,128)(2,1)}, u32[]{:S(2)}, u32[]{:S(2)}) collective-permute-start(bf16[2,768,256]{2,1,0:T(8,128)(2,1)S(1)} %pad_maximum_fusion.refs_1_.refs_3_), channel_id=1, source_target_pairs={{0,64},{64,0},{1,65},{65,1},{2,66},{66,2},{3,67},{67,3},{4,68},{68... | collective-permute-start | bytes 2359304 | tf_op jit(solution)/shard_map/ppermute | solution.py:39
  7.7 30.0 %collective-permute-start.1 = (bf16[2,1280,128]{2,1,0:T(8,128)(2,1)}, bf16[2,1280,128]{2,1,0:T(8,128)(2,1)}, u32[]{:S(2)}, u32[]{:S(2)}) collective-permute-start(bf16[2,1280,128]{2,1,0:T(8,128)(2,1)} %pad_maximum_fusion.1.refs_0_), channel_id=1, source_target_pairs={{0,32},{16,48},{32,0},{48,16},{1,33},{17,49},{33,1},{49,17},{2,34}... | collective-permute-start | bytes 1966088 | tf_op jit(solution)/shard_map/ppermute | solution.py:35
  10.6 29.0 %collective-permute-start.2 = (bf16[2,1280,128]{2,1,0:T(8,128)(2,1)}, bf16[2,1280,128]{2,1,0:T(8,128)(2,1)}, u32[]{:S(2)}, u32[]{:S(2)}) collective-permute-start(bf16[2,1280,128]{2,1,0:T(8,128)(2,1)} %pad_maximum_fusion.1.refs_0_), channel_id=1, source_target_pairs={{0,48},{16,0},{32,16},{48,32},{1,49},{17,1},{33,17},{49,33},{2,50}... | collective-permute-start | bytes 1966088 | tf_op jit(solution)/shard_map/ppermute | solution.py:35
  11.4 28.8 %collective-permute-start.3 = (bf16[2,1280,128]{2,1,0:T(8,128)(2,1)}, bf16[2,1280,128]{2,1,0:T(8,128)(2,1)}, u32[]{:S(2)}, u32[]{:S(2)}) collective-permute-start(bf16[2,1280,128]{2,1,0:T(8,128)(2,1)} %pad_maximum_fusion.1.refs_0_), channel_id=1, source_target_pairs={{0,16},{16,32},{32,48},{48,0},{1,17},{17,33},{33,49},{49,1},{2,18}... | collective-permute-start | bytes 1966088 | tf_op jit(solution)/shard_map/ppermute | solution.py:35
  12.1 28.1 %collective-permute-start.4 = (bf16[2,1280,128]{2,1,0:T(8,128)(2,1)}, bf16[2,1280,128]{2,1,0:T(8,128)(2,1)}, u32[]{:S(2)}, u32[]{:S(2)}) collective-permute-start(bf16[2,1280,128]{2,1,0:T(8,128)(2,1)} %pad_maximum_fusion.1.refs_0_), channel_id=1, source_target_pairs={{0,64},{64,0},{1,65},{65,1},{2,66},{66,2},{3,67},{67,3},{4,68},{68... | collective-permute-start | bytes 1966088 | tf_op jit(solution)/shard_map/ppermute | solution.py:39
  40.2 25.2 %collective-permute-start.9 = (bf16[256,2048]{1,0:T(8,128)(2,1)S(1)}, bf16[256,2048]{1,0:T(8,128)(2,1)}, u32[]{:S(2)}, u32[]{:S(2)}) collective-permute-start(bf16[256,2048]{1,0:T(8,128)(2,1)S(1)} %normalise.1.own), channel_id=1, source_target_pairs={{0,8},{8,0},{1,9},{9,1},{2,10},{10,2},{3,11},{11,3},{4,12},{12,4},... | collective-permute-start | bytes 3145736 | tf_op jit(solution)/shard_map/ppermute | solution.py:47
  43.3 16.6 %collective-permute-start.10 = (bf16[2,1280,128]{2,1,0:T(8,128)(2,1)}, bf16[2,1280,128]{2,1,0:T(8,128)(2,1)S(1)}, u32[]{:S(2)}, u32[]{:S(2)}) collective-permute-start(bf16[2,1280,128]{2,1,0:T(8,128)(2,1)} %collective-permute-done.4.refs_1_), channel_id=1, source_target_pairs={{0,48},{16,0},{32,16},{48,32},{1,49},{17,1},{33,17},{49,33},{2,50}... | collective-permute-start | bytes 1966088 | tf_op jit(solution)/shard_map/ppermute | solution.py:35
  45.3 17.5 %collective-permute-start.11 = (bf16[2,1280,128]{2,1,0:T(8,128)(2,1)}, bf16[2,1280,128]{2,1,0:T(8,128)(2,1)}, u32[]{:S(2)}, u32[]{:S(2)}) collective-permute-start(bf16[2,1280,128]{2,1,0:T(8,128)(2,1)} %collective-permute-done.4.refs_1_), channel_id=1, source_target_pairs={{0,16},{16,32},{32,48},{48,0},{1,17},{17,33},{33,49},{49,1},{2,18}... | collective-permute-start | bytes 1966088 | tf_op jit(solution)/shard_map/ppermute | solution.py:35
  45.3 20.1 %collective-permute-start.12 = (bf16[2,1280,128]{2,1,0:T(8,128)(2,1)}, bf16[2,1280,128]{2,1,0:T(8,128)(2,1)}, u32[]{:S(2)}, u32[]{:S(2)}) collective-permute-start(bf16[2,1280,128]{2,1,0:T(8,128)(2,1)} %collective-permute-done.1.refs_4_), channel_id=1, source_target_pairs={{0,64},{64,0},{1,65},{65,1},{2,66},{66,2},{3,67},{67,3},{4,68},{68... | collective-permute-start | bytes 1966088 | tf_op jit(solution)/shard_map/ppermute | solution.py:39
  62.8 12.6 %collective-permute-start.13 = (bf16[2048,128]{1,0:T(8,128)(2,1)}, bf16[2048,128]{1,0:T(8,128)(2,1)S(1)}, u32[]{:S(2)}, u32[]{:S(2)}) collective-permute-start(bf16[2048,128]{1,0:T(8,128)(2,1)} %refs_0_.1), channel_id=1, source_target_pairs={{0,48},{16,0},{32,16},{48,32},{1,49},{17,1},{33,17},{49,33},{2,50}... | collective-permute-start | bytes 1572872 | tf_op jit(solution)/shard_map/ppermute | solution.py:35
  63.9 13.7 %collective-permute-start.14 = (bf16[2048,128]{1,0:T(8,128)(2,1)}, bf16[2048,128]{1,0:T(8,128)(2,1)S(1)}, u32[]{:S(2)}, u32[]{:S(2)}) collective-permute-start(bf16[2048,128]{1,0:T(8,128)(2,1)} %refs_0_.1), channel_id=1, source_target_pairs={{0,16},{16,32},{32,48},{48,0},{1,17},{17,33},{33,49},{49,1},{2,18}... | collective-permute-start | bytes 1572872 | tf_op jit(solution)/shard_map/ppermute | solution.py:35
  64.2 14.1 %collective-permute-start.15 = (bf16[2048,128]{1,0:T(8,128)(2,1)}, bf16[2048,128]{1,0:T(8,128)(2,1)}, u32[]{:S(2)}, u32[]{:S(2)}) collective-permute-start(bf16[2048,128]{1,0:T(8,128)(2,1)} %refs_0_.1), channel_id=1, source_target_pairs={{0,64},{64,0},{1,65},{65,1},{2,66},{66,2},{3,67},{67,3},{4,68},{68... | collective-permute-start | bytes 1572872 | tf_op jit(solution)/shard_map/ppermute | solution.py:39
  73.2 30.4 %copy-start.1 = (bf16[1024,128]{1,0:T(8,128)(2,1)}, bf16[1024,128]{1,0:T(8,128)(2,1)S(1)}, u32[]{:S(2)}) copy-start(bf16[1024,128]{1,0:T(8,128)(2,1)S(1)} %get-tuple-element.53.refs_0_) | copy-start | bytes 786436
  73.3 8.5 %collective-permute-start.16 = (bf16[512,256]{1,0:T(8,128)(2,1)S(1)}, bf16[512,256]{1,0:T(8,128)(2,1)S(1)}, u32[]{:S(2)}, u32[]{:S(2)}) collective-permute-start(bf16[512,256]{1,0:T(8,128)(2,1)S(1)} %get-tuple-element.56.refs_3_.refs_5_), channel_id=1, source_target_pairs={{0,64},{64,0},{1,65},{65,1},{2,66},{66,2},{3,67},{67,3},{4,68},{68... | collective-permute-start | bytes 786440 | tf_op jit(solution)/shard_map/ppermute | solution.py:39
  73.6 11.4 %collective-permute-start.17 = (bf16[1024,128]{1,0:T(8,128)(2,1)S(1)}, bf16[1024,128]{1,0:T(8,128)(2,1)S(1)}, u32[]{:S(2)}, u32[]{:S(2)}) collective-permute-start(bf16[1024,128]{1,0:T(8,128)(2,1)S(1)} %get-tuple-element.53.refs_0_), channel_id=1, source_target_pairs={{0,16},{16,32},{32,48},{48,0},{1,17},{17,33},{33,49},{49,1},{2,18}... | collective-permute-start | bytes 786440 | tf_op jit(solution)/shard_map/ppermute | solution.py:35
  75.3 11.7 %collective-permute-start.18 = (bf16[1024,128]{1,0:T(8,128)(2,1)S(1)}, bf16[1024,128]{1,0:T(8,128)(2,1)S(1)}, u32[]{:S(2)}, u32[]{:S(2)}) collective-permute-start(bf16[1024,128]{1,0:T(8,128)(2,1)S(1)} %get-tuple-element.53.refs_0_), channel_id=1, source_target_pairs={{0,32},{16,48},{32,0},{48,16},{1,33},{17,49},{33,1},{49,17},{2,34}... | collective-permute-start | bytes 786440 | tf_op jit(solution)/shard_map/ppermute | solution.py:35
  77.6 11.8 %collective-permute-start.19 = (bf16[1024,128]{1,0:T(8,128)(2,1)S(1)}, bf16[1024,128]{1,0:T(8,128)(2,1)}, u32[]{:S(2)}, u32[]{:S(2)}) collective-permute-start(bf16[1024,128]{1,0:T(8,128)(2,1)S(1)} %get-tuple-element.53.refs_0_), channel_id=1, source_target_pairs={{0,48},{16,0},{32,16},{48,32},{1,49},{17,1},{33,17},{49,33},{2,50}... | collective-permute-start | bytes 786440 | tf_op jit(solution)/shard_map/ppermute | solution.py:35
  78.3 25.4 %collective-permute-start.22 = (bf16[2048,128]{1,0:T(8,128)(2,1)S(1)}, bf16[2048,128]{1,0:T(8,128)(2,1)S(1)}, u32[]{:S(2)}, u32[]{:S(2)}) collective-permute-start(bf16[2048,128]{1,0:T(8,128)(2,1)S(1)} %collective-permute-done.13.refs_2_), channel_id=1, source_target_pairs={{0,64},{64,0},{1,65},{65,1},{2,66},{66,2},{3,67},{67,3},{4,68},{68... | collective-permute-start | bytes 1572872 | tf_op jit(solution)/shard_map/ppermute | solution.py:39
  81.8 22.5 %collective-permute-start.23 = (bf16[2048,128]{1,0:T(8,128)(2,1)S(1)}, bf16[2048,128]{1,0:T(8,128)(2,1)S(1)}, u32[]{:S(2)}, u32[]{:S(2)}) collective-permute-start(bf16[2048,128]{1,0:T(8,128)(2,1)S(1)} %collective-permute-done.14.refs_4_), channel_id=1, source_target_pairs={{0,64},{64,0},{1,65},{65,1},{2,66},{66,2},{3,67},{67,3},{4,68},{68... | collective-permute-start | bytes 1572872 | tf_op jit(solution)/shard_map/ppermute | solution.py:39
  85.0 18.6 %collective-permute-start.20 = (bf16[1024,128]{1,0:T(8,128)(2,1)S(1)}, bf16[1024,128]{1,0:T(8,128)(2,1)S(1)}, u32[]{:S(2)}, u32[]{:S(2)}) collective-permute-start(bf16[1024,128]{1,0:T(8,128)(2,1)S(1)} %slice.6), channel_id=1, source_target_pairs={{0,16},{16,32},{32,48},{48,0},{1,17},{17,33},{33,49},{49,1},{2,18}... | collective-permute-start | bytes 786440 | tf_op jit(solution)/shard_map/ppermute | solution.py:35
  87.1 16.6 %collective-permute-start.21 = (bf16[1024,128]{1,0:T(8,128)(2,1)S(1)}, bf16[1024,128]{1,0:T(8,128)(2,1)S(1)}, u32[]{:S(2)}, u32[]{:S(2)}) collective-permute-start(bf16[1024,128]{1,0:T(8,128)(2,1)S(1)} %slice.7), channel_id=1, source_target_pairs={{0,48},{16,0},{32,16},{48,32},{1,49},{17,1},{33,17},{49,33},{2,50}... | collective-permute-start | bytes 786440 | tf_op jit(solution)/shard_map/ppermute | solution.py:35
  104.2 13.6 %collective-permute-start.24 = (bf16[144,1024]{1,0:T(8,128)(2,1)S(1)}, bf16[144,1024]{1,0:T(8,128)(2,1)S(1)}, u32[]{:S(2)}, u32[]{:S(2)}) collective-permute-start(bf16[144,1024]{1,0:T(8,128)(2,1)S(1)} %get-tuple-element.65), channel_id=1, source_target_pairs={{0,48},{16,0},{32,16},{48,32},{1,49},{17,1},{33,17},{49,33},{2,50}... | collective-permute-start | bytes 884744 | tf_op jit(solution)/shard_map/ppermute | solution.py:35
  106.8 11.0 %collective-permute-start.25 = (bf16[144,1024]{1,0:T(8,128)(2,1)S(1)}, bf16[144,1024]{1,0:T(8,128)(2,1)S(1)}, u32[]{:S(2)}, u32[]{:S(2)}) collective-permute-start(bf16[144,1024]{1,0:T(8,128)(2,1)S(1)} %get-tuple-element.66), channel_id=1, source_target_pairs={{0,32},{16,48},{32,0},{48,16},{1,33},{17,49},{33,1},{49,17},{2,34}... | collective-permute-start | bytes 884744 | tf_op jit(solution)/shard_map/ppermute | solution.py:35
  106.8 16.1 %collective-permute-start.26 = (bf16[144,1024]{1,0:T(8,128)(2,1)S(1)}, bf16[144,1024]{1,0:T(8,128)(2,1)S(1)}, u32[]{:S(2)}, u32[]{:S(2)}) collective-permute-start(bf16[144,1024]{1,0:T(8,128)(2,1)S(1)} %get-tuple-element.67), channel_id=1, source_target_pairs={{0,16},{16,32},{32,48},{48,0},{1,17},{17,33},{33,49},{49,1},{2,18}... | collective-permute-start | bytes 884744 | tf_op jit(solution)/shard_map/ppermute | solution.py:35
  107.4 8.8 %collective-permute-start.27 = (bf16[1024,128]{1,0:T(8,128)(2,1)S(1)}, bf16[1024,128]{1,0:T(8,128)(2,1)S(1)}, u32[]{:S(2)}, u32[]{:S(2)}) collective-permute-start(bf16[1024,128]{1,0:T(8,128)(2,1)S(1)} %collective-permute-done.20.refs_6_), channel_id=1, source_target_pairs={{0,64},{64,0},{1,65},{65,1},{2,66},{66,2},{3,67},{67,3},{4,68},{68... | collective-permute-start | bytes 786440 | tf_op jit(solution)/shard_map/ppermute | solution.py:39
  108.6 9.3 %collective-permute-start.28 = (bf16[1024,128]{1,0:T(8,128)(2,1)S(1)}, bf16[1024,128]{1,0:T(8,128)(2,1)S(1)}, u32[]{:S(2)}, u32[]{:S(2)}) collective-permute-start(bf16[1024,128]{1,0:T(8,128)(2,1)S(1)} %collective-permute-done.21.refs_7_), channel_id=1, source_target_pairs={{0,64},{64,0},{1,65},{65,1},{2,66},{66,2},{3,67},{67,3},{4,68},{68... | collective-permute-start | bytes 786440 | tf_op jit(solution)/shard_map/ppermute | solution.py:39
  123.3 2.3 %collective-permute-start.29 = (bf16[1024,128]{1,0:T(8,128)(2,1)S(1)}, bf16[1024,128]{1,0:T(8,128)(2,1)S(1)}, u32[]{:S(2)}, u32[]{:S(2)}) collective-permute-start(bf16[1024,128]{1,0:T(8,128)(2,1)S(1)} %combine.1.own), channel_id=1, source_target_pairs={{0,8},{8,0},{1,9},{9,1},{2,10},{10,2},{3,11},{11,3},{4,12},{12,4},... | collective-permute-start | bytes 786440 | tf_op jit(solution)/shard_map/ppermute | solution.py:47
  151.8 2.8 %collective-permute-start.30 = (bf16[256,128]{1,0:T(8,128)(2,1)S(1)}, bf16[256,128]{1,0:T(8,128)(2,1)S(1)}, u32[]{:S(2)}, u32[]{:S(2)}) collective-permute-start(bf16[256,128]{1,0:T(8,128)(2,1)S(1)} %get-tuple-element.84), channel_id=1, source_target_pairs={{0,8},{8,0},{1,9},{9,1},{2,10},{10,2},{3,11},{11,3},{4,12},{12,4},... | collective-permute-start | bytes 196616 | tf_op jit(solution)/shard_map/ppermute | solution.py:47
  (23 other events, 273.0 us)

commit v14 on v12

--- a/solution.py
+++ b/solution.py
@@ -388,9 +388,9 @@
     core = idx[8]
     copies = []
     for k, slot in enumerate((0, 1, 2, 3, 6, 7)):
-        copies.append(pltpu.make_async_copy(blocks[k], held.at[slot], sem.at[k]))
+        copies.append(pltpu.make_async_copy(blocks[k], held.at[idx[slot]], sem.at[k]))
     for k in range(6, 10):
-        target = held.at[4 + (k - 6) // 2, pl.ds((k % 2) * 1024, 1024)]
+        target = held.at[idx[4 + (k - 6) // 2], pl.ds((k % 2) * 1024, 1024)]
         copies.append(pltpu.make_async_copy(blocks[k], target, sem.at[k]))
     for c in copies:
         c.start()
@@ -405,13 +405,13 @@
                 value = jnp.where(wanted[1] == e, second, 0.0)
                 value = jnp.where(wanted[0] == e, first, value).astype(BF16)
                 padded[rows, pl.ds(pl.multiple_of((head * E + e) * H, H), H)] = value
-    for k, arrived in ((0, copies[0:2]), (2, copies[2:4]), (6, copies[4:6]), (4, copies[6:])):
-        for c in arrived:
-            c.wait()
+    for c in copies:
+        c.wait()
+    for k in range(0, 8, 2):
         w = jnp.concatenate([held[k], held[k + 1]], axis=1)
         value = jnp.dot(padded[...], w, preferred_element_type=F32)
         for s in range(2):
-            out[idx[k + s]] = value[:, s * H : (s + 1) * H].astype(BF16)
+            out[k + s] = value[:, s * H : (s + 1) * H].astype(BF16)
 
 
 def project_out(idx, routes, own, other, blocks):

time: 157 us -> 160 us (1.019)
  Pallas kernels: 39.7 us -> 30.1 us
  starting transfers between devices: 41 us -> 48.3 us
  waiting for transfers between devices: 24.7 us -> 28.9 us
    pallas_call x3, Pallas kernels: 23.2 us -> 15.3 us  [attend(): pl.pallas_call(functools.partial(attend_kernel, count), out_shape=tuple((...]
    ppermute x15, starting transfers between devices: 16.5 us -> 20.4 us  [along_y(): return lax.ppermute(x, 'y', [(i, (i + k) % 4) for i in range(4)])]
    ppermute x6, starting transfers between devices: 14.4 us -> 17.8 us  [across_core(): return lax.ppermute(x, 'c', [(0, 1), (1, 0)])]
    ppermute x15, waiting for transfers between devices: 19.8 us -> 22.4 us  [along_y(): return lax.ppermute(x, 'y', [(i, (i + k) % 4) for i in range(4)])]
    ppermute x9, waiting for transfers between devices: 2.28 us -> 4 us  [across_x(): return lax.ppermute(x, 'xl', [(0, 1), (1, 0)])]
    pallas_call x1, Pallas kernels: 7.42 us -> 5.72 us  [project_out(): pl.pallas_call(out_kernel, out_shape=jax.ShapeDtypeStruct((8, 512, H), BF...]
  transfers between devices with their start and end apart: 31 -> 31, of which waited for: 10 -> 13; matrix products, arithmetic and copies ran while one was open for 2% -> 2% of each run, Pallas kernels for 20% -> 15%
where the time goes in v14:
time: 160 us; the launch traced here: 158 us
  starting transfers between devices  48.3 us (30%)
  blocking collectives  44.2 us (28%)
  Pallas kernels  30.1 us (19%)
  waiting for transfers between devices  28.9 us (18%)
  local copies, waits for them, and re-layouts  3.82 us (2%)
  other arithmetic  1.9 us (1%)
    all_gather x2, blocking collectives, on_device(): blocks = [lax.all_gather(v, 'z', axis=0) for v in (tokens, half_row)]  23.6 us
    ppermute x15, waiting for transfers between devices, along_y(): return lax.ppermute(x, 'y', [(i, (i + k) % 4) for i in range(4)])  22.4 us
    all_to_all x1, blocking collectives, on_device(): sums = lax.all_to_all(sums, NARROW, 0, 0, tiled=True)  20.6 us
    ppermute x15, starting transfers between devices, along_y(): return lax.ppermute(x, 'y', [(i, (i + k) % 4) for i in range(4)])  20.4 us
    ppermute x6, starting transfers between devices, across_core(): return lax.ppermute(x, 'c', [(0, 1), (1, 0)])  17.8 us
    pallas_call x3, Pallas kernels, attend(): pl.pallas_call(functools.partial(attend_kernel, count), out_shape=tuple((...  15.3 us
    ppermute x9, starting transfers between devices, across_x(): return lax.ppermute(x, 'xl', [(0, 1), (1, 0)])  8.27 us
    pallas_call x1, Pallas kernels, project(): pl.pallas_call(project_kernel, out_shape=(jax.ShapeDtypeStruct((1024, H),...  7.39 us
  transfers between devices with their start and end apart: 31, of which 13 were waited for; matrix products, arithmetic and copies ran while one was open for 2% of the time, Pallas kernels for 15%

profile of v14, /device:TPU:3, one launch (start us, length us, event | category | flops | bytes accessed | tf_op | source)
XLA Modules:
  0.0 157.7 jit_solution(3992913819100926559)
XLA Ops:
  0.0 1.8 %collective-permute-start.5 = (bf16[256,256]{1,0:T(8,128)(2,1)}, bf16[256,256]{1,0:T(8,128)(2,1)S(1)}, u32[]{:S(2)}, u32[]{:S(2)}) collective-permute-start(bf16[256,256]{1,0:T(8,128)(2,1)} %param.10), channel_id=1, source_target_pairs={{0,1},{1,0},{2,3},{3,2},{4,5},{5,4},{6,7},{7,6},{8,9},{9,8},{10,11... | collective-permute-start | bytes 393224 | tf_op jit(solution)/shard_map/ppermute | solution.py:43
  1.9 1.2 dynamic-slice_bitcast_fusion
  5.5 1.2 collective-permute-start.7
  7.7 2.9 %collective-permute-start.1 = (bf16[2,1280,128]{2,1,0:T(8,128)(2,1)}, bf16[2,1280,128]{2,1,0:T(8,128)(2,1)}, u32[]{:S(2)}, u32[]{:S(2)}) collective-permute-start(bf16[2,1280,128]{2,1,0:T(8,128)(2,1)} %pad_maximum_fusion.1.refs_0_), channel_id=1, source_target_pairs={{0,32},{16,48},{32,0},{48,16},{1,33},{17,49},{33,1},{49,17},{2,34}... | collective-permute-start | bytes 1966088 | tf_op jit(solution)/shard_map/ppermute | solution.py:35
  12.4 12.5 %all-gather = bf16[1024,256]{1,0:T(8,128)(2,1)S(1)} all-gather(bf16[256,256]{1,0:T(8,128)(2,1)S(1)} %copy-done.8), channel_id=2, replica_groups=mesh['xl'=2,'y'=4,'c'=2,'z'=4,'xh'=2] {'z'}, dimensions={0}, use_global_device_ids=true | all-gather | bytes 655360 | tf_op jit(solution)/shard_map/all_gather | solution.py:475
  25.2 11.1 %all-gather.1 = bf16[1024,256]{1,0:T(8,128)(2,1)S(1)} all-gather(bf16[256,256]{1,0:T(8,128)(2,1)S(1)} %collective-permute-done.5), channel_id=3, replica_groups=mesh['xl'=2,'y'=4,'c'=2,'z'=4,'xh'=2] {'z'}, dimensions={0}, use_global_device_ids=true | all-gather | bytes 655360 | tf_op jit(solution)/shard_map/all_gather | solution.py:475
  36.3 1.3 normalise.1.own
  37.7 1.9 %collective-permute-done.2.refs_2_ = bf16[2,1280,128]{2,1,0:T(8,128)(2,1)} collective-permute-done((bf16[2,1280,128]{2,1,0:T(8,128)(2,1)}, bf16[2,1280,128]{2,1,0:T(8,128)(2,1)}, u32[]{:S(2)}, u32[]{:S(2)}) %collective-permute-start.2) | collective-permute-done | bytes 655392 | tf_op jit(solution)/shard_map/ppermute | solution.py:35
  40.2 3.1 %collective-permute-start.9 = (bf16[256,2048]{1,0:T(8,128)(2,1)S(1)}, bf16[256,2048]{1,0:T(8,128)(2,1)}, u32[]{:S(2)}, u32[]{:S(2)}) collective-permute-start(bf16[256,2048]{1,0:T(8,128)(2,1)S(1)} %normalise.1.own), channel_id=1, source_target_pairs={{0,8},{8,0},{1,9},{9,1},{2,10},{10,2},{3,11},{11,3},{4,12},{12,4},... | collective-permute-start | bytes 3145736 | tf_op jit(solution)/shard_map/ppermute | solution.py:47
  43.3 2.0 %collective-permute-start.10 = (bf16[2,1280,128]{2,1,0:T(8,128)(2,1)}, bf16[2,1280,128]{2,1,0:T(8,128)(2,1)S(1)}, u32[]{:S(2)}, u32[]{:S(2)}) collective-permute-start(bf16[2,1280,128]{2,1,0:T(8,128)(2,1)} %collective-permute-done.4.refs_1_), channel_id=1, source_target_pairs={{0,48},{16,0},{32,16},{48,32},{1,49},{17,1},{33,17},{49,33},{2,50}... | collective-permute-start | bytes 1966088 | tf_op jit(solution)/shard_map/ppermute | solution.py:35
  45.3 1.2 collective-permute-start.12
  46.5 13.4 %collective-permute-done.10.refs_3_ = bf16[2,1280,128]{2,1,0:T(8,128)(2,1)S(1)} collective-permute-done((bf16[2,1280,128]{2,1,0:T(8,128)(2,1)}, bf16[2,1280,128]{2,1,0:T(8,128)(2,1)S(1)}, u32[]{:S(2)}, u32[]{:S(2)}) %collective-permute-start.10) | collective-permute-done | bytes 655392 | tf_op jit(solution)/shard_map/ppermute | solution.py:35
  60.8 2.0 %collective-permute-done.11.refs_7_ = bf16[2,1280,128]{2,1,0:T(8,128)(2,1)} collective-permute-done((bf16[2,1280,128]{2,1,0:T(8,128)(2,1)}, bf16[2,1280,128]{2,1,0:T(8,128)(2,1)}, u32[]{:S(2)}, u32[]{:S(2)}) %collective-permute-start.11) | collective-permute-done | bytes 655392 | tf_op jit(solution)/shard_map/ppermute | solution.py:35
  64.2 1.2 collective-permute-start.14
  65.4 7.4 %project.1 = (bf16[1024,128]{1,0:T(8,128)(2,1)S(1)}, bf16[512,256]{1,0:T(8,128)(2,1)S(1)}, f32[512,2]{1,0:T(8,128)S(1)}) custom-call(s32[9]{0:T(128)S(1)} %stack.162.idx, s32[512,2]{1,0:T(8,128)S(1)} %broadcast_select_fusion.routes, bf16[8,2048]{1,0:T(8,128)(2,1)S(1)} %bitcast.47, bf16[256,2048]{1,0:T(8,128)(2,1)} %copy-done, ...), custom_call_target="tpu_custom_call" | custom-call | flops 6442450944 | bytes 8388608 | tf_op jit(solution)/shard_map/project/pallas_call | solution.py:164
  75.3 1.2 collective-permute-start.18
  78.1 1.4 collective-permute-start.23
  79.5 2.3 %collective-permute-done.17.refs_4_.refs_5_ = bf16[512,256]{1,0:T(8,128)(2,1)S(1)} collective-permute-done((bf16[512,256]{1,0:T(8,128)(2,1)S(1)}, bf16[512,256]{1,0:T(8,128)(2,1)S(1)}, u32[]{:S(2)}, u32[]{:S(2)}) %collective-permute-start.17) | collective-permute-done | bytes 262176 | tf_op jit(solution)/shard_map/ppermute | solution.py:39
  83.7 3.9 %attend.3 = bf16[144,1024]{1,0:T(8,128)(2,1)S(1)} custom-call(s32[6]{0:T(128)S(1)} %stack.193.idx, s32[4]{0:T(128)S(1)} %copy-done.4, s32[4]{0:T(128)S(1)} %copy-done.5, bf16[1024,128]{1,0:T(8,128)(2,1)} %copy-done.18, bf16[2,768,256]{2,1,0:T(8,128)(2,1)} %copy-done.6, bf16[2,768,256]{2,1,0:T(8,128)(2,1)} %collective-permute-done.7.refs_2_.refs_3_, ...), custom_call_target="tpu_custom_call" | custom-call | flops 3221225472 | bytes 4194304 | tf_op jit(solution)/shard_map/attend/pallas_call | solution.py:330
  87.6 1.6 collective-permute-done.18.refs_0_
  89.1 4.8 %collective-permute-start.21 = (bf16[1024,128]{1,0:T(8,128)(2,1)S(1)}, bf16[1024,128]{1,0:T(8,128)(2,1)S(1)}, u32[]{:S(2)}, u32[]{:S(2)}) collective-permute-start(bf16[1024,128]{1,0:T(8,128)(2,1)S(1)} %slice.6), channel_id=1, source_target_pairs={{0,16},{16,32},{32,48},{48,0},{1,17},{17,33},{33,49},{49,1},{2,18}... | collective-permute-start | bytes 786440 | tf_op jit(solution)/shard_map/ppermute | solution.py:35
  93.9 1.9 %collective-permute-start.20 = (bf16[144,1024]{1,0:T(8,128)(2,1)S(1)}, bf16[144,1024]{1,0:T(8,128)(2,1)S(1)}, u32[]{:S(2)}, u32[]{:S(2)}) collective-permute-start(bf16[144,1024]{1,0:T(8,128)(2,1)S(1)} %attend.3), channel_id=1, source_target_pairs={{0,32},{16,48},{32,0},{48,16},{1,33},{17,49},{33,1},{49,17},{2,34}... | collective-permute-start | bytes 884744 | tf_op jit(solution)/shard_map/ppermute | solution.py:35
  95.8 6.7 %attend.5 = (bf16[144,1024]{1,0:T(8,128)(2,1)S(1)}, bf16[144,1024]{1,0:T(8,128)(2,1)S(1)}) custom-call(s32[7]{0:T(128)S(1)} %stack.196.idx, s32[4]{0:T(128)S(1)} %copy-done.4, s32[4]{0:T(128)S(1)} %copy-done.5, bf16[1024,128]{1,0:T(8,128)(2,1)} %copy-done.21, bf16[1024,128]{1,0:T(8,128)(2,1)} %copy-done.23, bf16[2,768,256]{2,1,0:T(8,128)(2,1)} %copy-done.6, ...), custom_call_target="tpu_custom_call" | custom-call | flops 6442450944 | bytes 4194304 | tf_op jit(solution)/shard_map/attend/pallas_call | solution.py:330
  103.5 2.3 %collective-permute-start.25 = (bf16[144,1024]{1,0:T(8,128)(2,1)S(1)}, bf16[144,1024]{1,0:T(8,128)(2,1)S(1)}, u32[]{:S(2)}, u32[]{:S(2)}) collective-permute-start(bf16[144,1024]{1,0:T(8,128)(2,1)S(1)} %get-tuple-element.71), channel_id=1, source_target_pairs={{0,48},{16,0},{32,16},{48,32},{1,49},{17,1},{33,17},{49,33},{2,50}... | collective-permute-start | bytes 884744 | tf_op jit(solution)/shard_map/ppermute | solution.py:35
  107.0 1.4 collective-permute-start.28
  108.4 4.8 %attend.4.p0 = bf16[144,1024]{1,0:T(8,128)(2,1)S(1)} custom-call(s32[6]{0:T(128)S(1)} %stack.191.idx, s32[4]{0:T(128)S(1)} %copy-done.4, s32[4]{0:T(128)S(1)} %copy-done.5, bf16[1024,128]{1,0:T(8,128)(2,1)} %copy-done.1, bf16[2,768,256]{2,1,0:T(8,128)(2,1)} %copy-done.6, bf16[2,768,256]{2,1,0:T(8,128)(2,1)} %collective-permute-done.7.refs_2_.refs_3_, ...), custom_call_target="tpu_custom_call" | custom-call | flops 3221225472 | bytes 4194304 | tf_op jit(solution)/shard_map/attend/pallas_call | solution.py:330
  113.2 1.7 %collective-permute-done.28.refs_9_ = bf16[1024,128]{1,0:T(8,128)(2,1)S(1)} collective-permute-done((bf16[1024,128]{1,0:T(8,128)(2,1)S(1)}, bf16[1024,128]{1,0:T(8,128)(2,1)S(1)}, u32[]{:S(2)}, u32[]{:S(2)}) %collective-permute-start.28) | collective-permute-done | bytes 262176 | tf_op jit(solution)/shard_map/ppermute | solution.py:39
  115.3 11.2 %collective-permute-start.29 = (bf16[1024,128]{1,0:T(8,128)(2,1)S(1)}, bf16[1024,128]{1,0:T(8,128)(2,1)S(1)}, u32[]{:S(2)}, u32[]{:S(2)}) collective-permute-start(bf16[1024,128]{1,0:T(8,128)(2,1)S(1)} %combine.1.own), channel_id=1, source_target_pairs={{0,8},{8,0},{1,9},{9,1},{2,10},{10,2},{3,11},{11,3},{4,12},{12,4},... | collective-permute-start | bytes 786440 | tf_op jit(solution)/shard_map/ppermute | solution.py:47
  126.5 1.2 collective-permute-done.29.other
  127.6 5.7 %project_out.1 = bf16[8,512,128]{2,1,0:T(8,128)(2,1)S(1)} custom-call(s32[9]{0:T(128)S(1)} %stack.162.idx, s32[512,2]{1,0:T(8,128)S(1)} %broadcast_select_fusion.routes, bf16[1024,128]{1,0:T(8,128)(2,1)S(1)} %combine.1.own, bf16[1024,128]{1,0:T(8,128)(2,1)S(1)} %collective-permute-done.29.other, bf16[2048,128]{1,0:T(8,128)(2,1)} %refs_0_.1, ...), custom_call_target="tpu_custom_call" | custom-call | flops 4294967296 | bytes 6291456 | tf_op jit(solution)/shard_map/project_out/pallas_call | solution.py:418
  133.4 20.6 %all_to_all.5 = bf16[8,512,128]{2,1,0:T(8,128)(2,1)S(1)} all-to-all(bf16[8,512,128]{2,1,0:T(8,128)(2,1)S(1)} %project_out.1), channel_id=1, replica_groups=mesh['xl'=2,'y'=4,'c'=2,'z'=4,'xh'=2] {'z','xh'}, dimensions={0} | all-to-all | bytes 2097152 | tf_op jit(solution)/shard_map/all_to_all | solution.py:523
  154.2 1.9 %collective-permute-start.30 = (bf16[256,128]{1,0:T(8,128)(2,1)S(1)}, bf16[256,128]{1,0:T(8,128)(2,1)S(1)}, u32[]{:S(2)}, u32[]{:S(2)}) collective-permute-start(bf16[256,128]{1,0:T(8,128)(2,1)S(1)} %get-tuple-element.90), channel_id=1, source_target_pairs={{0,8},{8,0},{1,9},{9,1},{2,10},{10,2},{3,11},{11,3},{4,12},{12,4},... | collective-permute-start | bytes 196616 | tf_op jit(solution)/shard_map/ppermute | solution.py:47
  (114 shorter events, 18.7 us)
Async XLA Ops:
  0.0 12.0 %collective-permute-start.5 = (bf16[256,256]{1,0:T(8,128)(2,1)}, bf16[256,256]{1,0:T(8,128)(2,1)S(1)}, u32[]{:S(2)}, u32[]{:S(2)}) collective-permute-start(bf16[256,256]{1,0:T(8,128)(2,1)} %param.10), channel_id=1, source_target_pairs={{0,1},{1,0},{2,3},{3,2},{4,5},{5,4},{6,7},{7,6},{8,9},{9,8},{10,11... | collective-permute-start | bytes 393224 | tf_op jit(solution)/shard_map/ppermute | solution.py:43
  3.0 2.4 %collective-permute-start.6 = (bf16[768,256]{1,0:T(8,128)(2,1)S(1)}, bf16[768,256]{1,0:T(8,128)(2,1)S(1)}, u32[]{:S(2)}, u32[]{:S(2)}) collective-permute-start(bf16[768,256]{1,0:T(8,128)(2,1)S(1)} %get-tuple-element.86), channel_id=1, source_target_pairs={{0,8},{8,0},{1,9},{9,1},{2,10},{10,2},{3,11},{11,3},{4,12},{12,4},... | collective-permute-start | bytes 1179656 | tf_op jit(solution)/shard_map/ppermute | solution.py:47
  4.2 2.6 %collective-permute-start = (bf16[1280,128]{1,0:T(8,128)(2,1)S(1)}, bf16[1280,128]{1,0:T(8,128)(2,1)S(1)}, u32[]{:S(2)}, u32[]{:S(2)}) collective-permute-start(bf16[1280,128]{1,0:T(8,128)(2,1)S(1)} %pad_maximum_fusion.2), channel_id=1, source_target_pairs={{0,8},{8,0},{1,9},{9,1},{2,10},{10,2},{3,11},{11,3},{4,12},{12,4},... | collective-permute-start | bytes 983048 | tf_op jit(solution)/shard_map/ppermute | solution.py:47
  4.3 7.0 %collective-permute-start.8 = (s32[256,2]{0,1:T(2,128)S(1)}, s32[256,2]{0,1:T(2,128)S(1)}, u32[]{:S(2)}, u32[]{:S(2)}) collective-permute-start(s32[256,2]{0,1:T(2,128)S(1)} %copy-done.13), channel_id=1, source_target_pairs={{0,8},{8,0},{1,9},{9,1},{2,10},{10,2},{3,11},{11,3},{4,12},{12,4},... | collective-permute-start | bytes 6152 | tf_op jit(solution)/shard_map/ppermute | solution.py:47
  5.5 34.7 %collective-permute-start.7 = (bf16[2,768,256]{2,1,0:T(8,128)(2,1)S(1)}, bf16[2,768,256]{2,1,0:T(8,128)(2,1)}, u32[]{:S(2)}, u32[]{:S(2)}) collective-permute-start(bf16[2,768,256]{2,1,0:T(8,128)(2,1)S(1)} %pad_maximum_fusion.refs_1_.refs_2_), channel_id=1, source_target_pairs={{0,64},{64,0},{1,65},{65,1},{2,66},{66,2},{3,67},{67,3},{4,68},{68... | collective-permute-start | bytes 2359304 | tf_op jit(solution)/shard_map/ppermute | solution.py:39
  7.7 30.0 %collective-permute-start.1 = (bf16[2,1280,128]{2,1,0:T(8,128)(2,1)}, bf16[2,1280,128]{2,1,0:T(8,128)(2,1)}, u32[]{:S(2)}, u32[]{:S(2)}) collective-permute-start(bf16[2,1280,128]{2,1,0:T(8,128)(2,1)} %pad_maximum_fusion.1.refs_0_), channel_id=1, source_target_pairs={{0,32},{16,48},{32,0},{48,16},{1,33},{17,49},{33,1},{49,17},{2,34}... | collective-permute-start | bytes 1966088 | tf_op jit(solution)/shard_map/ppermute | solution.py:35
  10.6 29.0 %collective-permute-start.2 = (bf16[2,1280,128]{2,1,0:T(8,128)(2,1)}, bf16[2,1280,128]{2,1,0:T(8,128)(2,1)}, u32[]{:S(2)}, u32[]{:S(2)}) collective-permute-start(bf16[2,1280,128]{2,1,0:T(8,128)(2,1)} %pad_maximum_fusion.1.refs_0_), channel_id=1, source_target_pairs={{0,48},{16,0},{32,16},{48,32},{1,49},{17,1},{33,17},{49,33},{2,50}... | collective-permute-start | bytes 1966088 | tf_op jit(solution)/shard_map/ppermute | solution.py:35
  11.4 28.8 %collective-permute-start.3 = (bf16[2,1280,128]{2,1,0:T(8,128)(2,1)}, bf16[2,1280,128]{2,1,0:T(8,128)(2,1)}, u32[]{:S(2)}, u32[]{:S(2)}) collective-permute-start(bf16[2,1280,128]{2,1,0:T(8,128)(2,1)} %pad_maximum_fusion.1.refs_0_), channel_id=1, source_target_pairs={{0,16},{16,32},{32,48},{48,0},{1,17},{17,33},{33,49},{49,1},{2,18}... | collective-permute-start | bytes 1966088 | tf_op jit(solution)/shard_map/ppermute | solution.py:35
  12.1 28.1 %collective-permute-start.4 = (bf16[2,1280,128]{2,1,0:T(8,128)(2,1)}, bf16[2,1280,128]{2,1,0:T(8,128)(2,1)}, u32[]{:S(2)}, u32[]{:S(2)}) collective-permute-start(bf16[2,1280,128]{2,1,0:T(8,128)(2,1)} %pad_maximum_fusion.1.refs_0_), channel_id=1, source_target_pairs={{0,64},{64,0},{1,65},{65,1},{2,66},{66,2},{3,67},{67,3},{4,68},{68... | collective-permute-start | bytes 1966088 | tf_op jit(solution)/shard_map/ppermute | solution.py:39
  36.3 29.1 %copy-start.3 = (bf16[2048,8]{0,1:T(8,128)(2,1)S(1)}, bf16[2048,8]{0,1:T(8,128)(2,1)}, u32[]{:S(2)}) copy-start(bf16[2048,8]{0,1:T(8,128)(2,1)} %param.12) | copy-start | bytes 98308
  40.2 25.2 %collective-permute-start.9 = (bf16[256,2048]{1,0:T(8,128)(2,1)S(1)}, bf16[256,2048]{1,0:T(8,128)(2,1)}, u32[]{:S(2)}, u32[]{:S(2)}) collective-permute-start(bf16[256,2048]{1,0:T(8,128)(2,1)S(1)} %normalise.1.own), channel_id=1, source_target_pairs={{0,8},{8,0},{1,9},{9,1},{2,10},{10,2},{3,11},{11,3},{4,12},{12,4},... | collective-permute-start | bytes 3145736 | tf_op jit(solution)/shard_map/ppermute | solution.py:47
  43.3 16.6 %collective-permute-start.10 = (bf16[2,1280,128]{2,1,0:T(8,128)(2,1)}, bf16[2,1280,128]{2,1,0:T(8,128)(2,1)S(1)}, u32[]{:S(2)}, u32[]{:S(2)}) collective-permute-start(bf16[2,1280,128]{2,1,0:T(8,128)(2,1)} %collective-permute-done.4.refs_1_), channel_id=1, source_target_pairs={{0,48},{16,0},{32,16},{48,32},{1,49},{17,1},{33,17},{49,33},{2,50}... | collective-permute-start | bytes 1966088 | tf_op jit(solution)/shard_map/ppermute | solution.py:35
  45.3 17.5 %collective-permute-start.11 = (bf16[2,1280,128]{2,1,0:T(8,128)(2,1)}, bf16[2,1280,128]{2,1,0:T(8,128)(2,1)}, u32[]{:S(2)}, u32[]{:S(2)}) collective-permute-start(bf16[2,1280,128]{2,1,0:T(8,128)(2,1)} %collective-permute-done.4.refs_1_), channel_id=1, source_target_pairs={{0,16},{16,32},{32,48},{48,0},{1,17},{17,33},{33,49},{49,1},{2,18}... | collective-permute-start | bytes 1966088 | tf_op jit(solution)/shard_map/ppermute | solution.py:35
  45.3 20.1 %collective-permute-start.12 = (bf16[2,1280,128]{2,1,0:T(8,128)(2,1)}, bf16[2,1280,128]{2,1,0:T(8,128)(2,1)}, u32[]{:S(2)}, u32[]{:S(2)}) collective-permute-start(bf16[2,1280,128]{2,1,0:T(8,128)(2,1)} %collective-permute-done.1.refs_4_), channel_id=1, source_target_pairs={{0,64},{64,0},{1,65},{65,1},{2,66},{66,2},{3,67},{67,3},{4,68},{68... | collective-permute-start | bytes 1966088 | tf_op jit(solution)/shard_map/ppermute | solution.py:39
  62.8 12.6 %collective-permute-start.15 = (bf16[2048,128]{1,0:T(8,128)(2,1)}, bf16[2048,128]{1,0:T(8,128)(2,1)S(1)}, u32[]{:S(2)}, u32[]{:S(2)}) collective-permute-start(bf16[2048,128]{1,0:T(8,128)(2,1)} %refs_0_.1), channel_id=1, source_target_pairs={{0,48},{16,0},{32,16},{48,32},{1,49},{17,1},{33,17},{49,33},{2,50}... | collective-permute-start | bytes 1572872 | tf_op jit(solution)/shard_map/ppermute | solution.py:35
  63.9 13.7 %collective-permute-start.16 = (bf16[2048,128]{1,0:T(8,128)(2,1)}, bf16[2048,128]{1,0:T(8,128)(2,1)S(1)}, u32[]{:S(2)}, u32[]{:S(2)}) collective-permute-start(bf16[2048,128]{1,0:T(8,128)(2,1)} %refs_0_.1), channel_id=1, source_target_pairs={{0,16},{16,32},{32,48},{48,0},{1,17},{17,33},{33,49},{49,1},{2,18}... | collective-permute-start | bytes 1572872 | tf_op jit(solution)/shard_map/ppermute | solution.py:35
  64.2 13.8 %collective-permute-start.14 = (bf16[2048,128]{1,0:T(8,128)(2,1)}, bf16[2048,128]{1,0:T(8,128)(2,1)}, u32[]{:S(2)}, u32[]{:S(2)}) collective-permute-start(bf16[2048,128]{1,0:T(8,128)(2,1)} %refs_0_.1), channel_id=1, source_target_pairs={{0,64},{64,0},{1,65},{65,1},{2,66},{66,2},{3,67},{67,3},{4,68},{68... | collective-permute-start | bytes 1572872 | tf_op jit(solution)/shard_map/ppermute | solution.py:39
  72.9 8.9 %collective-permute-start.17 = (bf16[512,256]{1,0:T(8,128)(2,1)S(1)}, bf16[512,256]{1,0:T(8,128)(2,1)S(1)}, u32[]{:S(2)}, u32[]{:S(2)}) collective-permute-start(bf16[512,256]{1,0:T(8,128)(2,1)S(1)} %get-tuple-element.57.refs_3_.refs_4_), channel_id=1, source_target_pairs={{0,64},{64,0},{1,65},{65,1},{2,66},{66,2},{3,67},{67,3},{4,68},{68... | collective-permute-start | bytes 786440 | tf_op jit(solution)/shard_map/ppermute | solution.py:39
  73.3 9.7 %collective-permute-start.13 = (bf16[1024,128]{1,0:T(8,128)(2,1)S(1)}, bf16[1024,128]{1,0:T(8,128)(2,1)S(1)}, u32[]{:S(2)}, u32[]{:S(2)}) collective-permute-start(bf16[1024,128]{1,0:T(8,128)(2,1)S(1)} %get-tuple-element.64.refs_0_), channel_id=1, source_target_pairs={{0,32},{16,48},{32,0},{48,16},{1,33},{17,49},{33,1},{49,17},{2,34}... | collective-permute-start | bytes 786440 | tf_op jit(solution)/shard_map/ppermute | solution.py:35
  75.3 13.8 %collective-permute-start.18 = (bf16[1024,128]{1,0:T(8,128)(2,1)S(1)}, bf16[1024,128]{1,0:T(8,128)(2,1)S(1)}, u32[]{:S(2)}, u32[]{:S(2)}) collective-permute-start(bf16[1024,128]{1,0:T(8,128)(2,1)S(1)} %get-tuple-element.64.refs_0_), channel_id=1, source_target_pairs={{0,16},{16,32},{32,48},{48,0},{1,17},{17,33},{33,49},{49,1},{2,18}... | collective-permute-start | bytes 786440 | tf_op jit(solution)/shard_map/ppermute | solution.py:35
  77.6 11.6 %collective-permute-start.19 = (bf16[1024,128]{1,0:T(8,128)(2,1)S(1)}, bf16[1024,128]{1,0:T(8,128)(2,1)S(1)}, u32[]{:S(2)}, u32[]{:S(2)}) collective-permute-start(bf16[1024,128]{1,0:T(8,128)(2,1)S(1)} %get-tuple-element.64.refs_0_), channel_id=1, source_target_pairs={{0,48},{16,0},{32,16},{48,32},{1,49},{17,1},{33,17},{49,33},{2,50}... | collective-permute-start | bytes 786440 | tf_op jit(solution)/shard_map/ppermute | solution.py:35
  78.1 25.4 %collective-permute-start.23 = (bf16[2048,128]{1,0:T(8,128)(2,1)S(1)}, bf16[2048,128]{1,0:T(8,128)(2,1)S(1)}, u32[]{:S(2)}, u32[]{:S(2)}) collective-permute-start(bf16[2048,128]{1,0:T(8,128)(2,1)S(1)} %collective-permute-done.15.refs_2_), channel_id=1, source_target_pairs={{0,64},{64,0},{1,65},{65,1},{2,66},{66,2},{3,67},{67,3},{4,68},{68... | collective-permute-start | bytes 1572872 | tf_op jit(solution)/shard_map/ppermute | solution.py:39
  81.8 21.8 %collective-permute-start.24 = (bf16[2048,128]{1,0:T(8,128)(2,1)S(1)}, bf16[2048,128]{1,0:T(8,128)(2,1)S(1)}, u32[]{:S(2)}, u32[]{:S(2)}) collective-permute-start(bf16[2048,128]{1,0:T(8,128)(2,1)S(1)} %collective-permute-done.16.refs_4_), channel_id=1, source_target_pairs={{0,64},{64,0},{1,65},{65,1},{2,66},{66,2},{3,67},{67,3},{4,68},{68... | collective-permute-start | bytes 1572872 | tf_op jit(solution)/shard_map/ppermute | solution.py:39
  89.1 14.3 %collective-permute-start.21 = (bf16[1024,128]{1,0:T(8,128)(2,1)S(1)}, bf16[1024,128]{1,0:T(8,128)(2,1)S(1)}, u32[]{:S(2)}, u32[]{:S(2)}) collective-permute-start(bf16[1024,128]{1,0:T(8,128)(2,1)S(1)} %slice.6), channel_id=1, source_target_pairs={{0,16},{16,32},{32,48},{48,0},{1,17},{17,33},{33,49},{49,1},{2,18}... | collective-permute-start | bytes 786440 | tf_op jit(solution)/shard_map/ppermute | solution.py:35
  93.9 9.5 %collective-permute-start.22 = (bf16[1024,128]{1,0:T(8,128)(2,1)S(1)}, bf16[1024,128]{1,0:T(8,128)(2,1)S(1)}, u32[]{:S(2)}, u32[]{:S(2)}) collective-permute-start(bf16[1024,128]{1,0:T(8,128)(2,1)S(1)} %slice.7), channel_id=1, source_target_pairs={{0,48},{16,0},{32,16},{48,32},{1,49},{17,1},{33,17},{49,33},{2,50}... | collective-permute-start | bytes 786440 | tf_op jit(solution)/shard_map/ppermute | solution.py:35
  93.9 9.5 %collective-permute-start.20 = (bf16[144,1024]{1,0:T(8,128)(2,1)S(1)}, bf16[144,1024]{1,0:T(8,128)(2,1)S(1)}, u32[]{:S(2)}, u32[]{:S(2)}) collective-permute-start(bf16[144,1024]{1,0:T(8,128)(2,1)S(1)} %attend.3), channel_id=1, source_target_pairs={{0,32},{16,48},{32,0},{48,16},{1,33},{17,49},{33,1},{49,17},{2,34}... | collective-permute-start | bytes 884744 | tf_op jit(solution)/shard_map/ppermute | solution.py:35
  103.5 11.4 %collective-permute-start.25 = (bf16[144,1024]{1,0:T(8,128)(2,1)S(1)}, bf16[144,1024]{1,0:T(8,128)(2,1)S(1)}, u32[]{:S(2)}, u32[]{:S(2)}) collective-permute-start(bf16[144,1024]{1,0:T(8,128)(2,1)S(1)} %get-tuple-element.71), channel_id=1, source_target_pairs={{0,48},{16,0},{32,16},{48,32},{1,49},{17,1},{33,17},{49,33},{2,50}... | collective-permute-start | bytes 884744 | tf_op jit(solution)/shard_map/ppermute | solution.py:35
  105.8 9.1 %collective-permute-start.26 = (bf16[144,1024]{1,0:T(8,128)(2,1)S(1)}, bf16[144,1024]{1,0:T(8,128)(2,1)S(1)}, u32[]{:S(2)}, u32[]{:S(2)}) collective-permute-start(bf16[144,1024]{1,0:T(8,128)(2,1)S(1)} %get-tuple-element.73), channel_id=1, source_target_pairs={{0,16},{16,32},{32,48},{48,0},{1,17},{17,33},{33,49},{49,1},{2,18}... | collective-permute-start | bytes 884744 | tf_op jit(solution)/shard_map/ppermute | solution.py:35
  106.9 6.3 %collective-permute-start.27 = (bf16[1024,128]{1,0:T(8,128)(2,1)S(1)}, bf16[1024,128]{1,0:T(8,128)(2,1)S(1)}, u32[]{:S(2)}, u32[]{:S(2)}) collective-permute-start(bf16[1024,128]{1,0:T(8,128)(2,1)S(1)} %collective-permute-done.21.refs_6_), channel_id=1, source_target_pairs={{0,64},{64,0},{1,65},{65,1},{2,66},{66,2},{3,67},{67,3},{4,68},{68... | collective-permute-start | bytes 786440 | tf_op jit(solution)/shard_map/ppermute | solution.py:39
  107.0 7.9 %collective-permute-start.28 = (bf16[1024,128]{1,0:T(8,128)(2,1)S(1)}, bf16[1024,128]{1,0:T(8,128)(2,1)S(1)}, u32[]{:S(2)}, u32[]{:S(2)}) collective-permute-start(bf16[1024,128]{1,0:T(8,128)(2,1)S(1)} %collective-permute-done.22.refs_7_), channel_id=1, source_target_pairs={{0,64},{64,0},{1,65},{65,1},{2,66},{66,2},{3,67},{67,3},{4,68},{68... | collective-permute-start | bytes 786440 | tf_op jit(solution)/shard_map/ppermute | solution.py:39
  115.3 12.4 %collective-permute-start.29 = (bf16[1024,128]{1,0:T(8,128)(2,1)S(1)}, bf16[1024,128]{1,0:T(8,128)(2,1)S(1)}, u32[]{:S(2)}, u32[]{:S(2)}) collective-permute-start(bf16[1024,128]{1,0:T(8,128)(2,1)S(1)} %combine.1.own), channel_id=1, source_target_pairs={{0,8},{8,0},{1,9},{9,1},{2,10},{10,2},{3,11},{11,3},{4,12},{12,4},... | collective-permute-start | bytes 786440 | tf_op jit(solution)/shard_map/ppermute | solution.py:47
  154.2 2.8 %collective-permute-start.30 = (bf16[256,128]{1,0:T(8,128)(2,1)S(1)}, bf16[256,128]{1,0:T(8,128)(2,1)S(1)}, u32[]{:S(2)}, u32[]{:S(2)}) collective-permute-start(bf16[256,128]{1,0:T(8,128)(2,1)S(1)} %get-tuple-element.90), channel_id=1, source_target_pairs={{0,8},{8,0},{1,9},{9,1},{2,10},{10,2},{3,11},{11,3},{4,12},{12,4},... | collective-permute-start | bytes 196616 | tf_op jit(solution)/shard_map/ppermute | solution.py:47
  (24 other events, 214.9 us)
